TPU v7x, 256 devices: a whole 4x4x8 slice. The times are simulated.
256 devices in a mesh: shot: 8 (over y, x_lo), tile: 32 (over x_hi, z, core).
Axes of the slice: x: 4 (x_hi: 2, x_lo: 2; x = x_hi * 2 + x_lo), y: 4, z: 8, core: 2. Of those that a mesh axis runs over, the one named last changes fastest.
Arguments:
- p_now: float32 [8, 4096, 16, 128], P('shot', 'tile'), may hold values from -6 to 6
- p_prev: float32 [8, 4096, 16, 128], P('shot', 'tile'), may hold values from -6 to 6
- adj_now: float32 [8, 4096, 16, 128], P('shot', 'tile'), may hold values from -60 to 60
- adj_next: float32 [8, 4096, 16, 128], P('shot', 'tile'), may hold values from -60 to 60
- coef_old: float32 [2048, 512], P('tile'), may hold values from 0.14 to 0.28
- signs: int32 [8, 2048], P('shot', 'tile'), may hold values from 0 to 1
- elem_index: int32 [2048], P('tile'), may hold values from 0 to 262143
- wavelet: float32 [5], replicated, may hold values from -4 to 4
Outputs:
- direction: float32 [2048, 512], P('tile')
- p_last: float32 [8, 4096, 16, 128], P('shot', 'tile')
All inputs are finite; a program needn't handle non-finite values.
Results may differ from a plain program's by a relative error of at most 0.0003.
Values sent between devices are 32-bit elements; how exact they have to be, the bound alone decides.
No kernel may reach another device: no remote copies, remote signals or barrier semaphores. Data moves between devices by JAX's collectives and lax.ppermute only.
A program may use at most 64 MiB of HBM per device.

v0:
```python
import functools

import jax
import jax.numpy as jnp
import ml_dtypes
import numpy as np
from jax import lax
from jax.experimental import pallas as pl
from jax.experimental.pallas import tpu as pltpu
from jax.sharding import Mesh
from jax.sharding import PartitionSpec as P

CX = 128
CZ = 128
CY = 16
OV = 8
STEPS = 4
ELEMS = 64
CXC = 64
CYC = 8
CZC = 64
ROWS = 72
LEARN = 0.02
EPSILON = 1e-06
BF = jnp.bfloat16
F32 = jnp.float32
SHOT = ("y", "xl")
TILE = ("xh", "z", "core")


def spectral_second(length):
    index = np.arange(length)
    number = np.minimum(index, length - index) * (2.0 * np.pi / length)
    phase = (index[:, None, None] - index[None, :, None]) * index[None, None, :] % length
    return -np.sum(number**2 * np.cos(2.0 * np.pi / length * phase), axis=2) / length


def spline_units(offset):
    mag = np.abs(offset)
    inner = 2.0 / 3.0 - mag**2 + 0.5 * mag**3
    outer = (2.0 - mag) ** 3 / 6.0
    return np.round(384.0 * np.where(mag < 1.0, inner, np.where(mag < 2.0, outer, 0.0)))


def halves(matrix):
    high = matrix.astype(np.float32).astype(ml_dtypes.bfloat16)
    low = (matrix - high.astype(np.float64)).astype(np.float32).astype(ml_dtypes.bfloat16)
    return high, low


@functools.cache
def constants():
    out = {}
    second_x = spectral_second(CX + 2 * OV)[OV : OV + CX]
    ramp = np.sin(0.5 * np.pi * (np.arange(OV) + 0.5) / OV) ** 2
    left = second_x[:, :OV] * ramp[None, :]
    right = second_x[:, OV + CX :] * ramp[None, ::-1]
    high, low = halves(second_x[:, OV : OV + CX])
    out["own_x"] = np.block([[high, high], [low, np.zeros_like(low)]])
    sides = []
    for pair in ((right, left), (left, right)):
        high, low = halves(np.concatenate(pair, axis=1))
        sides.append(np.concatenate([high, high, low], axis=1))
    out["halo_x"] = np.stack(sides)
    high, low = halves(spectral_second(CZ) - 2.0 * np.eye(CZ))
    out["own_z"] = np.block([[high, low], [high, np.zeros_like(low)]])

    fine_z = np.arange(CZ)[:, None]
    coarse_z = np.arange(CZC)[None, :]
    weight_z = sum(
        spline_units((fine_z - 2 * coarse_z + image * CZ - 0.5) * 0.5) for image in range(-2, 3)
    )
    zero = np.zeros_like(weight_z.T)
    pair = np.block([[weight_z.T, zero], [zero, weight_z.T]])
    out["grow_z"] = np.concatenate([pair, pair], axis=0)
    zero = np.zeros_like(weight_z)
    out["shrink_z"] = np.block(
        [[weight_z, zero], [weight_z, zero], [zero, weight_z], [zero, weight_z]]
    )

    def column(coarse):
        return spline_units((np.arange(CX) - 2 * coarse - 0.5) * 0.5)

    own = np.stack([column(j) for j in range(CXC)], axis=1)
    lower = {j: column(j) for j in (-2, -1, 0, 1)}
    upper = {j: column(j) for j in (62, 63, 64, 65)}
    stack = lambda d: np.stack([d[j] for j in sorted(d)], axis=1)
    grow_old, grow_new, shrink = [], [], []
    inner = own.copy()
    inner[:, [0, 1, 62, 63]] = 0.0
    for core in range(2):
        near, far = (upper, lower) if core == 0 else (lower, upper)
        outside = lambda d: np.stack([d[j] for j in sorted(d) if j < 0 or j > 63], axis=1)
        old = np.concatenate([own, outside(near), outside(far), np.zeros((CX, 4))], axis=1)
        new = np.concatenate([inner, stack(near), stack(far)], axis=1)
        every = np.concatenate([own, stack(near), stack(far)], axis=1)
        grow_old.append(np.concatenate([old, old], axis=1))
        grow_new.append(np.concatenate([new, new], axis=1))
        shrink.append(np.concatenate([every.T, every.T], axis=1))
    out["grow_old"] = np.stack(grow_old)
    out["grow_new"] = np.stack(grow_new)
    out["shrink_x"] = np.stack(shrink)
    return {name: np.asarray(value).astype(ml_dtypes.bfloat16) for name, value in out.items()}


def taps():
    return [
        [
            (j, float(w))
            for j in range(CYC)
            for w in [
                sum(
                    spline_units(np.float64((i - 2 * j + image * CY - 0.5) * 0.5))
                    for image in range(-2, 3)
                )
            ]
            if w
        ]
        for i in range(CY)
    ]


def split(value):
    high = value.astype(BF)
    return high, (value - high.astype(F32)).astype(BF)


def dot(left, right):
    return jnp.dot(left, right, preferred_element_type=F32)


def cat(parts, axis):
    return jnp.concatenate(parts, axis=axis)


def interior(v, own_x, own_z, out):
    for j in range(CY // 2):
        one, two = 2 * j, 2 * j + 1
        high1, low1 = split(v[one])
        high2, low2 = split(v[two])
        x = dot(own_x[...], cat([cat([high1, high2], 1), cat([low1, low2], 1)], 0))
        z = dot(cat([cat([high1, low1], 1), cat([high2, low2], 1)], 0), own_z[...])
        x = x[:CX] + x[CX:]
        z = z[:, :CZ] + z[:, CZ:]
        beside = v[(one - 1) % CY] + v[two]
        out[one] = x[:, :CZ] + z[:CX] + beside
        beside = v[one] + v[(two + 1) % CY]
        out[two] = x[:, CZ:] + z[CX:] + beside


def halo_part(near, far, field, halo_x, pair):
    parts = []
    for y in (2 * pair, 2 * pair + 1):
        start = (field * CY + y) * OV
        high, low = split(cat([near[start : start + OV], far[start : start + OV]], 0))
        parts.append(cat([high, low, high], 0))
    return dot(halo_x, cat(parts, 1))


def edge_rows(v, core, near, far, field):
    near_row = pl.multiple_of((1 - core) * (CX - OV), OV)
    far_row = pl.multiple_of(core * (CX - OV), OV)
    for y in range(CY):
        start = (field * CY + y) * OV
        near[start : start + OV] = v[y, pl.ds(near_row, OV), :]
        far[start : start + OV] = v[y, pl.ds(far_row, OV), :]


def first_edges(p_lo, p_hi, q_lo, q_hi, coef, near, far):
    core = lax.axis_index("core")

    def fill(low, high, field):
        for y in range(CY):
            start = (field * CY + y) * OV
            rows = pl.ds(y, OV, stride=CY)
            first, last = low[rows, :], high[rows, :]
            near[start : start + OV] = jnp.where(core == 0, last, first)
            far[start : start + OV] = jnp.where(core == 0, first, last)

    fill(p_lo, p_hi, 0)
    fill(q_lo, q_hi, 1)
    base = 2 * CY * OV
    for row in range(2):
        for part in range(4):
            lanes = slice(part * 128, part * 128 + 128)
            first = coef[row : row + 1, lanes]
            last = coef[CXC - 2 + row : CXC - 1 + row, lanes]
            spot = base + row * 4 + part
            near[spot : spot + 1] = jnp.where(core == 0, last, first)
            far[spot : spot + 1] = jnp.where(core == 0, first, last)


def reorder(source, target):
    for y in range(CY):
        target[y] = source[pl.ds(y, CX, stride=CY), :]


def prepare(
    signs, index, wavelet, p_now, p_prev, q_now, q_prev, own_x, own_z,
    p0, p1, q0, q1, lap_p, lap_q, source, amounts,
):
    reorder(p_now, p0)
    reorder(q_now, q0)
    interior(p0, own_x, own_z, lap_p)
    interior(q0, own_x, own_z, lap_q)
    reorder(p_prev, p1)
    reorder(q_prev, q1)
    source[...] = jnp.zeros_like(source)
    lane = lax.broadcasted_iota(jnp.int32, (1, CZ), 1)

    def add(e, carry):
        spot = index[e]
        x, rest = spot // (CY * CZ), spot % (CY * CZ)
        y, z = rest // CZ, rest % CZ
        amount = (2 * signs[e] - 1).astype(F32)
        row = source[y, pl.ds(x, 1), :]
        source[y, pl.ds(x, 1), :] = row + jnp.where(lane == z, amount, 0.0)
        return carry

    lax.fori_loop(0, ELEMS, add, 0)
    for step in range(STEPS + 1):
        amounts[step] = jnp.full((8, CZ), wavelet[step], F32)


def grow(coef, grow_z, grow_x, write):
    wide = []
    for pair in range(CYC // 2):
        high, low = split(coef[:, pair * 128 : pair * 128 + 128])
        both = dot(cat([high, low], 1), grow_z[...])
        wide += [both[:, :CZ], both[:, CZ:]]
    weights = taps()
    for pair in range(CY // 2):
        parts = []
        for y in (2 * pair, 2 * pair + 1):
            mixed = None
            for j, w in weights[y]:
                term = wide[j] * w
                mixed = term if mixed is None else mixed + term
            parts.append(mixed)
        high, low = split(cat(parts, 1))
        fine = dot(grow_x, cat([high, low], 0))
        write(2 * pair, fine[:, :CZ])
        write(2 * pair + 1, fine[:, CZ:])


UNIT = 1.0 / 384.0**3


def speed(coef, near, far, grow_z, grow_old, sigma, squared, held):
    core = lax.axis_index("core")
    held[:CXC] = coef[...]
    held[CXC:] = jnp.zeros((ROWS - CXC, CYC * CZC), F32)
    base = 2 * CY * OV
    for row in range(2):
        for part in range(4):
            lanes = slice(part * 128, part * 128 + 128)
            spot = base + row * 4 + part
            held[CXC + row : CXC + row + 1, lanes] = near[spot : spot + 1]
            held[CXC + 2 + row : CXC + 3 + row, lanes] = far[spot : spot + 1]

    def write(y, fine):
        fine = fine * UNIT
        sigma[y] = fine
        squared[y] = fine * fine

    grow(held[...], grow_z, grow_old[core], write)


def advance(step, *refs):
    (near, far, p, p_before, q, q_before, lap_p, lap_q, squared, source, amounts, halo_x) = refs[:12]
    refs = refs[12:]
    core = lax.axis_index("core")
    columns = halo_x[core]
    weight = amounts[step, :1, :]
    if step == 2:
        old_lap, refs = refs[0], refs[1:]
    if step == 3:
        (old_lap, older_q, gathered, sigma), refs = refs[:4], refs[4:]
    if step < 3:
        p_new, q_new, near_out, far_out = refs[:4]
    else:
        p_new, near_out, far_out, image = refs[:4]
    refs = refs[4:]
    if step < 2:
        lap_out = refs[0]
    if step == 2:
        gathered = refs[0]
    for pair in range(CY // 2):
        extra_p = halo_part(near, far, 0, columns, pair)
        extra_q = halo_part(near, far, 1, columns, pair)
        for side in range(2):
            y = 2 * pair + side
            lanes = slice(side * CZ, side * CZ + CZ)
            lap = lap_p[y] + extra_p[:, lanes]
            lap_adj = lap_q[y] + extra_q[:, lanes]
            sq = squared[y]
            p_new[y] = 2.0 * p[y] - p_before[y] + sq * lap + source[y] * weight
            new_q = 2.0 * q[y] - q_before[y] + sq * lap_adj
            if step < 3:
                q_new[y] = new_q
            if step < 2:
                lap_out[y] = lap
            if step == 2:
                gathered[y] = q[y] * lap + new_q * old_lap[y]
            if step == 3:
                total = gathered[y] + older_q[y] * lap + new_q * old_lap[y]
                image[y] = 2.0 * sigma[y] * total
    edge_rows(p_new, core, near_out, far_out, 0)
    if step < 3:
        edge_rows(q_new, core, near_out, far_out, 1)


def inside(p, q, own_x, own_z, lap_p, lap_q):
    interior(p, own_x, own_z, lap_p)
    interior(q, own_x, own_z, lap_q)


def inside_one(p, own_x, own_z, lap_p):
    interior(p, own_x, own_z, lap_p)


def shrink(image, near_in, far_in, shrink_x, shrink_z, own, near, far):
    core = lax.axis_index("core")
    rows_x = shrink_x[core]
    narrow = [None] * CYC
    weights = taps()
    for pair in range(CY // 2):
        high, low = split(cat([image[2 * pair], image[2 * pair + 1]], 1))
        both = dot(rows_x, cat([high, low], 0))
        for side in range(2):
            part = both[:, side * CZ : side * CZ + CZ]
            for j, w in weights[2 * pair + side]:
                term = part * w
                narrow[j] = term if narrow[j] is None else narrow[j] + term
    pieces = []
    for pair in range(CYC // 2):
        parts = []
        for j in (2 * pair, 2 * pair + 1):
            parts += list(split(narrow[j]))
        pieces.append(dot(cat(parts, 1), shrink_z[...]) * UNIT)
    own[...] = cat(pieces, 1)
    field = CY * OV
    near[:field] = near_in[...]
    far[:field] = far_in[...]
    for row in range(4):
        for part in range(4):
            lanes = slice(part * 128, part * 128 + 128)
            spot = field + row * 4 + part
            near[spot : spot + 1] = own[CXC + row : CXC + row + 1, lanes]
            far[spot : spot + 1] = own[CXC + 4 + row : CXC + 5 + row, lanes]


def merge(own, near, far, out):
    out[...] = own[...]
    field = CY * OV
    for row in range(4):
        for part in range(4):
            lanes = slice(part * 128, part * 128 + 128)
            spot = field + row * 4 + part
            a, b = CXC + row, CXC + 4 + row
            out[a : a + 1, lanes] = own[a : a + 1, lanes] + near[spot : spot + 1]
            out[b : b + 1, lanes] = own[b : b + 1, lanes] + far[spot : spot + 1]


def squares(a, b, total, squared):
    core = lax.axis_index("core")
    total[...] = a[...] + b[...]
    chip = lax.axis_index("xh") * lax.axis_size("z") + lax.axis_index("z")
    chips = lax.axis_size("xh") * lax.axis_size("z")
    first = (core == 0) & (chip == 0)
    last = (core == 1) & (chip == chips - 1)
    total[CXC + 4 : CXC + 6] = jnp.where(first, 0.0, total[CXC + 4 : CXC + 6])
    total[CXC + 6 : CXC + 8] = jnp.where(last, 0.0, total[CXC + 6 : CXC + 8])
    total[0:2] = jnp.where(core == 0, total[CXC + 6 : CXC + 8], total[CXC + 2 : CXC + 4])
    total[CXC - 2 : CXC] = jnp.where(core == 0, total[CXC : CXC + 2], total[CXC + 4 : CXC + 6])
    value = total[:CXC]
    value = value * value
    rows = value[0:8]
    for r in range(1, CXC // 8):
        rows = rows + value[8 * r : 8 * r + 8]
    folded = rows[:, :128]
    for c in range(1, 4):
        folded = folded + rows[:, 128 * c : 128 * c + 128]
    squared[...] = folded


def last_terms(
    total, near, far, p, p_before, lap_p, source, amounts, halo_x, grow_z, grow_new,
    lap_out, base, change,
):
    core = lax.axis_index("core")
    columns = halo_x[core]
    weight = amounts[STEPS, :1, :]
    for pair in range(CY // 2):
        extra = halo_part(near, far, 0, columns, pair)
        for side in range(2):
            y = 2 * pair + side
            lap_out[y] = lap_p[y] + extra[:, side * CZ : side * CZ + CZ]
            base[y] = 2.0 * p[y] - p_before[y] + source[y] * weight

    def write(y, fine):
        change[y] = fine * UNIT

    grow(total[...], grow_z, grow_new[core], write)


def finish(count, parts, total, sigma, lap, base, change, direction, p_last):
    value = parts[0]
    for k in range(1, parts.shape[0]):
        value = value + parts[k]
    value = jnp.sum(jnp.sum(value, axis=0, keepdims=True), axis=1, keepdims=True)
    scale = jnp.sqrt(value * (1.0 / count) + EPSILON)
    inverse = 1.0 / scale
    direction[...] = total[:CXC] * inverse
    rate = LEARN * inverse
    for y in range(CY):
        new = sigma[y] - rate * change[y]
        p_last[pl.ds(y, CX, stride=CY), :] = base[y] + new * new * lap[y]


VM = pl.BlockSpec(memory_space=pltpu.VMEM)
SM = pl.BlockSpec(memory_space=pltpu.SMEM)
FIELD = jax.ShapeDtypeStruct((CY, CX, CZ), F32)
PARAMS = pltpu.CompilerParams(vmem_limit_bytes=16 * 2**20)


def rows_of(count, lanes=128):
    return jax.ShapeDtypeStruct((count, lanes), F32)


def call(body, outs, *args, smem=0, scratch=(), flops=0, name=None):
    size = sum(int(np.prod(a.shape)) * a.dtype.itemsize for a in args)
    return pl.pallas_call(
        body,
        out_shape=outs,
        in_specs=[SM] * smem + [VM] * (len(args) - smem),
        out_specs=jax.tree.map(lambda _: VM, outs),
        scratch_shapes=list(scratch),
        compiler_params=PARAMS,
        cost_estimate=pl.CostEstimate(flops=flops, bytes_accessed=size, transcendentals=0),
        name=name,
    )(*args)


def xor_swap(x, axis, mask):
    count = lax.axis_size(axis)
    if mask >= count:
        return jnp.zeros_like(x)
    return lax.ppermute(x, axis, [(i, i ^ mask) for i in range(count)])


def far_swap(x):
    count = lax.axis_size(TILE)
    pairs = [(i, i + 1) for i in range(1, count - 1, 2)]
    return lax.ppermute(x, TILE, pairs + [(b, a) for a, b in pairs])


def exchange(near, far):
    far = far_swap(far)
    near = xor_swap(near, "core", 1)
    return near, far


def on_device(p_now, p_prev, adj_now, adj_next, coef_old, signs, elem_index, wavelet):
    const = {name: jnp.asarray(value) for name, value in constants().items()}
    own_x, own_z, halo_x = const["own_x"], const["own_z"], const["halo_x"]
    flat = lambda a: a.reshape(CX * CY, CZ)
    p_now, p_prev, adj_now, adj_next = map(flat, (p_now, p_prev, adj_now, adj_next))

    edge = rows_of(2 * CY * OV)
    with_coef = rows_of(2 * CY * OV + 8)
    low = pl.BlockSpec((OV * CY, CZ), lambda i: (0, 0))
    high = pl.BlockSpec((OV * CY, CZ), lambda i: (CX // OV - 1, 0))
    near, far = pl.pallas_call(
        first_edges,
        grid=(1,),
        out_shape=(with_coef, with_coef),
        in_specs=[low, high, low, high, pl.BlockSpec((CXC, CYC * CZC), lambda i: (0, 0))],
        out_specs=(pl.BlockSpec(with_coef.shape, lambda i: (0, 0)),) * 2,
        name="first_edges",
    )(p_now, p_now, adj_now, adj_now, coef_old)
    near, far = exchange(near, far)

    p, p_before, q, q_before, lap_p, lap_q, source, amounts = call(
        prepare,
        (FIELD,) * 7 + (jax.ShapeDtypeStruct((STEPS + 1, 8, CZ), F32),),
        signs[0], elem_index, wavelet, p_now, p_prev, adj_now, adj_next, own_x, own_z,
        smem=3, flops=10**9, name="prepare",
    )
    sigma, squared = call(
        speed, (FIELD, FIELD), coef_old, near, far, const["grow_z"], const["grow_old"],
        scratch=[pltpu.VMEM((ROWS, CYC * CZC), F32)], flops=10**8, name="speed",
    )

    laps, qs = [], [q]
    gathered = None
    for step in range(STEPS):
        args = [near, far, p, p_before, q, q_before, lap_p, lap_q, squared, source, amounts, halo_x]
        body = functools.partial(advance, step)
        name = f"advance_{step}"
        if step < 2:
            outs = (FIELD, FIELD, edge, edge, FIELD)
        elif step == 2:
            args.append(laps[1])
            outs = (FIELD, FIELD, edge, edge, FIELD)
        else:
            args += [laps[0], qs[1], gathered, sigma]
            outs = (FIELD, rows_of(CY * OV), rows_of(CY * OV), FIELD)
        result = call(body, outs, *args, flops=10**8, name=name)
        if step < 3:
            p_new, q_new, near, far, other = result
            if step < 2:
                laps.append(other)
            else:
                gathered = other
            p, p_before = p_new, p
            q, q_before = q_new, q
            qs.append(q)
            near, far = exchange(near, far)
            lap_p, lap_q = call(
                inside, (FIELD, FIELD), p, q, own_x, own_z, flops=10**9, name=f"inside_{step}"
            )
        else:
            p_new, near, far, image = result
            p, p_before = p_new, p

    ends = rows_of(CY * OV + 16)
    own, near, far = call(
        shrink,
        (rows_of(ROWS, CYC * CZC), ends, ends),
        image, near, far, const["shrink_x"], const["shrink_z"], flops=10**8, name="shrink",
    )
    near, far = exchange(near, far)
    lap_p = call(inside_one, FIELD, p, own_x, own_z, flops=5 * 10**8, name="inside_last")
    partial = call(merge, rows_of(ROWS, CYC * CZC), own, near, far, name="merge")

    two, one, three = (xor_swap(partial, "y", m) for m in (2, 1, 3))
    partial = (partial + one) + (two + three)
    other = xor_swap(partial, "xl", 1)
    total, squared_sum = call(
        squares, (rows_of(ROWS, CYC * CZC), rows_of(8)), partial, other, name="squares"
    )
    squared_sum = squared_sum + xor_swap(squared_sum, "core", 1)
    squared_sum = squared_sum + xor_swap(squared_sum, "xh", 1)
    deep = lax.axis_size("z")
    parts = lax.all_to_all(
        jnp.broadcast_to(squared_sum, (deep, 8, 128)), "z", split_axis=0, concat_axis=0, tiled=True
    )
    lap_p, base, change = call(
        last_terms,
        (FIELD, FIELD, FIELD),
        total, near, far, p, p_before, lap_p, source, amounts, halo_x,
        const["grow_z"], const["grow_new"], flops=10**8, name="last_terms",
    )
    count = float(lax.axis_size(TILE) * CXC * CYC * CZC)
    direction, p_last = call(
        functools.partial(finish, count),
        (rows_of(CXC, CYC * CZC), rows_of(CX * CY)),
        parts, total, sigma, lap_p, base, change, name="finish",
    )
    return direction, p_last.reshape(1, CX, CY, CZ)


def solution(mesh):
    shots, tiles = mesh.shape["shot"], mesh.shape["tile"]
    fine = Mesh(
        mesh.devices.reshape(shots // 2, 2, 2, tiles // 4, 2), ("y", "xl", "xh", "z", "core")
    )
    placed = (
        P(SHOT, TILE, None, None),
        P(SHOT, TILE, None, None),
        P(SHOT, TILE, None, None),
        P(SHOT, TILE, None, None),
        P(TILE, None),
        P(SHOT, TILE),
        P(TILE),
        P(),
    )
    return jax.shard_map(
        on_device,
        mesh=fine,
        in_specs=placed,
        out_specs=(P(TILE, None), P(SHOT, TILE, None, None)),
        check_vma=False,
    )
```

profile of v0, /device:TPU:6, one launch (start us, length us, event | category | flops | bytes accessed | tf_op | source)
XLA Modules:
  0.0 104.8 jit_solution(8114616953131930348)
XLA Ops:
  0.7 2.0 %first_edges.1 = (f32[264,128]{1,0:T(8,128)}, f32[264,128]{1,0:T(8,128)}) custom-call(f32[2048,128]{1,0:T(8,128)} %bitcast.6, f32[2048,128]{1,0:T(8,128)} %bitcast.7, f32[2048,128]{1,0:T(8,128)} %bitcast.9, f32[2048,128]{1,0:T(8,128)} %bitcast.10, f32[64,512]{1,0:T(8,128)} %coef.3), custom_call_target="tpu_custom_call" | custom-call | tf_op jit(solution)/shard_map/first_edges/pallas_call | solution.py:474
  2.6 8.7 %collective-permute-start.1 = (f32[264,128]{1,0:T(8,128)}, f32[264,128]{1,0:T(8,128)S(1)}, u32[]{:S(2)}, u32[]{:S(2)}) collective-permute-start(f32[264,128]{1,0:T(8,128)} %get-tuple-element.50), channel_id=1, source_target_pairs={{1,2},{3,4},{5,6},{7,8},{9,10},{11,12},{13,14},{15,16},{17,18},{19... | collective-permute-start | bytes 405512 | tf_op jit(solution)/shard_map/ppermute | solution.py:455
  12.0 1.2 %copy-done.6 = f32[1,128,16,128]{3,2,1,0:T(8,128)S(1)} copy-done((f32[1,128,16,128]{3,2,1,0:T(8,128)S(1)}, f32[1,128,16,128]{3,2,1,0:T(8,128)}, u32[]{:S(2)}) %copy-start.6) | copy-done | bytes 1048600
  13.3 1.2 %copy-done.7 = f32[1,128,16,128]{3,2,1,0:T(8,128)S(1)} copy-done((f32[1,128,16,128]{3,2,1,0:T(8,128)S(1)}, f32[1,128,16,128]{3,2,1,0:T(8,128)}, u32[]{:S(2)}) %copy-start.7) | copy-done | bytes 1048600
  15.4 4.3 %prepare.1 = (f32[16,128,128]{2,1,0:T(8,128)S(1)}, f32[16,128,128]{2,1,0:T(8,128)S(1)}, f32[16,128,128]{2,1,0:T(8,128)S(1)}, f32[16,128,128]{2,1,0:T(8,128)S(1)}...) custom-call(s32[64]{0:T(128)S(1)} %bitcast.14, ...), custom_call_target="tpu_custom_call" | custom-call | flops 1000000000 | bytes 4456980 | tf_op jit(solution)/shard_map/prepare/pallas_call | solution.py:433
  21.5 3.0 %collective-permute-start.3 = (f32[256,128]{1,0:T(8,128)S(1)}, f32[256,128]{1,0:T(8,128)S(1)}, u32[]{:S(2)}, u32[]{:S(2)}) collective-permute-start(f32[256,128]{1,0:T(8,128)S(1)} %get-tuple-element.61), channel_id=1, source_target_pairs={{1,2},{3,4},{5,6},{7,8},{9,10},{11,12},{13,14},{15,16},{17,18},{19... | collective-permute-start | bytes 393224 | tf_op jit(solution)/shard_map/ppermute | solution.py:455
  24.5 1.4 %inside_0.1 = (f32[16,128,128]{2,1,0:T(8,128)S(1)}, f32[16,128,128]{2,1,0:T(8,128)S(1)}) custom-call(f32[16,128,128]{2,1,0:T(8,128)S(1)} %get-tuple-element.62.p.refs_2_.refs_3_, f32[16,128,128]{2,1,0:T(8,128)S(1)} %get-tuple-element.63.q.refs_4_.refs_5_.refs_13_, bf16[256,256]{1,0:T(8,128)(2,1)S(1)} %copy-done.18, bf16[256,256]{1,0:T(8,128)(2,1)S(1)} %copy-done.16), custom_call_target="tpu_custom_call" | custom-call | flops 1000000000 | bytes 2359296 | tf_op jit(solution)/shard_map/inside_0/pallas_call | solution.py:433
  26.0 5.4 %collective-permute-done.3.refs_1_ = f32[256,128]{1,0:T(8,128)S(1)} collective-permute-done((f32[256,128]{1,0:T(8,128)S(1)}, f32[256,128]{1,0:T(8,128)S(1)}, u32[]{:S(2)}, u32[]{:S(2)}) %collective-permute-start.3) | collective-permute-done | bytes 131104 | tf_op jit(solution)/shard_map/ppermute | solution.py:455
  32.4 3.0 %collective-permute-start.5 = (f32[256,128]{1,0:T(8,128)S(1)}, f32[256,128]{1,0:T(8,128)S(1)}, u32[]{:S(2)}, u32[]{:S(2)}) collective-permute-start(f32[256,128]{1,0:T(8,128)S(1)} %get-tuple-element.67), channel_id=1, source_target_pairs={{1,2},{3,4},{5,6},{7,8},{9,10},{11,12},{13,14},{15,16},{17,18},{19... | collective-permute-start | bytes 393224 | tf_op jit(solution)/shard_map/ppermute | solution.py:455
  35.4 1.4 %inside_1.1 = (f32[16,128,128]{2,1,0:T(8,128)S(1)}, f32[16,128,128]{2,1,0:T(8,128)S(1)}) custom-call(f32[16,128,128]{2,1,0:T(8,128)S(1)} %get-tuple-element.68.p.refs_2_.refs_3_, f32[16,128,128]{2,1,0:T(8,128)S(1)} %get-tuple-element.69.q.refs_4_.refs_5_, bf16[256,256]{1,0:T(8,128)(2,1)S(1)} %copy-done.18, bf16[256,256]{1,0:T(8,128)(2,1)S(1)} %copy-done.16), custom_call_target="tpu_custom_call" | custom-call | flops 1000000000 | bytes 2359296 | tf_op jit(solution)/shard_map/inside_1/pallas_call | solution.py:433
  36.8 5.5 %collective-permute-done.5.refs_1_ = f32[256,128]{1,0:T(8,128)S(1)} collective-permute-done((f32[256,128]{1,0:T(8,128)S(1)}, f32[256,128]{1,0:T(8,128)S(1)}, u32[]{:S(2)}, u32[]{:S(2)}) %collective-permute-start.5) | collective-permute-done | bytes 131104 | tf_op jit(solution)/shard_map/ppermute | solution.py:455
  43.3 3.2 %collective-permute-start.7 = (f32[256,128]{1,0:T(8,128)S(1)}, f32[256,128]{1,0:T(8,128)S(1)}, u32[]{:S(2)}, u32[]{:S(2)}) collective-permute-start(f32[256,128]{1,0:T(8,128)S(1)} %get-tuple-element.74), channel_id=1, source_target_pairs={{1,2},{3,4},{5,6},{7,8},{9,10},{11,12},{13,14},{15,16},{17,18},{19... | collective-permute-start | bytes 393224 | tf_op jit(solution)/shard_map/ppermute | solution.py:455
  46.5 1.4 %inside_2.1 = (f32[16,128,128]{2,1,0:T(8,128)S(1)}, f32[16,128,128]{2,1,0:T(8,128)S(1)}) custom-call(f32[16,128,128]{2,1,0:T(8,128)S(1)} %get-tuple-element.75.p.refs_2_.p_before, f32[16,128,128]{2,1,0:T(8,128)S(1)} %get-tuple-element.76.q.refs_4_, bf16[256,256]{1,0:T(8,128)(2,1)S(1)} %copy-done.19, bf16[256,256]{1,0:T(8,128)(2,1)S(1)} %copy-done.16), custom_call_target="tpu_custom_call" | custom-call | flops 1000000000 | bytes 2359296 | tf_op jit(solution)/shard_map/inside_2/pallas_call | solution.py:433
  47.9 5.3 %collective-permute-done.7.refs_1_ = f32[256,128]{1,0:T(8,128)S(1)} collective-permute-done((f32[256,128]{1,0:T(8,128)S(1)}, f32[256,128]{1,0:T(8,128)S(1)}, u32[]{:S(2)}, u32[]{:S(2)}) %collective-permute-start.7) | collective-permute-done | bytes 131104 | tf_op jit(solution)/shard_map/ppermute | solution.py:455
  53.2 1.3 %advance_3.1 = (f32[16,128,128]{2,1,0:T(8,128)S(1)}, f32[128,128]{1,0:T(8,128)S(1)}, f32[128,128]{1,0:T(8,128)S(1)}, f32[16,128,128]{2,1,0:T(8,128)S(1)}) custom-call(f32[256,128]{1,0:T(8,128)S(1)} %collective-permute-done.6.refs_0_, f32[256,128]{1,0:T(8,128)S(1)} %collective-permute-done.7.refs_1_, ...), custom_call_target="tpu_custom_call" | custom-call | flops 100000000 | bytes 12890112 | tf_op jit(solution)/shard_map/advance_3/pallas_call | solution.py:433
  54.5 1.0 copy-done.2
  56.1 3.0 %collective-permute-start.9 = (f32[144,128]{1,0:T(8,128)S(1)}, f32[144,128]{1,0:T(8,128)S(1)}, u32[]{:S(2)}, u32[]{:S(2)}) collective-permute-start(f32[144,128]{1,0:T(8,128)S(1)} %get-tuple-element.87), channel_id=1, source_target_pairs={{1,2},{3,4},{5,6},{7,8},{9,10},{11,12},{13,14},{15,16},{17,18},{19... | collective-permute-start | bytes 221192 | tf_op jit(solution)/shard_map/ppermute | solution.py:455
  59.1 6.2 %collective-permute-done.9.far = f32[144,128]{1,0:T(8,128)S(1)} collective-permute-done((f32[144,128]{1,0:T(8,128)S(1)}, f32[144,128]{1,0:T(8,128)S(1)}, u32[]{:S(2)}, u32[]{:S(2)}) %collective-permute-start.9) | collective-permute-done | bytes 73760 | tf_op jit(solution)/shard_map/ppermute | solution.py:455
  66.0 3.0 %collective-permute-start.12 = (f32[72,512]{1,0:T(8,128)S(1)}, f32[72,512]{1,0:T(8,128)S(1)}, u32[]{:S(2)}, u32[]{:S(2)}) collective-permute-start(f32[72,512]{1,0:T(8,128)S(1)} %merge.1), channel_id=1, source_target_pairs={{0,192},{64,128},{128,64},{192,0},{1,193},{65,129},{129,65},{193,1... | collective-permute-start | bytes 442376 | tf_op jit(solution)/shard_map/ppermute | solution.py:449
  70.1 3.2 %collective-permute-done.12 = f32[72,512]{1,0:T(8,128)S(1)} collective-permute-done((f32[72,512]{1,0:T(8,128)S(1)}, f32[72,512]{1,0:T(8,128)S(1)}, u32[]{:S(2)}, u32[]{:S(2)}) %collective-permute-start.12) | collective-permute-done | bytes 147488 | tf_op jit(solution)/shard_map/ppermute | solution.py:449
  73.3 2.4 %collective-permute-done.11 = f32[72,512]{1,0:T(8,128)S(1)} collective-permute-done((f32[72,512]{1,0:T(8,128)S(1)}, f32[72,512]{1,0:T(8,128)S(1)}, u32[]{:S(2)}, u32[]{:S(2)}) %collective-permute-start.11) | collective-permute-done | bytes 147488 | tf_op jit(solution)/shard_map/ppermute | solution.py:449
  75.8 5.1 %collective-permute-done.13.b = f32[72,512]{1,0:T(8,128)S(1)} collective-permute-done((f32[72,512]{1,0:T(8,128)S(1)}, f32[72,512]{1,0:T(8,128)S(1)}, u32[]{:S(2)}, u32[]{:S(2)}) %collective-permute-start.13) | collective-permute-done | bytes 147488 | tf_op jit(solution)/shard_map/ppermute | solution.py:449
  81.1 1.2 %collective-permute-done.14 = f32[8,128]{1,0:T(8,128)S(1)} collective-permute-done((f32[8,128]{1,0:T(8,128)S(1)}, f32[8,128]{1,0:T(8,128)S(1)}, u32[]{:S(2)}, u32[]{:S(2)}) %collective-permute-start.14) | collective-permute-done | bytes 4128 | tf_op jit(solution)/shard_map/ppermute | solution.py:449
  82.3 5.1 %collective-permute-done.15 = f32[8,128]{1,0:T(8,128)S(1)} collective-permute-done((f32[8,128]{1,0:T(8,128)S(1)}, f32[8,128]{1,0:T(8,128)S(1)}, u32[]{:S(2)}, u32[]{:S(2)}) %collective-permute-start.15) | collective-permute-done | bytes 4128 | tf_op jit(solution)/shard_map/ppermute | solution.py:449
  88.0 3.3 %all-to-all-start = ((f32[8,8,128]{2,1,0:T(8,128)}), f32[8,8,128]{2,1,0:T(8,128)S(1)}, u32[]{:S(2)}, u32[]{:S(2)}) async-start(f32[8,8,128]{2,1,0:T(8,128)} %broadcast_in_dim.3), calls=%async_computation | async-start | bytes 65536 | tf_op jit(solution)/shard_map/all_to_all | solution.py:546
  91.4 1.2 %copy-done.3 = f32[16,128,128]{2,1,0:T(8,128)S(1)} copy-done((f32[16,128,128]{2,1,0:T(8,128)S(1)}, f32[16,128,128]{2,1,0:T(8,128)}, u32[]{:S(2)}) %copy-start.3) | copy-done | bytes 1048600
  97.4 1.0 copy-done.10
  98.4 1.0 copy-done.12
  99.4 1.2 %copy-done.9 = f32[16,128,128]{2,1,0:T(8,128)S(1)} copy-done((f32[16,128,128]{2,1,0:T(8,128)S(1)}, f32[16,128,128]{2,1,0:T(8,128)}, u32[]{:S(2)}) %copy-start.9) | copy-done | bytes 1048600
  100.6 1.2 %copy-done.11 = f32[16,128,128]{2,1,0:T(8,128)S(1)} copy-done((f32[16,128,128]{2,1,0:T(8,128)S(1)}, f32[16,128,128]{2,1,0:T(8,128)}, u32[]{:S(2)}) %copy-start.11) | copy-done | bytes 1048600
  101.8 1.2 %copy-done.13 = f32[16,128,128]{2,1,0:T(8,128)S(1)} copy-done((f32[16,128,128]{2,1,0:T(8,128)S(1)}, f32[16,128,128]{2,1,0:T(8,128)}, u32[]{:S(2)}) %copy-start.13) | copy-done | bytes 1048600
  103.1 1.7 %finish.1 = (f32[64,512]{1,0:T(8,128)}, f32[2048,128]{1,0:T(8,128)}) custom-call(f32[8,8,128]{2,1,0:T(8,128)S(1)} %all-to-all-done.parts, f32[72,512]{1,0:T(8,128)S(1)} %get-tuple-element.89.total, f32[16,128,128]{2,1,0:T(8,128)S(1)} %get-tuple-element.81.refs_15_.sigma, f32[16,128,128]{2,1,0:T(8,128)S(1)} %copy-done.9, f32[16,128,128]{2,1,0:T(8,128)S(1)} %copy-done.11, ...), custom_call_target="tpu_custom_call" | custom-call | bytes 4374528 | tf_op jit(solution)/shard_map/finish/pallas_call | solution.py:433
  (86 shorter events, 13.4 us)
Async XLA Ops:
  0.6 10.8 %copy-start = (f32[1,128,16,128]{3,2,1,0:T(8,128)S(1)}, f32[1,128,16,128]{3,2,1,0:T(8,128)}, u32[]{:S(2)}) copy-start(f32[1,128,16,128]{3,2,1,0:T(8,128)} %param.16) | copy-start | bytes 3145732
  0.6 10.8 %copy-start.1 = (f32[1,128,16,128]{3,2,1,0:T(8,128)S(1)}, f32[1,128,16,128]{3,2,1,0:T(8,128)}, u32[]{:S(2)}) copy-start(f32[1,128,16,128]{3,2,1,0:T(8,128)} %param.18) | copy-start | bytes 3145732
  0.6 10.8 %copy-start.16 = (bf16[256,256]{1,0:T(8,128)(2,1)S(1)}, bf16[256,256]{1,0:T(8,128)(2,1)}, u32[]{:S(2)}) copy-start(bf16[256,256]{1,0:T(8,128)(2,1)} %constant.18.clone.own_z) | copy-start | bytes 393220
  2.6 17.1 %collective-permute-start = (f32[264,128]{1,0:T(8,128)}, f32[264,128]{1,0:T(8,128)S(1)}, u32[]{:S(2)}, u32[]{:S(2)}) collective-permute-start(f32[264,128]{1,0:T(8,128)} %get-tuple-element.49), channel_id=1, source_target_pairs={{0,1},{1,0},{2,3},{3,2},{4,5},{5,4},{6,7},{7,6},{8,9},{9,8},{10,11... | collective-permute-start | bytes 405512 | tf_op jit(solution)/shard_map/ppermute | solution.py:449
  2.6 17.1 %collective-permute-start.1 = (f32[264,128]{1,0:T(8,128)}, f32[264,128]{1,0:T(8,128)S(1)}, u32[]{:S(2)}, u32[]{:S(2)}) collective-permute-start(f32[264,128]{1,0:T(8,128)} %get-tuple-element.50), channel_id=1, source_target_pairs={{1,2},{3,4},{5,6},{7,8},{9,10},{11,12},{13,14},{15,16},{17,18},{19... | collective-permute-start | bytes 405512 | tf_op jit(solution)/shard_map/ppermute | solution.py:455
  15.4 4.3 %copy-start.14 = (f32[64,512]{1,0:T(8,128)S(1)}, f32[64,512]{1,0:T(8,128)}, u32[]{:S(2)}) copy-start(f32[64,512]{1,0:T(8,128)} %coef.3) | copy-start | bytes 393220
  15.4 4.3 %copy-start.15 = (bf16[256,256]{1,0:T(8,128)(2,1)S(1)}, bf16[256,256]{1,0:T(8,128)(2,1)}, u32[]{:S(2)}) copy-start(bf16[256,256]{1,0:T(8,128)(2,1)} %constant.19.clone.grow_z) | copy-start | bytes 393220
  15.4 4.3 %copy-start.26 = (bf16[2,128,144]{2,1,0:T(8,128)(2,1)S(1)}, bf16[2,128,144]{2,1,0:T(8,128)(2,1)}, u32[]{:S(2)}) copy-start(bf16[2,128,144]{2,1,0:T(8,128)(2,1)} %constant.21.clone.grow_old) | copy-start | bytes 221188
  21.4 4.5 %collective-permute-start.2 = (f32[256,128]{1,0:T(8,128)S(1)}, f32[256,128]{1,0:T(8,128)S(1)}, u32[]{:S(2)}, u32[]{:S(2)}) collective-permute-start(f32[256,128]{1,0:T(8,128)S(1)} %get-tuple-element.60), channel_id=1, source_target_pairs={{0,1},{1,0},{2,3},{3,2},{4,5},{5,4},{6,7},{7,6},{8,9},{9,8},{10,11... | collective-permute-start | bytes 393224 | tf_op jit(solution)/shard_map/ppermute | solution.py:449
  21.5 9.9 %collective-permute-start.3 = (f32[256,128]{1,0:T(8,128)S(1)}, f32[256,128]{1,0:T(8,128)S(1)}, u32[]{:S(2)}, u32[]{:S(2)}) collective-permute-start(f32[256,128]{1,0:T(8,128)S(1)} %get-tuple-element.61), channel_id=1, source_target_pairs={{1,2},{3,4},{5,6},{7,8},{9,10},{11,12},{13,14},{15,16},{17,18},{19... | collective-permute-start | bytes 393224 | tf_op jit(solution)/shard_map/ppermute | solution.py:455
  32.3 4.5 %collective-permute-start.4 = (f32[256,128]{1,0:T(8,128)S(1)}, f32[256,128]{1,0:T(8,128)S(1)}, u32[]{:S(2)}, u32[]{:S(2)}) collective-permute-start(f32[256,128]{1,0:T(8,128)S(1)} %get-tuple-element.66), channel_id=1, source_target_pairs={{0,1},{1,0},{2,3},{3,2},{4,5},{5,4},{6,7},{7,6},{8,9},{9,8},{10,11... | collective-permute-start | bytes 393224 | tf_op jit(solution)/shard_map/ppermute | solution.py:449
  32.4 9.9 %collective-permute-start.5 = (f32[256,128]{1,0:T(8,128)S(1)}, f32[256,128]{1,0:T(8,128)S(1)}, u32[]{:S(2)}, u32[]{:S(2)}) collective-permute-start(f32[256,128]{1,0:T(8,128)S(1)} %get-tuple-element.67), channel_id=1, source_target_pairs={{1,2},{3,4},{5,6},{7,8},{9,10},{11,12},{13,14},{15,16},{17,18},{19... | collective-permute-start | bytes 393224 | tf_op jit(solution)/shard_map/ppermute | solution.py:455
  42.3 4.2 %copy-start.19 = (bf16[256,256]{1,0:T(8,128)(2,1)S(1)}, bf16[256,256]{1,0:T(8,128)(2,1)}, u32[]{:S(2)}) copy-start(bf16[256,256]{1,0:T(8,128)(2,1)} %constant.16.clone.own_x) | copy-start | bytes 393220
  43.2 4.7 %collective-permute-start.6 = (f32[256,128]{1,0:T(8,128)S(1)}, f32[256,128]{1,0:T(8,128)S(1)}, u32[]{:S(2)}, u32[]{:S(2)}) collective-permute-start(f32[256,128]{1,0:T(8,128)S(1)} %get-tuple-element.73), channel_id=1, source_target_pairs={{0,1},{1,0},{2,3},{3,2},{4,5},{5,4},{6,7},{7,6},{8,9},{9,8},{10,11... | collective-permute-start | bytes 393224 | tf_op jit(solution)/shard_map/ppermute | solution.py:449
  43.3 9.9 %collective-permute-start.7 = (f32[256,128]{1,0:T(8,128)S(1)}, f32[256,128]{1,0:T(8,128)S(1)}, u32[]{:S(2)}, u32[]{:S(2)}) collective-permute-start(f32[256,128]{1,0:T(8,128)S(1)} %get-tuple-element.74), channel_id=1, source_target_pairs={{1,2},{3,4},{5,6},{7,8},{9,10},{11,12},{13,14},{15,16},{17,18},{19... | collective-permute-start | bytes 393224 | tf_op jit(solution)/shard_map/ppermute | solution.py:455
  53.2 2.2 %copy-start.27 = (bf16[512,128]{1,0:T(8,128)(2,1)S(1)}, bf16[512,128]{1,0:T(8,128)(2,1)}, u32[]{:S(2)}) copy-start(bf16[512,128]{1,0:T(8,128)(2,1)} %constant.20.clone.shrink_z) | copy-start | bytes 393220
  53.2 2.2 %copy-start.28 = (bf16[2,72,256]{2,1,0:T(8,128)(2,1)S(1)}, bf16[2,72,256]{2,1,0:T(8,128)(2,1)}, u32[]{:S(2)}) copy-start(bf16[2,72,256]{2,1,0:T(8,128)(2,1)} %constant.23.clone.shrink_x) | copy-start | bytes 221188
  56.0 3.1 %collective-permute-start.8 = (f32[144,128]{1,0:T(8,128)S(1)}, f32[144,128]{1,0:T(8,128)S(1)}, u32[]{:S(2)}, u32[]{:S(2)}) collective-permute-start(f32[144,128]{1,0:T(8,128)S(1)} %get-tuple-element.86), channel_id=1, source_target_pairs={{0,1},{1,0},{2,3},{3,2},{4,5},{5,4},{6,7},{7,6},{8,9},{9,8},{10,11... | collective-permute-start | bytes 221192 | tf_op jit(solution)/shard_map/ppermute | solution.py:449
  56.1 9.3 %collective-permute-start.9 = (f32[144,128]{1,0:T(8,128)S(1)}, f32[144,128]{1,0:T(8,128)S(1)}, u32[]{:S(2)}, u32[]{:S(2)}) collective-permute-start(f32[144,128]{1,0:T(8,128)S(1)} %get-tuple-element.87), channel_id=1, source_target_pairs={{1,2},{3,4},{5,6},{7,8},{9,10},{11,12},{13,14},{15,16},{17,18},{19... | collective-permute-start | bytes 221192 | tf_op jit(solution)/shard_map/ppermute | solution.py:455
  59.1 6.3 %copy-start.21 = (f32[144,128]{1,0:T(8,128)}, f32[144,128]{1,0:T(8,128)S(1)}, u32[]{:S(2)}) copy-start(f32[144,128]{1,0:T(8,128)S(1)} %collective-permute-done.8.near) | copy-start | bytes 221188
  66.0 7.3 %collective-permute-start.12 = (f32[72,512]{1,0:T(8,128)S(1)}, f32[72,512]{1,0:T(8,128)S(1)}, u32[]{:S(2)}, u32[]{:S(2)}) collective-permute-start(f32[72,512]{1,0:T(8,128)S(1)} %merge.1), channel_id=1, source_target_pairs={{0,192},{64,128},{128,64},{192,0},{1,193},{65,129},{129,65},{193,1... | collective-permute-start | bytes 442376 | tf_op jit(solution)/shard_map/ppermute | solution.py:449
  69.0 6.6 %collective-permute-start.11 = (f32[72,512]{1,0:T(8,128)S(1)}, f32[72,512]{1,0:T(8,128)S(1)}, u32[]{:S(2)}, u32[]{:S(2)}) collective-permute-start(f32[72,512]{1,0:T(8,128)S(1)} %merge.1), channel_id=1, source_target_pairs={{0,128},{64,192},{128,0},{192,64},{1,129},{65,193},{129,1},{193,65... | collective-permute-start | bytes 442376 | tf_op jit(solution)/shard_map/ppermute | solution.py:449
  69.7 6.0 %collective-permute-start.10 = (f32[72,512]{1,0:T(8,128)S(1)}, f32[72,512]{1,0:T(8,128)S(1)}, u32[]{:S(2)}, u32[]{:S(2)}) collective-permute-start(f32[72,512]{1,0:T(8,128)S(1)} %merge.1), channel_id=1, source_target_pairs={{0,64},{64,0},{128,192},{192,128},{1,65},{65,1},{129,193},{193,129... | collective-permute-start | bytes 442376 | tf_op jit(solution)/shard_map/ppermute | solution.py:449
  75.7 5.2 %collective-permute-start.13 = (f32[72,512]{1,0:T(8,128)S(1)}, f32[72,512]{1,0:T(8,128)S(1)}, u32[]{:S(2)}, u32[]{:S(2)}) collective-permute-start(f32[72,512]{1,0:T(8,128)S(1)} %add_add_fusion.a), channel_id=1, source_target_pairs={{0,32},{32,0},{1,33},{33,1},{2,34},{34,2},{3,35},{35,3},{4,36},{36... | collective-permute-start | bytes 442376 | tf_op jit(solution)/shard_map/ppermute | solution.py:449
  81.0 1.3 %collective-permute-start.14 = (f32[8,128]{1,0:T(8,128)S(1)}, f32[8,128]{1,0:T(8,128)S(1)}, u32[]{:S(2)}, u32[]{:S(2)}) collective-permute-start(f32[8,128]{1,0:T(8,128)S(1)} %get-tuple-element.88), channel_id=1, source_target_pairs={{0,1},{1,0},{2,3},{3,2},{4,5},{5,4},{6,7},{7,6},{8,9},{9,8},{10,11... | collective-permute-start | bytes 12296 | tf_op jit(solution)/shard_map/ppermute | solution.py:449
  82.3 5.1 %collective-permute-start.15 = (f32[8,128]{1,0:T(8,128)S(1)}, f32[8,128]{1,0:T(8,128)S(1)}, u32[]{:S(2)}, u32[]{:S(2)}) collective-permute-start(f32[8,128]{1,0:T(8,128)S(1)} %add.18), channel_id=1, source_target_pairs={{0,16},{16,0},{1,17},{17,1},{2,18},{18,2},{3,19},{19,3},{4,20},{20... | collective-permute-start | bytes 12296 | tf_op jit(solution)/shard_map/ppermute | solution.py:449
  88.0 11.4 %all-to-all-start = ((f32[8,8,128]{2,1,0:T(8,128)}), f32[8,8,128]{2,1,0:T(8,128)S(1)}, u32[]{:S(2)}, u32[]{:S(2)}) async-start(f32[8,8,128]{2,1,0:T(8,128)} %broadcast_in_dim.3), calls=%async_computation | async-start | bytes 65536 | tf_op jit(solution)/shard_map/all_to_all | solution.py:546
  91.3 1.2 %copy-start.3 = (f32[16,128,128]{2,1,0:T(8,128)S(1)}, f32[16,128,128]{2,1,0:T(8,128)}, u32[]{:S(2)}) copy-start(f32[16,128,128]{2,1,0:T(8,128)} %copy-done.2) | copy-start | bytes 3145732
  94.4 1.2 %copy-start.22 = (f32[144,128]{1,0:T(8,128)S(1)}, f32[144,128]{1,0:T(8,128)}, u32[]{:S(2)}) copy-start(f32[144,128]{1,0:T(8,128)} %copy-done.21) | copy-start | bytes 221188
  94.4 1.2 %copy-start.24 = (f32[144,128]{1,0:T(8,128)S(1)}, f32[144,128]{1,0:T(8,128)}, u32[]{:S(2)}) copy-start(f32[144,128]{1,0:T(8,128)} %copy-done.23) | copy-start | bytes 221188
  94.4 1.3 %copy-start.25 = (bf16[2,128,144]{2,1,0:T(8,128)(2,1)S(1)}, bf16[2,128,144]{2,1,0:T(8,128)(2,1)}, u32[]{:S(2)}) copy-start(bf16[2,128,144]{2,1,0:T(8,128)(2,1)} %constant.22.clone.grow_new) | copy-start | bytes 221188
  99.4 1.2 %copy-start.9 = (f32[16,128,128]{2,1,0:T(8,128)S(1)}, f32[16,128,128]{2,1,0:T(8,128)}, u32[]{:S(2)}) copy-start(f32[16,128,128]{2,1,0:T(8,128)} %copy-done.8) | copy-start | bytes 3145732
  (17 other events, 16.3 us)
where the time goes:
time: 105 us
  waiting for transfers between devices  39.4 us (38%)
  starting transfers between devices  28.9 us (28%)
  Pallas kernels  18.8 us (18%)
  local copies, waits for them, and re-layouts  16.6 us (16%)
  between operations  1.05 us (1%)
    ppermute x5, waiting for transfers between devices, far_swap(): return lax.ppermute(x, TILE, pairs + [(b, a) for a, b in pairs])  22.4 us
    ppermute x5, starting transfers between devices, far_swap(): return lax.ppermute(x, TILE, pairs + [(b, a) for a, b in pairs])  20.9 us
    ppermute x11, waiting for transfers between devices, xor_swap(): return lax.ppermute(x, axis, [(i, i ^ mask) for i in range(count)])  17 us
    pallas_call x15, Pallas kernels, call(): pl.pallas_call(body, out_shape=outs, in_specs=[SM] * smem + [VM] * (len(a...  16.8 us
    unnamed x64, local copies, waits for them, and re-layouts  16 us
    ppermute x11, starting transfers between devices, xor_swap(): return lax.ppermute(x, axis, [(i, i ^ mask) for i in range(count)])  4.65 us
    all_to_all x1, starting transfers between devices, on_device(): lax.all_to_all(jnp.broadcast_to(squared_sum, (deep, 8, 128)), 'z', split_...  3.33 us
  transfers between devices with their start and end apart: 17, of which 9 were waited for; matrix products, arithmetic and copies ran while one was open for 0% of the time, Pallas kernels for 10%

commit v1 on v0

--- a/solution.py
+++ b/solution.py
@@ -166,8 +166,24 @@
         far[start : start + OV] = v[y, pl.ds(far_row, OV), :]
 
 
-def first_edges(p_lo, p_hi, q_lo, q_hi, coef, near, far):
+def first_edges(p, q, coef, near, far, p_lo, p_hi, q_lo, q_hi, c_lo, c_hi, sems):
     core = lax.axis_index("core")
+    block = OV * CY
+    copies = [
+        pltpu.make_async_copy(source.at[pl.ds(start, size)], target, sems.at[k])
+        for k, (source, start, size, target) in enumerate(
+            (
+                (p, 0, block, p_lo),
+                (p, CX * CY - block, block, p_hi),
+                (q, 0, block, q_lo),
+                (q, CX * CY - block, block, q_hi),
+                (coef, 0, 8, c_lo),
+                (coef, CXC - 8, 8, c_hi),
+            )
+        )
+    ]
+    for copy in copies:
+        copy.start()
 
     def fill(low, high, field):
         for y in range(CY):
@@ -177,14 +193,20 @@
             near[start : start + OV] = jnp.where(core == 0, last, first)
             far[start : start + OV] = jnp.where(core == 0, first, last)
 
+    copies[0].wait()
+    copies[1].wait()
     fill(p_lo, p_hi, 0)
+    copies[2].wait()
+    copies[3].wait()
     fill(q_lo, q_hi, 1)
+    copies[4].wait()
+    copies[5].wait()
     base = 2 * CY * OV
     for row in range(2):
         for part in range(4):
             lanes = slice(part * 128, part * 128 + 128)
-            first = coef[row : row + 1, lanes]
-            last = coef[CXC - 2 + row : CXC - 1 + row, lanes]
+            first = c_lo[row : row + 1, lanes]
+            last = c_hi[6 + row : 7 + row, lanes]
             spot = base + row * 4 + part
             near[spot : spot + 1] = jnp.where(core == 0, last, first)
             far[spot : spot + 1] = jnp.where(core == 0, first, last)
@@ -196,15 +218,13 @@
 
 
 def prepare(
-    signs, index, wavelet, p_now, p_prev, q_now, q_prev, own_x, own_z,
-    p0, p1, q0, q1, lap_p, lap_q, source, amounts,
+    signs, index, wavelet, p_now, q_now, own_x, own_z,
+    p0, q0, lap_p, lap_q, source, amounts,
 ):
     reorder(p_now, p0)
     reorder(q_now, q0)
     interior(p0, own_x, own_z, lap_p)
     interior(q0, own_x, own_z, lap_q)
-    reorder(p_prev, p1)
-    reorder(q_prev, q1)
     source[...] = jnp.zeros_like(source)
     lane = lax.broadcasted_iota(jnp.int32, (1, CZ), 1)
 
@@ -294,8 +314,13 @@
             lap = lap_p[y] + extra_p[:, lanes]
             lap_adj = lap_q[y] + extra_q[:, lanes]
             sq = squared[y]
-            p_new[y] = 2.0 * p[y] - p_before[y] + sq * lap + source[y] * weight
-            new_q = 2.0 * q[y] - q_before[y] + sq * lap_adj
+            if step == 0:
+                rows = pl.ds(y, CX, stride=CY)
+                old_p, old_q = p_before[rows, :], q_before[rows, :]
+            else:
+                old_p, old_q = p_before[y], q_before[y]
+            p_new[y] = 2.0 * p[y] - old_p + sq * lap + source[y] * weight
+            new_q = 2.0 * q[y] - old_q + sq * lap_adj
             if step < 3:
                 q_new[y] = new_q
             if step < 2:
@@ -384,10 +409,7 @@
     squared[...] = folded
 
 
-def last_terms(
-    total, near, far, p, p_before, lap_p, source, amounts, halo_x, grow_z, grow_new,
-    lap_out, base, change,
-):
+def last_fields(near, far, p, p_before, lap_p, source, amounts, halo_x, lap_out, base):
     core = lax.axis_index("core")
     columns = halo_x[core]
     weight = amounts[STEPS, :1, :]
@@ -398,13 +420,32 @@
             lap_out[y] = lap_p[y] + extra[:, side * CZ : side * CZ + CZ]
             base[y] = 2.0 * p[y] - p_before[y] + source[y] * weight
 
+
+def add_four(own, one, two, three, out):
+    out[...] = (own[...] + one[...]) + (two[...] + three[...])
+
+
+def spread(total, sigma, lap, base, grow_z, grow_new, zeroth, first, second):
+    core = lax.axis_index("core")
+
     def write(y, fine):
-        change[y] = fine * UNIT
+        change = fine * UNIT
+        old, curve = sigma[y], lap[y]
+        scaled = change * curve
+        zeroth[y] = base[y] + old * old * curve
+        first[y] = -2.0 * old * scaled
+        second[y] = change * scaled
 
     grow(total[...], grow_z, grow_new[core], write)
 
 
-def finish(count, parts, total, sigma, lap, base, change, direction, p_last):
+def widen(a, b, out):
+    value = a[...] + b[...]
+    for k in range(out.shape[0]):
+        out[k] = value
+
+
+def finish(count, parts, total, zeroth, first, second, direction, p_last):
     value = parts[0]
     for k in range(1, parts.shape[0]):
         value = value + parts[k]
@@ -414,32 +455,39 @@
     direction[...] = total[:CXC] * inverse
     rate = LEARN * inverse
     for y in range(CY):
-        new = sigma[y] - rate * change[y]
-        p_last[pl.ds(y, CX, stride=CY), :] = base[y] + new * new * lap[y]
+        value = zeroth[y] + rate * (first[y] + rate * second[y])
+        p_last[pl.ds(y, CX, stride=CY), :] = value
 
 
 VM = pl.BlockSpec(memory_space=pltpu.VMEM)
 SM = pl.BlockSpec(memory_space=pltpu.SMEM)
 FIELD = jax.ShapeDtypeStruct((CY, CX, CZ), F32)
-PARAMS = pltpu.CompilerParams(vmem_limit_bytes=16 * 2**20)
+PARAMS = pltpu.CompilerParams(vmem_limit_bytes=4 * 2**20)
 
 
 def rows_of(count, lanes=128):
     return jax.ShapeDtypeStruct((count, lanes), F32)
 
 
-def call(body, outs, *args, smem=0, scratch=(), flops=0, name=None):
+def call(body, outs, *args, smem=0, scratch=(), flops=0, name=None, held=()):
     size = sum(int(np.prod(a.shape)) * a.dtype.itemsize for a in args)
+    count = len(args)
+
+    def run(*refs):
+        body(*refs[:count], *refs[count + len(held) :])
+
     return pl.pallas_call(
-        body,
+        run,
         out_shape=outs,
-        in_specs=[SM] * smem + [VM] * (len(args) - smem),
+        in_specs=[SM] * smem
+        + [VM] * (count - smem)
+        + [pl.BlockSpec(memory_space=pl.ANY)] * len(held),
         out_specs=jax.tree.map(lambda _: VM, outs),
         scratch_shapes=list(scratch),
         compiler_params=PARAMS,
         cost_estimate=pl.CostEstimate(flops=flops, bytes_accessed=size, transcendentals=0),
         name=name,
-    )(*args)
+    )(*args, *held)
 
 
 def xor_swap(x, axis, mask):
@@ -469,22 +517,23 @@
 
     edge = rows_of(2 * CY * OV)
     with_coef = rows_of(2 * CY * OV + 8)
-    low = pl.BlockSpec((OV * CY, CZ), lambda i: (0, 0))
-    high = pl.BlockSpec((OV * CY, CZ), lambda i: (CX // OV - 1, 0))
+    block = pltpu.VMEM((OV * CY, CZ), F32)
+    few = pltpu.VMEM((8, CYC * CZC), F32)
     near, far = pl.pallas_call(
         first_edges,
-        grid=(1,),
         out_shape=(with_coef, with_coef),
-        in_specs=[low, high, low, high, pl.BlockSpec((CXC, CYC * CZC), lambda i: (0, 0))],
-        out_specs=(pl.BlockSpec(with_coef.shape, lambda i: (0, 0)),) * 2,
+        in_specs=[pl.BlockSpec(memory_space=pltpu.HBM)] * 3,
+        out_specs=(VM, VM),
+        scratch_shapes=[block] * 4 + [few] * 2 + [pltpu.SemaphoreType.DMA((6,))],
+        compiler_params=PARAMS,
         name="first_edges",
-    )(p_now, p_now, adj_now, adj_now, coef_old)
+    )(*(pltpu.with_memory_space_constraint(a, pltpu.HBM) for a in (p_now, adj_now, coef_old)))
     near, far = exchange(near, far)
 
-    p, p_before, q, q_before, lap_p, lap_q, source, amounts = call(
+    p, q, lap_p, lap_q, source, amounts = call(
         prepare,
-        (FIELD,) * 7 + (jax.ShapeDtypeStruct((STEPS + 1, 8, CZ), F32),),
-        signs[0], elem_index, wavelet, p_now, p_prev, adj_now, adj_next, own_x, own_z,
+        (FIELD,) * 5 + (jax.ShapeDtypeStruct((STEPS + 1, 8, CZ), F32),),
+        signs[0], elem_index, wavelet, p_now, adj_now, own_x, own_z,
         smem=3, flops=10**9, name="prepare",
     )
     sigma, squared = call(
@@ -492,6 +541,7 @@
         scratch=[pltpu.VMEM((ROWS, CYC * CZC), F32)], flops=10**8, name="speed",
     )
 
+    p_before, q_before = p_prev, adj_next
     laps, qs = [], [q]
     gathered = None
     for step in range(STEPS):
@@ -535,28 +585,35 @@
     partial = call(merge, rows_of(ROWS, CYC * CZC), own, near, far, name="merge")
 
     two, one, three = (xor_swap(partial, "y", m) for m in (2, 1, 3))
-    partial = (partial + one) + (two + three)
+    lap_p, base = call(
+        last_fields, (FIELD, FIELD), near, far, p, p_before, lap_p, source, amounts, halo_x,
+        flops=10**8, name="last_fields",
+    )
+    held = (lap_p, base)
+    partial = call(
+        add_four, rows_of(ROWS, CYC * CZC), partial, one, two, three, name="add_four", held=held
+    )
     other = xor_swap(partial, "xl", 1)
     total, squared_sum = call(
-        squares, (rows_of(ROWS, CYC * CZC), rows_of(8)), partial, other, name="squares"
+        squares, (rows_of(ROWS, CYC * CZC), rows_of(8)), partial, other, name="squares",
+        held=held,
     )
     squared_sum = squared_sum + xor_swap(squared_sum, "core", 1)
-    squared_sum = squared_sum + xor_swap(squared_sum, "xh", 1)
+    terms = call(
+        spread, (FIELD,) * 3, total, sigma, lap_p, base, const["grow_z"], const["grow_new"],
+        flops=10**8, name="spread",
+    )
     deep = lax.axis_size("z")
-    parts = lax.all_to_all(
-        jnp.broadcast_to(squared_sum, (deep, 8, 128)), "z", split_axis=0, concat_axis=0, tiled=True
-    )
-    lap_p, base, change = call(
-        last_terms,
-        (FIELD, FIELD, FIELD),
-        total, near, far, p, p_before, lap_p, source, amounts, halo_x,
-        const["grow_z"], const["grow_new"], flops=10**8, name="last_terms",
-    )
+    copies = call(
+        widen, jax.ShapeDtypeStruct((deep, 8, 128), F32),
+        squared_sum, xor_swap(squared_sum, "xh", 1), name="widen", held=terms,
+    )
+    parts = lax.all_to_all(copies, "z", split_axis=0, concat_axis=0, tiled=True)
     count = float(lax.axis_size(TILE) * CXC * CYC * CZC)
     direction, p_last = call(
         functools.partial(finish, count),
         (rows_of(CXC, CYC * CZC), rows_of(CX * CY)),
-        parts, total, sigma, lap_p, base, change, name="finish",
+        parts, total, *terms, name="finish",
     )
     return direction, p_last.reshape(1, CX, CY, CZ)
 

time: 105 us -> 94.3 us (0.90)
  local copies, waits for them, and re-layouts: 16.6 us -> 1.16 us
  waiting for transfers between devices: 39.4 us -> 28.6 us
  blocking collectives: 0 us -> 10.4 us
  starting transfers between devices: 28.9 us -> 34.4 us
    unnamed x64 -> x34, local copies, waits for them, and re-layouts: 16 us -> 1.16 us
    all_to_all x0 -> x1, blocking collectives: none -> 10.4 us  [on_device(): parts = lax.all_to_all(copies, 'z', split_axis=0, concat_axis=0, tiled=True)]
    ppermute x5, waiting for transfers between devices: 22.4 us -> 13.6 us  [far_swap(): return lax.ppermute(x, TILE, pairs + [(b, a) for a, b in pairs])]
    ppermute x5, starting transfers between devices: 20.9 us -> 29.6 us  [far_swap(): return lax.ppermute(x, TILE, pairs + [(b, a) for a, b in pairs])]
    all_to_all x1 -> x0, starting transfers between devices: 3.33 us -> none  [on_device(): lax.all_to_all(jnp.broadcast_to(squared_sum, (deep, 8, 128)), 'z', split_...]
    ppermute x11, waiting for transfers between devices: 17 us -> 15 us  [xor_swap(): return lax.ppermute(x, axis, [(i, i ^ mask) for i in range(count)])]
    pallas_call x16 -> x19, Pallas kernels: 18.8 us -> 18.3 us  [the longest x18 17.1 us: call(): pl.pallas_call(run, out_shape=outs, in_specs=[SM] * smem + [VM] * (count...]
  transfers between devices with their start and end apart: 17 -> 16, of which waited for: 9 -> 9; matrix products, arithmetic and copies ran while one was open for 0% -> 0% of each run, Pallas kernels for 10% -> 11%
where the time goes in v1:
time: 94.3 us; the launch traced here: 94 us
  starting transfers between devices  34.4 us (36%)
  waiting for transfers between devices  28.6 us (30%)
  Pallas kernels  18.3 us (19%)
  blocking collectives  10.4 us (11%)
  local copies, waits for them, and re-layouts  1.16 us (1%)
  between operations  1.08 us (1%)
    ppermute x5, starting transfers between devices, far_swap(): return lax.ppermute(x, TILE, pairs + [(b, a) for a, b in pairs])  29.6 us
    pallas_call x18, Pallas kernels, call(): pl.pallas_call(run, out_shape=outs, in_specs=[SM] * smem + [VM] * (count...  17.1 us
    ppermute x11, waiting for transfers between devices, xor_swap(): return lax.ppermute(x, axis, [(i, i ^ mask) for i in range(count)])  15 us
    ppermute x5, waiting for transfers between devices, far_swap(): return lax.ppermute(x, TILE, pairs + [(b, a) for a, b in pairs])  13.6 us
    all_to_all x1, blocking collectives, on_device(): parts = lax.all_to_all(copies, 'z', split_axis=0, concat_axis=0, tiled=True)  10.4 us
    ppermute x11, starting transfers between devices, xor_swap(): return lax.ppermute(x, axis, [(i, i ^ mask) for i in range(count)])  4.83 us
  transfers between devices with their start and end apart: 16, of which 9 were waited for; matrix products, arithmetic and copies ran while one was open for 0% of the time, Pallas kernels for 11%

profile of v1, /device:TPU:6, one launch (start us, length us, event | category | flops | bytes accessed | tf_op | source)
XLA Modules:
  0.0 94.0 jit_solution(18006187476455052038)
XLA Ops:
  0.7 1.2 %first_edges.1 = (f32[264,128]{1,0:T(8,128)S(1)}, f32[264,128]{1,0:T(8,128)S(1)}) custom-call(f32[2048,128]{1,0:T(8,128)} %bitcast.8, f32[2048,128]{1,0:T(8,128)} %bitcast.10, f32[64,512]{1,0:T(8,128)} %refs_0_.1), custom_call_target="tpu_custom_call" | custom-call | tf_op jit(solution)/shard_map/first_edges/pallas_call | solution.py:522
  2.0 8.8 %collective-permute-start.1 = (f32[264,128]{1,0:T(8,128)S(1)}, f32[264,128]{1,0:T(8,128)S(1)}, u32[]{:S(2)}, u32[]{:S(2)}) collective-permute-start(f32[264,128]{1,0:T(8,128)S(1)} %get-tuple-element.50), channel_id=1, source_target_pairs={{1,2},{3,4},{5,6},{7,8},{9,10},{11,12},{13,14},{15,16},{17,18},{19... | collective-permute-start | bytes 405512 | tf_op jit(solution)/shard_map/ppermute | solution.py:503
  10.9 0.9 copy-done.9
  11.8 3.6 %prepare.1 = (f32[16,128,128]{2,1,0:T(8,128)S(1)}, f32[16,128,128]{2,1,0:T(8,128)S(1)}, f32[16,128,128]{2,1,0:T(8,128)S(1)}, f32[16,128,128]{2,1,0:T(8,128)S(1)}...) custom-call(s32[64]{0:T(128)S(1)} %bitcast.12, s32[64]{0:T(128)S(1)} %copy-done.15, f32[5]{0:T(128)S(1)} %copy-done.16, ...), custom_call_target="tpu_custom_call" | custom-call | flops 1000000000 | bytes 2359828 | tf_op jit(solution)/shard_map/prepare/pallas_call | solution.py:479
  15.4 0.6 speed.1
  16.2 1.3 %advance_0.1 = (f32[16,128,128]{2,1,0:T(8,128)S(1)}, f32[16,128,128]{2,1,0:T(8,128)S(1)}, f32[256,128]{1,0:T(8,128)S(1)}, f32[256,128]{1,0:T(8,128)S(1)}, f32[16,128,128]{2,1,0:T(8,128)S(1)}) custom-call(f32[264,128]{1,0:T(8,128)S(1)} %collective-permute-done.refs_1_.refs_0_, f32[264,128]{1,0:T(8,128)S(1)} %collective-permute-done.1.refs_2_.refs_1_, ...), custom_call_target="tpu_custom_call" | custom-call | flops 100000000 | bytes 8704000 | tf_op jit(solution)/shard_map/advance_0/pallas_call | solution.py:479
  17.6 5.1 %collective-permute-start.3 = (f32[256,128]{1,0:T(8,128)S(1)}, f32[256,128]{1,0:T(8,128)S(1)}, u32[]{:S(2)}, u32[]{:S(2)}) collective-permute-start(f32[256,128]{1,0:T(8,128)S(1)} %get-tuple-element.59), channel_id=1, source_target_pairs={{1,2},{3,4},{5,6},{7,8},{9,10},{11,12},{13,14},{15,16},{17,18},{19... | collective-permute-start | bytes 393224 | tf_op jit(solution)/shard_map/ppermute | solution.py:503
  22.8 1.5 %inside_0.1 = (f32[16,128,128]{2,1,0:T(8,128)S(1)}, f32[16,128,128]{2,1,0:T(8,128)S(1)}) custom-call(f32[16,128,128]{2,1,0:T(8,128)S(1)} %get-tuple-element.60.refs_0_.refs_2_.refs_3_, f32[16,128,128]{2,1,0:T(8,128)S(1)} %get-tuple-element.61.refs_1_.refs_4_.refs_5_.refs_13_, bf16[256,256]{1,0:T(8,128)(2,1)S(1)} %copy-done.9, bf16[256,256]{1,0:T(8,128)(2,1)S(1)} %copy-done.8), custom_call_target="tpu_custom_call" | custom-call | flops 1000000000 | bytes 2359296 | tf_op jit(solution)/shard_map/inside_0/pallas_call | solution.py:479
  24.3 3.2 %collective-permute-done.3.refs_1_ = f32[256,128]{1,0:T(8,128)S(1)} collective-permute-done((f32[256,128]{1,0:T(8,128)S(1)}, f32[256,128]{1,0:T(8,128)S(1)}, u32[]{:S(2)}, u32[]{:S(2)}) %collective-permute-start.3) | collective-permute-done | bytes 131104 | tf_op jit(solution)/shard_map/ppermute | solution.py:503
  27.5 0.8 advance_1.1
  28.4 5.2 %collective-permute-start.5 = (f32[256,128]{1,0:T(8,128)S(1)}, f32[256,128]{1,0:T(8,128)S(1)}, u32[]{:S(2)}, u32[]{:S(2)}) collective-permute-start(f32[256,128]{1,0:T(8,128)S(1)} %get-tuple-element.65), channel_id=1, source_target_pairs={{1,2},{3,4},{5,6},{7,8},{9,10},{11,12},{13,14},{15,16},{17,18},{19... | collective-permute-start | bytes 393224 | tf_op jit(solution)/shard_map/ppermute | solution.py:503
  33.6 1.5 %inside_1.1 = (f32[16,128,128]{2,1,0:T(8,128)S(1)}, f32[16,128,128]{2,1,0:T(8,128)S(1)}) custom-call(f32[16,128,128]{2,1,0:T(8,128)S(1)} %get-tuple-element.66.refs_0_.refs_2_.refs_3_, f32[16,128,128]{2,1,0:T(8,128)S(1)} %get-tuple-element.67.refs_1_.refs_4_.refs_5_, bf16[256,256]{1,0:T(8,128)(2,1)S(1)} %copy-done.9, bf16[256,256]{1,0:T(8,128)(2,1)S(1)} %copy-done.8), custom_call_target="tpu_custom_call" | custom-call | flops 1000000000 | bytes 2359296 | tf_op jit(solution)/shard_map/inside_1/pallas_call | solution.py:479
  35.2 3.2 %collective-permute-done.5.refs_1_ = f32[256,128]{1,0:T(8,128)S(1)} collective-permute-done((f32[256,128]{1,0:T(8,128)S(1)}, f32[256,128]{1,0:T(8,128)S(1)}, u32[]{:S(2)}, u32[]{:S(2)}) %collective-permute-start.5) | collective-permute-done | bytes 131104 | tf_op jit(solution)/shard_map/ppermute | solution.py:503
  38.3 0.9 advance_2.1
  39.4 5.3 %collective-permute-start.7 = (f32[256,128]{1,0:T(8,128)S(1)}, f32[256,128]{1,0:T(8,128)S(1)}, u32[]{:S(2)}, u32[]{:S(2)}) collective-permute-start(f32[256,128]{1,0:T(8,128)S(1)} %get-tuple-element.72), channel_id=1, source_target_pairs={{1,2},{3,4},{5,6},{7,8},{9,10},{11,12},{13,14},{15,16},{17,18},{19... | collective-permute-start | bytes 393224 | tf_op jit(solution)/shard_map/ppermute | solution.py:503
  44.7 1.5 %inside_2.1 = (f32[16,128,128]{2,1,0:T(8,128)S(1)}, f32[16,128,128]{2,1,0:T(8,128)S(1)}) custom-call(f32[16,128,128]{2,1,0:T(8,128)S(1)} %get-tuple-element.73.refs_0_.refs_2_.refs_3_, f32[16,128,128]{2,1,0:T(8,128)S(1)} %get-tuple-element.74.refs_1_.refs_4_, bf16[256,256]{1,0:T(8,128)(2,1)S(1)} %copy-done.10, bf16[256,256]{1,0:T(8,128)(2,1)S(1)} %copy-done.8), custom_call_target="tpu_custom_call" | custom-call | flops 1000000000 | bytes 2359296 | tf_op jit(solution)/shard_map/inside_2/pallas_call | solution.py:479
  46.2 3.1 %collective-permute-done.7.refs_1_ = f32[256,128]{1,0:T(8,128)S(1)} collective-permute-done((f32[256,128]{1,0:T(8,128)S(1)}, f32[256,128]{1,0:T(8,128)S(1)}, u32[]{:S(2)}, u32[]{:S(2)}) %collective-permute-start.7) | collective-permute-done | bytes 131104 | tf_op jit(solution)/shard_map/ppermute | solution.py:503
  49.3 1.2 %advance_3.1 = (f32[16,128,128]{2,1,0:T(8,128)S(1)}, f32[128,128]{1,0:T(8,128)S(1)}, f32[128,128]{1,0:T(8,128)S(1)}, f32[16,128,128]{2,1,0:T(8,128)S(1)}) custom-call(f32[256,128]{1,0:T(8,128)S(1)} %collective-permute-done.6.refs_0_, f32[256,128]{1,0:T(8,128)S(1)} %collective-permute-done.7.refs_1_, ...), custom_call_target="tpu_custom_call" | custom-call | flops 100000000 | bytes 12890112 | tf_op jit(solution)/shard_map/advance_3/pallas_call | solution.py:479
  50.5 0.5 shrink.1
  51.1 5.2 %collective-permute-start.9 = (f32[144,128]{1,0:T(8,128)S(1)}, f32[144,128]{1,0:T(8,128)S(1)}, u32[]{:S(2)}, u32[]{:S(2)}) collective-permute-start(f32[144,128]{1,0:T(8,128)S(1)} %get-tuple-element.85), channel_id=1, source_target_pairs={{1,2},{3,4},{5,6},{7,8},{9,10},{11,12},{13,14},{15,16},{17,18},{19... | collective-permute-start | bytes 221192 | tf_op jit(solution)/shard_map/ppermute | solution.py:503
  56.3 4.1 %collective-permute-done.9.refs_2_.refs_1_ = f32[144,128]{1,0:T(8,128)S(1)} collective-permute-done((f32[144,128]{1,0:T(8,128)S(1)}, f32[144,128]{1,0:T(8,128)S(1)}, u32[]{:S(2)}, u32[]{:S(2)}) %collective-permute-start.9) | collective-permute-done | bytes 73760 | tf_op jit(solution)/shard_map/ppermute | solution.py:503
  60.4 3.1 %collective-permute-start.12 = (f32[72,512]{1,0:T(8,128)S(1)}, f32[72,512]{1,0:T(8,128)S(1)}, u32[]{:S(2)}, u32[]{:S(2)}) collective-permute-start(f32[72,512]{1,0:T(8,128)S(1)} %merge.1.refs_0_), channel_id=1, source_target_pairs={{0,192},{64,128},{128,64},{192,0},{1,193},{65,129},{129,65},{193,1... | collective-permute-start | bytes 442376 | tf_op jit(solution)/shard_map/ppermute | solution.py:497
  63.5 0.6 collective-permute-start.11
  64.6 0.8 inside_last.1.refs_4_
  65.8 2.0 %collective-permute-done.12.refs_3_ = f32[72,512]{1,0:T(8,128)S(1)} collective-permute-done((f32[72,512]{1,0:T(8,128)S(1)}, f32[72,512]{1,0:T(8,128)S(1)}, u32[]{:S(2)}, u32[]{:S(2)}) %collective-permute-start.12) | collective-permute-done | bytes 147488 | tf_op jit(solution)/shard_map/ppermute | solution.py:497
  67.8 2.4 %collective-permute-done.11.refs_2_ = f32[72,512]{1,0:T(8,128)S(1)} collective-permute-done((f32[72,512]{1,0:T(8,128)S(1)}, f32[72,512]{1,0:T(8,128)S(1)}, u32[]{:S(2)}, u32[]{:S(2)}) %collective-permute-start.11) | collective-permute-done | bytes 147488 | tf_op jit(solution)/shard_map/ppermute | solution.py:497
  70.3 5.1 %collective-permute-done.13.refs_1_ = f32[72,512]{1,0:T(8,128)S(1)} collective-permute-done((f32[72,512]{1,0:T(8,128)S(1)}, f32[72,512]{1,0:T(8,128)S(1)}, u32[]{:S(2)}, u32[]{:S(2)}) %collective-permute-start.13) | collective-permute-done | bytes 147488 | tf_op jit(solution)/shard_map/ppermute | solution.py:497
  75.6 1.2 %collective-permute-done.14 = f32[8,128]{1,0:T(8,128)S(1)} collective-permute-done((f32[8,128]{1,0:T(8,128)S(1)}, f32[8,128]{1,0:T(8,128)S(1)}, u32[]{:S(2)}, u32[]{:S(2)}) %collective-permute-start.14) | collective-permute-done | bytes 4128 | tf_op jit(solution)/shard_map/ppermute | solution.py:497
  76.8 0.7 spread.1
  77.5 4.4 %collective-permute-done.15.refs_1_ = f32[8,128]{1,0:T(8,128)S(1)} collective-permute-done((f32[8,128]{1,0:T(8,128)S(1)}, f32[8,128]{1,0:T(8,128)S(1)}, u32[]{:S(2)}, u32[]{:S(2)}) %collective-permute-start.15) | collective-permute-done | bytes 4128 | tf_op jit(solution)/shard_map/ppermute | solution.py:497
  81.9 10.4 %all_to_all.5.refs_0_ = f32[8,8,128]{2,1,0:T(8,128)S(1)} all-to-all(f32[8,8,128]{2,1,0:T(8,128)S(1)} %widen.1), channel_id=1, replica_groups=mesh['y'=4,'xl'=2,'xh'=2,'z'=8,'core'=2] {'z'}, dimensions={0} | all-to-all | bytes 65536 | tf_op jit(solution)/shard_map/all_to_all | solution.py:611
  92.3 1.7 %finish.1 = (f32[64,512]{1,0:T(8,128)}, f32[2048,128]{1,0:T(8,128)}) custom-call(f32[8,8,128]{2,1,0:T(8,128)S(1)} %all_to_all.5.refs_0_, f32[72,512]{1,0:T(8,128)S(1)} %get-tuple-element.90.refs_0_.refs_1_, f32[16,128,128]{2,1,0:T(8,128)S(1)} %get-tuple-element.91.refs_2_, f32[16,128,128]{2,1,0:T(8,128)S(1)} %get-tuple-element.92.refs_3_, ...), custom_call_target="tpu_custom_call" | custom-call | bytes 3325952 | tf_op jit(solution)/shard_map/finish/pallas_call | solution.py:479
  (55 shorter events, 1.9 us)
Async XLA Ops:
  0.6 10.2 %copy-start.3 = (f32[1,128,16,128]{3,2,1,0:T(8,128)S(1)}, f32[1,128,16,128]{3,2,1,0:T(8,128)}, u32[]{:S(2)}) copy-start(f32[1,128,16,128]{3,2,1,0:T(8,128)} %param.16) | copy-start | bytes 3145732
  0.6 10.2 %copy-start.4 = (f32[1,128,16,128]{3,2,1,0:T(8,128)S(1)}, f32[1,128,16,128]{3,2,1,0:T(8,128)}, u32[]{:S(2)}) copy-start(f32[1,128,16,128]{3,2,1,0:T(8,128)} %param.18) | copy-start | bytes 3145732
  0.6 10.2 %copy-start.8 = (bf16[256,256]{1,0:T(8,128)(2,1)S(1)}, bf16[256,256]{1,0:T(8,128)(2,1)}, u32[]{:S(2)}) copy-start(bf16[256,256]{1,0:T(8,128)(2,1)} %constant.18.clone.refs_6_.refs_3_.refs_2_) | copy-start | bytes 393220
  1.9 13.5 %collective-permute-start = (f32[264,128]{1,0:T(8,128)S(1)}, f32[264,128]{1,0:T(8,128)S(1)}, u32[]{:S(2)}, u32[]{:S(2)}) collective-permute-start(f32[264,128]{1,0:T(8,128)S(1)} %get-tuple-element.49), channel_id=1, source_target_pairs={{0,1},{1,0},{2,3},{3,2},{4,5},{5,4},{6,7},{7,6},{8,9},{9,8},{10,11... | collective-permute-start | bytes 405512 | tf_op jit(solution)/shard_map/ppermute | solution.py:497
  2.0 8.9 %copy-start.14 = (s32[1,64]{1,0:T(1,128)S(1)}, s32[1,64]{1,0:T(1,128)}, u32[]{:S(2)}) copy-start(s32[1,64]{1,0:T(1,128)} %param.21) | copy-start | bytes 772
  2.0 8.9 %copy-start.15 = (s32[64]{0:T(128)S(1)}, s32[64]{0:T(128)}, u32[]{:S(2)}) copy-start(s32[64]{0:T(128)} %refs_1_.2) | copy-start | bytes 772
  2.0 8.9 %copy-start.16 = (f32[5]{0:T(128)S(1)}, f32[5]{0:T(128)}, u32[]{:S(2)}) copy-start(f32[5]{0:T(128)} %refs_2_.5) | copy-start | bytes 64
  2.0 13.4 %collective-permute-start.1 = (f32[264,128]{1,0:T(8,128)S(1)}, f32[264,128]{1,0:T(8,128)S(1)}, u32[]{:S(2)}, u32[]{:S(2)}) collective-permute-start(f32[264,128]{1,0:T(8,128)S(1)} %get-tuple-element.50), channel_id=1, source_target_pairs={{1,2},{3,4},{5,6},{7,8},{9,10},{11,12},{13,14},{15,16},{17,18},{19... | collective-permute-start | bytes 405512 | tf_op jit(solution)/shard_map/ppermute | solution.py:503
  10.9 0.9 copy-start.9
  11.8 3.6 %copy-start.5 = (bf16[256,256]{1,0:T(8,128)(2,1)S(1)}, bf16[256,256]{1,0:T(8,128)(2,1)}, u32[]{:S(2)}) copy-start(bf16[256,256]{1,0:T(8,128)(2,1)} %constant.19.clone.refs_3_.refs_4_) | copy-start | bytes 393220
  11.8 3.7 %copy-start.6 = (f32[64,512]{1,0:T(8,128)S(1)}, f32[64,512]{1,0:T(8,128)}, u32[]{:S(2)}) copy-start(f32[64,512]{1,0:T(8,128)} %refs_0_.1) | copy-start | bytes 393220
  11.8 3.7 %copy-start.11 = (bf16[2,128,144]{2,1,0:T(8,128)(2,1)S(1)}, bf16[2,128,144]{2,1,0:T(8,128)(2,1)}, u32[]{:S(2)}) copy-start(bf16[2,128,144]{2,1,0:T(8,128)(2,1)} %constant.21.clone.refs_4_) | copy-start | bytes 221188
  11.8 4.2 %copy-start.1 = (f32[1,128,16,128]{3,2,1,0:T(8,128)S(1)}, f32[1,128,16,128]{3,2,1,0:T(8,128)}, u32[]{:S(2)}) copy-start(f32[1,128,16,128]{3,2,1,0:T(8,128)} %param.17) | copy-start | bytes 3145732
  11.8 4.2 %copy-start.2 = (f32[1,128,16,128]{3,2,1,0:T(8,128)S(1)}, f32[1,128,16,128]{3,2,1,0:T(8,128)}, u32[]{:S(2)}) copy-start(f32[1,128,16,128]{3,2,1,0:T(8,128)} %param.19) | copy-start | bytes 3145732
  17.5 6.8 %collective-permute-start.2 = (f32[256,128]{1,0:T(8,128)S(1)}, f32[256,128]{1,0:T(8,128)S(1)}, u32[]{:S(2)}, u32[]{:S(2)}) collective-permute-start(f32[256,128]{1,0:T(8,128)S(1)} %get-tuple-element.58), channel_id=1, source_target_pairs={{0,1},{1,0},{2,3},{3,2},{4,5},{5,4},{6,7},{7,6},{8,9},{9,8},{10,11... | collective-permute-start | bytes 393224 | tf_op jit(solution)/shard_map/ppermute | solution.py:497
  17.6 9.9 %collective-permute-start.3 = (f32[256,128]{1,0:T(8,128)S(1)}, f32[256,128]{1,0:T(8,128)S(1)}, u32[]{:S(2)}, u32[]{:S(2)}) collective-permute-start(f32[256,128]{1,0:T(8,128)S(1)} %get-tuple-element.59), channel_id=1, source_target_pairs={{1,2},{3,4},{5,6},{7,8},{9,10},{11,12},{13,14},{15,16},{17,18},{19... | collective-permute-start | bytes 393224 | tf_op jit(solution)/shard_map/ppermute | solution.py:503
  28.3 6.8 %collective-permute-start.4 = (f32[256,128]{1,0:T(8,128)S(1)}, f32[256,128]{1,0:T(8,128)S(1)}, u32[]{:S(2)}, u32[]{:S(2)}) collective-permute-start(f32[256,128]{1,0:T(8,128)S(1)} %get-tuple-element.64), channel_id=1, source_target_pairs={{0,1},{1,0},{2,3},{3,2},{4,5},{5,4},{6,7},{7,6},{8,9},{9,8},{10,11... | collective-permute-start | bytes 393224 | tf_op jit(solution)/shard_map/ppermute | solution.py:497
  28.4 9.9 %collective-permute-start.5 = (f32[256,128]{1,0:T(8,128)S(1)}, f32[256,128]{1,0:T(8,128)S(1)}, u32[]{:S(2)}, u32[]{:S(2)}) collective-permute-start(f32[256,128]{1,0:T(8,128)S(1)} %get-tuple-element.65), channel_id=1, source_target_pairs={{1,2},{3,4},{5,6},{7,8},{9,10},{11,12},{13,14},{15,16},{17,18},{19... | collective-permute-start | bytes 393224 | tf_op jit(solution)/shard_map/ppermute | solution.py:503
  38.3 6.4 %copy-start.10 = (bf16[256,256]{1,0:T(8,128)(2,1)S(1)}, bf16[256,256]{1,0:T(8,128)(2,1)}, u32[]{:S(2)}) copy-start(bf16[256,256]{1,0:T(8,128)(2,1)} %constant.16.clone.refs_5_.refs_2_.refs_1_) | copy-start | bytes 393220
  39.3 6.9 %collective-permute-start.6 = (f32[256,128]{1,0:T(8,128)S(1)}, f32[256,128]{1,0:T(8,128)S(1)}, u32[]{:S(2)}, u32[]{:S(2)}) collective-permute-start(f32[256,128]{1,0:T(8,128)S(1)} %get-tuple-element.71), channel_id=1, source_target_pairs={{0,1},{1,0},{2,3},{3,2},{4,5},{5,4},{6,7},{7,6},{8,9},{9,8},{10,11... | collective-permute-start | bytes 393224 | tf_op jit(solution)/shard_map/ppermute | solution.py:497
  39.4 9.9 %collective-permute-start.7 = (f32[256,128]{1,0:T(8,128)S(1)}, f32[256,128]{1,0:T(8,128)S(1)}, u32[]{:S(2)}, u32[]{:S(2)}) collective-permute-start(f32[256,128]{1,0:T(8,128)S(1)} %get-tuple-element.72), channel_id=1, source_target_pairs={{1,2},{3,4},{5,6},{7,8},{9,10},{11,12},{13,14},{15,16},{17,18},{19... | collective-permute-start | bytes 393224 | tf_op jit(solution)/shard_map/ppermute | solution.py:503
  49.3 1.2 %copy-start.12 = (bf16[512,128]{1,0:T(8,128)(2,1)S(1)}, bf16[512,128]{1,0:T(8,128)(2,1)}, u32[]{:S(2)}) copy-start(bf16[512,128]{1,0:T(8,128)(2,1)} %constant.20.clone.refs_4_) | copy-start | bytes 393220
  49.3 1.2 %copy-start.13 = (bf16[2,72,256]{2,1,0:T(8,128)(2,1)S(1)}, bf16[2,72,256]{2,1,0:T(8,128)(2,1)}, u32[]{:S(2)}) copy-start(bf16[2,72,256]{2,1,0:T(8,128)(2,1)} %constant.23.clone.refs_3_) | copy-start | bytes 221188
  51.0 5.3 %collective-permute-start.8 = (f32[144,128]{1,0:T(8,128)S(1)}, f32[144,128]{1,0:T(8,128)S(1)}, u32[]{:S(2)}, u32[]{:S(2)}) collective-permute-start(f32[144,128]{1,0:T(8,128)S(1)} %get-tuple-element.84), channel_id=1, source_target_pairs={{0,1},{1,0},{2,3},{3,2},{4,5},{5,4},{6,7},{7,6},{8,9},{9,8},{10,11... | collective-permute-start | bytes 221192 | tf_op jit(solution)/shard_map/ppermute | solution.py:497
  51.1 9.3 %collective-permute-start.9 = (f32[144,128]{1,0:T(8,128)S(1)}, f32[144,128]{1,0:T(8,128)S(1)}, u32[]{:S(2)}, u32[]{:S(2)}) collective-permute-start(f32[144,128]{1,0:T(8,128)S(1)} %get-tuple-element.85), channel_id=1, source_target_pairs={{1,2},{3,4},{5,6},{7,8},{9,10},{11,12},{13,14},{15,16},{17,18},{19... | collective-permute-start | bytes 221192 | tf_op jit(solution)/shard_map/ppermute | solution.py:503
  60.4 7.4 %collective-permute-start.12 = (f32[72,512]{1,0:T(8,128)S(1)}, f32[72,512]{1,0:T(8,128)S(1)}, u32[]{:S(2)}, u32[]{:S(2)}) collective-permute-start(f32[72,512]{1,0:T(8,128)S(1)} %merge.1.refs_0_), channel_id=1, source_target_pairs={{0,192},{64,128},{128,64},{192,0},{1,193},{65,129},{129,65},{193,1... | collective-permute-start | bytes 442376 | tf_op jit(solution)/shard_map/ppermute | solution.py:497
  63.5 6.6 %collective-permute-start.11 = (f32[72,512]{1,0:T(8,128)S(1)}, f32[72,512]{1,0:T(8,128)S(1)}, u32[]{:S(2)}, u32[]{:S(2)}) collective-permute-start(f32[72,512]{1,0:T(8,128)S(1)} %merge.1.refs_0_), channel_id=1, source_target_pairs={{0,128},{64,192},{128,0},{192,64},{1,129},{65,193},{129,1},{193,65... | collective-permute-start | bytes 442376 | tf_op jit(solution)/shard_map/ppermute | solution.py:497
  64.2 6.0 %collective-permute-start.10 = (f32[72,512]{1,0:T(8,128)S(1)}, f32[72,512]{1,0:T(8,128)S(1)}, u32[]{:S(2)}, u32[]{:S(2)}) collective-permute-start(f32[72,512]{1,0:T(8,128)S(1)} %merge.1.refs_0_), channel_id=1, source_target_pairs={{0,64},{64,0},{128,192},{192,128},{1,65},{65,1},{129,193},{193,129... | collective-permute-start | bytes 442376 | tf_op jit(solution)/shard_map/ppermute | solution.py:497
  70.2 6.6 %copy-start.7 = (bf16[2,128,144]{2,1,0:T(8,128)(2,1)S(1)}, bf16[2,128,144]{2,1,0:T(8,128)(2,1)}, u32[]{:S(2)}) copy-start(bf16[2,128,144]{2,1,0:T(8,128)(2,1)} %constant.22.clone.refs_5_) | copy-start | bytes 221188
  70.2 5.2 %collective-permute-start.13 = (f32[72,512]{1,0:T(8,128)S(1)}, f32[72,512]{1,0:T(8,128)S(1)}, u32[]{:S(2)}, u32[]{:S(2)}) collective-permute-start(f32[72,512]{1,0:T(8,128)S(1)} %add_four.1.refs_0_), channel_id=1, source_target_pairs={{0,32},{32,0},{1,33},{33,1},{2,34},{34,2},{3,35},{35,3},{4,36},{36... | collective-permute-start | bytes 442376 | tf_op jit(solution)/shard_map/ppermute | solution.py:497
  75.5 1.3 %collective-permute-start.14 = (f32[8,128]{1,0:T(8,128)S(1)}, f32[8,128]{1,0:T(8,128)S(1)}, u32[]{:S(2)}, u32[]{:S(2)}) collective-permute-start(f32[8,128]{1,0:T(8,128)S(1)} %get-tuple-element.89), channel_id=1, source_target_pairs={{0,1},{1,0},{2,3},{3,2},{4,5},{5,4},{6,7},{7,6},{8,9},{9,8},{10,11... | collective-permute-start | bytes 12296 | tf_op jit(solution)/shard_map/ppermute | solution.py:497
  76.8 5.1 %collective-permute-start.15 = (f32[8,128]{1,0:T(8,128)S(1)}, f32[8,128]{1,0:T(8,128)S(1)}, u32[]{:S(2)}, u32[]{:S(2)}) collective-permute-start(f32[8,128]{1,0:T(8,128)S(1)} %add.3.refs_0_), channel_id=1, source_target_pairs={{0,16},{16,0},{1,17},{17,1},{2,18},{18,2},{3,19},{19,3},{4,20},{20... | collective-permute-start | bytes 12296 | tf_op jit(solution)/shard_map/ppermute | solution.py:497
  (1 other events, 0.8 us)

commit v2 on v1

--- a/solution.py
+++ b/solution.py
@@ -48,6 +48,11 @@
     return high, low
 
 
+def narrow_band(matrix):
+    high, low = halves(np.pad(matrix, ((0, OV), (0, OV))))
+    return np.concatenate([high, high, low], axis=1)
+
+
 @functools.cache
 def constants():
     out = {}
@@ -62,6 +67,14 @@
         high, low = halves(np.concatenate(pair, axis=1))
         sides.append(np.concatenate([high, high, low], axis=1))
     out["halo_x"] = np.stack(sides)
+    near_part, cross_part = [], []
+    for core in range(2):
+        rows = slice(0, OV) if core == 0 else slice(CX - OV, CX)
+        near_part.append(narrow_band((right if core == 0 else left)[rows]))
+        rows = slice(CX - OV, CX) if core == 0 else slice(0, OV)
+        cross_part.append(narrow_band((right if core == 0 else left)[rows]))
+    out["near_x"] = np.stack(near_part)
+    out["cross_x"] = np.stack(cross_part)
     high, low = halves(spectral_second(CZ) - 2.0 * np.eye(CZ))
     out["own_z"] = np.block([[high, low], [high, np.zeros_like(low)]])
 
@@ -78,8 +91,8 @@
         [[weight_z, zero], [weight_z, zero], [zero, weight_z], [zero, weight_z]]
     )
 
-    def column(coarse):
-        return spline_units((np.arange(CX) - 2 * coarse - 0.5) * 0.5)
+    def column(coarse, start=0, count=CX):
+        return spline_units((np.arange(start, start + count) - 2 * coarse - 0.5) * 0.5)
 
     own = np.stack([column(j) for j in range(CXC)], axis=1)
     lower = {j: column(j) for j in (-2, -1, 0, 1)}
@@ -90,8 +103,15 @@
     inner[:, [0, 1, 62, 63]] = 0.0
     for core in range(2):
         near, far = (upper, lower) if core == 0 else (lower, upper)
-        outside = lambda d: np.stack([d[j] for j in sorted(d) if j < 0 or j > 63], axis=1)
-        old = np.concatenate([own, outside(near), outside(far), np.zeros((CX, 4))], axis=1)
+        near_two, far_six = ((64, 65), range(-6, 0)) if core == 0 else ((-2, -1), range(64, 70))
+        beyond = -OV if core == 0 else CX
+        old = np.stack(
+            [
+                np.concatenate([column(j), column(j, beyond, OV)])
+                for j in (*range(CXC), *near_two, *far_six)
+            ],
+            axis=1,
+        )
         new = np.concatenate([inner, stack(near), stack(far)], axis=1)
         every = np.concatenate([own, stack(near), stack(far)], axis=1)
         grow_old.append(np.concatenate([old, old], axis=1))
@@ -163,7 +183,8 @@
     for y in range(CY):
         start = (field * CY + y) * OV
         near[start : start + OV] = v[y, pl.ds(near_row, OV), :]
-        far[start : start + OV] = v[y, pl.ds(far_row, OV), :]
+        if far is not None:
+            far[start : start + OV] = v[y, pl.ds(far_row, OV), :]
 
 
 def first_edges(p, q, coef, near, far, p_lo, p_hi, q_lo, q_hi, c_lo, c_hi, sems):
@@ -202,13 +223,16 @@
     copies[4].wait()
     copies[5].wait()
     base = 2 * CY * OV
-    for row in range(2):
+    for row in range(6):
         for part in range(4):
             lanes = slice(part * 128, part * 128 + 128)
+            spot = base + row * 4 + part
+            if row < 2:
+                first = c_lo[row : row + 1, lanes]
+                last = c_hi[6 + row : 7 + row, lanes]
+                near[spot : spot + 1] = jnp.where(core == 0, last, first)
             first = c_lo[row : row + 1, lanes]
-            last = c_hi[6 + row : 7 + row, lanes]
-            spot = base + row * 4 + part
-            near[spot : spot + 1] = jnp.where(core == 0, last, first)
+            last = c_hi[2 + row : 3 + row, lanes]
             far[spot : spot + 1] = jnp.where(core == 0, first, last)
 
 
@@ -266,22 +290,32 @@
 UNIT = 1.0 / 384.0**3
 
 
-def speed(coef, near, far, grow_z, grow_old, sigma, squared, held):
+def grid_ends():
+    core = lax.axis_index("core")
+    chip = lax.axis_index("xh") * lax.axis_size("z") + lax.axis_index("z")
+    chips = lax.axis_size("xh") * lax.axis_size("z")
+    return (core == 0) & (chip == 0), (core == 1) & (chip == chips - 1)
+
+
+def speed(coef, near, far, grow_z, grow_old, sigma, squared, beyond, held):
     core = lax.axis_index("core")
     held[:CXC] = coef[...]
-    held[CXC:] = jnp.zeros((ROWS - CXC, CYC * CZC), F32)
     base = 2 * CY * OV
-    for row in range(2):
+    for row in range(6):
         for part in range(4):
             lanes = slice(part * 128, part * 128 + 128)
             spot = base + row * 4 + part
-            held[CXC + row : CXC + row + 1, lanes] = near[spot : spot + 1]
+            if row < 2:
+                held[CXC + row : CXC + row + 1, lanes] = near[spot : spot + 1]
             held[CXC + 2 + row : CXC + 3 + row, lanes] = far[spot : spot + 1]
+    first, last = grid_ends()
 
     def write(y, fine):
         fine = fine * UNIT
-        sigma[y] = fine
-        squared[y] = fine * fine
+        square = fine * fine
+        sigma[y] = fine[:CX]
+        squared[y] = square[:CX]
+        beyond[y * OV : y * OV + OV] = jnp.where(first | last, 0.0, square[CX:])
 
     grow(held[...], grow_z, grow_old[core], write)
 
@@ -292,15 +326,19 @@
     core = lax.axis_index("core")
     columns = halo_x[core]
     weight = amounts[step, :1, :]
+    if step == 1:
+        (sent, beyond, cross_x), refs = refs[:3], refs[3:]
+        cross = cross_x[core]
     if step == 2:
         old_lap, refs = refs[0], refs[1:]
     if step == 3:
         (old_lap, older_q, gathered, sigma), refs = refs[:4], refs[4:]
-    if step < 3:
-        p_new, q_new, near_out, far_out = refs[:4]
+    if step == 0:
+        (p_new, q_new, near_out), refs = refs[:3], refs[3:]
+    elif step < 3:
+        (p_new, q_new, near_out, far_out), refs = refs[:4], refs[4:]
     else:
         p_new, near_out, far_out, image = refs[:4]
-    refs = refs[4:]
     if step < 2:
         lap_out = refs[0]
     if step == 2:
@@ -330,9 +368,55 @@
             if step == 3:
                 total = gathered[y] + older_q[y] * lap + new_q * old_lap[y]
                 image[y] = 2.0 * sigma[y] * total
-    edge_rows(p_new, core, near_out, far_out, 0)
+    if step == 0 or step == 1:
+        far_out_used = None
+    else:
+        far_out_used = far_out
+    edge_rows(p_new, core, near_out, far_out_used, 0)
     if step < 3:
-        edge_rows(q_new, core, near_out, far_out, 1)
+        edge_rows(q_new, core, near_out, far_out_used, 1)
+    if step == 1:
+        size = CY * OV
+        for pair in range(CY // 2):
+            for field in range(2):
+                extra = halo_part(sent, sent, field, cross, pair)
+                for side in range(2):
+                    spot = (2 * pair + side) * OV
+                    known = far[(2 + field) * size + spot : (2 + field) * size + spot + OV]
+                    far_out[field * size + spot : field * size + spot + OV] = (
+                        known
+                        + beyond[spot : spot + OV] * extra[:OV, side * CZ : side * CZ + CZ]
+                    )
+
+
+def early(
+    near, p, p_before, q, q_before, lap_p, lap_q, squared, source, amounts, near_x, out,
+):
+    core = lax.axis_index("core")
+    row = pl.multiple_of(core * (CX - OV), OV)
+    weight = amounts[1, :1, :]
+    columns = near_x[core]
+    size = CY * OV
+    for pair in range(CY // 2):
+        extra_p = halo_part(near, near, 0, columns, pair)
+        extra_q = halo_part(near, near, 1, columns, pair)
+        for side in range(2):
+            y = 2 * pair + side
+            rows = pl.ds(row, OV)
+            lanes = slice(side * CZ, side * CZ + CZ)
+            sq = squared[y, rows, :]
+            lap = lap_p[y, rows, :] + extra_p[:OV, lanes]
+            lap_adj = lap_q[y, rows, :] + extra_q[:OV, lanes]
+            edge_p, edge_q = p[y, rows, :], q[y, rows, :]
+            spot = y * OV
+            out[spot : spot + OV] = edge_p
+            out[size + spot : size + spot + OV] = edge_q
+            out[2 * size + spot : 2 * size + spot + OV] = (
+                2.0 * edge_p - p_before[y, rows, :] + sq * lap + source[y, rows, :] * weight
+            )
+            out[3 * size + spot : 3 * size + spot + OV] = (
+                2.0 * edge_q - q_before[y, rows, :] + sq * lap_adj
+            )
 
 
 def inside(p, q, own_x, own_z, lap_p, lap_q):
@@ -390,10 +474,7 @@
 def squares(a, b, total, squared):
     core = lax.axis_index("core")
     total[...] = a[...] + b[...]
-    chip = lax.axis_index("xh") * lax.axis_size("z") + lax.axis_index("z")
-    chips = lax.axis_size("xh") * lax.axis_size("z")
-    first = (core == 0) & (chip == 0)
-    last = (core == 1) & (chip == chips - 1)
+    first, last = grid_ends()
     total[CXC + 4 : CXC + 6] = jnp.where(first, 0.0, total[CXC + 4 : CXC + 6])
     total[CXC + 6 : CXC + 8] = jnp.where(last, 0.0, total[CXC + 6 : CXC + 8])
     total[0:2] = jnp.where(core == 0, total[CXC + 6 : CXC + 8], total[CXC + 2 : CXC + 4])
@@ -516,12 +597,12 @@
     p_now, p_prev, adj_now, adj_next = map(flat, (p_now, p_prev, adj_now, adj_next))
 
     edge = rows_of(2 * CY * OV)
-    with_coef = rows_of(2 * CY * OV + 8)
+    with_two, with_six = rows_of(2 * CY * OV + 8), rows_of(2 * CY * OV + 24)
     block = pltpu.VMEM((OV * CY, CZ), F32)
     few = pltpu.VMEM((8, CYC * CZC), F32)
     near, far = pl.pallas_call(
         first_edges,
-        out_shape=(with_coef, with_coef),
+        out_shape=(with_two, with_six),
         in_specs=[pl.BlockSpec(memory_space=pltpu.HBM)] * 3,
         out_specs=(VM, VM),
         scratch_shapes=[block] * 4 + [few] * 2 + [pltpu.SemaphoreType.DMA((6,))],
@@ -536,8 +617,8 @@
         signs[0], elem_index, wavelet, p_now, adj_now, own_x, own_z,
         smem=3, flops=10**9, name="prepare",
     )
-    sigma, squared = call(
-        speed, (FIELD, FIELD), coef_old, near, far, const["grow_z"], const["grow_old"],
+    sigma, squared, beyond = call(
+        speed, (FIELD, FIELD, rows_of(CY * OV)), coef_old, near, far, const["grow_z"], const["grow_old"],
         scratch=[pltpu.VMEM((ROWS, CYC * CZC), F32)], flops=10**8, name="speed",
     )
 
@@ -548,7 +629,10 @@
         args = [near, far, p, p_before, q, q_before, lap_p, lap_q, squared, source, amounts, halo_x]
         body = functools.partial(advance, step)
         name = f"advance_{step}"
-        if step < 2:
+        if step == 0:
+            outs = (FIELD, FIELD, edge, FIELD)
+        elif step == 1:
+            args += [sent, beyond, const["cross_x"]]
             outs = (FIELD, FIELD, edge, edge, FIELD)
         elif step == 2:
             args.append(laps[1])
@@ -557,22 +641,33 @@
             args += [laps[0], qs[1], gathered, sigma]
             outs = (FIELD, rows_of(CY * OV), rows_of(CY * OV), FIELD)
         result = call(body, outs, *args, flops=10**8, name=name)
-        if step < 3:
-            p_new, q_new, near, far, other = result
-            if step < 2:
-                laps.append(other)
-            else:
-                gathered = other
-            p, p_before = p_new, p
-            q, q_before = q_new, q
-            qs.append(q)
-            near, far = exchange(near, far)
-            lap_p, lap_q = call(
-                inside, (FIELD, FIELD), p, q, own_x, own_z, flops=10**9, name=f"inside_{step}"
-            )
-        else:
+        if step == 3:
             p_new, near, far, image = result
             p, p_before = p_new, p
+            continue
+        p_new, q_new, *edges, other = result
+        if step < 2:
+            laps.append(other)
+        else:
+            gathered = other
+        p, p_before = p_new, p
+        q, q_before = q_new, q
+        qs.append(q)
+        if step == 2:
+            near, far = exchange(*edges)
+        else:
+            near = xor_swap(edges[0], "core", 1)
+        lap_p, lap_q = call(
+            inside, (FIELD, FIELD), p, q, own_x, own_z, flops=10**9, name=f"inside_{step}"
+        )
+        if step == 0:
+            sent = call(
+                early, rows_of(4 * CY * OV), near, p, p_before, q, q_before, lap_p, lap_q,
+                squared, source, amounts, const["near_x"], flops=10**7, name="early",
+            )
+            far = far_swap(sent)
+        elif step == 1:
+            far = edges[1]
 
     ends = rows_of(CY * OV + 16)
     own, near, far = call(

time: 94.3 us -> 89.4 us (0.948)
  starting transfers between devices: 34.4 us -> 27.4 us
  waiting for transfers between devices: 28.6 us -> 29.9 us
    ppermute x5 -> x4, starting transfers between devices: 29.6 us -> 22 us  [far_swap(): return lax.ppermute(x, TILE, pairs + [(b, a) for a, b in pairs])]
    ppermute x5 -> x4, waiting for transfers between devices: 13.6 us -> 15 us  [far_swap(): return lax.ppermute(x, TILE, pairs + [(b, a) for a, b in pairs])]
    pallas_call x18 -> x19, Pallas kernels: 17.1 us -> 17.4 us  [call(): pl.pallas_call(run, out_shape=outs, in_specs=[SM] * smem + [VM] * (count...]
  transfers between devices with their start and end apart: 16 -> 15, of which waited for: 9 -> 8; matrix products, arithmetic and copies ran while one was open for 0% -> 0% of each run, Pallas kernels for 11% -> 11%
where the time goes in v2:
time: 89.4 us; the launch traced here: 89 us
  waiting for transfers between devices  29.9 us (33%)
  starting transfers between devices  27.4 us (31%)
  Pallas kernels  18.6 us (21%)
  blocking collectives  10.4 us (12%)
  local copies, waits for them, and re-layouts  1.68 us (2%)
  between operations  1.05 us (1%)
    ppermute x4, starting transfers between devices, far_swap(): return lax.ppermute(x, TILE, pairs + [(b, a) for a, b in pairs])  22 us
    pallas_call x19, Pallas kernels, call(): pl.pallas_call(run, out_shape=outs, in_specs=[SM] * smem + [VM] * (count...  17.4 us
    ppermute x4, waiting for transfers between devices, far_swap(): return lax.ppermute(x, TILE, pairs + [(b, a) for a, b in pairs])  15 us
    ppermute x11, waiting for transfers between devices, xor_swap(): return lax.ppermute(x, axis, [(i, i ^ mask) for i in range(count)])  14.9 us
    all_to_all x1, blocking collectives, on_device(): parts = lax.all_to_all(copies, 'z', split_axis=0, concat_axis=0, tiled=True)  10.4 us
    ppermute x11, starting transfers between devices, xor_swap(): return lax.ppermute(x, axis, [(i, i ^ mask) for i in range(count)])  5.35 us
  transfers between devices with their start and end apart: 15, of which 8 were waited for; matrix products, arithmetic and copies ran while one was open for 0% of the time, Pallas kernels for 11%

profile of v2, /device:TPU:6, one launch (start us, length us, event | category | flops | bytes accessed | tf_op | source)
XLA Modules:
  0.0 89.0 jit_solution(12412181994614395150)
XLA Ops:
  0.7 1.2 %first_edges.1 = (f32[264,128]{1,0:T(8,128)S(1)}, f32[280,128]{1,0:T(8,128)S(1)}) custom-call(f32[2048,128]{1,0:T(8,128)} %bitcast.6, f32[2048,128]{1,0:T(8,128)} %bitcast.8, f32[64,512]{1,0:T(8,128)} %refs_0_.1), custom_call_target="tpu_custom_call" | custom-call | tf_op jit(solution)/shard_map/first_edges/pallas_call | solution.py:603
  1.9 8.0 %collective-permute-start.1 = (f32[280,128]{1,0:T(8,128)S(1)}, f32[280,128]{1,0:T(8,128)S(1)}, u32[]{:S(2)}, u32[]{:S(2)}) collective-permute-start(f32[280,128]{1,0:T(8,128)S(1)} %get-tuple-element.50), channel_id=1, source_target_pairs={{1,2},{3,4},{5,6},{7,8},{9,10},{11,12},{13,14},{15,16},{17,18},{19... | collective-permute-start | bytes 430088 | tf_op jit(solution)/shard_map/ppermute | solution.py:584
  10.6 0.9 %copy-done.10 = bf16[256,256]{1,0:T(8,128)(2,1)S(1)} copy-done((bf16[256,256]{1,0:T(8,128)(2,1)S(1)}, bf16[256,256]{1,0:T(8,128)(2,1)}, u32[]{:S(2)}) %copy-start.10) | copy-done | bytes 131096
  11.5 3.6 %prepare.1 = (f32[16,128,128]{2,1,0:T(8,128)S(1)}, f32[16,128,128]{2,1,0:T(8,128)S(1)}, f32[16,128,128]{2,1,0:T(8,128)S(1)}, f32[16,128,128]{2,1,0:T(8,128)S(1)}...) custom-call(s32[64]{0:T(128)S(1)} %bitcast.12, s32[64]{0:T(128)S(1)} %copy-done.17, f32[5]{0:T(128)S(1)} %copy-done.18, ...), custom_call_target="tpu_custom_call" | custom-call | flops 1000000000 | bytes 2359828 | tf_op jit(solution)/shard_map/prepare/pallas_call | solution.py:560
  15.2 0.6 speed.1
  16.0 1.3 %advance_0.1 = (f32[16,128,128]{2,1,0:T(8,128)S(1)}, f32[16,128,128]{2,1,0:T(8,128)S(1)}, f32[256,128]{1,0:T(8,128)S(1)}, f32[16,128,128]{2,1,0:T(8,128)S(1)}) custom-call(f32[264,128]{1,0:T(8,128)S(1)} %collective-permute-done.refs_1_.refs_0_, f32[280,128]{1,0:T(8,128)S(1)} %collective-permute-done.1.refs_2_.refs_1_, ...), custom_call_target="tpu_custom_call" | custom-call | flops 100000000 | bytes 8712192 | tf_op jit(solution)/shard_map/advance_0/pallas_call | solution.py:560
  17.4 1.5 %inside_0.1 = (f32[16,128,128]{2,1,0:T(8,128)S(1)}, f32[16,128,128]{2,1,0:T(8,128)S(1)}) custom-call(f32[16,128,128]{2,1,0:T(8,128)S(1)} %get-tuple-element.59.refs_0_.refs_1_.refs_2_.refs_3_, f32[16,128,128]{2,1,0:T(8,128)S(1)} %get-tuple-element.60.refs_1_.refs_3_.refs_4_.refs_5_.refs_13_, bf16[256,256]{1,0:T(8,128)(2,1)S(1)} %copy-done.10, ...), custom_call_target="tpu_custom_call" | custom-call | flops 1000000000 | bytes 2359296 | tf_op jit(solution)/shard_map/inside_0/pallas_call | solution.py:560
  19.2 4.6 %collective-permute-start.3 = (f32[512,128]{1,0:T(8,128)S(1)}, f32[512,128]{1,0:T(8,128)S(1)}, u32[]{:S(2)}, u32[]{:S(2)}) collective-permute-start(f32[512,128]{1,0:T(8,128)S(1)} %early.1.refs_12_), channel_id=1, source_target_pairs={{1,2},{3,4},{5,6},{7,8},{9,10},{11,12},{13,14},{15,16},{17,18},{19... | collective-permute-start | bytes 786440 | tf_op jit(solution)/shard_map/ppermute | solution.py:584
  23.8 6.7 %collective-permute-done.3.refs_1_ = f32[512,128]{1,0:T(8,128)S(1)} collective-permute-done((f32[512,128]{1,0:T(8,128)S(1)}, f32[512,128]{1,0:T(8,128)S(1)}, u32[]{:S(2)}, u32[]{:S(2)}) %collective-permute-start.3) | collective-permute-done | bytes 262176 | tf_op jit(solution)/shard_map/ppermute | solution.py:584
  30.5 0.9 advance_1.1
  31.4 1.5 %inside_1.1 = (f32[16,128,128]{2,1,0:T(8,128)S(1)}, f32[16,128,128]{2,1,0:T(8,128)S(1)}) custom-call(f32[16,128,128]{2,1,0:T(8,128)S(1)} %get-tuple-element.66.refs_0_.refs_2_.refs_3_, f32[16,128,128]{2,1,0:T(8,128)S(1)} %get-tuple-element.67.refs_1_.refs_4_.refs_5_, bf16[256,256]{1,0:T(8,128)(2,1)S(1)} %copy-done.10, bf16[256,256]{1,0:T(8,128)(2,1)S(1)} %copy-done.9), custom_call_target="tpu_custom_call" | custom-call | flops 1000000000 | bytes 2359296 | tf_op jit(solution)/shard_map/inside_1/pallas_call | solution.py:560
  33.0 0.9 %advance_2.1 = (f32[16,128,128]{2,1,0:T(8,128)S(1)}, f32[16,128,128]{2,1,0:T(8,128)S(1)}, f32[256,128]{1,0:T(8,128)S(1)}, f32[256,128]{1,0:T(8,128)S(1)}, f32[16,128,128]{2,1,0:T(8,128)S(1)}) custom-call(f32[256,128]{1,0:T(8,128)S(1)} %collective-permute-done.4.refs_0_, f32[256,128]{1,0:T(8,128)S(1)} %get-tuple-element.65.refs_1_, ...), custom_call_target="tpu_custom_call" | custom-call | flops 100000000 | bytes 9744384 | tf_op jit(solution)/shard_map/advance_2/pallas_call | solution.py:560
  33.9 0.6 collective-permute-start.5
  34.5 4.8 %collective-permute-start.6 = (f32[256,128]{1,0:T(8,128)S(1)}, f32[256,128]{1,0:T(8,128)S(1)}, u32[]{:S(2)}, u32[]{:S(2)}) collective-permute-start(f32[256,128]{1,0:T(8,128)S(1)} %get-tuple-element.72), channel_id=1, source_target_pairs={{1,2},{3,4},{5,6},{7,8},{9,10},{11,12},{13,14},{15,16},{17,18},{19... | collective-permute-start | bytes 393224 | tf_op jit(solution)/shard_map/ppermute | solution.py:584
  39.2 1.5 %inside_2.1 = (f32[16,128,128]{2,1,0:T(8,128)S(1)}, f32[16,128,128]{2,1,0:T(8,128)S(1)}) custom-call(f32[16,128,128]{2,1,0:T(8,128)S(1)} %get-tuple-element.73.refs_0_.refs_2_.refs_3_, f32[16,128,128]{2,1,0:T(8,128)S(1)} %get-tuple-element.74.refs_1_.refs_4_, bf16[256,256]{1,0:T(8,128)(2,1)S(1)} %copy-done.10, bf16[256,256]{1,0:T(8,128)(2,1)S(1)} %copy-done.9), custom_call_target="tpu_custom_call" | custom-call | flops 1000000000 | bytes 2359296 | tf_op jit(solution)/shard_map/inside_2/pallas_call | solution.py:560
  40.8 3.6 %collective-permute-done.6.refs_1_ = f32[256,128]{1,0:T(8,128)S(1)} collective-permute-done((f32[256,128]{1,0:T(8,128)S(1)}, f32[256,128]{1,0:T(8,128)S(1)}, u32[]{:S(2)}, u32[]{:S(2)}) %collective-permute-start.6) | collective-permute-done | bytes 131104 | tf_op jit(solution)/shard_map/ppermute | solution.py:584
  44.3 1.1 %advance_3.1 = (f32[16,128,128]{2,1,0:T(8,128)S(1)}, f32[128,128]{1,0:T(8,128)S(1)}, f32[128,128]{1,0:T(8,128)S(1)}, f32[16,128,128]{2,1,0:T(8,128)S(1)}) custom-call(f32[256,128]{1,0:T(8,128)S(1)} %collective-permute-done.5.refs_0_, f32[256,128]{1,0:T(8,128)S(1)} %collective-permute-done.6.refs_1_, ...), custom_call_target="tpu_custom_call" | custom-call | flops 100000000 | bytes 12890112 | tf_op jit(solution)/shard_map/advance_3/pallas_call | solution.py:560
  45.5 0.5 shrink.1
  46.2 4.6 %collective-permute-start.8 = (f32[144,128]{1,0:T(8,128)S(1)}, f32[144,128]{1,0:T(8,128)S(1)}, u32[]{:S(2)}, u32[]{:S(2)}) collective-permute-start(f32[144,128]{1,0:T(8,128)S(1)} %get-tuple-element.85), channel_id=1, source_target_pairs={{1,2},{3,4},{5,6},{7,8},{9,10},{11,12},{13,14},{15,16},{17,18},{19... | collective-permute-start | bytes 221192 | tf_op jit(solution)/shard_map/ppermute | solution.py:584
  50.8 4.8 %collective-permute-done.8.refs_2_.refs_1_ = f32[144,128]{1,0:T(8,128)S(1)} collective-permute-done((f32[144,128]{1,0:T(8,128)S(1)}, f32[144,128]{1,0:T(8,128)S(1)}, u32[]{:S(2)}, u32[]{:S(2)}) %collective-permute-start.8) | collective-permute-done | bytes 73760 | tf_op jit(solution)/shard_map/ppermute | solution.py:584
  55.6 3.0 %collective-permute-start.11 = (f32[72,512]{1,0:T(8,128)S(1)}, f32[72,512]{1,0:T(8,128)S(1)}, u32[]{:S(2)}, u32[]{:S(2)}) collective-permute-start(f32[72,512]{1,0:T(8,128)S(1)} %merge.1.refs_0_), channel_id=1, source_target_pairs={{0,192},{64,128},{128,64},{192,0},{1,193},{65,129},{129,65},{193,1... | collective-permute-start | bytes 442376 | tf_op jit(solution)/shard_map/ppermute | solution.py:578
  58.6 0.6 collective-permute-start.10
  59.2 0.6 collective-permute-start.9
  59.8 0.8 inside_last.1.refs_4_
  61.0 1.9 %collective-permute-done.11.refs_3_ = f32[72,512]{1,0:T(8,128)S(1)} collective-permute-done((f32[72,512]{1,0:T(8,128)S(1)}, f32[72,512]{1,0:T(8,128)S(1)}, u32[]{:S(2)}, u32[]{:S(2)}) %collective-permute-start.11) | collective-permute-done | bytes 147488 | tf_op jit(solution)/shard_map/ppermute | solution.py:578
  62.9 2.4 %collective-permute-done.10.refs_2_ = f32[72,512]{1,0:T(8,128)S(1)} collective-permute-done((f32[72,512]{1,0:T(8,128)S(1)}, f32[72,512]{1,0:T(8,128)S(1)}, u32[]{:S(2)}, u32[]{:S(2)}) %collective-permute-start.10) | collective-permute-done | bytes 147488 | tf_op jit(solution)/shard_map/ppermute | solution.py:578
  65.4 5.1 %collective-permute-done.12.refs_1_ = f32[72,512]{1,0:T(8,128)S(1)} collective-permute-done((f32[72,512]{1,0:T(8,128)S(1)}, f32[72,512]{1,0:T(8,128)S(1)}, u32[]{:S(2)}, u32[]{:S(2)}) %collective-permute-start.12) | collective-permute-done | bytes 147488 | tf_op jit(solution)/shard_map/ppermute | solution.py:578
  70.7 1.2 %collective-permute-done.13 = f32[8,128]{1,0:T(8,128)S(1)} collective-permute-done((f32[8,128]{1,0:T(8,128)S(1)}, f32[8,128]{1,0:T(8,128)S(1)}, u32[]{:S(2)}, u32[]{:S(2)}) %collective-permute-start.13) | collective-permute-done | bytes 4128 | tf_op jit(solution)/shard_map/ppermute | solution.py:578
  71.8 0.7 spread.1
  72.6 4.4 %collective-permute-done.14.refs_1_ = f32[8,128]{1,0:T(8,128)S(1)} collective-permute-done((f32[8,128]{1,0:T(8,128)S(1)}, f32[8,128]{1,0:T(8,128)S(1)}, u32[]{:S(2)}, u32[]{:S(2)}) %collective-permute-start.14) | collective-permute-done | bytes 4128 | tf_op jit(solution)/shard_map/ppermute | solution.py:578
  76.9 10.4 %all_to_all.5.refs_0_ = f32[8,8,128]{2,1,0:T(8,128)S(1)} all-to-all(f32[8,8,128]{2,1,0:T(8,128)S(1)} %widen.1), channel_id=1, replica_groups=mesh['y'=4,'xl'=2,'xh'=2,'z'=8,'core'=2] {'z'}, dimensions={0} | all-to-all | bytes 65536 | tf_op jit(solution)/shard_map/all_to_all | solution.py:706
  87.3 1.7 %finish.1 = (f32[64,512]{1,0:T(8,128)}, f32[2048,128]{1,0:T(8,128)}) custom-call(f32[8,8,128]{2,1,0:T(8,128)S(1)} %all_to_all.5.refs_0_, f32[72,512]{1,0:T(8,128)S(1)} %get-tuple-element.90.refs_0_.refs_1_, f32[16,128,128]{2,1,0:T(8,128)S(1)} %get-tuple-element.91.refs_2_, f32[16,128,128]{2,1,0:T(8,128)S(1)} %get-tuple-element.92.refs_3_, ...), custom_call_target="tpu_custom_call" | custom-call | bytes 3325952 | tf_op jit(solution)/shard_map/finish/pallas_call | solution.py:560
  (58 shorter events, 2.0 us)
Async XLA Ops:
  0.6 9.4 %copy-start.1 = (f32[1,128,16,128]{3,2,1,0:T(8,128)S(1)}, f32[1,128,16,128]{3,2,1,0:T(8,128)}, u32[]{:S(2)}) copy-start(f32[1,128,16,128]{3,2,1,0:T(8,128)} %param.18) | copy-start | bytes 3145732
  0.6 9.4 %copy-start.2 = (f32[1,128,16,128]{3,2,1,0:T(8,128)S(1)}, f32[1,128,16,128]{3,2,1,0:T(8,128)}, u32[]{:S(2)}) copy-start(f32[1,128,16,128]{3,2,1,0:T(8,128)} %param.20) | copy-start | bytes 3145732
  0.6 9.4 %copy-start.9 = (bf16[256,256]{1,0:T(8,128)(2,1)S(1)}, bf16[256,256]{1,0:T(8,128)(2,1)}, u32[]{:S(2)}) copy-start(bf16[256,256]{1,0:T(8,128)(2,1)} %constant.24.clone.refs_6_.refs_3_.refs_2_) | copy-start | bytes 393220
  1.9 13.3 %collective-permute-start.1 = (f32[280,128]{1,0:T(8,128)S(1)}, f32[280,128]{1,0:T(8,128)S(1)}, u32[]{:S(2)}, u32[]{:S(2)}) collective-permute-start(f32[280,128]{1,0:T(8,128)S(1)} %get-tuple-element.50), channel_id=1, source_target_pairs={{1,2},{3,4},{5,6},{7,8},{9,10},{11,12},{13,14},{15,16},{17,18},{19... | collective-permute-start | bytes 430088 | tf_op jit(solution)/shard_map/ppermute | solution.py:584
  9.9 0.7 copy-start.18
  10.0 5.2 %collective-permute-start = (f32[264,128]{1,0:T(8,128)S(1)}, f32[264,128]{1,0:T(8,128)S(1)}, u32[]{:S(2)}, u32[]{:S(2)}) collective-permute-start(f32[264,128]{1,0:T(8,128)S(1)} %get-tuple-element.49), channel_id=1, source_target_pairs={{0,1},{1,0},{2,3},{3,2},{4,5},{5,4},{6,7},{7,6},{8,9},{9,8},{10,11... | collective-permute-start | bytes 405512 | tf_op jit(solution)/shard_map/ppermute | solution.py:578
  10.6 0.9 %copy-start.10 = (bf16[256,256]{1,0:T(8,128)(2,1)S(1)}, bf16[256,256]{1,0:T(8,128)(2,1)}, u32[]{:S(2)}) copy-start(bf16[256,256]{1,0:T(8,128)(2,1)} %constant.20.clone.refs_5_.refs_2_.refs_1_) | copy-start | bytes 393220
  11.5 3.6 %copy-start.5 = (bf16[256,256]{1,0:T(8,128)(2,1)S(1)}, bf16[256,256]{1,0:T(8,128)(2,1)}, u32[]{:S(2)}) copy-start(bf16[256,256]{1,0:T(8,128)(2,1)} %constant.25.clone.refs_3_.refs_4_) | copy-start | bytes 393220
  11.5 3.7 %copy-start.6 = (f32[64,512]{1,0:T(8,128)S(1)}, f32[64,512]{1,0:T(8,128)}, u32[]{:S(2)}) copy-start(f32[64,512]{1,0:T(8,128)} %refs_0_.1) | copy-start | bytes 393220
  11.5 3.7 %copy-start.7 = (bf16[2,136,144]{2,1,0:T(8,128)(2,1)S(1)}, bf16[2,136,144]{2,1,0:T(8,128)(2,1)}, u32[]{:S(2)}) copy-start(bf16[2,136,144]{2,1,0:T(8,128)(2,1)} %constant.27.clone.refs_4_) | copy-start | bytes 235012
  11.5 4.3 %copy-start.3 = (f32[1,128,16,128]{3,2,1,0:T(8,128)S(1)}, f32[1,128,16,128]{3,2,1,0:T(8,128)}, u32[]{:S(2)}) copy-start(f32[1,128,16,128]{3,2,1,0:T(8,128)} %param.19) | copy-start | bytes 3145732
  11.5 4.3 %copy-start.4 = (f32[1,128,16,128]{3,2,1,0:T(8,128)S(1)}, f32[1,128,16,128]{3,2,1,0:T(8,128)}, u32[]{:S(2)}) copy-start(f32[1,128,16,128]{3,2,1,0:T(8,128)} %param.21) | copy-start | bytes 3145732
  15.1 0.8 copy-start
  17.3 1.6 %collective-permute-start.2 = (f32[256,128]{1,0:T(8,128)S(1)}, f32[256,128]{1,0:T(8,128)S(1)}, u32[]{:S(2)}, u32[]{:S(2)}) collective-permute-start(f32[256,128]{1,0:T(8,128)S(1)} %get-tuple-element.58), channel_id=1, source_target_pairs={{0,1},{1,0},{2,3},{3,2},{4,5},{5,4},{6,7},{7,6},{8,9},{9,8},{10,11... | collective-permute-start | bytes 393224 | tf_op jit(solution)/shard_map/ppermute | solution.py:578
  17.4 1.5 %copy-start.15 = (bf16[2,16,48]{2,1,0:T(8,128)(2,1)S(1)}, bf16[2,16,48]{2,1,0:T(8,128)(2,1)}, u32[]{:S(2)}) copy-start(bf16[2,16,48]{2,1,0:T(8,128)(2,1)} %constant.22.clone.refs_10_) | copy-start | bytes 9220
  19.0 11.5 %copy-start.14 = (bf16[2,16,48]{2,1,0:T(8,128)(2,1)S(1)}, bf16[2,16,48]{2,1,0:T(8,128)(2,1)}, u32[]{:S(2)}) copy-start(bf16[2,16,48]{2,1,0:T(8,128)(2,1)} %constant.23.clone.refs_14_) | copy-start | bytes 9220
  19.2 11.3 %collective-permute-start.3 = (f32[512,128]{1,0:T(8,128)S(1)}, f32[512,128]{1,0:T(8,128)S(1)}, u32[]{:S(2)}, u32[]{:S(2)}) collective-permute-start(f32[512,128]{1,0:T(8,128)S(1)} %early.1.refs_12_), channel_id=1, source_target_pairs={{1,2},{3,4},{5,6},{7,8},{9,10},{11,12},{13,14},{15,16},{17,18},{19... | collective-permute-start | bytes 786440 | tf_op jit(solution)/shard_map/ppermute | solution.py:584
  31.3 1.6 %collective-permute-start.4 = (f32[256,128]{1,0:T(8,128)S(1)}, f32[256,128]{1,0:T(8,128)S(1)}, u32[]{:S(2)}, u32[]{:S(2)}) collective-permute-start(f32[256,128]{1,0:T(8,128)S(1)} %get-tuple-element.64), channel_id=1, source_target_pairs={{0,1},{1,0},{2,3},{3,2},{4,5},{5,4},{6,7},{7,6},{8,9},{9,8},{10,11... | collective-permute-start | bytes 393224 | tf_op jit(solution)/shard_map/ppermute | solution.py:578
  33.9 6.9 %collective-permute-start.5 = (f32[256,128]{1,0:T(8,128)S(1)}, f32[256,128]{1,0:T(8,128)S(1)}, u32[]{:S(2)}, u32[]{:S(2)}) collective-permute-start(f32[256,128]{1,0:T(8,128)S(1)} %get-tuple-element.71), channel_id=1, source_target_pairs={{0,1},{1,0},{2,3},{3,2},{4,5},{5,4},{6,7},{7,6},{8,9},{9,8},{10,11... | collective-permute-start | bytes 393224 | tf_op jit(solution)/shard_map/ppermute | solution.py:578
  34.5 9.9 %collective-permute-start.6 = (f32[256,128]{1,0:T(8,128)S(1)}, f32[256,128]{1,0:T(8,128)S(1)}, u32[]{:S(2)}, u32[]{:S(2)}) collective-permute-start(f32[256,128]{1,0:T(8,128)S(1)} %get-tuple-element.72), channel_id=1, source_target_pairs={{1,2},{3,4},{5,6},{7,8},{9,10},{11,12},{13,14},{15,16},{17,18},{19... | collective-permute-start | bytes 393224 | tf_op jit(solution)/shard_map/ppermute | solution.py:584
  44.3 1.2 %copy-start.12 = (bf16[512,128]{1,0:T(8,128)(2,1)S(1)}, bf16[512,128]{1,0:T(8,128)(2,1)}, u32[]{:S(2)}) copy-start(bf16[512,128]{1,0:T(8,128)(2,1)} %constant.26.clone.refs_4_) | copy-start | bytes 393220
  44.3 1.2 %copy-start.13 = (bf16[2,72,256]{2,1,0:T(8,128)(2,1)S(1)}, bf16[2,72,256]{2,1,0:T(8,128)(2,1)}, u32[]{:S(2)}) copy-start(bf16[2,72,256]{2,1,0:T(8,128)(2,1)} %constant.29.clone.refs_3_) | copy-start | bytes 221188
  46.1 4.7 %collective-permute-start.7 = (f32[144,128]{1,0:T(8,128)S(1)}, f32[144,128]{1,0:T(8,128)S(1)}, u32[]{:S(2)}, u32[]{:S(2)}) collective-permute-start(f32[144,128]{1,0:T(8,128)S(1)} %get-tuple-element.84), channel_id=1, source_target_pairs={{0,1},{1,0},{2,3},{3,2},{4,5},{5,4},{6,7},{7,6},{8,9},{9,8},{10,11... | collective-permute-start | bytes 221192 | tf_op jit(solution)/shard_map/ppermute | solution.py:578
  46.2 9.4 %collective-permute-start.8 = (f32[144,128]{1,0:T(8,128)S(1)}, f32[144,128]{1,0:T(8,128)S(1)}, u32[]{:S(2)}, u32[]{:S(2)}) collective-permute-start(f32[144,128]{1,0:T(8,128)S(1)} %get-tuple-element.85), channel_id=1, source_target_pairs={{1,2},{3,4},{5,6},{7,8},{9,10},{11,12},{13,14},{15,16},{17,18},{19... | collective-permute-start | bytes 221192 | tf_op jit(solution)/shard_map/ppermute | solution.py:584
  55.6 4.2 %copy-start.11 = (bf16[256,256]{1,0:T(8,128)(2,1)S(1)}, bf16[256,256]{1,0:T(8,128)(2,1)}, u32[]{:S(2)}) copy-start(bf16[256,256]{1,0:T(8,128)(2,1)} %constant.20.clone.refs_5_.refs_2_.refs_1_) | copy-start | bytes 393220
  55.6 7.3 %collective-permute-start.11 = (f32[72,512]{1,0:T(8,128)S(1)}, f32[72,512]{1,0:T(8,128)S(1)}, u32[]{:S(2)}, u32[]{:S(2)}) collective-permute-start(f32[72,512]{1,0:T(8,128)S(1)} %merge.1.refs_0_), channel_id=1, source_target_pairs={{0,192},{64,128},{128,64},{192,0},{1,193},{65,129},{129,65},{193,1... | collective-permute-start | bytes 442376 | tf_op jit(solution)/shard_map/ppermute | solution.py:578
  58.6 6.6 %collective-permute-start.10 = (f32[72,512]{1,0:T(8,128)S(1)}, f32[72,512]{1,0:T(8,128)S(1)}, u32[]{:S(2)}, u32[]{:S(2)}) collective-permute-start(f32[72,512]{1,0:T(8,128)S(1)} %merge.1.refs_0_), channel_id=1, source_target_pairs={{0,128},{64,192},{128,0},{192,64},{1,129},{65,193},{129,1},{193,65... | collective-permute-start | bytes 442376 | tf_op jit(solution)/shard_map/ppermute | solution.py:578
  59.2 6.0 %collective-permute-start.9 = (f32[72,512]{1,0:T(8,128)S(1)}, f32[72,512]{1,0:T(8,128)S(1)}, u32[]{:S(2)}, u32[]{:S(2)}) collective-permute-start(f32[72,512]{1,0:T(8,128)S(1)} %merge.1.refs_0_), channel_id=1, source_target_pairs={{0,64},{64,0},{128,192},{192,128},{1,65},{65,1},{129,193},{193,129... | collective-permute-start | bytes 442376 | tf_op jit(solution)/shard_map/ppermute | solution.py:578
  65.3 6.6 %copy-start.8 = (bf16[2,128,144]{2,1,0:T(8,128)(2,1)S(1)}, bf16[2,128,144]{2,1,0:T(8,128)(2,1)}, u32[]{:S(2)}) copy-start(bf16[2,128,144]{2,1,0:T(8,128)(2,1)} %constant.28.clone.refs_5_) | copy-start | bytes 221188
  65.3 5.2 %collective-permute-start.12 = (f32[72,512]{1,0:T(8,128)S(1)}, f32[72,512]{1,0:T(8,128)S(1)}, u32[]{:S(2)}, u32[]{:S(2)}) collective-permute-start(f32[72,512]{1,0:T(8,128)S(1)} %add_four.1.refs_0_), channel_id=1, source_target_pairs={{0,32},{32,0},{1,33},{33,1},{2,34},{34,2},{3,35},{35,3},{4,36},{36... | collective-permute-start | bytes 442376 | tf_op jit(solution)/shard_map/ppermute | solution.py:578
  70.6 1.3 %collective-permute-start.13 = (f32[8,128]{1,0:T(8,128)S(1)}, f32[8,128]{1,0:T(8,128)S(1)}, u32[]{:S(2)}, u32[]{:S(2)}) collective-permute-start(f32[8,128]{1,0:T(8,128)S(1)} %get-tuple-element.89), channel_id=1, source_target_pairs={{0,1},{1,0},{2,3},{3,2},{4,5},{5,4},{6,7},{7,6},{8,9},{9,8},{10,11... | collective-permute-start | bytes 12296 | tf_op jit(solution)/shard_map/ppermute | solution.py:578
  71.8 5.1 %collective-permute-start.14 = (f32[8,128]{1,0:T(8,128)S(1)}, f32[8,128]{1,0:T(8,128)S(1)}, u32[]{:S(2)}, u32[]{:S(2)}) collective-permute-start(f32[8,128]{1,0:T(8,128)S(1)} %add.3.refs_0_), channel_id=1, source_target_pairs={{0,16},{16,0},{1,17},{17,1},{2,18},{18,2},{3,19},{19,3},{4,20},{20... | collective-permute-start | bytes 12296 | tf_op jit(solution)/shard_map/ppermute | solution.py:578
  (2 other events, 1.3 us)

commit v3 on v2

--- a/solution.py
+++ b/solution.py
@@ -98,12 +98,12 @@
     lower = {j: column(j) for j in (-2, -1, 0, 1)}
     upper = {j: column(j) for j in (62, 63, 64, 65)}
     stack = lambda d: np.stack([d[j] for j in sorted(d)], axis=1)
-    grow_old, grow_new, shrink = [], [], []
-    inner = own.copy()
-    inner[:, [0, 1, 62, 63]] = 0.0
+    grow_old, grow_new, shrink, shrink_far = [], [], [], []
+    blank = np.zeros((CX, 2))
     for core in range(2):
-        near, far = (upper, lower) if core == 0 else (lower, upper)
+        near = upper if core == 0 else lower
         near_two, far_six = ((64, 65), range(-6, 0)) if core == 0 else ((-2, -1), range(64, 70))
+        far_two = (-2, -1) if core == 0 else (64, 65)
         beyond = -OV if core == 0 else CX
         old = np.stack(
             [
@@ -112,11 +112,19 @@
             ],
             axis=1,
         )
-        new = np.concatenate([inner, stack(near), stack(far)], axis=1)
-        every = np.concatenate([own, stack(near), stack(far)], axis=1)
+        inner = own.copy()
+        inner[:, [62, 63] if core == 0 else [0, 1]] = 0.0
+        outer = np.stack([column(j) for j in far_two], axis=1)
+        new = np.concatenate([inner, stack(near), outer, blank], axis=1)
+        every = np.concatenate([own, stack(near), outer, blank], axis=1).T
+        past = np.zeros((ROWS, OV))
+        for row, j in (*enumerate(range(CXC)), *zip((CXC + 4, CXC + 5), far_two)):
+            past[row] = column(j, beyond, OV)
         grow_old.append(np.concatenate([old, old], axis=1))
         grow_new.append(np.concatenate([new, new], axis=1))
-        shrink.append(np.concatenate([every.T, every.T], axis=1))
+        shrink.append(np.concatenate([every, every], axis=1))
+        shrink_far.append(np.concatenate([past, past], axis=1))
+    out["shrink_far"] = np.stack(shrink_far)
     out["grow_old"] = np.stack(grow_old)
     out["grow_new"] = np.stack(grow_new)
     out["shrink_x"] = np.stack(shrink)
@@ -177,14 +185,11 @@
     return dot(halo_x, cat(parts, 1))
 
 
-def edge_rows(v, core, near, far, field):
-    near_row = pl.multiple_of((1 - core) * (CX - OV), OV)
-    far_row = pl.multiple_of(core * (CX - OV), OV)
+def edge_rows(v, core, near, field):
+    row = pl.multiple_of((1 - core) * (CX - OV), OV)
     for y in range(CY):
         start = (field * CY + y) * OV
-        near[start : start + OV] = v[y, pl.ds(near_row, OV), :]
-        if far is not None:
-            far[start : start + OV] = v[y, pl.ds(far_row, OV), :]
+        near[start : start + OV] = v[y, pl.ds(row, OV), :]
 
 
 def first_edges(p, q, coef, near, far, p_lo, p_hi, q_lo, q_hi, c_lo, c_hi, sems):
@@ -315,9 +320,14 @@
         square = fine * fine
         sigma[y] = fine[:CX]
         squared[y] = square[:CX]
-        beyond[y * OV : y * OV + OV] = jnp.where(first | last, 0.0, square[CX:])
+        beyond[y * OV : y * OV + OV] = jnp.where(first | last, 0.0, fine[CX:])
 
     grow(held[...], grow_z, grow_old[core], write)
+
+
+def squared_at(beyond, spot):
+    value = beyond[spot : spot + OV]
+    return value * value
 
 
 def advance(step, *refs):
@@ -326,19 +336,19 @@
     core = lax.axis_index("core")
     columns = halo_x[core]
     weight = amounts[step, :1, :]
-    if step == 1:
+    if step in (1, 3):
         (sent, beyond, cross_x), refs = refs[:3], refs[3:]
         cross = cross_x[core]
     if step == 2:
         old_lap, refs = refs[0], refs[1:]
     if step == 3:
-        (old_lap, older_q, gathered, sigma), refs = refs[:4], refs[4:]
-    if step == 0:
+        (old_lap, older_q, gathered, sigma, older_far), refs = refs[:5], refs[5:]
+    if step in (0, 2):
         (p_new, q_new, near_out), refs = refs[:3], refs[3:]
-    elif step < 3:
+    elif step == 1:
         (p_new, q_new, near_out, far_out), refs = refs[:4], refs[4:]
     else:
-        p_new, near_out, far_out, image = refs[:4]
+        p_new, near_out, far_out, image, image_far = refs[:5]
     if step < 2:
         lap_out = refs[0]
     if step == 2:
@@ -368,13 +378,9 @@
             if step == 3:
                 total = gathered[y] + older_q[y] * lap + new_q * old_lap[y]
                 image[y] = 2.0 * sigma[y] * total
-    if step == 0 or step == 1:
-        far_out_used = None
-    else:
-        far_out_used = far_out
-    edge_rows(p_new, core, near_out, far_out_used, 0)
+    edge_rows(p_new, core, near_out, 0)
     if step < 3:
-        edge_rows(q_new, core, near_out, far_out_used, 1)
+        edge_rows(q_new, core, near_out, 1)
     if step == 1:
         size = CY * OV
         for pair in range(CY // 2):
@@ -385,38 +391,56 @@
                     known = far[(2 + field) * size + spot : (2 + field) * size + spot + OV]
                     far_out[field * size + spot : field * size + spot + OV] = (
                         known
-                        + beyond[spot : spot + OV] * extra[:OV, side * CZ : side * CZ + CZ]
+                        + squared_at(beyond, spot) * extra[:OV, side * CZ : side * CZ + CZ]
                     )
-
-
-def early(
-    near, p, p_before, q, q_before, lap_p, lap_q, squared, source, amounts, near_x, out,
-):
-    core = lax.axis_index("core")
-    row = pl.multiple_of(core * (CX - OV), OV)
-    weight = amounts[1, :1, :]
+    if step == 3:
+        size = CY * OV
+        for pair in range(CY // 2):
+            extra_p = halo_part(sent, sent, 0, cross, pair)
+            extra_q = halo_part(sent, sent, 1, cross, pair)
+            for side in range(2):
+                spot = (2 * pair + side) * OV
+                lanes = slice(side * CZ, side * CZ + CZ)
+                part_p, part_q = extra_p[:OV, lanes], extra_q[:OV, lanes]
+                rows = lambda k: far[k * size + spot : k * size + spot + OV]
+                far_out[spot : spot + OV] = rows(2) + squared_at(beyond, spot) * part_p
+                near_q = older_far[size + spot : size + spot + OV]
+                image_far[spot : spot + OV] = (
+                    rows(3) + 2.0 * beyond[spot : spot + OV] * near_q * part_p + rows(4) * part_q
+                )
+
+
+def early(step, *refs):
+    (near, p, p_before, q, q_before, lap_p, lap_q, squared, source, amounts, near_x) = refs[:11]
+    if step == 3:
+        older_q, old_lap, gathered, sigma = refs[11:15]
+    out = refs[-1]
+    core = lax.axis_index("core")
+    rows = pl.ds(pl.multiple_of(core * (CX - OV), OV), OV)
+    weight = amounts[step, :1, :]
     columns = near_x[core]
-    size = CY * OV
     for pair in range(CY // 2):
         extra_p = halo_part(near, near, 0, columns, pair)
         extra_q = halo_part(near, near, 1, columns, pair)
         for side in range(2):
             y = 2 * pair + side
-            rows = pl.ds(row, OV)
             lanes = slice(side * CZ, side * CZ + CZ)
             sq = squared[y, rows, :]
             lap = lap_p[y, rows, :] + extra_p[:OV, lanes]
             lap_adj = lap_q[y, rows, :] + extra_q[:OV, lanes]
             edge_p, edge_q = p[y, rows, :], q[y, rows, :]
-            spot = y * OV
-            out[spot : spot + OV] = edge_p
-            out[size + spot : size + spot + OV] = edge_q
-            out[2 * size + spot : 2 * size + spot + OV] = (
-                2.0 * edge_p - p_before[y, rows, :] + sq * lap + source[y, rows, :] * weight
-            )
-            out[3 * size + spot : 3 * size + spot + OV] = (
-                2.0 * edge_q - q_before[y, rows, :] + sq * lap_adj
-            )
+            next_p = 2.0 * edge_p - p_before[y, rows, :] + sq * lap + source[y, rows, :] * weight
+            next_q = 2.0 * edge_q - q_before[y, rows, :] + sq * lap_adj
+            if step == 1:
+                sets = (edge_p, edge_q, next_p, next_q)
+            else:
+                twice = 2.0 * sigma[y, rows, :]
+                old = old_lap[y, rows, :]
+                known = gathered[y, rows, :] + older_q[y, rows, :] * lap + next_q * old
+                sets = (edge_p, edge_q, next_p, twice * known, twice * sq * old)
+            for k, value in enumerate(sets):
+                spot = (k * CY + y) * OV
+                out[spot : spot + OV] = value
 
 
 def inside(p, q, own_x, own_z, lap_p, lap_q):
@@ -428,14 +452,18 @@
     interior(p, own_x, own_z, lap_p)
 
 
-def shrink(image, near_in, far_in, shrink_x, shrink_z, own, near, far):
+def shrink(image, image_far, near_in, shrink_x, shrink_far, shrink_z, own, near):
     core = lax.axis_index("core")
     rows_x = shrink_x[core]
+    rows_far = shrink_far[core]
     narrow = [None] * CYC
     weights = taps()
     for pair in range(CY // 2):
         high, low = split(cat([image[2 * pair], image[2 * pair + 1]], 1))
         both = dot(rows_x, cat([high, low], 0))
+        spots = [slice(y * OV, y * OV + OV) for y in (2 * pair, 2 * pair + 1)]
+        high, low = split(cat([image_far[spots[0]], image_far[spots[1]]], 1))
+        both = both + dot(rows_far, cat([high, low], 0))
         for side in range(2):
             part = both[:, side * CZ : side * CZ + CZ]
             for j, w in weights[2 * pair + side]:
@@ -450,35 +478,31 @@
     own[...] = cat(pieces, 1)
     field = CY * OV
     near[:field] = near_in[...]
-    far[:field] = far_in[...]
     for row in range(4):
         for part in range(4):
             lanes = slice(part * 128, part * 128 + 128)
             spot = field + row * 4 + part
             near[spot : spot + 1] = own[CXC + row : CXC + row + 1, lanes]
-            far[spot : spot + 1] = own[CXC + 4 + row : CXC + 5 + row, lanes]
-
-
-def merge(own, near, far, out):
+
+
+def merge(own, near, out):
     out[...] = own[...]
     field = CY * OV
     for row in range(4):
         for part in range(4):
             lanes = slice(part * 128, part * 128 + 128)
             spot = field + row * 4 + part
-            a, b = CXC + row, CXC + 4 + row
-            out[a : a + 1, lanes] = own[a : a + 1, lanes] + near[spot : spot + 1]
-            out[b : b + 1, lanes] = own[b : b + 1, lanes] + far[spot : spot + 1]
+            at = slice(CXC + row, CXC + row + 1)
+            out[at, lanes] = own[at, lanes] + near[spot : spot + 1]
 
 
 def squares(a, b, total, squared):
     core = lax.axis_index("core")
     total[...] = a[...] + b[...]
     first, last = grid_ends()
-    total[CXC + 4 : CXC + 6] = jnp.where(first, 0.0, total[CXC + 4 : CXC + 6])
-    total[CXC + 6 : CXC + 8] = jnp.where(last, 0.0, total[CXC + 6 : CXC + 8])
-    total[0:2] = jnp.where(core == 0, total[CXC + 6 : CXC + 8], total[CXC + 2 : CXC + 4])
-    total[CXC - 2 : CXC] = jnp.where(core == 0, total[CXC : CXC + 2], total[CXC + 4 : CXC + 6])
+    total[CXC + 4 : CXC + 6] = jnp.where(first | last, 0.0, total[CXC + 4 : CXC + 6])
+    total[0:2] = jnp.where(core == 0, total[0:2], total[CXC + 2 : CXC + 4])
+    total[CXC - 2 : CXC] = jnp.where(core == 0, total[CXC : CXC + 2], total[CXC - 2 : CXC])
     value = total[:CXC]
     value = value * value
     rows = value[0:8]
@@ -596,7 +620,7 @@
     flat = lambda a: a.reshape(CX * CY, CZ)
     p_now, p_prev, adj_now, adj_next = map(flat, (p_now, p_prev, adj_now, adj_next))
 
-    edge = rows_of(2 * CY * OV)
+    half, edge = rows_of(CY * OV), rows_of(2 * CY * OV)
     with_two, with_six = rows_of(2 * CY * OV + 8), rows_of(2 * CY * OV + 24)
     block = pltpu.VMEM((OV * CY, CZ), F32)
     few = pltpu.VMEM((8, CYC * CZC), F32)
@@ -634,15 +658,16 @@
         elif step == 1:
             args += [sent, beyond, const["cross_x"]]
             outs = (FIELD, FIELD, edge, edge, FIELD)
+            older_far = far
         elif step == 2:
             args.append(laps[1])
-            outs = (FIELD, FIELD, edge, edge, FIELD)
+            outs = (FIELD, FIELD, edge, FIELD)
         else:
-            args += [laps[0], qs[1], gathered, sigma]
-            outs = (FIELD, rows_of(CY * OV), rows_of(CY * OV), FIELD)
+            args += [sent, beyond, const["cross_x"], laps[0], qs[1], gathered, sigma, older_far]
+            outs = (FIELD, half, half, FIELD, half)
         result = call(body, outs, *args, flops=10**8, name=name)
         if step == 3:
-            p_new, near, far, image = result
+            p_new, near, far, image, image_far = result
             p, p_before = p_new, p
             continue
         p_new, q_new, *edges, other = result
@@ -653,31 +678,32 @@
         p, p_before = p_new, p
         q, q_before = q_new, q
         qs.append(q)
-        if step == 2:
-            near, far = exchange(*edges)
-        else:
-            near = xor_swap(edges[0], "core", 1)
+        near = xor_swap(edges[0], "core", 1)
         lap_p, lap_q = call(
             inside, (FIELD, FIELD), p, q, own_x, own_z, flops=10**9, name=f"inside_{step}"
         )
-        if step == 0:
-            sent = call(
-                early, rows_of(4 * CY * OV), near, p, p_before, q, q_before, lap_p, lap_q,
-                squared, source, amounts, const["near_x"], flops=10**7, name="early",
-            )
-            far = far_swap(sent)
-        elif step == 1:
+        if step == 1:
             far = edges[1]
-
-    ends = rows_of(CY * OV + 16)
-    own, near, far = call(
+            continue
+        args = [near, p, p_before, q, q_before, lap_p, lap_q, squared, source, amounts]
+        args.append(const["near_x"])
+        if step == 2:
+            args += [qs[1], laps[0], gathered, sigma]
+        sent = call(
+            functools.partial(early, step + 1), rows_of((4 if step == 0 else 5) * CY * OV),
+            *args, flops=10**7, name=f"early_{step + 1}",
+        )
+        far = far_swap(sent)
+
+    own, near = call(
         shrink,
-        (rows_of(ROWS, CYC * CZC), ends, ends),
-        image, near, far, const["shrink_x"], const["shrink_z"], flops=10**8, name="shrink",
-    )
-    near, far = exchange(near, far)
+        (rows_of(ROWS, CYC * CZC), rows_of(CY * OV + 16)),
+        image, image_far, near, const["shrink_x"], const["shrink_far"], const["shrink_z"],
+        flops=10**8, name="shrink",
+    )
+    near = xor_swap(near, "core", 1)
     lap_p = call(inside_one, FIELD, p, own_x, own_z, flops=5 * 10**8, name="inside_last")
-    partial = call(merge, rows_of(ROWS, CYC * CZC), own, near, far, name="merge")
+    partial = call(merge, rows_of(ROWS, CYC * CZC), own, near, name="merge")
 
     two, one, three = (xor_swap(partial, "y", m) for m in (2, 1, 3))
     lap_p, base = call(

time: 89.4 us -> 87.7 us (0.981)
  starting transfers between devices: 27.4 us -> 22.9 us
  waiting for transfers between devices: 29.9 us -> 31.7 us
    ppermute x4 -> x3, starting transfers between devices: 22 us -> 17.6 us  [far_swap(): return lax.ppermute(x, TILE, pairs + [(b, a) for a, b in pairs])]
    ppermute x11, waiting for transfers between devices: 14.9 us -> 17.8 us  [xor_swap(): return lax.ppermute(x, axis, [(i, i ^ mask) for i in range(count)])]
    ppermute x4 -> x3, waiting for transfers between devices: 15 us -> 13.8 us  [far_swap(): return lax.ppermute(x, TILE, pairs + [(b, a) for a, b in pairs])]
    pallas_call x19 -> x20, Pallas kernels: 17.4 us -> 17.7 us  [call(): pl.pallas_call(run, out_shape=outs, in_specs=[SM] * smem + [VM] * (count...]
  transfers between devices with their start and end apart: 15 -> 14, of which waited for: 8 -> 8; matrix products, arithmetic and copies ran while one was open for 0% -> 0% of each run, Pallas kernels for 11% -> 12%
where the time goes in v3:
time: 87.7 us; the launch traced here: 86.7 us
  waiting for transfers between devices  31.7 us (36%)
  starting transfers between devices  22.9 us (26%)
  Pallas kernels  18.9 us (22%)
  blocking collectives  10.4 us (12%)
  local copies, waits for them, and re-layouts  1.7 us (2%)
  between operations  1.08 us (1%)
    ppermute x11, waiting for transfers between devices, xor_swap(): return lax.ppermute(x, axis, [(i, i ^ mask) for i in range(count)])  17.8 us
    pallas_call x20, Pallas kernels, call(): pl.pallas_call(run, out_shape=outs, in_specs=[SM] * smem + [VM] * (count...  17.7 us
    ppermute x3, starting transfers between devices, far_swap(): return lax.ppermute(x, TILE, pairs + [(b, a) for a, b in pairs])  17.6 us
    ppermute x3, waiting for transfers between devices, far_swap(): return lax.ppermute(x, TILE, pairs + [(b, a) for a, b in pairs])  13.8 us
    all_to_all x1, blocking collectives, on_device(): parts = lax.all_to_all(copies, 'z', split_axis=0, concat_axis=0, tiled=True)  10.4 us
    ppermute x11, starting transfers between devices, xor_swap(): return lax.ppermute(x, axis, [(i, i ^ mask) for i in range(count)])  5.3 us
  transfers between devices with their start and end apart: 14, of which 8 were waited for; matrix products, arithmetic and copies ran while one was open for 0% of the time, Pallas kernels for 12%

profile of v3, /device:TPU:6, one launch (start us, length us, event | category | flops | bytes accessed | tf_op | source)
XLA Modules:
  0.0 86.7 jit_solution(16042656854188605480)
XLA Ops:
  0.7 1.2 %first_edges.1 = (f32[264,128]{1,0:T(8,128)S(1)}, f32[280,128]{1,0:T(8,128)S(1)}) custom-call(f32[2048,128]{1,0:T(8,128)} %bitcast.6, f32[2048,128]{1,0:T(8,128)} %bitcast.8, f32[64,512]{1,0:T(8,128)} %refs_0_.1), custom_call_target="tpu_custom_call" | custom-call | tf_op jit(solution)/shard_map/first_edges/pallas_call | solution.py:627
  1.9 8.0 %collective-permute-start.1 = (f32[280,128]{1,0:T(8,128)S(1)}, f32[280,128]{1,0:T(8,128)S(1)}, u32[]{:S(2)}, u32[]{:S(2)}) collective-permute-start(f32[280,128]{1,0:T(8,128)S(1)} %get-tuple-element.49), channel_id=1, source_target_pairs={{1,2},{3,4},{5,6},{7,8},{9,10},{11,12},{13,14},{15,16},{17,18},{19... | collective-permute-start | bytes 430088 | tf_op jit(solution)/shard_map/ppermute | solution.py:608
  10.1 0.5 copy-done.17
  10.6 0.9 %copy-done.10 = bf16[256,256]{1,0:T(8,128)(2,1)S(1)} copy-done((bf16[256,256]{1,0:T(8,128)(2,1)S(1)}, bf16[256,256]{1,0:T(8,128)(2,1)}, u32[]{:S(2)}) %copy-start.10) | copy-done | bytes 131096
  11.5 3.5 %prepare.1 = (f32[16,128,128]{2,1,0:T(8,128)S(1)}, f32[16,128,128]{2,1,0:T(8,128)S(1)}, f32[16,128,128]{2,1,0:T(8,128)S(1)}, f32[16,128,128]{2,1,0:T(8,128)S(1)}...) custom-call(s32[64]{0:T(128)S(1)} %bitcast.12, s32[64]{0:T(128)S(1)} %copy-done.18, f32[5]{0:T(128)S(1)} %copy-done.19, ...), custom_call_target="tpu_custom_call" | custom-call | flops 1000000000 | bytes 2359828 | tf_op jit(solution)/shard_map/prepare/pallas_call | solution.py:584
  15.2 0.6 speed.1
  15.9 1.3 %advance_0.1 = (f32[16,128,128]{2,1,0:T(8,128)S(1)}, f32[16,128,128]{2,1,0:T(8,128)S(1)}, f32[256,128]{1,0:T(8,128)S(1)}, f32[16,128,128]{2,1,0:T(8,128)S(1)}) custom-call(f32[264,128]{1,0:T(8,128)S(1)} %collective-permute-done.refs_1_.refs_0_, f32[280,128]{1,0:T(8,128)S(1)} %collective-permute-done.1.refs_2_.refs_1_, ...), custom_call_target="tpu_custom_call" | custom-call | flops 100000000 | bytes 8712192 | tf_op jit(solution)/shard_map/advance_0/pallas_call | solution.py:584
  17.3 1.5 %inside_0.1 = (f32[16,128,128]{2,1,0:T(8,128)S(1)}, f32[16,128,128]{2,1,0:T(8,128)S(1)}) custom-call(f32[16,128,128]{2,1,0:T(8,128)S(1)} %get-tuple-element.58.refs_0_.refs_1_.refs_2_.refs_3_, f32[16,128,128]{2,1,0:T(8,128)S(1)} %get-tuple-element.59.refs_1_.refs_3_.refs_4_.refs_5_.refs_11_.refs_16_, bf16[256,256]{1,0:T(8,128)(2,1)S(1)} %copy-done.10, ...), custom_call_target="tpu_custom_call" | custom-call | flops 1000000000 | bytes 2359296 | tf_op jit(solution)/shard_map/inside_0/pallas_call | solution.py:584
  19.0 4.6 %collective-permute-start.3 = (f32[512,128]{1,0:T(8,128)S(1)}, f32[512,128]{1,0:T(8,128)S(1)}, u32[]{:S(2)}, u32[]{:S(2)}) collective-permute-start(f32[512,128]{1,0:T(8,128)S(1)} %early_1.1.refs_12_), channel_id=1, source_target_pairs={{1,2},{3,4},{5,6},{7,8},{9,10},{11,12},{13,14},{15,16},{17,18},{19... | collective-permute-start | bytes 786440 | tf_op jit(solution)/shard_map/ppermute | solution.py:608
  23.7 6.7 %collective-permute-done.3.refs_1_.refs_19_ = f32[512,128]{1,0:T(8,128)S(1)} collective-permute-done((f32[512,128]{1,0:T(8,128)S(1)}, f32[512,128]{1,0:T(8,128)S(1)}, u32[]{:S(2)}, u32[]{:S(2)}) %collective-permute-start.3) | collective-permute-done | bytes 262176 | tf_op jit(solution)/shard_map/ppermute | solution.py:608
  30.3 0.9 %advance_1.1 = (f32[16,128,128]{2,1,0:T(8,128)S(1)}, f32[16,128,128]{2,1,0:T(8,128)S(1)}, f32[256,128]{1,0:T(8,128)S(1)}, f32[256,128]{1,0:T(8,128)S(1)}, f32[16,128,128]{2,1,0:T(8,128)S(1)}) custom-call(f32[256,128]{1,0:T(8,128)S(1)} %collective-permute-done.2.refs_0_, f32[512,128]{1,0:T(8,128)S(1)} %collective-permute-done.3.refs_1_.refs_19_, ...), custom_call_target="tpu_custom_call" | custom-call | flops 100000000 | bytes 9157632 | tf_op jit(solution)/shard_map/advance_1/pallas_call | solution.py:584
  31.3 1.6 %inside_1.1 = (f32[16,128,128]{2,1,0:T(8,128)S(1)}, f32[16,128,128]{2,1,0:T(8,128)S(1)}) custom-call(f32[16,128,128]{2,1,0:T(8,128)S(1)} %get-tuple-element.65.refs_0_.refs_2_.refs_3_, f32[16,128,128]{2,1,0:T(8,128)S(1)} %get-tuple-element.66.refs_1_.refs_4_.refs_5_, bf16[256,256]{1,0:T(8,128)(2,1)S(1)} %copy-done.11, bf16[256,256]{1,0:T(8,128)(2,1)S(1)} %copy-done.9), custom_call_target="tpu_custom_call" | custom-call | flops 1000000000 | bytes 2359296 | tf_op jit(solution)/shard_map/inside_1/pallas_call | solution.py:584
  32.9 0.9 %advance_2.1 = (f32[16,128,128]{2,1,0:T(8,128)S(1)}, f32[16,128,128]{2,1,0:T(8,128)S(1)}, f32[256,128]{1,0:T(8,128)S(1)}, f32[16,128,128]{2,1,0:T(8,128)S(1)}) custom-call(f32[256,128]{1,0:T(8,128)S(1)} %collective-permute-done.4.refs_0_, f32[256,128]{1,0:T(8,128)S(1)} %get-tuple-element.64.refs_1_, ...), custom_call_target="tpu_custom_call" | custom-call | flops 100000000 | bytes 9744384 | tf_op jit(solution)/shard_map/advance_2/pallas_call | solution.py:584
  33.8 0.6 collective-permute-start.5
  34.4 1.5 %inside_2.1 = (f32[16,128,128]{2,1,0:T(8,128)S(1)}, f32[16,128,128]{2,1,0:T(8,128)S(1)}) custom-call(f32[16,128,128]{2,1,0:T(8,128)S(1)} %get-tuple-element.71.refs_0_.refs_1_.refs_2_.refs_3_, f32[16,128,128]{2,1,0:T(8,128)S(1)} %get-tuple-element.72.refs_1_.refs_3_.refs_4_, bf16[256,256]{1,0:T(8,128)(2,1)S(1)} %copy-done.11, bf16[256,256]{1,0:T(8,128)(2,1)S(1)} %copy-done.9), custom_call_target="tpu_custom_call" | custom-call | flops 1000000000 | bytes 2359296 | tf_op jit(solution)/shard_map/inside_2/pallas_call | solution.py:584
  36.2 5.0 %collective-permute-start.6 = (f32[640,128]{1,0:T(8,128)S(1)}, f32[640,128]{1,0:T(8,128)S(1)}, u32[]{:S(2)}, u32[]{:S(2)}) collective-permute-start(f32[640,128]{1,0:T(8,128)S(1)} %early_3.1.refs_12_), channel_id=1, source_target_pairs={{1,2},{3,4},{5,6},{7,8},{9,10},{11,12},{13,14},{15,16},{17,18},{19... | collective-permute-start | bytes 983048 | tf_op jit(solution)/shard_map/ppermute | solution.py:608
  41.1 7.2 %collective-permute-done.6.refs_1_ = f32[640,128]{1,0:T(8,128)S(1)} collective-permute-done((f32[640,128]{1,0:T(8,128)S(1)}, f32[640,128]{1,0:T(8,128)S(1)}, u32[]{:S(2)}, u32[]{:S(2)}) %collective-permute-start.6) | collective-permute-done | bytes 327712 | tf_op jit(solution)/shard_map/ppermute | solution.py:608
  48.3 1.2 %advance_3.1 = (f32[16,128,128]{2,1,0:T(8,128)S(1)}, f32[128,128]{1,0:T(8,128)S(1)}, f32[128,128]{1,0:T(8,128)S(1)}, f32[16,128,128]{2,1,0:T(8,128)S(1)}, f32[128,128]{1,0:T(8,128)S(1)}) custom-call(f32[256,128]{1,0:T(8,128)S(1)} %collective-permute-done.5.refs_0_, f32[640,128]{1,0:T(8,128)S(1)} %collective-permute-done.6.refs_1_, ...), custom_call_target="tpu_custom_call" | custom-call | flops 100000000 | bytes 13745152 | tf_op jit(solution)/shard_map/advance_3/pallas_call | solution.py:584
  49.5 0.7 shrink.1
  50.3 1.3 %collective-permute-done.7.refs_1_.refs_0_ = f32[144,128]{1,0:T(8,128)S(1)} collective-permute-done((f32[144,128]{1,0:T(8,128)S(1)}, f32[144,128]{1,0:T(8,128)S(1)}, u32[]{:S(2)}, u32[]{:S(2)}) %collective-permute-start.7) | collective-permute-done | bytes 73760 | tf_op jit(solution)/shard_map/ppermute | solution.py:602
  51.6 3.1 %collective-permute-start.10 = (f32[72,512]{1,0:T(8,128)S(1)}, f32[72,512]{1,0:T(8,128)S(1)}, u32[]{:S(2)}, u32[]{:S(2)}) collective-permute-start(f32[72,512]{1,0:T(8,128)S(1)} %merge.1.refs_0_), channel_id=1, source_target_pairs={{0,192},{64,128},{128,64},{192,0},{1,193},{65,129},{129,65},{193,1... | collective-permute-start | bytes 442376 | tf_op jit(solution)/shard_map/ppermute | solution.py:602
  54.7 0.6 collective-permute-start.9
  55.3 0.4 collective-permute-start.8
  55.8 0.8 inside_last.1.refs_4_
  57.0 4.3 %collective-permute-done.10.refs_3_ = f32[72,512]{1,0:T(8,128)S(1)} collective-permute-done((f32[72,512]{1,0:T(8,128)S(1)}, f32[72,512]{1,0:T(8,128)S(1)}, u32[]{:S(2)}, u32[]{:S(2)}) %collective-permute-start.10) | collective-permute-done | bytes 147488 | tf_op jit(solution)/shard_map/ppermute | solution.py:602
  61.3 1.6 %collective-permute-done.9.refs_2_ = f32[72,512]{1,0:T(8,128)S(1)} collective-permute-done((f32[72,512]{1,0:T(8,128)S(1)}, f32[72,512]{1,0:T(8,128)S(1)}, u32[]{:S(2)}, u32[]{:S(2)}) %collective-permute-start.9) | collective-permute-done | bytes 147488 | tf_op jit(solution)/shard_map/ppermute | solution.py:602
  63.1 5.1 %collective-permute-done.11.refs_1_ = f32[72,512]{1,0:T(8,128)S(1)} collective-permute-done((f32[72,512]{1,0:T(8,128)S(1)}, f32[72,512]{1,0:T(8,128)S(1)}, u32[]{:S(2)}, u32[]{:S(2)}) %collective-permute-start.11) | collective-permute-done | bytes 147488 | tf_op jit(solution)/shard_map/ppermute | solution.py:602
  68.3 1.2 %collective-permute-done.12 = f32[8,128]{1,0:T(8,128)S(1)} collective-permute-done((f32[8,128]{1,0:T(8,128)S(1)}, f32[8,128]{1,0:T(8,128)S(1)}, u32[]{:S(2)}, u32[]{:S(2)}) %collective-permute-start.12) | collective-permute-done | bytes 4128 | tf_op jit(solution)/shard_map/ppermute | solution.py:602
  69.5 0.7 spread.1
  70.3 4.3 %collective-permute-done.13.refs_1_ = f32[8,128]{1,0:T(8,128)S(1)} collective-permute-done((f32[8,128]{1,0:T(8,128)S(1)}, f32[8,128]{1,0:T(8,128)S(1)}, u32[]{:S(2)}, u32[]{:S(2)}) %collective-permute-start.13) | collective-permute-done | bytes 4128 | tf_op jit(solution)/shard_map/ppermute | solution.py:602
  74.6 10.4 %all_to_all.5.refs_0_ = f32[8,8,128]{2,1,0:T(8,128)S(1)} all-to-all(f32[8,8,128]{2,1,0:T(8,128)S(1)} %widen.1), channel_id=1, replica_groups=mesh['y'=4,'xl'=2,'xh'=2,'z'=8,'core'=2] {'z'}, dimensions={0} | all-to-all | bytes 65536 | tf_op jit(solution)/shard_map/all_to_all | solution.py:732
  85.0 1.7 %finish.1 = (f32[64,512]{1,0:T(8,128)}, f32[2048,128]{1,0:T(8,128)}) custom-call(f32[8,8,128]{2,1,0:T(8,128)S(1)} %all_to_all.5.refs_0_, f32[72,512]{1,0:T(8,128)S(1)} %get-tuple-element.88.refs_0_.refs_1_, f32[16,128,128]{2,1,0:T(8,128)S(1)} %get-tuple-element.89.refs_2_, f32[16,128,128]{2,1,0:T(8,128)S(1)} %get-tuple-element.90.refs_3_, ...), custom_call_target="tpu_custom_call" | custom-call | bytes 3325952 | tf_op jit(solution)/shard_map/finish/pallas_call | solution.py:584
  (59 shorter events, 1.7 us)
Async XLA Ops:
  0.6 9.4 %copy-start.1 = (f32[1,128,16,128]{3,2,1,0:T(8,128)S(1)}, f32[1,128,16,128]{3,2,1,0:T(8,128)}, u32[]{:S(2)}) copy-start(f32[1,128,16,128]{3,2,1,0:T(8,128)} %param.19) | copy-start | bytes 3145732
  0.6 9.4 %copy-start.2 = (f32[1,128,16,128]{3,2,1,0:T(8,128)S(1)}, f32[1,128,16,128]{3,2,1,0:T(8,128)}, u32[]{:S(2)}) copy-start(f32[1,128,16,128]{3,2,1,0:T(8,128)} %param.21) | copy-start | bytes 3145732
  0.6 9.4 %copy-start.9 = (bf16[256,256]{1,0:T(8,128)(2,1)S(1)}, bf16[256,256]{1,0:T(8,128)(2,1)}, u32[]{:S(2)}) copy-start(bf16[256,256]{1,0:T(8,128)(2,1)} %constant.26.clone.refs_6_.refs_3_.refs_2_) | copy-start | bytes 393220
  1.9 13.3 %collective-permute-start.1 = (f32[280,128]{1,0:T(8,128)S(1)}, f32[280,128]{1,0:T(8,128)S(1)}, u32[]{:S(2)}, u32[]{:S(2)}) collective-permute-start(f32[280,128]{1,0:T(8,128)S(1)} %get-tuple-element.49), channel_id=1, source_target_pairs={{1,2},{3,4},{5,6},{7,8},{9,10},{11,12},{13,14},{15,16},{17,18},{19... | collective-permute-start | bytes 430088 | tf_op jit(solution)/shard_map/ppermute | solution.py:608
  9.9 0.7 copy-start.19
  10.0 5.2 %collective-permute-start = (f32[264,128]{1,0:T(8,128)S(1)}, f32[264,128]{1,0:T(8,128)S(1)}, u32[]{:S(2)}, u32[]{:S(2)}) collective-permute-start(f32[264,128]{1,0:T(8,128)S(1)} %get-tuple-element.48), channel_id=1, source_target_pairs={{0,1},{1,0},{2,3},{3,2},{4,5},{5,4},{6,7},{7,6},{8,9},{9,8},{10,11... | collective-permute-start | bytes 405512 | tf_op jit(solution)/shard_map/ppermute | solution.py:602
  10.6 0.9 %copy-start.10 = (bf16[256,256]{1,0:T(8,128)(2,1)S(1)}, bf16[256,256]{1,0:T(8,128)(2,1)}, u32[]{:S(2)}) copy-start(bf16[256,256]{1,0:T(8,128)(2,1)} %constant.22.clone.refs_5_.refs_2_.refs_1_) | copy-start | bytes 393220
  11.5 3.6 %copy-start.5 = (bf16[256,256]{1,0:T(8,128)(2,1)S(1)}, bf16[256,256]{1,0:T(8,128)(2,1)}, u32[]{:S(2)}) copy-start(bf16[256,256]{1,0:T(8,128)(2,1)} %constant.27.clone.refs_3_.refs_4_) | copy-start | bytes 393220
  11.5 3.6 %copy-start.6 = (f32[64,512]{1,0:T(8,128)S(1)}, f32[64,512]{1,0:T(8,128)}, u32[]{:S(2)}) copy-start(f32[64,512]{1,0:T(8,128)} %refs_0_.1) | copy-start | bytes 393220
  11.5 3.6 %copy-start.7 = (bf16[2,136,144]{2,1,0:T(8,128)(2,1)S(1)}, bf16[2,136,144]{2,1,0:T(8,128)(2,1)}, u32[]{:S(2)}) copy-start(bf16[2,136,144]{2,1,0:T(8,128)(2,1)} %constant.30.clone.refs_4_) | copy-start | bytes 235012
  11.5 4.2 %copy-start.3 = (f32[1,128,16,128]{3,2,1,0:T(8,128)S(1)}, f32[1,128,16,128]{3,2,1,0:T(8,128)}, u32[]{:S(2)}) copy-start(f32[1,128,16,128]{3,2,1,0:T(8,128)} %param.20) | copy-start | bytes 3145732
  11.5 4.2 %copy-start.4 = (f32[1,128,16,128]{3,2,1,0:T(8,128)S(1)}, f32[1,128,16,128]{3,2,1,0:T(8,128)}, u32[]{:S(2)}) copy-start(f32[1,128,16,128]{3,2,1,0:T(8,128)} %param.22) | copy-start | bytes 3145732
  15.1 0.8 copy-start
  17.2 1.6 %collective-permute-start.2 = (f32[256,128]{1,0:T(8,128)S(1)}, f32[256,128]{1,0:T(8,128)S(1)}, u32[]{:S(2)}, u32[]{:S(2)}) collective-permute-start(f32[256,128]{1,0:T(8,128)S(1)} %get-tuple-element.57), channel_id=1, source_target_pairs={{0,1},{1,0},{2,3},{3,2},{4,5},{5,4},{6,7},{7,6},{8,9},{9,8},{10,11... | collective-permute-start | bytes 393224 | tf_op jit(solution)/shard_map/ppermute | solution.py:602
  17.3 1.5 %copy-start.16 = (bf16[2,16,48]{2,1,0:T(8,128)(2,1)S(1)}, bf16[2,16,48]{2,1,0:T(8,128)(2,1)}, u32[]{:S(2)}) copy-start(bf16[2,16,48]{2,1,0:T(8,128)(2,1)} %constant.24.clone.refs_10_) | copy-start | bytes 9220
  18.8 11.5 %copy-start.15 = (bf16[2,16,48]{2,1,0:T(8,128)(2,1)S(1)}, bf16[2,16,48]{2,1,0:T(8,128)(2,1)}, u32[]{:S(2)}) copy-start(bf16[2,16,48]{2,1,0:T(8,128)(2,1)} %constant.25.clone.refs_14_) | copy-start | bytes 9220
  19.0 11.3 %collective-permute-start.3 = (f32[512,128]{1,0:T(8,128)S(1)}, f32[512,128]{1,0:T(8,128)S(1)}, u32[]{:S(2)}, u32[]{:S(2)}) collective-permute-start(f32[512,128]{1,0:T(8,128)S(1)} %early_1.1.refs_12_), channel_id=1, source_target_pairs={{1,2},{3,4},{5,6},{7,8},{9,10},{11,12},{13,14},{15,16},{17,18},{19... | collective-permute-start | bytes 786440 | tf_op jit(solution)/shard_map/ppermute | solution.py:608
  30.3 1.0 %copy-start.11 = (bf16[256,256]{1,0:T(8,128)(2,1)S(1)}, bf16[256,256]{1,0:T(8,128)(2,1)}, u32[]{:S(2)}) copy-start(bf16[256,256]{1,0:T(8,128)(2,1)} %constant.22.clone.refs_5_.refs_2_.refs_1_) | copy-start | bytes 393220
  31.2 1.7 %collective-permute-start.4 = (f32[256,128]{1,0:T(8,128)S(1)}, f32[256,128]{1,0:T(8,128)S(1)}, u32[]{:S(2)}, u32[]{:S(2)}) collective-permute-start(f32[256,128]{1,0:T(8,128)S(1)} %get-tuple-element.63), channel_id=1, source_target_pairs={{0,1},{1,0},{2,3},{3,2},{4,5},{5,4},{6,7},{7,6},{8,9},{9,8},{10,11... | collective-permute-start | bytes 393224 | tf_op jit(solution)/shard_map/ppermute | solution.py:602
  33.8 2.1 %collective-permute-start.5 = (f32[256,128]{1,0:T(8,128)S(1)}, f32[256,128]{1,0:T(8,128)S(1)}, u32[]{:S(2)}, u32[]{:S(2)}) collective-permute-start(f32[256,128]{1,0:T(8,128)S(1)} %get-tuple-element.70), channel_id=1, source_target_pairs={{0,1},{1,0},{2,3},{3,2},{4,5},{5,4},{6,7},{7,6},{8,9},{9,8},{10,11... | collective-permute-start | bytes 393224 | tf_op jit(solution)/shard_map/ppermute | solution.py:602
  36.1 13.4 %copy-start.12 = (bf16[512,128]{1,0:T(8,128)(2,1)S(1)}, bf16[512,128]{1,0:T(8,128)(2,1)}, u32[]{:S(2)}) copy-start(bf16[512,128]{1,0:T(8,128)(2,1)} %constant.28.clone.refs_5_) | copy-start | bytes 393220
  36.1 13.4 %copy-start.13 = (bf16[2,72,256]{2,1,0:T(8,128)(2,1)S(1)}, bf16[2,72,256]{2,1,0:T(8,128)(2,1)}, u32[]{:S(2)}) copy-start(bf16[2,72,256]{2,1,0:T(8,128)(2,1)} %constant.32.clone.refs_3_) | copy-start | bytes 221188
  36.2 13.4 %copy-start.14 = (bf16[2,72,16]{2,1,0:T(8,128)(2,1)S(1)}, bf16[2,72,16]{2,1,0:T(8,128)(2,1)}, u32[]{:S(2)}) copy-start(bf16[2,72,16]{2,1,0:T(8,128)(2,1)} %constant.29.clone.refs_4_) | copy-start | bytes 13828
  36.2 12.1 %collective-permute-start.6 = (f32[640,128]{1,0:T(8,128)S(1)}, f32[640,128]{1,0:T(8,128)S(1)}, u32[]{:S(2)}, u32[]{:S(2)}) collective-permute-start(f32[640,128]{1,0:T(8,128)S(1)} %early_3.1.refs_12_), channel_id=1, source_target_pairs={{1,2},{3,4},{5,6},{7,8},{9,10},{11,12},{13,14},{15,16},{17,18},{19... | collective-permute-start | bytes 983048 | tf_op jit(solution)/shard_map/ppermute | solution.py:608
  50.2 1.4 %collective-permute-start.7 = (f32[144,128]{1,0:T(8,128)S(1)}, f32[144,128]{1,0:T(8,128)S(1)}, u32[]{:S(2)}, u32[]{:S(2)}) collective-permute-start(f32[144,128]{1,0:T(8,128)S(1)} %get-tuple-element.82), channel_id=1, source_target_pairs={{0,1},{1,0},{2,3},{3,2},{4,5},{5,4},{6,7},{7,6},{8,9},{9,8},{10,11... | collective-permute-start | bytes 221192 | tf_op jit(solution)/shard_map/ppermute | solution.py:602
  51.6 9.7 %collective-permute-start.10 = (f32[72,512]{1,0:T(8,128)S(1)}, f32[72,512]{1,0:T(8,128)S(1)}, u32[]{:S(2)}, u32[]{:S(2)}) collective-permute-start(f32[72,512]{1,0:T(8,128)S(1)} %merge.1.refs_0_), channel_id=1, source_target_pairs={{0,192},{64,128},{128,64},{192,0},{1,193},{65,129},{129,65},{193,1... | collective-permute-start | bytes 442376 | tf_op jit(solution)/shard_map/ppermute | solution.py:602
  54.7 8.2 %collective-permute-start.9 = (f32[72,512]{1,0:T(8,128)S(1)}, f32[72,512]{1,0:T(8,128)S(1)}, u32[]{:S(2)}, u32[]{:S(2)}) collective-permute-start(f32[72,512]{1,0:T(8,128)S(1)} %merge.1.refs_0_), channel_id=1, source_target_pairs={{0,128},{64,192},{128,0},{192,64},{1,129},{65,193},{129,1},{193,65... | collective-permute-start | bytes 442376 | tf_op jit(solution)/shard_map/ppermute | solution.py:602
  55.3 7.6 %collective-permute-start.8 = (f32[72,512]{1,0:T(8,128)S(1)}, f32[72,512]{1,0:T(8,128)S(1)}, u32[]{:S(2)}, u32[]{:S(2)}) collective-permute-start(f32[72,512]{1,0:T(8,128)S(1)} %merge.1.refs_0_), channel_id=1, source_target_pairs={{0,64},{64,0},{128,192},{192,128},{1,65},{65,1},{129,193},{193,129... | collective-permute-start | bytes 442376 | tf_op jit(solution)/shard_map/ppermute | solution.py:602
  63.0 6.5 %copy-start.8 = (bf16[2,128,144]{2,1,0:T(8,128)(2,1)S(1)}, bf16[2,128,144]{2,1,0:T(8,128)(2,1)}, u32[]{:S(2)}) copy-start(bf16[2,128,144]{2,1,0:T(8,128)(2,1)} %constant.31.clone.refs_5_) | copy-start | bytes 221188
  63.0 5.2 %collective-permute-start.11 = (f32[72,512]{1,0:T(8,128)S(1)}, f32[72,512]{1,0:T(8,128)S(1)}, u32[]{:S(2)}, u32[]{:S(2)}) collective-permute-start(f32[72,512]{1,0:T(8,128)S(1)} %add_four.1.refs_0_), channel_id=1, source_target_pairs={{0,32},{32,0},{1,33},{33,1},{2,34},{34,2},{3,35},{35,3},{4,36},{36... | collective-permute-start | bytes 442376 | tf_op jit(solution)/shard_map/ppermute | solution.py:602
  68.2 1.3 %collective-permute-start.12 = (f32[8,128]{1,0:T(8,128)S(1)}, f32[8,128]{1,0:T(8,128)S(1)}, u32[]{:S(2)}, u32[]{:S(2)}) collective-permute-start(f32[8,128]{1,0:T(8,128)S(1)} %get-tuple-element.87), channel_id=1, source_target_pairs={{0,1},{1,0},{2,3},{3,2},{4,5},{5,4},{6,7},{7,6},{8,9},{9,8},{10,11... | collective-permute-start | bytes 12296 | tf_op jit(solution)/shard_map/ppermute | solution.py:602
  69.5 5.1 %collective-permute-start.13 = (f32[8,128]{1,0:T(8,128)S(1)}, f32[8,128]{1,0:T(8,128)S(1)}, u32[]{:S(2)}, u32[]{:S(2)}) collective-permute-start(f32[8,128]{1,0:T(8,128)S(1)} %add.3.refs_0_), channel_id=1, source_target_pairs={{0,16},{16,0},{1,17},{17,1},{2,18},{18,2},{3,19},{19,3},{4,20},{20... | collective-permute-start | bytes 12296 | tf_op jit(solution)/shard_map/ppermute | solution.py:602
  (2 other events, 1.3 us)

commit v4 on v3

--- a/solution.py
+++ b/solution.py
@@ -452,7 +452,7 @@
     interior(p, own_x, own_z, lap_p)
 
 
-def shrink(image, image_far, near_in, shrink_x, shrink_far, shrink_z, own, near):
+def shrink(image, image_far, shrink_x, shrink_far, shrink_z, own):
     core = lax.axis_index("core")
     rows_x = shrink_x[core]
     rows_far = shrink_far[core]
@@ -476,42 +476,47 @@
             parts += list(split(narrow[j]))
         pieces.append(dot(cat(parts, 1), shrink_z[...]) * UNIT)
     own[...] = cat(pieces, 1)
-    field = CY * OV
-    near[:field] = near_in[...]
-    for row in range(4):
-        for part in range(4):
-            lanes = slice(part * 128, part * 128 + 128)
-            spot = field + row * 4 + part
-            near[spot : spot + 1] = own[CXC + row : CXC + row + 1, lanes]
-
-
-def merge(own, near, out):
-    out[...] = own[...]
-    field = CY * OV
-    for row in range(4):
-        for part in range(4):
-            lanes = slice(part * 128, part * 128 + 128)
-            spot = field + row * 4 + part
-            at = slice(CXC + row, CXC + row + 1)
-            out[at, lanes] = own[at, lanes] + near[spot : spot + 1]
-
-
-def squares(a, b, total, squared):
-    core = lax.axis_index("core")
-    total[...] = a[...] + b[...]
-    first, last = grid_ends()
-    total[CXC + 4 : CXC + 6] = jnp.where(first | last, 0.0, total[CXC + 4 : CXC + 6])
-    total[0:2] = jnp.where(core == 0, total[0:2], total[CXC + 2 : CXC + 4])
-    total[CXC - 2 : CXC] = jnp.where(core == 0, total[CXC : CXC + 2], total[CXC - 2 : CXC])
-    value = total[:CXC]
-    value = value * value
+
+
+def fold(value):
     rows = value[0:8]
-    for r in range(1, CXC // 8):
+    for r in range(1, value.shape[0] // 8):
         rows = rows + value[8 * r : 8 * r + 8]
     folded = rows[:, :128]
     for c in range(1, 4):
         folded = folded + rows[:, 128 * c : 128 * c + 128]
-    squared[...] = folded
+    return folded
+
+
+def squares(a, b, total, near):
+    core = lax.axis_index("core")
+    total[...] = a[...] + b[...]
+    first, last = grid_ends()
+    total[CXC + 4 : CXC + 6] = jnp.where(first | last, 0.0, total[CXC + 4 : CXC + 6])
+    row = lax.broadcasted_iota(jnp.int32, (CXC, CYC * CZC), 0)
+    start = (1 - core) * (CXC - 2)
+    value = jnp.where((row >= start) & (row < start + 2), 0.0, total[:CXC])
+    for r in range(4):
+        for part in range(4):
+            lanes = slice(part * 128, part * 128 + 128)
+            spot = r * 4 + part
+            near[spot : spot + 1] = total[CXC + r : CXC + r + 1, lanes]
+    near[16:24] = fold(value * value)
+
+
+def pair_up(total, mine, other, out, squared):
+    core = lax.axis_index("core")
+    out[...] = total[...]
+    edge = mine[0:16] + other[0:16]
+    for r in range(4):
+        for part in range(4):
+            lanes = slice(part * 128, part * 128 + 128)
+            spot = r * 4 + part
+            out[CXC + r : CXC + r + 1, lanes] = edge[spot : spot + 1]
+    out[0:2] = jnp.where(core == 0, out[0:2], out[CXC + 2 : CXC + 4])
+    out[CXC - 2 : CXC] = jnp.where(core == 0, out[CXC : CXC + 2], out[CXC - 2 : CXC])
+    edge = edge * edge
+    squared[...] = (mine[16:24] + other[16:24]) + (edge[0:8] + edge[8:16])
 
 
 def last_fields(near, far, p, p_before, lap_p, source, amounts, halo_x, lap_out, base):
@@ -526,8 +531,8 @@
             base[y] = 2.0 * p[y] - p_before[y] + source[y] * weight
 
 
-def add_four(own, one, two, three, out):
-    out[...] = (own[...] + one[...]) + (two[...] + three[...])
+def add_two(a, b, out):
+    out[...] = a[...] + b[...]
 
 
 def spread(total, sigma, lap, base, grow_z, grow_new, zeroth, first, second):
@@ -550,18 +555,27 @@
         out[k] = value
 
 
-def finish(count, parts, total, zeroth, first, second, direction, p_last):
+def finish(count, parts, total, zeroth, first, second, direction, p_last, held, sems):
     value = parts[0]
     for k in range(1, parts.shape[0]):
         value = value + parts[k]
     value = jnp.sum(jnp.sum(value, axis=0, keepdims=True), axis=1, keepdims=True)
-    scale = jnp.sqrt(value * (1.0 / count) + EPSILON)
-    inverse = 1.0 / scale
+    inverse = 1.0 / jnp.sqrt(value * (1.0 / count) + EPSILON)
+    rate = LEARN * inverse
+    chunks = sems.shape[0]
+    step = CX // chunks
+    copies = []
+    for c in range(chunks):
+        rows = slice(c * step, c * step + step)
+        for y in range(CY):
+            value = zeroth[y, rows] + rate * (first[y, rows] + rate * second[y, rows])
+            held[pl.ds(c * step * CY + y, step, stride=CY), :] = value
+        block = pl.ds(c * step * CY, step * CY)
+        copies.append(pltpu.make_async_copy(held.at[block], p_last.at[block], sems.at[c]))
+        copies[-1].start()
     direction[...] = total[:CXC] * inverse
-    rate = LEARN * inverse
-    for y in range(CY):
-        value = zeroth[y] + rate * (first[y] + rate * second[y])
-        p_last[pl.ds(y, CX, stride=CY), :] = value
+    for copy in copies:
+        copy.wait()
 
 
 VM = pl.BlockSpec(memory_space=pltpu.VMEM)
@@ -574,7 +588,7 @@
     return jax.ShapeDtypeStruct((count, lanes), F32)
 
 
-def call(body, outs, *args, smem=0, scratch=(), flops=0, name=None, held=()):
+def call(body, outs, *args, smem=0, scratch=(), flops=0, name=None, held=(), out_specs=None):
     size = sum(int(np.prod(a.shape)) * a.dtype.itemsize for a in args)
     count = len(args)
 
@@ -587,7 +601,7 @@
         in_specs=[SM] * smem
         + [VM] * (count - smem)
         + [pl.BlockSpec(memory_space=pl.ANY)] * len(held),
-        out_specs=jax.tree.map(lambda _: VM, outs),
+        out_specs=jax.tree.map(lambda _: VM, outs) if out_specs is None else out_specs,
         scratch_shapes=list(scratch),
         compiler_params=PARAMS,
         cost_estimate=pl.CostEstimate(flops=flops, bytes_accessed=size, transcendentals=0),
@@ -695,31 +709,34 @@
         )
         far = far_swap(sent)
 
-    own, near = call(
-        shrink,
-        (rows_of(ROWS, CYC * CZC), rows_of(CY * OV + 16)),
-        image, image_far, near, const["shrink_x"], const["shrink_far"], const["shrink_z"],
+    partial = call(
+        shrink, rows_of(ROWS, CYC * CZC),
+        image, image_far, const["shrink_x"], const["shrink_far"], const["shrink_z"],
         flops=10**8, name="shrink",
     )
+    other = xor_swap(partial, "y", 1)
     near = xor_swap(near, "core", 1)
     lap_p = call(inside_one, FIELD, p, own_x, own_z, flops=5 * 10**8, name="inside_last")
-    partial = call(merge, rows_of(ROWS, CYC * CZC), own, near, name="merge")
-
-    two, one, three = (xor_swap(partial, "y", m) for m in (2, 1, 3))
     lap_p, base = call(
         last_fields, (FIELD, FIELD), near, far, p, p_before, lap_p, source, amounts, halo_x,
         flops=10**8, name="last_fields",
     )
     held = (lap_p, base)
     partial = call(
-        add_four, rows_of(ROWS, CYC * CZC), partial, one, two, three, name="add_four", held=held
-    )
-    other = xor_swap(partial, "xl", 1)
+        add_two, rows_of(ROWS, CYC * CZC), partial, other, name="add_y1", held=held
+    )
+    partial = call(
+        add_two, rows_of(ROWS, CYC * CZC), partial, xor_swap(partial, "y", 3), name="add_y3",
+        held=held,
+    )
+    total, mine = call(
+        squares, (rows_of(ROWS, CYC * CZC), rows_of(24)), partial, xor_swap(partial, "xl", 1),
+        name="squares", held=held,
+    )
     total, squared_sum = call(
-        squares, (rows_of(ROWS, CYC * CZC), rows_of(8)), partial, other, name="squares",
-        held=held,
-    )
-    squared_sum = squared_sum + xor_swap(squared_sum, "core", 1)
+        pair_up, (rows_of(ROWS, CYC * CZC), rows_of(8)), total, mine, xor_swap(mine, "core", 1),
+        name="pair_up", held=held,
+    )
     terms = call(
         spread, (FIELD,) * 3, total, sigma, lap_p, base, const["grow_z"], const["grow_new"],
         flops=10**8, name="spread",
@@ -733,8 +750,10 @@
     count = float(lax.axis_size(TILE) * CXC * CYC * CZC)
     direction, p_last = call(
         functools.partial(finish, count),
-        (rows_of(CXC, CYC * CZC), rows_of(CX * CY)),
+        (rows_of(CXC, CYC * CZC), pltpu.HBM((CX * CY, CZ), F32)),
         parts, total, *terms, name="finish",
+        scratch=[pltpu.VMEM((CX * CY, CZ), F32), pltpu.SemaphoreType.DMA((4,))],
+        out_specs=(VM, pl.BlockSpec(memory_space=pltpu.HBM)),
     )
     return direction, p_last.reshape(1, CX, CY, CZ)
 

time: 87.7 us -> 87 us (level)
  waiting for transfers between devices: 31.7 us -> 29.4 us
    ppermute x11 -> x10, waiting for transfers between devices: 17.8 us -> 15.6 us  [xor_swap(): return lax.ppermute(x, axis, [(i, i ^ mask) for i in range(count)])]
    ppermute x11 -> x10, starting transfers between devices: 5.3 us -> 5.88 us  [xor_swap(): return lax.ppermute(x, axis, [(i, i ^ mask) for i in range(count)])]
    pallas_call x20 -> x21, Pallas kernels: 17.7 us -> 18 us  [call(): pl.pallas_call(run, out_shape=outs, in_specs=[SM] * smem + [VM] * (count...]
  transfers between devices with their start and end apart: 14 -> 13, of which waited for: 8 -> 8; matrix products, arithmetic and copies ran while one was open for 0% -> 0% of each run, Pallas kernels for 12% -> 12%
where the time goes in v4:
time: 87 us; the launch traced here: 86.2 us
  waiting for transfers between devices  29.4 us (34%)
  starting transfers between devices  23.5 us (27%)
  Pallas kernels  19.2 us (22%)
  blocking collectives  10.4 us (12%)
  local copies, waits for them, and re-layouts  2.47 us (3%)
  between operations  1.24 us (1%)
    pallas_call x21, Pallas kernels, call(): pl.pallas_call(run, out_shape=outs, in_specs=[SM] * smem + [VM] * (count...  18 us
    ppermute x3, starting transfers between devices, far_swap(): return lax.ppermute(x, TILE, pairs + [(b, a) for a, b in pairs])  17.6 us
    ppermute x10, waiting for transfers between devices, xor_swap(): return lax.ppermute(x, axis, [(i, i ^ mask) for i in range(count)])  15.6 us
    ppermute x3, waiting for transfers between devices, far_swap(): return lax.ppermute(x, TILE, pairs + [(b, a) for a, b in pairs])  13.8 us
    all_to_all x1, blocking collectives, on_device(): parts = lax.all_to_all(copies, 'z', split_axis=0, concat_axis=0, tiled=True)  10.4 us
    ppermute x10, starting transfers between devices, xor_swap(): return lax.ppermute(x, axis, [(i, i ^ mask) for i in range(count)])  5.88 us
    unnamed x40, local copies, waits for them, and re-layouts  2.47 us
  transfers between devices with their start and end apart: 13, of which 8 were waited for; matrix products, arithmetic and copies ran while one was open for 0% of the time, Pallas kernels for 12%

profile of v4, /device:TPU:6, one launch (start us, length us, event | category | flops | bytes accessed | tf_op | source)
XLA Modules:
  0.0 86.2 jit_solution(13956958976549803461)
XLA Ops:
  0.7 1.2 %first_edges.1 = (f32[264,128]{1,0:T(8,128)S(1)}, f32[280,128]{1,0:T(8,128)S(1)}) custom-call(f32[2048,128]{1,0:T(8,128)} %bitcast.6, f32[2048,128]{1,0:T(8,128)} %bitcast.8, f32[64,512]{1,0:T(8,128)} %refs_0_.1), custom_call_target="tpu_custom_call" | custom-call | tf_op jit(solution)/shard_map/first_edges/pallas_call | solution.py:641
  1.9 8.0 %collective-permute-start.1 = (f32[280,128]{1,0:T(8,128)S(1)}, f32[280,128]{1,0:T(8,128)S(1)}, u32[]{:S(2)}, u32[]{:S(2)}) collective-permute-start(f32[280,128]{1,0:T(8,128)S(1)} %get-tuple-element.49), channel_id=1, source_target_pairs={{1,2},{3,4},{5,6},{7,8},{9,10},{11,12},{13,14},{15,16},{17,18},{19... | collective-permute-start | bytes 430088 | tf_op jit(solution)/shard_map/ppermute | solution.py:622
  10.1 0.5 copy-done.17
  10.6 0.9 %copy-done.10 = bf16[256,256]{1,0:T(8,128)(2,1)S(1)} copy-done((bf16[256,256]{1,0:T(8,128)(2,1)S(1)}, bf16[256,256]{1,0:T(8,128)(2,1)}, u32[]{:S(2)}) %copy-start.10) | copy-done | bytes 131096
  11.5 3.5 %prepare.1 = (f32[16,128,128]{2,1,0:T(8,128)S(1)}, f32[16,128,128]{2,1,0:T(8,128)S(1)}, f32[16,128,128]{2,1,0:T(8,128)S(1)}, f32[16,128,128]{2,1,0:T(8,128)S(1)}...) custom-call(s32[64]{0:T(128)S(1)} %bitcast.12, s32[64]{0:T(128)S(1)} %copy-done.18, f32[5]{0:T(128)S(1)} %copy-done.19, ...), custom_call_target="tpu_custom_call" | custom-call | flops 1000000000 | bytes 2359828 | tf_op jit(solution)/shard_map/prepare/pallas_call | solution.py:598
  15.2 0.6 speed.1
  15.9 1.3 %advance_0.1 = (f32[16,128,128]{2,1,0:T(8,128)S(1)}, f32[16,128,128]{2,1,0:T(8,128)S(1)}, f32[256,128]{1,0:T(8,128)S(1)}, f32[16,128,128]{2,1,0:T(8,128)S(1)}) custom-call(f32[264,128]{1,0:T(8,128)S(1)} %collective-permute-done.refs_1_.refs_0_, f32[280,128]{1,0:T(8,128)S(1)} %collective-permute-done.1.refs_2_.refs_1_, ...), custom_call_target="tpu_custom_call" | custom-call | flops 100000000 | bytes 8712192 | tf_op jit(solution)/shard_map/advance_0/pallas_call | solution.py:598
  17.3 1.5 %inside_0.1 = (f32[16,128,128]{2,1,0:T(8,128)S(1)}, f32[16,128,128]{2,1,0:T(8,128)S(1)}) custom-call(f32[16,128,128]{2,1,0:T(8,128)S(1)} %get-tuple-element.58.refs_0_.refs_1_.refs_2_.refs_3_, f32[16,128,128]{2,1,0:T(8,128)S(1)} %get-tuple-element.59.refs_1_.refs_3_.refs_4_.refs_5_.refs_11_.refs_16_, bf16[256,256]{1,0:T(8,128)(2,1)S(1)} %copy-done.10, ...), custom_call_target="tpu_custom_call" | custom-call | flops 1000000000 | bytes 2359296 | tf_op jit(solution)/shard_map/inside_0/pallas_call | solution.py:598
  19.0 4.6 %collective-permute-start.3 = (f32[512,128]{1,0:T(8,128)S(1)}, f32[512,128]{1,0:T(8,128)S(1)}, u32[]{:S(2)}, u32[]{:S(2)}) collective-permute-start(f32[512,128]{1,0:T(8,128)S(1)} %early_1.1.refs_12_), channel_id=1, source_target_pairs={{1,2},{3,4},{5,6},{7,8},{9,10},{11,12},{13,14},{15,16},{17,18},{19... | collective-permute-start | bytes 786440 | tf_op jit(solution)/shard_map/ppermute | solution.py:622
  23.7 6.7 %collective-permute-done.3.refs_1_.refs_19_ = f32[512,128]{1,0:T(8,128)S(1)} collective-permute-done((f32[512,128]{1,0:T(8,128)S(1)}, f32[512,128]{1,0:T(8,128)S(1)}, u32[]{:S(2)}, u32[]{:S(2)}) %collective-permute-start.3) | collective-permute-done | bytes 262176 | tf_op jit(solution)/shard_map/ppermute | solution.py:622
  30.3 0.9 %advance_1.1 = (f32[16,128,128]{2,1,0:T(8,128)S(1)}, f32[16,128,128]{2,1,0:T(8,128)S(1)}, f32[256,128]{1,0:T(8,128)S(1)}, f32[256,128]{1,0:T(8,128)S(1)}, f32[16,128,128]{2,1,0:T(8,128)S(1)}) custom-call(f32[256,128]{1,0:T(8,128)S(1)} %collective-permute-done.2.refs_0_, f32[512,128]{1,0:T(8,128)S(1)} %collective-permute-done.3.refs_1_.refs_19_, ...), custom_call_target="tpu_custom_call" | custom-call | flops 100000000 | bytes 9157632 | tf_op jit(solution)/shard_map/advance_1/pallas_call | solution.py:598
  31.3 1.6 %inside_1.1 = (f32[16,128,128]{2,1,0:T(8,128)S(1)}, f32[16,128,128]{2,1,0:T(8,128)S(1)}) custom-call(f32[16,128,128]{2,1,0:T(8,128)S(1)} %get-tuple-element.65.refs_0_.refs_2_.refs_3_, f32[16,128,128]{2,1,0:T(8,128)S(1)} %get-tuple-element.66.refs_1_.refs_4_.refs_5_, bf16[256,256]{1,0:T(8,128)(2,1)S(1)} %copy-done.11, bf16[256,256]{1,0:T(8,128)(2,1)S(1)} %copy-done.9), custom_call_target="tpu_custom_call" | custom-call | flops 1000000000 | bytes 2359296 | tf_op jit(solution)/shard_map/inside_1/pallas_call | solution.py:598
  32.9 0.9 %advance_2.1 = (f32[16,128,128]{2,1,0:T(8,128)S(1)}, f32[16,128,128]{2,1,0:T(8,128)S(1)}, f32[256,128]{1,0:T(8,128)S(1)}, f32[16,128,128]{2,1,0:T(8,128)S(1)}) custom-call(f32[256,128]{1,0:T(8,128)S(1)} %collective-permute-done.4.refs_0_, f32[256,128]{1,0:T(8,128)S(1)} %get-tuple-element.64.refs_1_, ...), custom_call_target="tpu_custom_call" | custom-call | flops 100000000 | bytes 9744384 | tf_op jit(solution)/shard_map/advance_2/pallas_call | solution.py:598
  33.8 0.6 collective-permute-start.5
  34.4 1.5 %inside_2.1 = (f32[16,128,128]{2,1,0:T(8,128)S(1)}, f32[16,128,128]{2,1,0:T(8,128)S(1)}) custom-call(f32[16,128,128]{2,1,0:T(8,128)S(1)} %get-tuple-element.71.refs_0_.refs_1_.refs_2_.refs_3_, f32[16,128,128]{2,1,0:T(8,128)S(1)} %get-tuple-element.72.refs_1_.refs_3_.refs_4_, bf16[256,256]{1,0:T(8,128)(2,1)S(1)} %copy-done.11, bf16[256,256]{1,0:T(8,128)(2,1)S(1)} %copy-done.9), custom_call_target="tpu_custom_call" | custom-call | flops 1000000000 | bytes 2359296 | tf_op jit(solution)/shard_map/inside_2/pallas_call | solution.py:598
  36.2 5.0 %collective-permute-start.6 = (f32[640,128]{1,0:T(8,128)S(1)}, f32[640,128]{1,0:T(8,128)S(1)}, u32[]{:S(2)}, u32[]{:S(2)}) collective-permute-start(f32[640,128]{1,0:T(8,128)S(1)} %early_3.1.refs_12_), channel_id=1, source_target_pairs={{1,2},{3,4},{5,6},{7,8},{9,10},{11,12},{13,14},{15,16},{17,18},{19... | collective-permute-start | bytes 983048 | tf_op jit(solution)/shard_map/ppermute | solution.py:622
  41.1 7.2 %collective-permute-done.6.refs_1_ = f32[640,128]{1,0:T(8,128)S(1)} collective-permute-done((f32[640,128]{1,0:T(8,128)S(1)}, f32[640,128]{1,0:T(8,128)S(1)}, u32[]{:S(2)}, u32[]{:S(2)}) %collective-permute-start.6) | collective-permute-done | bytes 327712 | tf_op jit(solution)/shard_map/ppermute | solution.py:622
  48.3 1.2 %advance_3.1 = (f32[16,128,128]{2,1,0:T(8,128)S(1)}, f32[128,128]{1,0:T(8,128)S(1)}, f32[128,128]{1,0:T(8,128)S(1)}, f32[16,128,128]{2,1,0:T(8,128)S(1)}, f32[128,128]{1,0:T(8,128)S(1)}) custom-call(f32[256,128]{1,0:T(8,128)S(1)} %collective-permute-done.5.refs_0_, f32[640,128]{1,0:T(8,128)S(1)} %collective-permute-done.6.refs_1_, ...), custom_call_target="tpu_custom_call" | custom-call | flops 100000000 | bytes 13745152 | tf_op jit(solution)/shard_map/advance_3/pallas_call | solution.py:598
  49.5 0.6 shrink.1.refs_0_
  50.2 1.7 %collective-permute-start.7 = (f32[72,512]{1,0:T(8,128)S(1)}, f32[72,512]{1,0:T(8,128)S(1)}, u32[]{:S(2)}, u32[]{:S(2)}) collective-permute-start(f32[72,512]{1,0:T(8,128)S(1)} %shrink.1.refs_0_), channel_id=1, source_target_pairs={{0,64},{64,0},{128,192},{192,128},{1,65},{65,1},{129,193},{193,129... | collective-permute-start | bytes 442376 | tf_op jit(solution)/shard_map/ppermute | solution.py:616
  51.9 0.8 inside_last.1.refs_4_
  52.7 0.4 collective-permute-done.8.refs_0_
  53.5 2.0 %collective-permute-done.7.refs_1_ = f32[72,512]{1,0:T(8,128)S(1)} collective-permute-done((f32[72,512]{1,0:T(8,128)S(1)}, f32[72,512]{1,0:T(8,128)S(1)}, u32[]{:S(2)}, u32[]{:S(2)}) %collective-permute-start.7) | collective-permute-done | bytes 147488 | tf_op jit(solution)/shard_map/ppermute | solution.py:616
  55.4 3.1 %collective-permute-start.9 = (f32[72,512]{1,0:T(8,128)S(1)}, f32[72,512]{1,0:T(8,128)S(1)}, u32[]{:S(2)}, u32[]{:S(2)}) collective-permute-start(f32[72,512]{1,0:T(8,128)S(1)} %add_y1.1.refs_0_), channel_id=1, source_target_pairs={{0,192},{64,128},{128,64},{192,0},{1,193},{65,129},{129,65},{193,1... | collective-permute-start | bytes 442376 | tf_op jit(solution)/shard_map/ppermute | solution.py:616
  58.5 3.3 %collective-permute-done.9.refs_1_ = f32[72,512]{1,0:T(8,128)S(1)} collective-permute-done((f32[72,512]{1,0:T(8,128)S(1)}, f32[72,512]{1,0:T(8,128)S(1)}, u32[]{:S(2)}, u32[]{:S(2)}) %collective-permute-start.9) | collective-permute-done | bytes 147488 | tf_op jit(solution)/shard_map/ppermute | solution.py:616
  62.0 5.1 %collective-permute-done.10.refs_1_ = f32[72,512]{1,0:T(8,128)S(1)} collective-permute-done((f32[72,512]{1,0:T(8,128)S(1)}, f32[72,512]{1,0:T(8,128)S(1)}, u32[]{:S(2)}, u32[]{:S(2)}) %collective-permute-start.10) | collective-permute-done | bytes 147488 | tf_op jit(solution)/shard_map/ppermute | solution.py:616
  67.3 1.2 %collective-permute-done.11.refs_2_ = f32[24,128]{1,0:T(8,128)S(1)} collective-permute-done((f32[24,128]{1,0:T(8,128)S(1)}, f32[24,128]{1,0:T(8,128)S(1)}, u32[]{:S(2)}, u32[]{:S(2)}) %collective-permute-start.11) | collective-permute-done | bytes 12320 | tf_op jit(solution)/shard_map/ppermute | solution.py:616
  68.6 0.8 copy-done.8
  69.3 0.8 spread.1
  70.1 3.5 %collective-permute-done.12.refs_1_ = f32[8,128]{1,0:T(8,128)S(1)} collective-permute-done((f32[8,128]{1,0:T(8,128)S(1)}, f32[8,128]{1,0:T(8,128)S(1)}, u32[]{:S(2)}, u32[]{:S(2)}) %collective-permute-start.12) | collective-permute-done | bytes 4128 | tf_op jit(solution)/shard_map/ppermute | solution.py:616
  73.7 10.4 %all_to_all.5.refs_0_ = f32[8,8,128]{2,1,0:T(8,128)S(1)} all-to-all(f32[8,8,128]{2,1,0:T(8,128)S(1)} %widen.1), channel_id=1, replica_groups=mesh['y'=4,'xl'=2,'xh'=2,'z'=8,'core'=2] {'z'}, dimensions={0} | all-to-all | bytes 65536 | tf_op jit(solution)/shard_map/all_to_all | solution.py:749
  84.1 2.0 %finish.1 = (f32[64,512]{1,0:T(8,128)}, f32[2048,128]{1,0:T(8,128)}) custom-call(f32[8,8,128]{2,1,0:T(8,128)S(1)} %all_to_all.5.refs_0_, f32[72,512]{1,0:T(8,128)S(1)} %get-tuple-element.88.refs_0_.refs_1_, f32[16,128,128]{2,1,0:T(8,128)S(1)} %get-tuple-element.89.refs_2_, f32[16,128,128]{2,1,0:T(8,128)S(1)} %get-tuple-element.90.refs_3_, ...), custom_call_target="tpu_custom_call" | custom-call | bytes 3325952 | tf_op jit(solution)/shard_map/finish/pallas_call | solution.py:598
  (57 shorter events, 1.7 us)
Async XLA Ops:
  0.6 9.4 %copy-start.1 = (f32[1,128,16,128]{3,2,1,0:T(8,128)S(1)}, f32[1,128,16,128]{3,2,1,0:T(8,128)}, u32[]{:S(2)}) copy-start(f32[1,128,16,128]{3,2,1,0:T(8,128)} %param.19) | copy-start | bytes 3145732
  0.6 9.4 %copy-start.2 = (f32[1,128,16,128]{3,2,1,0:T(8,128)S(1)}, f32[1,128,16,128]{3,2,1,0:T(8,128)}, u32[]{:S(2)}) copy-start(f32[1,128,16,128]{3,2,1,0:T(8,128)} %param.21) | copy-start | bytes 3145732
  0.6 9.4 %copy-start.9 = (bf16[256,256]{1,0:T(8,128)(2,1)S(1)}, bf16[256,256]{1,0:T(8,128)(2,1)}, u32[]{:S(2)}) copy-start(bf16[256,256]{1,0:T(8,128)(2,1)} %constant.26.clone.refs_6_.refs_3_.refs_2_) | copy-start | bytes 393220
  1.9 13.3 %collective-permute-start.1 = (f32[280,128]{1,0:T(8,128)S(1)}, f32[280,128]{1,0:T(8,128)S(1)}, u32[]{:S(2)}, u32[]{:S(2)}) collective-permute-start(f32[280,128]{1,0:T(8,128)S(1)} %get-tuple-element.49), channel_id=1, source_target_pairs={{1,2},{3,4},{5,6},{7,8},{9,10},{11,12},{13,14},{15,16},{17,18},{19... | collective-permute-start | bytes 430088 | tf_op jit(solution)/shard_map/ppermute | solution.py:622
  9.9 0.7 copy-start.18
  9.9 0.7 copy-start.19
  10.0 5.2 %collective-permute-start = (f32[264,128]{1,0:T(8,128)S(1)}, f32[264,128]{1,0:T(8,128)S(1)}, u32[]{:S(2)}, u32[]{:S(2)}) collective-permute-start(f32[264,128]{1,0:T(8,128)S(1)} %get-tuple-element.48), channel_id=1, source_target_pairs={{0,1},{1,0},{2,3},{3,2},{4,5},{5,4},{6,7},{7,6},{8,9},{9,8},{10,11... | collective-permute-start | bytes 405512 | tf_op jit(solution)/shard_map/ppermute | solution.py:616
  10.6 0.9 %copy-start.10 = (bf16[256,256]{1,0:T(8,128)(2,1)S(1)}, bf16[256,256]{1,0:T(8,128)(2,1)}, u32[]{:S(2)}) copy-start(bf16[256,256]{1,0:T(8,128)(2,1)} %constant.22.clone.refs_5_.refs_2_.refs_1_) | copy-start | bytes 393220
  11.5 3.6 %copy-start.5 = (bf16[256,256]{1,0:T(8,128)(2,1)S(1)}, bf16[256,256]{1,0:T(8,128)(2,1)}, u32[]{:S(2)}) copy-start(bf16[256,256]{1,0:T(8,128)(2,1)} %constant.27.clone.refs_3_.refs_4_) | copy-start | bytes 393220
  11.5 3.6 %copy-start.6 = (f32[64,512]{1,0:T(8,128)S(1)}, f32[64,512]{1,0:T(8,128)}, u32[]{:S(2)}) copy-start(f32[64,512]{1,0:T(8,128)} %refs_0_.1) | copy-start | bytes 393220
  11.5 3.6 %copy-start.7 = (bf16[2,136,144]{2,1,0:T(8,128)(2,1)S(1)}, bf16[2,136,144]{2,1,0:T(8,128)(2,1)}, u32[]{:S(2)}) copy-start(bf16[2,136,144]{2,1,0:T(8,128)(2,1)} %constant.30.clone.refs_4_) | copy-start | bytes 235012
  11.5 4.2 %copy-start.3 = (f32[1,128,16,128]{3,2,1,0:T(8,128)S(1)}, f32[1,128,16,128]{3,2,1,0:T(8,128)}, u32[]{:S(2)}) copy-start(f32[1,128,16,128]{3,2,1,0:T(8,128)} %param.20) | copy-start | bytes 3145732
  11.5 4.2 %copy-start.4 = (f32[1,128,16,128]{3,2,1,0:T(8,128)S(1)}, f32[1,128,16,128]{3,2,1,0:T(8,128)}, u32[]{:S(2)}) copy-start(f32[1,128,16,128]{3,2,1,0:T(8,128)} %param.22) | copy-start | bytes 3145732
  15.1 0.8 copy-start
  17.2 1.6 %collective-permute-start.2 = (f32[256,128]{1,0:T(8,128)S(1)}, f32[256,128]{1,0:T(8,128)S(1)}, u32[]{:S(2)}, u32[]{:S(2)}) collective-permute-start(f32[256,128]{1,0:T(8,128)S(1)} %get-tuple-element.57), channel_id=1, source_target_pairs={{0,1},{1,0},{2,3},{3,2},{4,5},{5,4},{6,7},{7,6},{8,9},{9,8},{10,11... | collective-permute-start | bytes 393224 | tf_op jit(solution)/shard_map/ppermute | solution.py:616
  17.3 1.5 %copy-start.16 = (bf16[2,16,48]{2,1,0:T(8,128)(2,1)S(1)}, bf16[2,16,48]{2,1,0:T(8,128)(2,1)}, u32[]{:S(2)}) copy-start(bf16[2,16,48]{2,1,0:T(8,128)(2,1)} %constant.24.clone.refs_10_) | copy-start | bytes 9220
  18.8 11.5 %copy-start.15 = (bf16[2,16,48]{2,1,0:T(8,128)(2,1)S(1)}, bf16[2,16,48]{2,1,0:T(8,128)(2,1)}, u32[]{:S(2)}) copy-start(bf16[2,16,48]{2,1,0:T(8,128)(2,1)} %constant.25.clone.refs_14_) | copy-start | bytes 9220
  19.0 11.3 %collective-permute-start.3 = (f32[512,128]{1,0:T(8,128)S(1)}, f32[512,128]{1,0:T(8,128)S(1)}, u32[]{:S(2)}, u32[]{:S(2)}) collective-permute-start(f32[512,128]{1,0:T(8,128)S(1)} %early_1.1.refs_12_), channel_id=1, source_target_pairs={{1,2},{3,4},{5,6},{7,8},{9,10},{11,12},{13,14},{15,16},{17,18},{19... | collective-permute-start | bytes 786440 | tf_op jit(solution)/shard_map/ppermute | solution.py:622
  30.3 1.0 %copy-start.11 = (bf16[256,256]{1,0:T(8,128)(2,1)S(1)}, bf16[256,256]{1,0:T(8,128)(2,1)}, u32[]{:S(2)}) copy-start(bf16[256,256]{1,0:T(8,128)(2,1)} %constant.22.clone.refs_5_.refs_2_.refs_1_) | copy-start | bytes 393220
  31.2 1.7 %collective-permute-start.4 = (f32[256,128]{1,0:T(8,128)S(1)}, f32[256,128]{1,0:T(8,128)S(1)}, u32[]{:S(2)}, u32[]{:S(2)}) collective-permute-start(f32[256,128]{1,0:T(8,128)S(1)} %get-tuple-element.63), channel_id=1, source_target_pairs={{0,1},{1,0},{2,3},{3,2},{4,5},{5,4},{6,7},{7,6},{8,9},{9,8},{10,11... | collective-permute-start | bytes 393224 | tf_op jit(solution)/shard_map/ppermute | solution.py:616
  33.8 2.1 %collective-permute-start.5 = (f32[256,128]{1,0:T(8,128)S(1)}, f32[256,128]{1,0:T(8,128)S(1)}, u32[]{:S(2)}, u32[]{:S(2)}) collective-permute-start(f32[256,128]{1,0:T(8,128)S(1)} %get-tuple-element.70), channel_id=1, source_target_pairs={{0,1},{1,0},{2,3},{3,2},{4,5},{5,4},{6,7},{7,6},{8,9},{9,8},{10,11... | collective-permute-start | bytes 393224 | tf_op jit(solution)/shard_map/ppermute | solution.py:616
  36.1 13.4 %copy-start.12 = (bf16[512,128]{1,0:T(8,128)(2,1)S(1)}, bf16[512,128]{1,0:T(8,128)(2,1)}, u32[]{:S(2)}) copy-start(bf16[512,128]{1,0:T(8,128)(2,1)} %constant.28.clone.refs_4_) | copy-start | bytes 393220
  36.1 13.4 %copy-start.13 = (bf16[2,72,256]{2,1,0:T(8,128)(2,1)S(1)}, bf16[2,72,256]{2,1,0:T(8,128)(2,1)}, u32[]{:S(2)}) copy-start(bf16[2,72,256]{2,1,0:T(8,128)(2,1)} %constant.32.clone.refs_2_) | copy-start | bytes 221188
  36.2 13.4 %copy-start.14 = (bf16[2,72,16]{2,1,0:T(8,128)(2,1)S(1)}, bf16[2,72,16]{2,1,0:T(8,128)(2,1)}, u32[]{:S(2)}) copy-start(bf16[2,72,16]{2,1,0:T(8,128)(2,1)} %constant.29.clone.refs_3_) | copy-start | bytes 13828
  36.2 12.1 %collective-permute-start.6 = (f32[640,128]{1,0:T(8,128)S(1)}, f32[640,128]{1,0:T(8,128)S(1)}, u32[]{:S(2)}, u32[]{:S(2)}) collective-permute-start(f32[640,128]{1,0:T(8,128)S(1)} %early_3.1.refs_12_), channel_id=1, source_target_pairs={{1,2},{3,4},{5,6},{7,8},{9,10},{11,12},{13,14},{15,16},{17,18},{19... | collective-permute-start | bytes 983048 | tf_op jit(solution)/shard_map/ppermute | solution.py:622
  50.2 5.2 %collective-permute-start.7 = (f32[72,512]{1,0:T(8,128)S(1)}, f32[72,512]{1,0:T(8,128)S(1)}, u32[]{:S(2)}, u32[]{:S(2)}) collective-permute-start(f32[72,512]{1,0:T(8,128)S(1)} %shrink.1.refs_0_), channel_id=1, source_target_pairs={{0,64},{64,0},{128,192},{192,128},{1,65},{65,1},{129,193},{193,129... | collective-permute-start | bytes 442376 | tf_op jit(solution)/shard_map/ppermute | solution.py:616
  51.9 1.3 %collective-permute-start.8 = (f32[128,128]{1,0:T(8,128)S(1)}, f32[128,128]{1,0:T(8,128)S(1)}, u32[]{:S(2)}, u32[]{:S(2)}) collective-permute-start(f32[128,128]{1,0:T(8,128)S(1)} %get-tuple-element.80), channel_id=1, source_target_pairs={{0,1},{1,0},{2,3},{3,2},{4,5},{5,4},{6,7},{7,6},{8,9},{9,8},{10,11... | collective-permute-start | bytes 196616 | tf_op jit(solution)/shard_map/ppermute | solution.py:616
  55.4 6.4 %collective-permute-start.9 = (f32[72,512]{1,0:T(8,128)S(1)}, f32[72,512]{1,0:T(8,128)S(1)}, u32[]{:S(2)}, u32[]{:S(2)}) collective-permute-start(f32[72,512]{1,0:T(8,128)S(1)} %add_y1.1.refs_0_), channel_id=1, source_target_pairs={{0,192},{64,128},{128,64},{192,0},{1,193},{65,129},{129,65},{193,1... | collective-permute-start | bytes 442376 | tf_op jit(solution)/shard_map/ppermute | solution.py:616
  61.9 5.2 %collective-permute-start.10 = (f32[72,512]{1,0:T(8,128)S(1)}, f32[72,512]{1,0:T(8,128)S(1)}, u32[]{:S(2)}, u32[]{:S(2)}) collective-permute-start(f32[72,512]{1,0:T(8,128)S(1)} %add_y3.1.refs_0_), channel_id=1, source_target_pairs={{0,32},{32,0},{1,33},{33,1},{2,34},{34,2},{3,35},{35,3},{4,36},{36... | collective-permute-start | bytes 442376 | tf_op jit(solution)/shard_map/ppermute | solution.py:616
  67.2 1.3 %collective-permute-start.11 = (f32[24,128]{1,0:T(8,128)S(1)}, f32[24,128]{1,0:T(8,128)S(1)}, u32[]{:S(2)}, u32[]{:S(2)}) collective-permute-start(f32[24,128]{1,0:T(8,128)S(1)} %get-tuple-element.86.refs_1_), channel_id=1, source_target_pairs={{0,1},{1,0},{2,3},{3,2},{4,5},{5,4},{6,7},{7,6},{8,9},{9,8},{10,11... | collective-permute-start | bytes 36872 | tf_op jit(solution)/shard_map/ppermute | solution.py:616
  68.4 0.9 %copy-start.8 = (bf16[2,128,144]{2,1,0:T(8,128)(2,1)S(1)}, bf16[2,128,144]{2,1,0:T(8,128)(2,1)}, u32[]{:S(2)}) copy-start(bf16[2,128,144]{2,1,0:T(8,128)(2,1)} %constant.31.clone.refs_5_) | copy-start | bytes 221188
  68.5 5.2 %collective-permute-start.12 = (f32[8,128]{1,0:T(8,128)S(1)}, f32[8,128]{1,0:T(8,128)S(1)}, u32[]{:S(2)}, u32[]{:S(2)}) collective-permute-start(f32[8,128]{1,0:T(8,128)S(1)} %get-tuple-element.87.refs_0_), channel_id=1, source_target_pairs={{0,16},{16,0},{1,17},{17,1},{2,18},{18,2},{3,19},{19,3},{4,20},{20... | collective-permute-start | bytes 12296 | tf_op jit(solution)/shard_map/ppermute | solution.py:616
  (1 other events, 0.7 us)

commit v5 on v4

--- a/solution.py
+++ b/solution.py
@@ -20,6 +20,7 @@
 CYC = 8
 CZC = 64
 ROWS = 72
+THIRD = 24
 LEARN = 0.02
 EPSILON = 1e-06
 BF = jnp.bfloat16
@@ -61,7 +62,7 @@
     left = second_x[:, :OV] * ramp[None, :]
     right = second_x[:, OV + CX :] * ramp[None, ::-1]
     high, low = halves(second_x[:, OV : OV + CX])
-    out["own_x"] = np.block([[high, high], [low, np.zeros_like(low)]])
+    out["own_x"] = np.block([[high, high], [low, low]])
     sides = []
     for pair in ((right, left), (left, right)):
         high, low = halves(np.concatenate(pair, axis=1))
@@ -76,7 +77,7 @@
     out["near_x"] = np.stack(near_part)
     out["cross_x"] = np.stack(cross_part)
     high, low = halves(spectral_second(CZ) - 2.0 * np.eye(CZ))
-    out["own_z"] = np.block([[high, low], [high, np.zeros_like(low)]])
+    out["own_z"] = np.block([[high, low], [high, low]])
 
     fine_z = np.arange(CZ)[:, None]
     coarse_z = np.arange(CZC)[None, :]
@@ -452,7 +453,7 @@
     interior(p, own_x, own_z, lap_p)
 
 
-def shrink(image, image_far, shrink_x, shrink_far, shrink_z, own):
+def shrink(image, image_far, shrink_x, shrink_far, shrink_z, *thirds):
     core = lax.axis_index("core")
     rows_x = shrink_x[core]
     rows_far = shrink_far[core]
@@ -475,7 +476,9 @@
         for j in (2 * pair, 2 * pair + 1):
             parts += list(split(narrow[j]))
         pieces.append(dot(cat(parts, 1), shrink_z[...]) * UNIT)
-    own[...] = cat(pieces, 1)
+    whole = cat(pieces, 1)
+    for k, third in enumerate(thirds):
+        third[...] = whole[k * THIRD : k * THIRD + THIRD]
 
 
 def fold(value):
@@ -488,9 +491,11 @@
     return folded
 
 
-def squares(a, b, total, near):
-    core = lax.axis_index("core")
-    total[...] = a[...] + b[...]
+def squares(*refs):
+    core = lax.axis_index("core")
+    total, near = refs[6:]
+    for k in range(3):
+        total[k * THIRD : k * THIRD + THIRD] = refs[k][...] + refs[3 + k][...]
     first, last = grid_ends()
     total[CXC + 4 : CXC + 6] = jnp.where(first | last, 0.0, total[CXC + 4 : CXC + 6])
     row = lax.broadcasted_iota(jnp.int32, (CXC, CYC * CZC), 0)
@@ -531,8 +536,9 @@
             base[y] = 2.0 * p[y] - p_before[y] + source[y] * weight
 
 
-def add_two(a, b, out):
-    out[...] = a[...] + b[...]
+def add_thirds(*refs):
+    for mine, other, out in zip(refs[:3], refs[3:6], refs[6:]):
+        out[...] = mine[...] + other[...]
 
 
 def spread(total, sigma, lap, base, grow_z, grow_new, zeroth, first, second):
@@ -555,27 +561,17 @@
         out[k] = value
 
 
-def finish(count, parts, total, zeroth, first, second, direction, p_last, held, sems):
+def finish(count, parts, total, zeroth, first, second, direction, p_last):
     value = parts[0]
     for k in range(1, parts.shape[0]):
         value = value + parts[k]
     value = jnp.sum(jnp.sum(value, axis=0, keepdims=True), axis=1, keepdims=True)
     inverse = 1.0 / jnp.sqrt(value * (1.0 / count) + EPSILON)
     rate = LEARN * inverse
-    chunks = sems.shape[0]
-    step = CX // chunks
-    copies = []
-    for c in range(chunks):
-        rows = slice(c * step, c * step + step)
-        for y in range(CY):
-            value = zeroth[y, rows] + rate * (first[y, rows] + rate * second[y, rows])
-            held[pl.ds(c * step * CY + y, step, stride=CY), :] = value
-        block = pl.ds(c * step * CY, step * CY)
-        copies.append(pltpu.make_async_copy(held.at[block], p_last.at[block], sems.at[c]))
-        copies[-1].start()
+    for y in range(CY):
+        value = zeroth[y] + rate * (first[y] + rate * second[y])
+        p_last[pl.ds(y, CX, stride=CY), :] = value
     direction[...] = total[:CXC] * inverse
-    for copy in copies:
-        copy.wait()
 
 
 VM = pl.BlockSpec(memory_space=pltpu.VMEM)
@@ -709,12 +705,18 @@
         )
         far = far_swap(sent)
 
+    thirds = (rows_of(THIRD, CYC * CZC),) * 3
     partial = call(
-        shrink, rows_of(ROWS, CYC * CZC),
+        shrink, thirds,
         image, image_far, const["shrink_x"], const["shrink_far"], const["shrink_z"],
         flops=10**8, name="shrink",
     )
-    other = xor_swap(partial, "y", 1)
+    ways = (("xl", 1), ("y", 1), ("y", 3))
+
+    def swapped(stage):
+        return [xor_swap(x, *ways[(k + stage) % 3]) for k, x in enumerate(partial)]
+
+    other = swapped(0)
     near = xor_swap(near, "core", 1)
     lap_p = call(inside_one, FIELD, p, own_x, own_z, flops=5 * 10**8, name="inside_last")
     lap_p, base = call(
@@ -722,15 +724,10 @@
         flops=10**8, name="last_fields",
     )
     held = (lap_p, base)
-    partial = call(
-        add_two, rows_of(ROWS, CYC * CZC), partial, other, name="add_y1", held=held
-    )
-    partial = call(
-        add_two, rows_of(ROWS, CYC * CZC), partial, xor_swap(partial, "y", 3), name="add_y3",
-        held=held,
-    )
+    partial = call(add_thirds, thirds, *partial, *other, name="add_1", held=held)
+    partial = call(add_thirds, thirds, *partial, *swapped(1), name="add_2", held=held)
     total, mine = call(
-        squares, (rows_of(ROWS, CYC * CZC), rows_of(24)), partial, xor_swap(partial, "xl", 1),
+        squares, (rows_of(ROWS, CYC * CZC), rows_of(24)), *partial, *swapped(2),
         name="squares", held=held,
     )
     total, squared_sum = call(
@@ -750,10 +747,8 @@
     count = float(lax.axis_size(TILE) * CXC * CYC * CZC)
     direction, p_last = call(
         functools.partial(finish, count),
-        (rows_of(CXC, CYC * CZC), pltpu.HBM((CX * CY, CZ), F32)),
+        (rows_of(CXC, CYC * CZC), rows_of(CX * CY)),
         parts, total, *terms, name="finish",
-        scratch=[pltpu.VMEM((CX * CY, CZ), F32), pltpu.SemaphoreType.DMA((4,))],
-        out_specs=(VM, pl.BlockSpec(memory_space=pltpu.HBM)),
     )
     return direction, p_last.reshape(1, CX, CY, CZ)
 

time: 87 us -> 91.2 us (1.048)
  starting transfers between devices: 23.5 us -> 30.8 us
  waiting for transfers between devices: 29.4 us -> 26.1 us
    ppermute x10 -> x16, starting transfers between devices: 5.88 us -> 13.1 us  [xor_swap(): return lax.ppermute(x, axis, [(i, i ^ mask) for i in range(count)])]
    ppermute x10 -> x16, waiting for transfers between devices: 15.6 us -> 12.3 us  [xor_swap(): return lax.ppermute(x, axis, [(i, i ^ mask) for i in range(count)])]
  transfers between devices with their start and end apart: 13 -> 19, of which waited for: 8 -> 9; matrix products, arithmetic and copies ran while one was open for 0% -> 0% of each run, Pallas kernels for 12% -> 12%
where the time goes in v5:
time: 91.2 us; the launch traced here: 89.8 us
  starting transfers between devices  30.8 us (34%)
  waiting for transfers between devices  26.1 us (29%)
  Pallas kernels  19 us (21%)
  blocking collectives  10.4 us (11%)
  local copies, waits for them, and re-layouts  2.47 us (3%)
  between operations  1.12 us (1%)
    pallas_call x21, Pallas kernels, call(): pl.pallas_call(run, out_shape=outs, in_specs=[SM] * smem + [VM] * (count...  17.8 us
    ppermute x3, starting transfers between devices, far_swap(): return lax.ppermute(x, TILE, pairs + [(b, a) for a, b in pairs])  17.6 us
    ppermute x3, waiting for transfers between devices, far_swap(): return lax.ppermute(x, TILE, pairs + [(b, a) for a, b in pairs])  13.8 us
    ppermute x16, starting transfers between devices, xor_swap(): return lax.ppermute(x, axis, [(i, i ^ mask) for i in range(count)])  13.1 us
    ppermute x16, waiting for transfers between devices, xor_swap(): return lax.ppermute(x, axis, [(i, i ^ mask) for i in range(count)])  12.3 us
    all_to_all x1, blocking collectives, on_device(): parts = lax.all_to_all(copies, 'z', split_axis=0, concat_axis=0, tiled=True)  10.4 us
    unnamed x40, local copies, waits for them, and re-layouts  2.47 us
  transfers between devices with their start and end apart: 19, of which 9 were waited for; matrix products, arithmetic and copies ran while one was open for 0% of the time, Pallas kernels for 12%

profile of v5, /device:TPU:6, one launch (start us, length us, event | category | flops | bytes accessed | tf_op | source)
XLA Modules:
  0.0 89.8 jit_solution(13250594021861294498)
XLA Ops:
  0.7 1.2 %first_edges.1 = (f32[264,128]{1,0:T(8,128)S(1)}, f32[280,128]{1,0:T(8,128)S(1)}) custom-call(f32[2048,128]{1,0:T(8,128)} %bitcast.6, f32[2048,128]{1,0:T(8,128)} %bitcast.8, f32[64,512]{1,0:T(8,128)} %refs_0_.1), custom_call_target="tpu_custom_call" | custom-call | tf_op jit(solution)/shard_map/first_edges/pallas_call | solution.py:637
  1.9 8.0 %collective-permute-start.1 = (f32[280,128]{1,0:T(8,128)S(1)}, f32[280,128]{1,0:T(8,128)S(1)}, u32[]{:S(2)}, u32[]{:S(2)}) collective-permute-start(f32[280,128]{1,0:T(8,128)S(1)} %get-tuple-element.58), channel_id=1, source_target_pairs={{1,2},{3,4},{5,6},{7,8},{9,10},{11,12},{13,14},{15,16},{17,18},{19... | collective-permute-start | bytes 430088 | tf_op jit(solution)/shard_map/ppermute | solution.py:618
  10.6 0.9 %copy-done.10 = bf16[256,256]{1,0:T(8,128)(2,1)S(1)} copy-done((bf16[256,256]{1,0:T(8,128)(2,1)S(1)}, bf16[256,256]{1,0:T(8,128)(2,1)}, u32[]{:S(2)}) %copy-start.10) | copy-done | bytes 131096
  11.5 3.5 %prepare.1 = (f32[16,128,128]{2,1,0:T(8,128)S(1)}, f32[16,128,128]{2,1,0:T(8,128)S(1)}, f32[16,128,128]{2,1,0:T(8,128)S(1)}, f32[16,128,128]{2,1,0:T(8,128)S(1)}...) custom-call(s32[64]{0:T(128)S(1)} %bitcast.12, s32[64]{0:T(128)S(1)} %copy-done.18, f32[5]{0:T(128)S(1)} %copy-done.19, ...), custom_call_target="tpu_custom_call" | custom-call | flops 1000000000 | bytes 2359828 | tf_op jit(solution)/shard_map/prepare/pallas_call | solution.py:594
  15.9 1.3 %advance_0.1 = (f32[16,128,128]{2,1,0:T(8,128)S(1)}, f32[16,128,128]{2,1,0:T(8,128)S(1)}, f32[256,128]{1,0:T(8,128)S(1)}, f32[16,128,128]{2,1,0:T(8,128)S(1)}) custom-call(f32[264,128]{1,0:T(8,128)S(1)} %collective-permute-done.refs_1_.refs_0_, f32[280,128]{1,0:T(8,128)S(1)} %collective-permute-done.1.refs_2_.refs_1_, ...), custom_call_target="tpu_custom_call" | custom-call | flops 100000000 | bytes 8712192 | tf_op jit(solution)/shard_map/advance_0/pallas_call | solution.py:594
  17.3 1.5 %inside_0.1 = (f32[16,128,128]{2,1,0:T(8,128)S(1)}, f32[16,128,128]{2,1,0:T(8,128)S(1)}) custom-call(f32[16,128,128]{2,1,0:T(8,128)S(1)} %get-tuple-element.67.refs_0_.refs_1_.refs_2_.refs_3_, f32[16,128,128]{2,1,0:T(8,128)S(1)} %get-tuple-element.68.refs_1_.refs_3_.refs_4_.refs_5_.refs_11_.refs_16_, bf16[256,256]{1,0:T(8,128)(2,1)S(1)} %copy-done.10, ...), custom_call_target="tpu_custom_call" | custom-call | flops 1000000000 | bytes 2359296 | tf_op jit(solution)/shard_map/inside_0/pallas_call | solution.py:594
  19.0 4.6 %collective-permute-start.3 = (f32[512,128]{1,0:T(8,128)S(1)}, f32[512,128]{1,0:T(8,128)S(1)}, u32[]{:S(2)}, u32[]{:S(2)}) collective-permute-start(f32[512,128]{1,0:T(8,128)S(1)} %early_1.1.refs_12_), channel_id=1, source_target_pairs={{1,2},{3,4},{5,6},{7,8},{9,10},{11,12},{13,14},{15,16},{17,18},{19... | collective-permute-start | bytes 786440 | tf_op jit(solution)/shard_map/ppermute | solution.py:618
  23.7 6.7 %collective-permute-done.3.refs_1_.refs_19_ = f32[512,128]{1,0:T(8,128)S(1)} collective-permute-done((f32[512,128]{1,0:T(8,128)S(1)}, f32[512,128]{1,0:T(8,128)S(1)}, u32[]{:S(2)}, u32[]{:S(2)}) %collective-permute-start.3) | collective-permute-done | bytes 262176 | tf_op jit(solution)/shard_map/ppermute | solution.py:618
  30.3 0.9 advance_1.1
  31.3 1.6 %inside_1.1 = (f32[16,128,128]{2,1,0:T(8,128)S(1)}, f32[16,128,128]{2,1,0:T(8,128)S(1)}) custom-call(f32[16,128,128]{2,1,0:T(8,128)S(1)} %get-tuple-element.74.refs_0_.refs_2_.refs_3_, f32[16,128,128]{2,1,0:T(8,128)S(1)} %get-tuple-element.75.refs_1_.refs_4_.refs_5_, bf16[256,256]{1,0:T(8,128)(2,1)S(1)} %copy-done.11, bf16[256,256]{1,0:T(8,128)(2,1)S(1)} %copy-done.9), custom_call_target="tpu_custom_call" | custom-call | flops 1000000000 | bytes 2359296 | tf_op jit(solution)/shard_map/inside_1/pallas_call | solution.py:594
  32.9 0.9 %advance_2.1 = (f32[16,128,128]{2,1,0:T(8,128)S(1)}, f32[16,128,128]{2,1,0:T(8,128)S(1)}, f32[256,128]{1,0:T(8,128)S(1)}, f32[16,128,128]{2,1,0:T(8,128)S(1)}) custom-call(f32[256,128]{1,0:T(8,128)S(1)} %collective-permute-done.4.refs_0_, f32[256,128]{1,0:T(8,128)S(1)} %get-tuple-element.73.refs_1_, ...), custom_call_target="tpu_custom_call" | custom-call | flops 100000000 | bytes 9744384 | tf_op jit(solution)/shard_map/advance_2/pallas_call | solution.py:594
  34.4 1.5 %inside_2.1 = (f32[16,128,128]{2,1,0:T(8,128)S(1)}, f32[16,128,128]{2,1,0:T(8,128)S(1)}) custom-call(f32[16,128,128]{2,1,0:T(8,128)S(1)} %get-tuple-element.80.refs_0_.refs_1_.refs_2_.refs_3_, f32[16,128,128]{2,1,0:T(8,128)S(1)} %get-tuple-element.81.refs_1_.refs_3_.refs_4_, bf16[256,256]{1,0:T(8,128)(2,1)S(1)} %copy-done.11, bf16[256,256]{1,0:T(8,128)(2,1)S(1)} %copy-done.9), custom_call_target="tpu_custom_call" | custom-call | flops 1000000000 | bytes 2359296 | tf_op jit(solution)/shard_map/inside_2/pallas_call | solution.py:594
  36.2 5.0 %collective-permute-start.6 = (f32[640,128]{1,0:T(8,128)S(1)}, f32[640,128]{1,0:T(8,128)S(1)}, u32[]{:S(2)}, u32[]{:S(2)}) collective-permute-start(f32[640,128]{1,0:T(8,128)S(1)} %early_3.1.refs_12_), channel_id=1, source_target_pairs={{1,2},{3,4},{5,6},{7,8},{9,10},{11,12},{13,14},{15,16},{17,18},{19... | collective-permute-start | bytes 983048 | tf_op jit(solution)/shard_map/ppermute | solution.py:618
  41.1 7.2 %collective-permute-done.6.refs_1_ = f32[640,128]{1,0:T(8,128)S(1)} collective-permute-done((f32[640,128]{1,0:T(8,128)S(1)}, f32[640,128]{1,0:T(8,128)S(1)}, u32[]{:S(2)}, u32[]{:S(2)}) %collective-permute-start.6) | collective-permute-done | bytes 327712 | tf_op jit(solution)/shard_map/ppermute | solution.py:618
  48.3 1.2 %advance_3.1 = (f32[16,128,128]{2,1,0:T(8,128)S(1)}, f32[128,128]{1,0:T(8,128)S(1)}, f32[128,128]{1,0:T(8,128)S(1)}, f32[16,128,128]{2,1,0:T(8,128)S(1)}, f32[128,128]{1,0:T(8,128)S(1)}) custom-call(f32[256,128]{1,0:T(8,128)S(1)} %collective-permute-done.5.refs_0_, f32[640,128]{1,0:T(8,128)S(1)} %collective-permute-done.6.refs_1_, ...), custom_call_target="tpu_custom_call" | custom-call | flops 100000000 | bytes 13745152 | tf_op jit(solution)/shard_map/advance_3/pallas_call | solution.py:594
  50.4 1.7 %collective-permute-start.8 = (f32[24,512]{1,0:T(8,128)S(1)}, f32[24,512]{1,0:T(8,128)S(1)}, u32[]{:S(2)}, u32[]{:S(2)}) collective-permute-start(f32[24,512]{1,0:T(8,128)S(1)} %get-tuple-element.90.refs_1_), channel_id=1, source_target_pairs={{0,64},{64,0},{128,192},{192,128},{1,65},{65,1},{129,193},{193,129... | collective-permute-start | bytes 147464 | tf_op jit(solution)/shard_map/ppermute | solution.py:612
  52.1 2.2 %collective-permute-start.9 = (f32[24,512]{1,0:T(8,128)S(1)}, f32[24,512]{1,0:T(8,128)S(1)}, u32[]{:S(2)}, u32[]{:S(2)}) collective-permute-start(f32[24,512]{1,0:T(8,128)S(1)} %get-tuple-element.91.refs_2_), channel_id=1, source_target_pairs={{0,192},{64,128},{128,64},{192,0},{1,193},{65,129},{129,65},{193,1... | collective-permute-start | bytes 147464 | tf_op jit(solution)/shard_map/ppermute | solution.py:612
  54.2 0.8 inside_last.1.refs_4_
  55.5 1.9 %collective-permute-done.9.refs_5_ = f32[24,512]{1,0:T(8,128)S(1)} collective-permute-done((f32[24,512]{1,0:T(8,128)S(1)}, f32[24,512]{1,0:T(8,128)S(1)}, u32[]{:S(2)}, u32[]{:S(2)}) %collective-permute-start.9) | collective-permute-done | bytes 49184 | tf_op jit(solution)/shard_map/ppermute | solution.py:612
  57.5 2.3 %collective-permute-start.12 = (f32[24,512]{1,0:T(8,128)S(1)}, f32[24,512]{1,0:T(8,128)S(1)}, u32[]{:S(2)}, u32[]{:S(2)}) collective-permute-start(f32[24,512]{1,0:T(8,128)S(1)} %get-tuple-element.98.refs_1_), channel_id=1, source_target_pairs={{0,192},{64,128},{128,64},{192,0},{1,193},{65,129},{129,65},{193,1... | collective-permute-start | bytes 147464 | tf_op jit(solution)/shard_map/ppermute | solution.py:612
  59.7 1.9 %collective-permute-start.13 = (f32[24,512]{1,0:T(8,128)S(1)}, f32[24,512]{1,0:T(8,128)S(1)}, u32[]{:S(2)}, u32[]{:S(2)}) collective-permute-start(f32[24,512]{1,0:T(8,128)S(1)} %get-tuple-element.99.refs_2_), channel_id=1, source_target_pairs={{0,32},{32,0},{1,33},{33,1},{2,34},{34,2},{3,35},{35,3},{4,36},{36... | collective-permute-start | bytes 147464 | tf_op jit(solution)/shard_map/ppermute | solution.py:612
  61.7 1.2 %collective-permute-done.12.refs_4_ = f32[24,512]{1,0:T(8,128)S(1)} collective-permute-done((f32[24,512]{1,0:T(8,128)S(1)}, f32[24,512]{1,0:T(8,128)S(1)}, u32[]{:S(2)}, u32[]{:S(2)}) %collective-permute-start.12) | collective-permute-done | bytes 49184 | tf_op jit(solution)/shard_map/ppermute | solution.py:612
  62.9 1.0 %collective-permute-done.13.refs_5_ = f32[24,512]{1,0:T(8,128)S(1)} collective-permute-done((f32[24,512]{1,0:T(8,128)S(1)}, f32[24,512]{1,0:T(8,128)S(1)}, u32[]{:S(2)}, u32[]{:S(2)}) %collective-permute-start.13) | collective-permute-done | bytes 49184 | tf_op jit(solution)/shard_map/ppermute | solution.py:612
  63.9 1.3 %collective-permute-start.14 = (f32[24,512]{1,0:T(8,128)S(1)}, f32[24,512]{1,0:T(8,128)S(1)}, u32[]{:S(2)}, u32[]{:S(2)}) collective-permute-start(f32[24,512]{1,0:T(8,128)S(1)} %get-tuple-element.100.refs_0_), channel_id=1, source_target_pairs={{0,192},{64,128},{128,64},{192,0},{1,193},{65,129},{129,65},{193,1... | collective-permute-start | bytes 147464 | tf_op jit(solution)/shard_map/ppermute | solution.py:612
  65.2 1.9 %collective-permute-start.15 = (f32[24,512]{1,0:T(8,128)S(1)}, f32[24,512]{1,0:T(8,128)S(1)}, u32[]{:S(2)}, u32[]{:S(2)}) collective-permute-start(f32[24,512]{1,0:T(8,128)S(1)} %get-tuple-element.101.refs_1_), channel_id=1, source_target_pairs={{0,32},{32,0},{1,33},{33,1},{2,34},{34,2},{3,35},{35,3},{4,36},{36... | collective-permute-start | bytes 147464 | tf_op jit(solution)/shard_map/ppermute | solution.py:612
  67.7 1.6 %collective-permute-done.14.refs_3_ = f32[24,512]{1,0:T(8,128)S(1)} collective-permute-done((f32[24,512]{1,0:T(8,128)S(1)}, f32[24,512]{1,0:T(8,128)S(1)}, u32[]{:S(2)}, u32[]{:S(2)}) %collective-permute-start.14) | collective-permute-done | bytes 49184 | tf_op jit(solution)/shard_map/ppermute | solution.py:612
  69.3 1.9 %collective-permute-done.16.refs_5_ = f32[24,512]{1,0:T(8,128)S(1)} collective-permute-done((f32[24,512]{1,0:T(8,128)S(1)}, f32[24,512]{1,0:T(8,128)S(1)}, u32[]{:S(2)}, u32[]{:S(2)}) %collective-permute-start.16) | collective-permute-done | bytes 49184 | tf_op jit(solution)/shard_map/ppermute | solution.py:612
  71.3 1.2 %collective-permute-done.17.refs_2_ = f32[24,128]{1,0:T(8,128)S(1)} collective-permute-done((f32[24,128]{1,0:T(8,128)S(1)}, f32[24,128]{1,0:T(8,128)S(1)}, u32[]{:S(2)}, u32[]{:S(2)}) %collective-permute-start.17) | collective-permute-done | bytes 12320 | tf_op jit(solution)/shard_map/ppermute | solution.py:612
  73.4 0.8 spread.1
  74.2 3.5 %collective-permute-done.18.refs_1_ = f32[8,128]{1,0:T(8,128)S(1)} collective-permute-done((f32[8,128]{1,0:T(8,128)S(1)}, f32[8,128]{1,0:T(8,128)S(1)}, u32[]{:S(2)}, u32[]{:S(2)}) %collective-permute-start.18) | collective-permute-done | bytes 4128 | tf_op jit(solution)/shard_map/ppermute | solution.py:612
  77.7 10.4 %all_to_all.5.refs_0_ = f32[8,8,128]{2,1,0:T(8,128)S(1)} all-to-all(f32[8,8,128]{2,1,0:T(8,128)S(1)} %widen.1), channel_id=1, replica_groups=mesh['y'=4,'xl'=2,'xh'=2,'z'=8,'core'=2] {'z'}, dimensions={0} | all-to-all | bytes 65536 | tf_op jit(solution)/shard_map/all_to_all | solution.py:746
  88.1 1.7 %finish.1 = (f32[64,512]{1,0:T(8,128)}, f32[2048,128]{1,0:T(8,128)}) custom-call(f32[8,8,128]{2,1,0:T(8,128)S(1)} %all_to_all.5.refs_0_, f32[72,512]{1,0:T(8,128)S(1)} %get-tuple-element.106.refs_0_.refs_1_, f32[16,128,128]{2,1,0:T(8,128)S(1)} %get-tuple-element.107.refs_2_, f32[16,128,128]{2,1,0:T(8,128)S(1)} %get-tuple-element.108.refs_3_, ...), custom_call_target="tpu_custom_call" | custom-call | bytes 3325952 | tf_op jit(solution)/shard_map/finish/pallas_call | solution.py:594
  (69 shorter events, 5.5 us)
Async XLA Ops:
  0.6 9.4 %copy-start.1 = (f32[1,128,16,128]{3,2,1,0:T(8,128)S(1)}, f32[1,128,16,128]{3,2,1,0:T(8,128)}, u32[]{:S(2)}) copy-start(f32[1,128,16,128]{3,2,1,0:T(8,128)} %param.19) | copy-start | bytes 3145732
  0.6 9.4 %copy-start.2 = (f32[1,128,16,128]{3,2,1,0:T(8,128)S(1)}, f32[1,128,16,128]{3,2,1,0:T(8,128)}, u32[]{:S(2)}) copy-start(f32[1,128,16,128]{3,2,1,0:T(8,128)} %param.21) | copy-start | bytes 3145732
  0.6 9.4 %copy-start.9 = (bf16[256,256]{1,0:T(8,128)(2,1)S(1)}, bf16[256,256]{1,0:T(8,128)(2,1)}, u32[]{:S(2)}) copy-start(bf16[256,256]{1,0:T(8,128)(2,1)} %constant.26.clone.refs_6_.refs_3_.refs_2_) | copy-start | bytes 393220
  1.9 13.3 %collective-permute-start.1 = (f32[280,128]{1,0:T(8,128)S(1)}, f32[280,128]{1,0:T(8,128)S(1)}, u32[]{:S(2)}, u32[]{:S(2)}) collective-permute-start(f32[280,128]{1,0:T(8,128)S(1)} %get-tuple-element.58), channel_id=1, source_target_pairs={{1,2},{3,4},{5,6},{7,8},{9,10},{11,12},{13,14},{15,16},{17,18},{19... | collective-permute-start | bytes 430088 | tf_op jit(solution)/shard_map/ppermute | solution.py:618
  10.0 5.2 %collective-permute-start = (f32[264,128]{1,0:T(8,128)S(1)}, f32[264,128]{1,0:T(8,128)S(1)}, u32[]{:S(2)}, u32[]{:S(2)}) collective-permute-start(f32[264,128]{1,0:T(8,128)S(1)} %get-tuple-element.57), channel_id=1, source_target_pairs={{0,1},{1,0},{2,3},{3,2},{4,5},{5,4},{6,7},{7,6},{8,9},{9,8},{10,11... | collective-permute-start | bytes 405512 | tf_op jit(solution)/shard_map/ppermute | solution.py:612
  11.5 3.6 %copy-start.5 = (bf16[256,256]{1,0:T(8,128)(2,1)S(1)}, bf16[256,256]{1,0:T(8,128)(2,1)}, u32[]{:S(2)}) copy-start(bf16[256,256]{1,0:T(8,128)(2,1)} %constant.27.clone.refs_3_.refs_4_) | copy-start | bytes 393220
  11.5 3.6 %copy-start.6 = (f32[64,512]{1,0:T(8,128)S(1)}, f32[64,512]{1,0:T(8,128)}, u32[]{:S(2)}) copy-start(f32[64,512]{1,0:T(8,128)} %refs_0_.1) | copy-start | bytes 393220
  11.5 3.6 %copy-start.7 = (bf16[2,136,144]{2,1,0:T(8,128)(2,1)S(1)}, bf16[2,136,144]{2,1,0:T(8,128)(2,1)}, u32[]{:S(2)}) copy-start(bf16[2,136,144]{2,1,0:T(8,128)(2,1)} %constant.30.clone.refs_4_) | copy-start | bytes 235012
  11.5 4.2 %copy-start.3 = (f32[1,128,16,128]{3,2,1,0:T(8,128)S(1)}, f32[1,128,16,128]{3,2,1,0:T(8,128)}, u32[]{:S(2)}) copy-start(f32[1,128,16,128]{3,2,1,0:T(8,128)} %param.20) | copy-start | bytes 3145732
  11.5 4.2 %copy-start.4 = (f32[1,128,16,128]{3,2,1,0:T(8,128)S(1)}, f32[1,128,16,128]{3,2,1,0:T(8,128)}, u32[]{:S(2)}) copy-start(f32[1,128,16,128]{3,2,1,0:T(8,128)} %param.22) | copy-start | bytes 3145732
  17.2 1.6 %collective-permute-start.2 = (f32[256,128]{1,0:T(8,128)S(1)}, f32[256,128]{1,0:T(8,128)S(1)}, u32[]{:S(2)}, u32[]{:S(2)}) collective-permute-start(f32[256,128]{1,0:T(8,128)S(1)} %get-tuple-element.66), channel_id=1, source_target_pairs={{0,1},{1,0},{2,3},{3,2},{4,5},{5,4},{6,7},{7,6},{8,9},{9,8},{10,11... | collective-permute-start | bytes 393224 | tf_op jit(solution)/shard_map/ppermute | solution.py:612
  17.3 1.5 %copy-start.16 = (bf16[2,16,48]{2,1,0:T(8,128)(2,1)S(1)}, bf16[2,16,48]{2,1,0:T(8,128)(2,1)}, u32[]{:S(2)}) copy-start(bf16[2,16,48]{2,1,0:T(8,128)(2,1)} %constant.24.clone.refs_10_) | copy-start | bytes 9220
  18.8 11.5 %copy-start.15 = (bf16[2,16,48]{2,1,0:T(8,128)(2,1)S(1)}, bf16[2,16,48]{2,1,0:T(8,128)(2,1)}, u32[]{:S(2)}) copy-start(bf16[2,16,48]{2,1,0:T(8,128)(2,1)} %constant.25.clone.refs_14_) | copy-start | bytes 9220
  19.0 11.3 %collective-permute-start.3 = (f32[512,128]{1,0:T(8,128)S(1)}, f32[512,128]{1,0:T(8,128)S(1)}, u32[]{:S(2)}, u32[]{:S(2)}) collective-permute-start(f32[512,128]{1,0:T(8,128)S(1)} %early_1.1.refs_12_), channel_id=1, source_target_pairs={{1,2},{3,4},{5,6},{7,8},{9,10},{11,12},{13,14},{15,16},{17,18},{19... | collective-permute-start | bytes 786440 | tf_op jit(solution)/shard_map/ppermute | solution.py:618
  31.2 1.7 %collective-permute-start.4 = (f32[256,128]{1,0:T(8,128)S(1)}, f32[256,128]{1,0:T(8,128)S(1)}, u32[]{:S(2)}, u32[]{:S(2)}) collective-permute-start(f32[256,128]{1,0:T(8,128)S(1)} %get-tuple-element.72), channel_id=1, source_target_pairs={{0,1},{1,0},{2,3},{3,2},{4,5},{5,4},{6,7},{7,6},{8,9},{9,8},{10,11... | collective-permute-start | bytes 393224 | tf_op jit(solution)/shard_map/ppermute | solution.py:612
  33.8 2.1 %collective-permute-start.5 = (f32[256,128]{1,0:T(8,128)S(1)}, f32[256,128]{1,0:T(8,128)S(1)}, u32[]{:S(2)}, u32[]{:S(2)}) collective-permute-start(f32[256,128]{1,0:T(8,128)S(1)} %get-tuple-element.79), channel_id=1, source_target_pairs={{0,1},{1,0},{2,3},{3,2},{4,5},{5,4},{6,7},{7,6},{8,9},{9,8},{10,11... | collective-permute-start | bytes 393224 | tf_op jit(solution)/shard_map/ppermute | solution.py:612
  36.1 13.5 %copy-start.12 = (bf16[512,128]{1,0:T(8,128)(2,1)S(1)}, bf16[512,128]{1,0:T(8,128)(2,1)}, u32[]{:S(2)}) copy-start(bf16[512,128]{1,0:T(8,128)(2,1)} %constant.28.clone.refs_4_) | copy-start | bytes 393220
  36.1 13.5 %copy-start.13 = (bf16[2,72,256]{2,1,0:T(8,128)(2,1)S(1)}, bf16[2,72,256]{2,1,0:T(8,128)(2,1)}, u32[]{:S(2)}) copy-start(bf16[2,72,256]{2,1,0:T(8,128)(2,1)} %constant.32.clone.refs_2_) | copy-start | bytes 221188
  36.2 13.5 %copy-start.14 = (bf16[2,72,16]{2,1,0:T(8,128)(2,1)S(1)}, bf16[2,72,16]{2,1,0:T(8,128)(2,1)}, u32[]{:S(2)}) copy-start(bf16[2,72,16]{2,1,0:T(8,128)(2,1)} %constant.29.clone.refs_3_) | copy-start | bytes 13828
  36.2 12.1 %collective-permute-start.6 = (f32[640,128]{1,0:T(8,128)S(1)}, f32[640,128]{1,0:T(8,128)S(1)}, u32[]{:S(2)}, u32[]{:S(2)}) collective-permute-start(f32[640,128]{1,0:T(8,128)S(1)} %early_3.1.refs_12_), channel_id=1, source_target_pairs={{1,2},{3,4},{5,6},{7,8},{9,10},{11,12},{13,14},{15,16},{17,18},{19... | collective-permute-start | bytes 983048 | tf_op jit(solution)/shard_map/ppermute | solution.py:618
  49.5 5.6 %collective-permute-start.10 = (f32[128,128]{1,0:T(8,128)S(1)}, f32[128,128]{1,0:T(8,128)S(1)}, u32[]{:S(2)}, u32[]{:S(2)}) collective-permute-start(f32[128,128]{1,0:T(8,128)S(1)} %get-tuple-element.92), channel_id=1, source_target_pairs={{0,1},{1,0},{2,3},{3,2},{4,5},{5,4},{6,7},{7,6},{8,9},{9,8},{10,11... | collective-permute-start | bytes 196616 | tf_op jit(solution)/shard_map/ppermute | solution.py:612
  50.3 5.2 %collective-permute-start.7 = (f32[24,512]{1,0:T(8,128)S(1)}, f32[24,512]{1,0:T(8,128)S(1)}, u32[]{:S(2)}, u32[]{:S(2)}) collective-permute-start(f32[24,512]{1,0:T(8,128)S(1)} %get-tuple-element.89.refs_0_), channel_id=1, source_target_pairs={{0,32},{32,0},{1,33},{33,1},{2,34},{34,2},{3,35},{35,3},{4,36},{36... | collective-permute-start | bytes 147464 | tf_op jit(solution)/shard_map/ppermute | solution.py:612
  50.4 5.1 %collective-permute-start.8 = (f32[24,512]{1,0:T(8,128)S(1)}, f32[24,512]{1,0:T(8,128)S(1)}, u32[]{:S(2)}, u32[]{:S(2)}) collective-permute-start(f32[24,512]{1,0:T(8,128)S(1)} %get-tuple-element.90.refs_1_), channel_id=1, source_target_pairs={{0,64},{64,0},{128,192},{192,128},{1,65},{65,1},{129,193},{193,129... | collective-permute-start | bytes 147464 | tf_op jit(solution)/shard_map/ppermute | solution.py:612
  52.1 5.3 %collective-permute-start.9 = (f32[24,512]{1,0:T(8,128)S(1)}, f32[24,512]{1,0:T(8,128)S(1)}, u32[]{:S(2)}, u32[]{:S(2)}) collective-permute-start(f32[24,512]{1,0:T(8,128)S(1)} %get-tuple-element.91.refs_2_), channel_id=1, source_target_pairs={{0,192},{64,128},{128,64},{192,0},{1,193},{65,129},{129,65},{193,1... | collective-permute-start | bytes 147464 | tf_op jit(solution)/shard_map/ppermute | solution.py:612
  57.4 4.3 %collective-permute-start.11 = (f32[24,512]{1,0:T(8,128)S(1)}, f32[24,512]{1,0:T(8,128)S(1)}, u32[]{:S(2)}, u32[]{:S(2)}) collective-permute-start(f32[24,512]{1,0:T(8,128)S(1)} %get-tuple-element.97.refs_0_), channel_id=1, source_target_pairs={{0,64},{64,0},{128,192},{192,128},{1,65},{65,1},{129,193},{193,129... | collective-permute-start | bytes 147464 | tf_op jit(solution)/shard_map/ppermute | solution.py:612
  57.5 5.4 %collective-permute-start.12 = (f32[24,512]{1,0:T(8,128)S(1)}, f32[24,512]{1,0:T(8,128)S(1)}, u32[]{:S(2)}, u32[]{:S(2)}) collective-permute-start(f32[24,512]{1,0:T(8,128)S(1)} %get-tuple-element.98.refs_1_), channel_id=1, source_target_pairs={{0,192},{64,128},{128,64},{192,0},{1,193},{65,129},{129,65},{193,1... | collective-permute-start | bytes 147464 | tf_op jit(solution)/shard_map/ppermute | solution.py:612
  59.7 4.1 %collective-permute-start.13 = (f32[24,512]{1,0:T(8,128)S(1)}, f32[24,512]{1,0:T(8,128)S(1)}, u32[]{:S(2)}, u32[]{:S(2)}) collective-permute-start(f32[24,512]{1,0:T(8,128)S(1)} %get-tuple-element.99.refs_2_), channel_id=1, source_target_pairs={{0,32},{32,0},{1,33},{33,1},{2,34},{34,2},{3,35},{35,3},{4,36},{36... | collective-permute-start | bytes 147464 | tf_op jit(solution)/shard_map/ppermute | solution.py:612
  63.9 5.4 %collective-permute-start.14 = (f32[24,512]{1,0:T(8,128)S(1)}, f32[24,512]{1,0:T(8,128)S(1)}, u32[]{:S(2)}, u32[]{:S(2)}) collective-permute-start(f32[24,512]{1,0:T(8,128)S(1)} %get-tuple-element.100.refs_0_), channel_id=1, source_target_pairs={{0,192},{64,128},{128,64},{192,0},{1,193},{65,129},{129,65},{193,1... | collective-permute-start | bytes 147464 | tf_op jit(solution)/shard_map/ppermute | solution.py:612
  65.2 4.1 %collective-permute-start.15 = (f32[24,512]{1,0:T(8,128)S(1)}, f32[24,512]{1,0:T(8,128)S(1)}, u32[]{:S(2)}, u32[]{:S(2)}) collective-permute-start(f32[24,512]{1,0:T(8,128)S(1)} %get-tuple-element.101.refs_1_), channel_id=1, source_target_pairs={{0,32},{32,0},{1,33},{33,1},{2,34},{34,2},{3,35},{35,3},{4,36},{36... | collective-permute-start | bytes 147464 | tf_op jit(solution)/shard_map/ppermute | solution.py:612
  67.1 4.1 %collective-permute-start.16 = (f32[24,512]{1,0:T(8,128)S(1)}, f32[24,512]{1,0:T(8,128)S(1)}, u32[]{:S(2)}, u32[]{:S(2)}) collective-permute-start(f32[24,512]{1,0:T(8,128)S(1)} %get-tuple-element.102.refs_2_), channel_id=1, source_target_pairs={{0,64},{64,0},{128,192},{192,128},{1,65},{65,1},{129,193},{193,129... | collective-permute-start | bytes 147464 | tf_op jit(solution)/shard_map/ppermute | solution.py:612
  71.2 1.3 %collective-permute-start.17 = (f32[24,128]{1,0:T(8,128)S(1)}, f32[24,128]{1,0:T(8,128)S(1)}, u32[]{:S(2)}, u32[]{:S(2)}) collective-permute-start(f32[24,128]{1,0:T(8,128)S(1)} %get-tuple-element.104.refs_1_), channel_id=1, source_target_pairs={{0,1},{1,0},{2,3},{3,2},{4,5},{5,4},{6,7},{7,6},{8,9},{9,8},{10,11... | collective-permute-start | bytes 36872 | tf_op jit(solution)/shard_map/ppermute | solution.py:612
  72.5 5.2 %collective-permute-start.18 = (f32[8,128]{1,0:T(8,128)S(1)}, f32[8,128]{1,0:T(8,128)S(1)}, u32[]{:S(2)}, u32[]{:S(2)}) collective-permute-start(f32[8,128]{1,0:T(8,128)S(1)} %get-tuple-element.105.refs_0_), channel_id=1, source_target_pairs={{0,16},{16,0},{1,17},{17,1},{2,18},{18,2},{3,19},{19,3},{4,20},{20... | collective-permute-start | bytes 12296 | tf_op jit(solution)/shard_map/ppermute | solution.py:612
  (7 other events, 5.6 us)

commit v6 on v4

--- a/solution.py
+++ b/solution.py
@@ -61,7 +61,7 @@
     left = second_x[:, :OV] * ramp[None, :]
     right = second_x[:, OV + CX :] * ramp[None, ::-1]
     high, low = halves(second_x[:, OV : OV + CX])
-    out["own_x"] = np.block([[high, high], [low, np.zeros_like(low)]])
+    out["own_x"] = np.block([[high, high], [low, low]])
     sides = []
     for pair in ((right, left), (left, right)):
         high, low = halves(np.concatenate(pair, axis=1))
@@ -76,7 +76,7 @@
     out["near_x"] = np.stack(near_part)
     out["cross_x"] = np.stack(cross_part)
     high, low = halves(spectral_second(CZ) - 2.0 * np.eye(CZ))
-    out["own_z"] = np.block([[high, low], [high, np.zeros_like(low)]])
+    out["own_z"] = np.block([[high, low], [high, low]])
 
     fine_z = np.arange(CZ)[:, None]
     coarse_z = np.arange(CZC)[None, :]
@@ -98,20 +98,16 @@
     lower = {j: column(j) for j in (-2, -1, 0, 1)}
     upper = {j: column(j) for j in (62, 63, 64, 65)}
     stack = lambda d: np.stack([d[j] for j in sorted(d)], axis=1)
-    grow_old, grow_new, shrink, shrink_far = [], [], [], []
+    grow_own, grow_rest, grow_new, shrink, shrink_far = [], [], [], [], []
     blank = np.zeros((CX, 2))
     for core in range(2):
         near = upper if core == 0 else lower
         near_two, far_six = ((64, 65), range(-6, 0)) if core == 0 else ((-2, -1), range(64, 70))
         far_two = (-2, -1) if core == 0 else (64, 65)
         beyond = -OV if core == 0 else CX
-        old = np.stack(
-            [
-                np.concatenate([column(j), column(j, beyond, OV)])
-                for j in (*range(CXC), *near_two, *far_six)
-            ],
-            axis=1,
-        )
+        both = lambda j: np.concatenate([column(j), column(j, beyond, OV)])
+        mine = np.stack([both(j) for j in range(CXC)], axis=1)
+        rest = np.stack([both(j) for j in (*near_two, *far_six)], axis=1)
         inner = own.copy()
         inner[:, [62, 63] if core == 0 else [0, 1]] = 0.0
         outer = np.stack([column(j) for j in far_two], axis=1)
@@ -120,12 +116,14 @@
         past = np.zeros((ROWS, OV))
         for row, j in (*enumerate(range(CXC)), *zip((CXC + 4, CXC + 5), far_two)):
             past[row] = column(j, beyond, OV)
-        grow_old.append(np.concatenate([old, old], axis=1))
+        grow_own.append(np.concatenate([mine, mine], axis=1))
+        grow_rest.append(np.concatenate([rest, rest], axis=1))
         grow_new.append(np.concatenate([new, new], axis=1))
         shrink.append(np.concatenate([every, every], axis=1))
         shrink_far.append(np.concatenate([past, past], axis=1))
     out["shrink_far"] = np.stack(shrink_far)
-    out["grow_old"] = np.stack(grow_old)
+    out["grow_own"] = np.stack(grow_own)
+    out["grow_rest"] = np.stack(grow_rest)
     out["grow_new"] = np.stack(grow_new)
     out["shrink_x"] = np.stack(shrink)
     return {name: np.asarray(value).astype(ml_dtypes.bfloat16) for name, value in out.items()}
@@ -247,13 +245,27 @@
 
 
 def prepare(
-    signs, index, wavelet, p_now, q_now, own_x, own_z,
-    p0, q0, lap_p, lap_q, source, amounts,
+    signs, index, wavelet, p_now, q_now, grow_z, own_x_in, own_z_in, p_prev_in, q_prev_in, coef_in, grow_own_in,
+    p0, q0, p1, q1, lap_p, lap_q, source, amounts, sigma_own,
+    own_x, own_z, p_prev, q_prev, coef, grow_own, sems,
 ):
+    copies = [
+        pltpu.make_async_copy(far, near, sems.at[k])
+        for k, (far, near) in enumerate(
+            (
+                (own_x_in, own_x),
+                (own_z_in, own_z),
+                (p_prev_in, p_prev),
+                (q_prev_in, q_prev),
+                (coef_in, coef),
+                (grow_own_in, grow_own),
+            )
+        )
+    ]
+    for copy in copies:
+        copy.start()
     reorder(p_now, p0)
     reorder(q_now, q0)
-    interior(p0, own_x, own_z, lap_p)
-    interior(q0, own_x, own_z, lap_q)
     source[...] = jnp.zeros_like(source)
     lane = lax.broadcasted_iota(jnp.int32, (1, CZ), 1)
 
@@ -269,6 +281,21 @@
     lax.fori_loop(0, ELEMS, add, 0)
     for step in range(STEPS + 1):
         amounts[step] = jnp.full((8, CZ), wavelet[step], F32)
+    copies[0].wait()
+    copies[1].wait()
+    interior(p0, own_x, own_z, lap_p)
+    interior(q0, own_x, own_z, lap_q)
+    copies[2].wait()
+    reorder(p_prev, p1)
+    copies[3].wait()
+    reorder(q_prev, q1)
+    copies[4].wait()
+    copies[5].wait()
+
+    def write(y, fine):
+        sigma_own[y] = fine
+
+    grow(coef[...], grow_z, grow_own[lax.axis_index("core")], write)
 
 
 def grow(coef, grow_z, grow_x, write):
@@ -302,27 +329,25 @@
     return (core == 0) & (chip == 0), (core == 1) & (chip == chips - 1)
 
 
-def speed(coef, near, far, grow_z, grow_old, sigma, squared, beyond, held):
-    core = lax.axis_index("core")
-    held[:CXC] = coef[...]
+def speed(sigma_own, near, far, grow_z, grow_rest, sigma, squared, beyond, held):
+    core = lax.axis_index("core")
     base = 2 * CY * OV
     for row in range(6):
         for part in range(4):
             lanes = slice(part * 128, part * 128 + 128)
             spot = base + row * 4 + part
             if row < 2:
-                held[CXC + row : CXC + row + 1, lanes] = near[spot : spot + 1]
-            held[CXC + 2 + row : CXC + 3 + row, lanes] = far[spot : spot + 1]
+                held[row : row + 1, lanes] = near[spot : spot + 1]
+            held[2 + row : 3 + row, lanes] = far[spot : spot + 1]
     first, last = grid_ends()
 
     def write(y, fine):
-        fine = fine * UNIT
-        square = fine * fine
+        fine = (sigma_own[y] + fine) * UNIT
         sigma[y] = fine[:CX]
-        squared[y] = square[:CX]
+        squared[y] = fine[:CX] * fine[:CX]
         beyond[y * OV : y * OV + OV] = jnp.where(first | last, 0.0, fine[CX:])
 
-    grow(held[...], grow_z, grow_old[core], write)
+    grow(held[...], grow_z, grow_rest[core], write)
 
 
 def squared_at(beyond, spot):
@@ -362,13 +387,8 @@
             lap = lap_p[y] + extra_p[:, lanes]
             lap_adj = lap_q[y] + extra_q[:, lanes]
             sq = squared[y]
-            if step == 0:
-                rows = pl.ds(y, CX, stride=CY)
-                old_p, old_q = p_before[rows, :], q_before[rows, :]
-            else:
-                old_p, old_q = p_before[y], q_before[y]
-            p_new[y] = 2.0 * p[y] - old_p + sq * lap + source[y] * weight
-            new_q = 2.0 * q[y] - old_q + sq * lap_adj
+            p_new[y] = 2.0 * p[y] - p_before[y] + sq * lap + source[y] * weight
+            new_q = 2.0 * q[y] - q_before[y] + sq * lap_adj
             if step < 3:
                 q_new[y] = new_q
             if step < 2:
@@ -531,8 +551,8 @@
             base[y] = 2.0 * p[y] - p_before[y] + source[y] * weight
 
 
-def add_two(a, b, out):
-    out[...] = a[...] + b[...]
+def add_four(own, one, two, three, out):
+    out[...] = (own[...] + one[...]) + (two[...] + three[...])
 
 
 def spread(total, sigma, lap, base, grow_z, grow_new, zeroth, first, second):
@@ -542,9 +562,10 @@
         change = fine * UNIT
         old, curve = sigma[y], lap[y]
         scaled = change * curve
-        zeroth[y] = base[y] + old * old * curve
-        first[y] = -2.0 * old * scaled
-        second[y] = change * scaled
+        rows = pl.ds(y, CX, stride=CY)
+        zeroth[rows, :] = base[y] + old * old * curve
+        first[rows, :] = -2.0 * old * scaled
+        second[rows, :] = change * scaled
 
     grow(total[...], grow_z, grow_new[core], write)
 
@@ -562,16 +583,12 @@
     value = jnp.sum(jnp.sum(value, axis=0, keepdims=True), axis=1, keepdims=True)
     inverse = 1.0 / jnp.sqrt(value * (1.0 / count) + EPSILON)
     rate = LEARN * inverse
-    chunks = sems.shape[0]
-    step = CX // chunks
+    size = CX * CY // sems.shape[0]
     copies = []
-    for c in range(chunks):
-        rows = slice(c * step, c * step + step)
-        for y in range(CY):
-            value = zeroth[y, rows] + rate * (first[y, rows] + rate * second[y, rows])
-            held[pl.ds(c * step * CY + y, step, stride=CY), :] = value
-        block = pl.ds(c * step * CY, step * CY)
-        copies.append(pltpu.make_async_copy(held.at[block], p_last.at[block], sems.at[c]))
+    for c in range(sems.shape[0]):
+        rows = slice(c * size, c * size + size)
+        held[rows] = zeroth[rows] + rate * (first[rows] + rate * second[rows])
+        copies.append(pltpu.make_async_copy(held.at[rows], p_last.at[rows], sems.at[c]))
         copies[-1].start()
     direction[...] = total[:CXC] * inverse
     for copy in copies:
@@ -581,14 +598,14 @@
 VM = pl.BlockSpec(memory_space=pltpu.VMEM)
 SM = pl.BlockSpec(memory_space=pltpu.SMEM)
 FIELD = jax.ShapeDtypeStruct((CY, CX, CZ), F32)
-PARAMS = pltpu.CompilerParams(vmem_limit_bytes=4 * 2**20)
+PARAMS = pltpu.CompilerParams(vmem_limit_bytes=6 * 2**20)
 
 
 def rows_of(count, lanes=128):
     return jax.ShapeDtypeStruct((count, lanes), F32)
 
 
-def call(body, outs, *args, smem=0, scratch=(), flops=0, name=None, held=(), out_specs=None):
+def call(body, outs, *args, smem=0, scratch=(), flops=0, name=None, held=(), in_specs=None, out_specs=None):
     size = sum(int(np.prod(a.shape)) * a.dtype.itemsize for a in args)
     count = len(args)
 
@@ -598,8 +615,7 @@
     return pl.pallas_call(
         run,
         out_shape=outs,
-        in_specs=[SM] * smem
-        + [VM] * (count - smem)
+        in_specs=([SM] * smem + [VM] * (count - smem) if in_specs is None else in_specs)
         + [pl.BlockSpec(memory_space=pl.ANY)] * len(held),
         out_specs=jax.tree.map(lambda _: VM, outs) if out_specs is None else out_specs,
         scratch_shapes=list(scratch),
@@ -649,18 +665,23 @@
     )(*(pltpu.with_memory_space_constraint(a, pltpu.HBM) for a in (p_now, adj_now, coef_old)))
     near, far = exchange(near, far)
 
-    p, q, lap_p, lap_q, source, amounts = call(
+    wide = jax.ShapeDtypeStruct((CY, CX + OV, CZ), F32)
+    later = [own_x, own_z, p_prev, adj_next, coef_old, const["grow_own"]]
+    p, q, p_before, q_before, lap_p, lap_q, source, amounts, sigma_own = call(
         prepare,
-        (FIELD,) * 5 + (jax.ShapeDtypeStruct((STEPS + 1, 8, CZ), F32),),
-        signs[0], elem_index, wavelet, p_now, adj_now, own_x, own_z,
-        smem=3, flops=10**9, name="prepare",
+        (FIELD,) * 7 + (jax.ShapeDtypeStruct((STEPS + 1, 8, CZ), F32), wide),
+        signs[0], elem_index, wavelet, p_now, adj_now, const["grow_z"],
+        *(pltpu.with_memory_space_constraint(a, pltpu.HBM) for a in later),
+        flops=10**9, name="prepare",
+        in_specs=[SM] * 3 + [VM] * 3 + [pl.BlockSpec(memory_space=pltpu.HBM)] * len(later),
+        scratch=[pltpu.VMEM(a.shape, a.dtype) for a in later]
+        + [pltpu.SemaphoreType.DMA((len(later),))],
     )
     sigma, squared, beyond = call(
-        speed, (FIELD, FIELD, rows_of(CY * OV)), coef_old, near, far, const["grow_z"], const["grow_old"],
-        scratch=[pltpu.VMEM((ROWS, CYC * CZC), F32)], flops=10**8, name="speed",
-    )
-
-    p_before, q_before = p_prev, adj_next
+        speed, (FIELD, FIELD, half), sigma_own, near, far, const["grow_z"], const["grow_rest"],
+        scratch=[pltpu.VMEM((8, CYC * CZC), F32)], flops=10**8, name="speed",
+    )
+
     laps, qs = [], [q]
     gathered = None
     for step in range(STEPS):
@@ -714,7 +735,7 @@
         image, image_far, const["shrink_x"], const["shrink_far"], const["shrink_z"],
         flops=10**8, name="shrink",
     )
-    other = xor_swap(partial, "y", 1)
+    two, three, one = (xor_swap(partial, "y", m) for m in (2, 3, 1))
     near = xor_swap(near, "core", 1)
     lap_p = call(inside_one, FIELD, p, own_x, own_z, flops=5 * 10**8, name="inside_last")
     lap_p, base = call(
@@ -723,11 +744,7 @@
     )
     held = (lap_p, base)
     partial = call(
-        add_two, rows_of(ROWS, CYC * CZC), partial, other, name="add_y1", held=held
-    )
-    partial = call(
-        add_two, rows_of(ROWS, CYC * CZC), partial, xor_swap(partial, "y", 3), name="add_y3",
-        held=held,
+        add_four, rows_of(ROWS, CYC * CZC), partial, one, two, three, name="add_four", held=held
     )
     total, mine = call(
         squares, (rows_of(ROWS, CYC * CZC), rows_of(24)), partial, xor_swap(partial, "xl", 1),
@@ -738,7 +755,7 @@
         name="pair_up", held=held,
     )
     terms = call(
-        spread, (FIELD,) * 3, total, sigma, lap_p, base, const["grow_z"], const["grow_new"],
+        spread, (rows_of(CX * CY),) * 3, total, sigma, lap_p, base, const["grow_z"], const["grow_new"],
         flops=10**8, name="spread",
     )
     deep = lax.axis_size("z")

time: 87 us -> 85 us (0.977)
  Pallas kernels: 19.2 us -> 21.1 us
  starting transfers between devices: 23.5 us -> 21.8 us
  local copies, waits for them, and re-layouts: 2.47 us -> 1.17 us
    ppermute x10 -> x11, waiting for transfers between devices: 15.6 us -> 13.3 us  [xor_swap(): return lax.ppermute(x, axis, [(i, i ^ mask) for i in range(count)])]
    ppermute x3, waiting for transfers between devices: 13.8 us -> 15.7 us  [far_swap(): return lax.ppermute(x, TILE, pairs + [(b, a) for a, b in pairs])]
    pallas_call x21 -> x20, Pallas kernels: 18 us -> 19.9 us  [call(): pl.pallas_call(run, out_shape=outs, in_specs=([SM] * smem + [VM] * (count...]
    ppermute x3, starting transfers between devices: 17.6 us -> 15.9 us  [far_swap(): return lax.ppermute(x, TILE, pairs + [(b, a) for a, b in pairs])]
    unnamed x40 -> x32, local copies, waits for them, and re-layouts: 2.47 us -> 1.17 us
    ppermute x10 -> x11, starting transfers between devices: 5.88 us -> 5.96 us  [xor_swap(): return lax.ppermute(x, axis, [(i, i ^ mask) for i in range(count)])]
  transfers between devices with their start and end apart: 13 -> 14, of which waited for: 8 -> 8; matrix products, arithmetic and copies ran while one was open for 0% -> 0% of each run, Pallas kernels for 12% -> 15%
where the time goes in v6:
time: 85 us; the launch traced here: 84.7 us
  waiting for transfers between devices  29 us (34%)
  starting transfers between devices  21.8 us (26%)
  Pallas kernels  21.1 us (25%)
  blocking collectives  10.4 us (12%)
  between operations  1.2 us (1%)
  local copies, waits for them, and re-layouts  1.17 us (1%)
    pallas_call x20, Pallas kernels, call(): pl.pallas_call(run, out_shape=outs, in_specs=([SM] * smem + [VM] * (count...  19.9 us
    ppermute x3, starting transfers between devices, far_swap(): return lax.ppermute(x, TILE, pairs + [(b, a) for a, b in pairs])  15.9 us
    ppermute x3, waiting for transfers between devices, far_swap(): return lax.ppermute(x, TILE, pairs + [(b, a) for a, b in pairs])  15.7 us
    ppermute x11, waiting for transfers between devices, xor_swap(): return lax.ppermute(x, axis, [(i, i ^ mask) for i in range(count)])  13.3 us
    all_to_all x1, blocking collectives, on_device(): parts = lax.all_to_all(copies, 'z', split_axis=0, concat_axis=0, tiled=True)  10.4 us
    ppermute x11, starting transfers between devices, xor_swap(): return lax.ppermute(x, axis, [(i, i ^ mask) for i in range(count)])  5.96 us
  transfers between devices with their start and end apart: 14, of which 8 were waited for; matrix products, arithmetic and copies ran while one was open for 0% of the time, Pallas kernels for 15%

profile of v6, /device:TPU:6, one launch (start us, length us, event | category | flops | bytes accessed | tf_op | source)
XLA Modules:
  0.0 84.7 jit_solution(617268881883809079)
XLA Ops:
  0.7 1.2 %first_edges.1 = (f32[264,128]{1,0:T(8,128)S(1)}, f32[280,128]{1,0:T(8,128)S(1)}) custom-call(f32[2048,128]{1,0:T(8,128)} %bitcast.6, f32[2048,128]{1,0:T(8,128)} %bitcast.8, f32[64,512]{1,0:T(8,128)} %refs_10_.3), custom_call_target="tpu_custom_call" | custom-call | tf_op jit(solution)/shard_map/first_edges/pallas_call | solution.py:657
  1.9 8.0 %collective-permute-start.1 = (f32[280,128]{1,0:T(8,128)S(1)}, f32[280,128]{1,0:T(8,128)S(1)}, u32[]{:S(2)}, u32[]{:S(2)}) collective-permute-start(f32[280,128]{1,0:T(8,128)S(1)} %get-tuple-element.52), channel_id=1, source_target_pairs={{1,2},{3,4},{5,6},{7,8},{9,10},{11,12},{13,14},{15,16},{17,18},{19... | collective-permute-start | bytes 430088 | tf_op jit(solution)/shard_map/ppermute | solution.py:638
  10.1 5.3 %prepare.1 = (f32[16,128,128]{2,1,0:T(8,128)S(1)}, f32[16,128,128]{2,1,0:T(8,128)S(1)}, f32[16,128,128]{2,1,0:T(8,128)S(1)}, f32[16,128,128]{2,1,0:T(8,128)S(1)}...) custom-call(s32[64]{0:T(128)S(1)} %bitcast.10, ...), custom_call_target="tpu_custom_call" | custom-call | flops 1000000000 | bytes 4788756 | tf_op jit(solution)/shard_map/prepare/pallas_call | solution.py:615
  15.4 0.5 speed.1
  16.2 0.8 advance_0.1
  17.0 0.6 collective-permute-start.2
  17.6 1.5 %inside_0.1 = (f32[16,128,128]{2,1,0:T(8,128)S(1)}, f32[16,128,128]{2,1,0:T(8,128)S(1)}) custom-call(f32[16,128,128]{2,1,0:T(8,128)S(1)} %get-tuple-element.64.refs_0_.refs_1_.refs_2_.refs_3_, f32[16,128,128]{2,1,0:T(8,128)S(1)} %get-tuple-element.65.refs_1_.refs_3_.refs_4_.refs_5_.refs_11_.refs_16_, bf16[256,256]{1,0:T(8,128)(2,1)S(1)} %copy-done.5, ...), custom_call_target="tpu_custom_call" | custom-call | flops 1000000000 | bytes 2359296 | tf_op jit(solution)/shard_map/inside_0/pallas_call | solution.py:615
  19.3 3.8 %collective-permute-start.3 = (f32[512,128]{1,0:T(8,128)S(1)}, f32[512,128]{1,0:T(8,128)S(1)}, u32[]{:S(2)}, u32[]{:S(2)}) collective-permute-start(f32[512,128]{1,0:T(8,128)S(1)} %early_1.1.refs_12_), channel_id=1, source_target_pairs={{1,2},{3,4},{5,6},{7,8},{9,10},{11,12},{13,14},{15,16},{17,18},{19... | collective-permute-start | bytes 786440 | tf_op jit(solution)/shard_map/ppermute | solution.py:638
  23.2 7.5 %collective-permute-done.3.refs_1_.refs_19_ = f32[512,128]{1,0:T(8,128)S(1)} collective-permute-done((f32[512,128]{1,0:T(8,128)S(1)}, f32[512,128]{1,0:T(8,128)S(1)}, u32[]{:S(2)}, u32[]{:S(2)}) %collective-permute-start.3) | collective-permute-done | bytes 262176 | tf_op jit(solution)/shard_map/ppermute | solution.py:638
  30.6 0.9 %advance_1.1 = (f32[16,128,128]{2,1,0:T(8,128)S(1)}, f32[16,128,128]{2,1,0:T(8,128)S(1)}, f32[256,128]{1,0:T(8,128)S(1)}, f32[256,128]{1,0:T(8,128)S(1)}, f32[16,128,128]{2,1,0:T(8,128)S(1)}) custom-call(f32[256,128]{1,0:T(8,128)S(1)} %collective-permute-done.2.refs_0_, f32[512,128]{1,0:T(8,128)S(1)} %collective-permute-done.3.refs_1_.refs_19_, ...), custom_call_target="tpu_custom_call" | custom-call | flops 100000000 | bytes 9157632 | tf_op jit(solution)/shard_map/advance_1/pallas_call | solution.py:615
  31.6 1.5 %inside_1.1 = (f32[16,128,128]{2,1,0:T(8,128)S(1)}, f32[16,128,128]{2,1,0:T(8,128)S(1)}) custom-call(f32[16,128,128]{2,1,0:T(8,128)S(1)} %get-tuple-element.71.refs_0_.refs_2_.refs_3_, f32[16,128,128]{2,1,0:T(8,128)S(1)} %get-tuple-element.72.refs_1_.refs_4_.refs_5_, bf16[256,256]{1,0:T(8,128)(2,1)S(1)} %copy-done.5, bf16[256,256]{1,0:T(8,128)(2,1)S(1)} %copy-done.4), custom_call_target="tpu_custom_call" | custom-call | flops 1000000000 | bytes 2359296 | tf_op jit(solution)/shard_map/inside_1/pallas_call | solution.py:615
  33.1 0.9 %advance_2.1 = (f32[16,128,128]{2,1,0:T(8,128)S(1)}, f32[16,128,128]{2,1,0:T(8,128)S(1)}, f32[256,128]{1,0:T(8,128)S(1)}, f32[16,128,128]{2,1,0:T(8,128)S(1)}) custom-call(f32[256,128]{1,0:T(8,128)S(1)} %collective-permute-done.4.refs_0_, f32[256,128]{1,0:T(8,128)S(1)} %get-tuple-element.70.refs_1_, ...), custom_call_target="tpu_custom_call" | custom-call | flops 100000000 | bytes 9744384 | tf_op jit(solution)/shard_map/advance_2/pallas_call | solution.py:615
  34.1 0.8 collective-permute-start.5
  34.8 1.5 %inside_2.1 = (f32[16,128,128]{2,1,0:T(8,128)S(1)}, f32[16,128,128]{2,1,0:T(8,128)S(1)}) custom-call(f32[16,128,128]{2,1,0:T(8,128)S(1)} %get-tuple-element.77.refs_0_.refs_1_.refs_2_.refs_3_, f32[16,128,128]{2,1,0:T(8,128)S(1)} %get-tuple-element.78.refs_1_.refs_3_.refs_4_, bf16[256,256]{1,0:T(8,128)(2,1)S(1)} %copy-done.5, bf16[256,256]{1,0:T(8,128)(2,1)S(1)} %copy-done.4), custom_call_target="tpu_custom_call" | custom-call | flops 1000000000 | bytes 2359296 | tf_op jit(solution)/shard_map/inside_2/pallas_call | solution.py:615
  36.6 4.0 %collective-permute-start.6 = (f32[640,128]{1,0:T(8,128)S(1)}, f32[640,128]{1,0:T(8,128)S(1)}, u32[]{:S(2)}, u32[]{:S(2)}) collective-permute-start(f32[640,128]{1,0:T(8,128)S(1)} %early_3.1.refs_12_), channel_id=1, source_target_pairs={{1,2},{3,4},{5,6},{7,8},{9,10},{11,12},{13,14},{15,16},{17,18},{19... | collective-permute-start | bytes 983048 | tf_op jit(solution)/shard_map/ppermute | solution.py:638
  40.6 8.2 %collective-permute-done.6.refs_1_ = f32[640,128]{1,0:T(8,128)S(1)} collective-permute-done((f32[640,128]{1,0:T(8,128)S(1)}, f32[640,128]{1,0:T(8,128)S(1)}, u32[]{:S(2)}, u32[]{:S(2)}) %collective-permute-start.6) | collective-permute-done | bytes 327712 | tf_op jit(solution)/shard_map/ppermute | solution.py:638
  48.8 1.2 %advance_3.1 = (f32[16,128,128]{2,1,0:T(8,128)S(1)}, f32[128,128]{1,0:T(8,128)S(1)}, f32[128,128]{1,0:T(8,128)S(1)}, f32[16,128,128]{2,1,0:T(8,128)S(1)}, f32[128,128]{1,0:T(8,128)S(1)}) custom-call(f32[256,128]{1,0:T(8,128)S(1)} %collective-permute-done.5.refs_0_, f32[640,128]{1,0:T(8,128)S(1)} %collective-permute-done.6.refs_1_, ...), custom_call_target="tpu_custom_call" | custom-call | flops 100000000 | bytes 13745152 | tf_op jit(solution)/shard_map/advance_3/pallas_call | solution.py:615
  50.1 0.6 shrink.1.refs_0_
  50.7 3.1 %collective-permute-start.9 = (f32[72,512]{1,0:T(8,128)S(1)}, f32[72,512]{1,0:T(8,128)S(1)}, u32[]{:S(2)}, u32[]{:S(2)}) collective-permute-start(f32[72,512]{1,0:T(8,128)S(1)} %shrink.1.refs_0_), channel_id=1, source_target_pairs={{0,192},{64,128},{128,64},{192,0},{1,193},{65,129},{129,65},{193,1... | collective-permute-start | bytes 442376 | tf_op jit(solution)/shard_map/ppermute | solution.py:632
  53.8 0.6 collective-permute-start.8
  54.5 0.4 collective-permute-start.7
  54.9 0.8 inside_last.1.refs_4_
  55.7 0.4 collective-permute-done.10.refs_0_
  56.5 1.6 %collective-permute-done.9.refs_3_ = f32[72,512]{1,0:T(8,128)S(1)} collective-permute-done((f32[72,512]{1,0:T(8,128)S(1)}, f32[72,512]{1,0:T(8,128)S(1)}, u32[]{:S(2)}, u32[]{:S(2)}) %collective-permute-start.9) | collective-permute-done | bytes 147488 | tf_op jit(solution)/shard_map/ppermute | solution.py:632
  58.1 2.4 %collective-permute-done.8.refs_2_ = f32[72,512]{1,0:T(8,128)S(1)} collective-permute-done((f32[72,512]{1,0:T(8,128)S(1)}, f32[72,512]{1,0:T(8,128)S(1)}, u32[]{:S(2)}, u32[]{:S(2)}) %collective-permute-start.8) | collective-permute-done | bytes 147488 | tf_op jit(solution)/shard_map/ppermute | solution.py:632
  60.6 5.1 %collective-permute-done.11.refs_1_ = f32[72,512]{1,0:T(8,128)S(1)} collective-permute-done((f32[72,512]{1,0:T(8,128)S(1)}, f32[72,512]{1,0:T(8,128)S(1)}, u32[]{:S(2)}, u32[]{:S(2)}) %collective-permute-start.11) | collective-permute-done | bytes 147488 | tf_op jit(solution)/shard_map/ppermute | solution.py:632
  65.9 1.2 %collective-permute-done.12.refs_2_ = f32[24,128]{1,0:T(8,128)S(1)} collective-permute-done((f32[24,128]{1,0:T(8,128)S(1)}, f32[24,128]{1,0:T(8,128)S(1)}, u32[]{:S(2)}, u32[]{:S(2)}) %collective-permute-start.12) | collective-permute-done | bytes 12320 | tf_op jit(solution)/shard_map/ppermute | solution.py:632
  67.2 0.8 copy-done.6
  68.0 1.7 %spread.1 = (f32[2048,128]{1,0:T(8,128)S(1)}, f32[2048,128]{1,0:T(8,128)S(1)}, f32[2048,128]{1,0:T(8,128)S(1)}) custom-call(f32[72,512]{1,0:T(8,128)S(1)} %get-tuple-element.94.refs_0_.refs_1_, f32[16,128,128]{2,1,0:T(8,128)S(1)} %get-tuple-element.83.refs_14_.refs_18_.refs_1_, f32[16,128,128]{2,1,0:T(8,128)S(1)} %get-tuple-element.89.refs_4_.refs_2_.refs_3_, ...), custom_call_target="tpu_custom_call" | custom-call | flops 100000000 | bytes 3497984 | tf_op jit(solution)/shard_map/spread/pallas_call | solution.py:615
  69.7 2.6 %collective-permute-done.13.refs_1_ = f32[8,128]{1,0:T(8,128)S(1)} collective-permute-done((f32[8,128]{1,0:T(8,128)S(1)}, f32[8,128]{1,0:T(8,128)S(1)}, u32[]{:S(2)}, u32[]{:S(2)}) %collective-permute-start.13) | collective-permute-done | bytes 4128 | tf_op jit(solution)/shard_map/ppermute | solution.py:632
  72.3 10.4 %all_to_all.5.refs_0_ = f32[8,8,128]{2,1,0:T(8,128)S(1)} all-to-all(f32[8,8,128]{2,1,0:T(8,128)S(1)} %widen.1), channel_id=1, replica_groups=mesh['y'=4,'xl'=2,'xh'=2,'z'=8,'core'=2] {'z'}, dimensions={0} | all-to-all | bytes 65536 | tf_op jit(solution)/shard_map/all_to_all | solution.py:766
  82.7 1.8 %finish.1 = (f32[64,512]{1,0:T(8,128)}, f32[2048,128]{1,0:T(8,128)}) custom-call(f32[8,8,128]{2,1,0:T(8,128)S(1)} %all_to_all.5.refs_0_, f32[72,512]{1,0:T(8,128)S(1)} %get-tuple-element.94.refs_0_.refs_1_, f32[2048,128]{1,0:T(8,128)S(1)} %get-tuple-element.95.refs_2_, f32[2048,128]{1,0:T(8,128)S(1)} %get-tuple-element.96.refs_3_, ...), custom_call_target="tpu_custom_call" | custom-call | bytes 3325952 | tf_op jit(solution)/shard_map/finish/pallas_call | solution.py:615
  (50 shorter events, 1.7 us)
Async XLA Ops:
  0.6 9.4 %copy-start = (f32[1,128,16,128]{3,2,1,0:T(8,128)S(1)}, f32[1,128,16,128]{3,2,1,0:T(8,128)}, u32[]{:S(2)}) copy-start(f32[1,128,16,128]{3,2,1,0:T(8,128)} %param.20) | copy-start | bytes 3145732
  0.6 9.4 %copy-start.1 = (f32[1,128,16,128]{3,2,1,0:T(8,128)S(1)}, f32[1,128,16,128]{3,2,1,0:T(8,128)}, u32[]{:S(2)}) copy-start(f32[1,128,16,128]{3,2,1,0:T(8,128)} %param.22) | copy-start | bytes 3145732
  0.7 9.4 %copy-start.3 = (bf16[256,256]{1,0:T(8,128)(2,1)S(1)}, bf16[256,256]{1,0:T(8,128)(2,1)}, u32[]{:S(2)}) copy-start(bf16[256,256]{1,0:T(8,128)(2,1)} %constant.29.clone.refs_5_.refs_3_.refs_4_) | copy-start | bytes 393220
  0.7 9.4 %copy-start.13 = (s32[1,64]{1,0:T(1,128)S(1)}, s32[1,64]{1,0:T(1,128)}, u32[]{:S(2)}) copy-start(s32[1,64]{1,0:T(1,128)} %param.25) | copy-start | bytes 772
  0.7 9.4 %copy-start.14 = (s32[64]{0:T(128)S(1)}, s32[64]{0:T(128)}, u32[]{:S(2)}) copy-start(s32[64]{0:T(128)} %refs_1_.2) | copy-start | bytes 772
  0.7 9.4 %copy-start.15 = (f32[5]{0:T(128)S(1)}, f32[5]{0:T(128)}, u32[]{:S(2)}) copy-start(f32[5]{0:T(128)} %refs_2_.6) | copy-start | bytes 64
  1.9 13.5 %collective-permute-start.1 = (f32[280,128]{1,0:T(8,128)S(1)}, f32[280,128]{1,0:T(8,128)S(1)}, u32[]{:S(2)}, u32[]{:S(2)}) collective-permute-start(f32[280,128]{1,0:T(8,128)S(1)} %get-tuple-element.52), channel_id=1, source_target_pairs={{1,2},{3,4},{5,6},{7,8},{9,10},{11,12},{13,14},{15,16},{17,18},{19... | collective-permute-start | bytes 430088 | tf_op jit(solution)/shard_map/ppermute | solution.py:638
  9.9 5.5 %collective-permute-start = (f32[264,128]{1,0:T(8,128)S(1)}, f32[264,128]{1,0:T(8,128)S(1)}, u32[]{:S(2)}, u32[]{:S(2)}) collective-permute-start(f32[264,128]{1,0:T(8,128)S(1)} %get-tuple-element.51), channel_id=1, source_target_pairs={{0,1},{1,0},{2,3},{3,2},{4,5},{5,4},{6,7},{7,6},{8,9},{9,8},{10,11... | collective-permute-start | bytes 405512 | tf_op jit(solution)/shard_map/ppermute | solution.py:632
  10.1 5.3 %copy-start.9 = (bf16[2,136,16]{2,1,0:T(8,128)(2,1)S(1)}, bf16[2,136,16]{2,1,0:T(8,128)(2,1)}, u32[]{:S(2)}) copy-start(bf16[2,136,16]{2,1,0:T(8,128)(2,1)} %constant.33.clone.refs_4_) | copy-start | bytes 26116
  15.4 0.8 copy-start.2
  16.2 1.4 %copy-start.4 = (bf16[256,256]{1,0:T(8,128)(2,1)S(1)}, bf16[256,256]{1,0:T(8,128)(2,1)}, u32[]{:S(2)}) copy-start(bf16[256,256]{1,0:T(8,128)(2,1)} %constant.28.clone.refs_7_.refs_3_.refs_2_) | copy-start | bytes 393220
  16.2 1.4 %copy-start.5 = (bf16[256,256]{1,0:T(8,128)(2,1)S(1)}, bf16[256,256]{1,0:T(8,128)(2,1)}, u32[]{:S(2)}) copy-start(bf16[256,256]{1,0:T(8,128)(2,1)} %constant.24.clone.refs_6_.refs_2_.refs_1_) | copy-start | bytes 393220
  17.0 2.1 %collective-permute-start.2 = (f32[256,128]{1,0:T(8,128)S(1)}, f32[256,128]{1,0:T(8,128)S(1)}, u32[]{:S(2)}, u32[]{:S(2)}) collective-permute-start(f32[256,128]{1,0:T(8,128)S(1)} %get-tuple-element.63), channel_id=1, source_target_pairs={{0,1},{1,0},{2,3},{3,2},{4,5},{5,4},{6,7},{7,6},{8,9},{9,8},{10,11... | collective-permute-start | bytes 393224 | tf_op jit(solution)/shard_map/ppermute | solution.py:632
  17.6 1.5 %copy-start.12 = (bf16[2,16,48]{2,1,0:T(8,128)(2,1)S(1)}, bf16[2,16,48]{2,1,0:T(8,128)(2,1)}, u32[]{:S(2)}) copy-start(bf16[2,16,48]{2,1,0:T(8,128)(2,1)} %constant.26.clone.refs_10_) | copy-start | bytes 9220
  19.1 11.5 %copy-start.11 = (bf16[2,16,48]{2,1,0:T(8,128)(2,1)S(1)}, bf16[2,16,48]{2,1,0:T(8,128)(2,1)}, u32[]{:S(2)}) copy-start(bf16[2,16,48]{2,1,0:T(8,128)(2,1)} %constant.27.clone.refs_14_) | copy-start | bytes 9220
  19.3 11.3 %collective-permute-start.3 = (f32[512,128]{1,0:T(8,128)S(1)}, f32[512,128]{1,0:T(8,128)S(1)}, u32[]{:S(2)}, u32[]{:S(2)}) collective-permute-start(f32[512,128]{1,0:T(8,128)S(1)} %early_1.1.refs_12_), channel_id=1, source_target_pairs={{1,2},{3,4},{5,6},{7,8},{9,10},{11,12},{13,14},{15,16},{17,18},{19... | collective-permute-start | bytes 786440 | tf_op jit(solution)/shard_map/ppermute | solution.py:638
  31.5 1.6 %collective-permute-start.4 = (f32[256,128]{1,0:T(8,128)S(1)}, f32[256,128]{1,0:T(8,128)S(1)}, u32[]{:S(2)}, u32[]{:S(2)}) collective-permute-start(f32[256,128]{1,0:T(8,128)S(1)} %get-tuple-element.69), channel_id=1, source_target_pairs={{0,1},{1,0},{2,3},{3,2},{4,5},{5,4},{6,7},{7,6},{8,9},{9,8},{10,11... | collective-permute-start | bytes 393224 | tf_op jit(solution)/shard_map/ppermute | solution.py:632
  34.1 2.3 %collective-permute-start.5 = (f32[256,128]{1,0:T(8,128)S(1)}, f32[256,128]{1,0:T(8,128)S(1)}, u32[]{:S(2)}, u32[]{:S(2)}) collective-permute-start(f32[256,128]{1,0:T(8,128)S(1)} %get-tuple-element.76), channel_id=1, source_target_pairs={{0,1},{1,0},{2,3},{3,2},{4,5},{5,4},{6,7},{7,6},{8,9},{9,8},{10,11... | collective-permute-start | bytes 393224 | tf_op jit(solution)/shard_map/ppermute | solution.py:632
  36.6 13.5 %copy-start.7 = (bf16[512,128]{1,0:T(8,128)(2,1)S(1)}, bf16[512,128]{1,0:T(8,128)(2,1)}, u32[]{:S(2)}) copy-start(bf16[512,128]{1,0:T(8,128)(2,1)} %constant.30.clone.refs_4_) | copy-start | bytes 393220
  36.6 13.5 %copy-start.8 = (bf16[2,72,256]{2,1,0:T(8,128)(2,1)S(1)}, bf16[2,72,256]{2,1,0:T(8,128)(2,1)}, u32[]{:S(2)}) copy-start(bf16[2,72,256]{2,1,0:T(8,128)(2,1)} %constant.35.clone.refs_2_) | copy-start | bytes 221188
  36.6 13.5 %copy-start.10 = (bf16[2,72,16]{2,1,0:T(8,128)(2,1)S(1)}, bf16[2,72,16]{2,1,0:T(8,128)(2,1)}, u32[]{:S(2)}) copy-start(bf16[2,72,16]{2,1,0:T(8,128)(2,1)} %constant.31.clone.refs_3_) | copy-start | bytes 13828
  36.6 12.2 %collective-permute-start.6 = (f32[640,128]{1,0:T(8,128)S(1)}, f32[640,128]{1,0:T(8,128)S(1)}, u32[]{:S(2)}, u32[]{:S(2)}) collective-permute-start(f32[640,128]{1,0:T(8,128)S(1)} %early_3.1.refs_12_), channel_id=1, source_target_pairs={{1,2},{3,4},{5,6},{7,8},{9,10},{11,12},{13,14},{15,16},{17,18},{19... | collective-permute-start | bytes 983048 | tf_op jit(solution)/shard_map/ppermute | solution.py:638
  50.7 7.4 %collective-permute-start.9 = (f32[72,512]{1,0:T(8,128)S(1)}, f32[72,512]{1,0:T(8,128)S(1)}, u32[]{:S(2)}, u32[]{:S(2)}) collective-permute-start(f32[72,512]{1,0:T(8,128)S(1)} %shrink.1.refs_0_), channel_id=1, source_target_pairs={{0,192},{64,128},{128,64},{192,0},{1,193},{65,129},{129,65},{193,1... | collective-permute-start | bytes 442376 | tf_op jit(solution)/shard_map/ppermute | solution.py:632
  53.8 6.6 %collective-permute-start.8 = (f32[72,512]{1,0:T(8,128)S(1)}, f32[72,512]{1,0:T(8,128)S(1)}, u32[]{:S(2)}, u32[]{:S(2)}) collective-permute-start(f32[72,512]{1,0:T(8,128)S(1)} %shrink.1.refs_0_), channel_id=1, source_target_pairs={{0,128},{64,192},{128,0},{192,64},{1,129},{65,193},{129,1},{193,65... | collective-permute-start | bytes 442376 | tf_op jit(solution)/shard_map/ppermute | solution.py:632
  54.5 6.0 %collective-permute-start.7 = (f32[72,512]{1,0:T(8,128)S(1)}, f32[72,512]{1,0:T(8,128)S(1)}, u32[]{:S(2)}, u32[]{:S(2)}) collective-permute-start(f32[72,512]{1,0:T(8,128)S(1)} %shrink.1.refs_0_), channel_id=1, source_target_pairs={{0,64},{64,0},{128,192},{192,128},{1,65},{65,1},{129,193},{193,129... | collective-permute-start | bytes 442376 | tf_op jit(solution)/shard_map/ppermute | solution.py:632
  54.9 1.3 %collective-permute-start.10 = (f32[128,128]{1,0:T(8,128)S(1)}, f32[128,128]{1,0:T(8,128)S(1)}, u32[]{:S(2)}, u32[]{:S(2)}) collective-permute-start(f32[128,128]{1,0:T(8,128)S(1)} %get-tuple-element.86), channel_id=1, source_target_pairs={{0,1},{1,0},{2,3},{3,2},{4,5},{5,4},{6,7},{7,6},{8,9},{9,8},{10,11... | collective-permute-start | bytes 196616 | tf_op jit(solution)/shard_map/ppermute | solution.py:632
  60.5 5.2 %collective-permute-start.11 = (f32[72,512]{1,0:T(8,128)S(1)}, f32[72,512]{1,0:T(8,128)S(1)}, u32[]{:S(2)}, u32[]{:S(2)}) collective-permute-start(f32[72,512]{1,0:T(8,128)S(1)} %add_four.1.refs_0_), channel_id=1, source_target_pairs={{0,32},{32,0},{1,33},{33,1},{2,34},{34,2},{3,35},{35,3},{4,36},{36... | collective-permute-start | bytes 442376 | tf_op jit(solution)/shard_map/ppermute | solution.py:632
  65.8 1.3 %collective-permute-start.12 = (f32[24,128]{1,0:T(8,128)S(1)}, f32[24,128]{1,0:T(8,128)S(1)}, u32[]{:S(2)}, u32[]{:S(2)}) collective-permute-start(f32[24,128]{1,0:T(8,128)S(1)} %get-tuple-element.92.refs_1_), channel_id=1, source_target_pairs={{0,1},{1,0},{2,3},{3,2},{4,5},{5,4},{6,7},{7,6},{8,9},{9,8},{10,11... | collective-permute-start | bytes 36872 | tf_op jit(solution)/shard_map/ppermute | solution.py:632
  67.1 0.9 %copy-start.6 = (bf16[2,128,144]{2,1,0:T(8,128)(2,1)S(1)}, bf16[2,128,144]{2,1,0:T(8,128)(2,1)}, u32[]{:S(2)}) copy-start(bf16[2,128,144]{2,1,0:T(8,128)(2,1)} %constant.34.clone.refs_5_) | copy-start | bytes 221188
  67.1 5.2 %collective-permute-start.13 = (f32[8,128]{1,0:T(8,128)S(1)}, f32[8,128]{1,0:T(8,128)S(1)}, u32[]{:S(2)}, u32[]{:S(2)}) collective-permute-start(f32[8,128]{1,0:T(8,128)S(1)} %get-tuple-element.93.refs_0_), channel_id=1, source_target_pairs={{0,16},{16,0},{1,17},{17,1},{2,18},{18,2},{3,19},{19,3},{4,20},{20... | collective-permute-start | bytes 12296 | tf_op jit(solution)/shard_map/ppermute | solution.py:632

commit v7 on v6

--- a/solution.py
+++ b/solution.py
@@ -67,6 +67,11 @@
         high, low = halves(np.concatenate(pair, axis=1))
         sides.append(np.concatenate([high, high, low], axis=1))
     out["halo_x"] = np.stack(sides)
+    edge = []
+    for rows in (slice(0, OV), slice(CX - OV, CX)):
+        high, low = halves(second_x[rows, OV : OV + CX])
+        edge.append(np.block([[high, high], [low, low]]))
+    out["edge_x"] = np.stack(edge)
     near_part, cross_part = [], []
     for core in range(2):
         rows = slice(0, OV) if core == 0 else slice(CX - OV, CX)
@@ -431,9 +436,9 @@
 
 
 def early(step, *refs):
-    (near, p, p_before, q, q_before, lap_p, lap_q, squared, source, amounts, near_x) = refs[:11]
+    (near, p, p_before, q, q_before, laps, squared, source, amounts, near_x) = refs[:10]
     if step == 3:
-        older_q, old_lap, gathered, sigma = refs[11:15]
+        older_q, old_lap, gathered, sigma = refs[10:14]
     out = refs[-1]
     core = lax.axis_index("core")
     rows = pl.ds(pl.multiple_of(core * (CX - OV), OV), OV)
@@ -446,8 +451,10 @@
             y = 2 * pair + side
             lanes = slice(side * CZ, side * CZ + CZ)
             sq = squared[y, rows, :]
-            lap = lap_p[y, rows, :] + extra_p[:OV, lanes]
-            lap_adj = lap_q[y, rows, :] + extra_q[:OV, lanes]
+            spot = y * OV
+            lap = laps[spot : spot + OV] + extra_p[:OV, lanes]
+            spot += CY * OV
+            lap_adj = laps[spot : spot + OV] + extra_q[:OV, lanes]
             edge_p, edge_q = p[y, rows, :], q[y, rows, :]
             next_p = 2.0 * edge_p - p_before[y, rows, :] + sq * lap + source[y, rows, :] * weight
             next_q = 2.0 * edge_q - q_before[y, rows, :] + sq * lap_adj
@@ -461,6 +468,33 @@
             for k, value in enumerate(sets):
                 spot = (k * CY + y) * OV
                 out[spot : spot + OV] = value
+
+
+def edge_interior(v, edge_x, own_z, first, out, field):
+    strips = []
+    for j in range(CY // 2):
+        one, two = 2 * j, 2 * j + 1
+        high1, low1 = split(v[one])
+        high2, low2 = split(v[two])
+        x = dot(edge_x, cat([cat([high1, high2], 1), cat([low1, low2], 1)], 0))
+        x = x[:OV] + x[OV:]
+        strips += [x[:, :CZ], x[:, CZ:]]
+    rows = pl.ds(first, OV)
+    edge = [v[y, rows, :] for y in range(CY)]
+    high, low = split(cat(edge, 0))
+    z = dot(cat([high, low], 1), own_z[...])
+    z = z[:, :CZ] + z[:, CZ:]
+    for y in range(CY):
+        beside = edge[(y - 1) % CY] + edge[(y + 1) % CY]
+        spot = (field * CY + y) * OV
+        out[spot : spot + OV] = strips[y] + z[y * OV : y * OV + OV] + beside
+
+
+def edge_inside(p, q, edge_x, own_z, out):
+    core = lax.axis_index("core")
+    first = pl.multiple_of(core * (CX - OV), OV)
+    edge_interior(p, edge_x[core], own_z, first, out, 0)
+    edge_interior(q, edge_x[core], own_z, first, out, 1)
 
 
 def inside(p, q, own_x, own_z, lap_p, lap_q):
@@ -672,7 +706,7 @@
         (FIELD,) * 7 + (jax.ShapeDtypeStruct((STEPS + 1, 8, CZ), F32), wide),
         signs[0], elem_index, wavelet, p_now, adj_now, const["grow_z"],
         *(pltpu.with_memory_space_constraint(a, pltpu.HBM) for a in later),
-        flops=10**9, name="prepare",
+        flops=10**9, name="prepare", held=(halo_x,),
         in_specs=[SM] * 3 + [VM] * 3 + [pl.BlockSpec(memory_space=pltpu.HBM)] * len(later),
         scratch=[pltpu.VMEM(a.shape, a.dtype) for a in later]
         + [pltpu.SemaphoreType.DMA((len(later),))],
@@ -714,13 +748,16 @@
         q, q_before = q_new, q
         qs.append(q)
         near = xor_swap(edges[0], "core", 1)
-        lap_p, lap_q = call(
-            inside, (FIELD, FIELD), p, q, own_x, own_z, flops=10**9, name=f"inside_{step}"
-        )
         if step == 1:
+            lap_p, lap_q = call(
+                inside, (FIELD, FIELD), p, q, own_x, own_z, flops=10**9, name="inside_1"
+            )
             far = edges[1]
             continue
-        args = [near, p, p_before, q, q_before, lap_p, lap_q, squared, source, amounts]
+        edge_laps = call(
+            edge_inside, edge, p, q, const["edge_x"], own_z, flops=10**8, name=f"edge_inside_{step}"
+        )
+        args = [near, p, p_before, q, q_before, edge_laps, squared, source, amounts]
         args.append(const["near_x"])
         if step == 2:
             args += [qs[1], laps[0], gathered, sigma]
@@ -729,6 +766,10 @@
             *args, flops=10**7, name=f"early_{step + 1}",
         )
         far = far_swap(sent)
+        lap_p, lap_q = call(
+            inside, (FIELD, FIELD), p, q, own_x, own_z, flops=10**9, name=f"inside_{step}",
+            held=(sent,),
+        )
 
     partial = call(
         shrink, rows_of(ROWS, CYC * CZC),

time: 85 us -> 84 us (0.988)
  waiting for transfers between devices: 29 us -> 27.3 us
    ppermute x3, waiting for transfers between devices: 15.7 us -> 13 us  [far_swap(): return lax.ppermute(x, TILE, pairs + [(b, a) for a, b in pairs])]
    ppermute x11, waiting for transfers between devices: 13.3 us -> 14.2 us  [xor_swap(): return lax.ppermute(x, axis, [(i, i ^ mask) for i in range(count)])]
    pallas_call x20 -> x22, Pallas kernels: 19.9 us -> 20.7 us  [call(): pl.pallas_call(run, out_shape=outs, in_specs=([SM] * smem + [VM] * (count...]
    unnamed x32 -> x36, local copies, waits for them, and re-layouts: 1.17 us -> 1.81 us
  transfers between devices with their start and end apart: 14 -> 14, of which waited for: 8 -> 10; matrix products, arithmetic and copies ran while one was open for 0% -> 0% of each run, Pallas kernels for 15% -> 16%
where the time goes in v7:
time: 84 us; the launch traced here: 83.8 us
  waiting for transfers between devices  27.3 us (32%)
  Pallas kernels  21.9 us (26%)
  starting transfers between devices  21.2 us (25%)
  blocking collectives  10.4 us (12%)
  local copies, waits for them, and re-layouts  1.81 us (2%)
  between operations  1.2 us (1%)
    pallas_call x22, Pallas kernels, call(): pl.pallas_call(run, out_shape=outs, in_specs=([SM] * smem + [VM] * (count...  20.7 us
    ppermute x3, starting transfers between devices, far_swap(): return lax.ppermute(x, TILE, pairs + [(b, a) for a, b in pairs])  15.4 us
    ppermute x11, waiting for transfers between devices, xor_swap(): return lax.ppermute(x, axis, [(i, i ^ mask) for i in range(count)])  14.2 us
    ppermute x3, waiting for transfers between devices, far_swap(): return lax.ppermute(x, TILE, pairs + [(b, a) for a, b in pairs])  13 us
    all_to_all x1, blocking collectives, on_device(): parts = lax.all_to_all(copies, 'z', split_axis=0, concat_axis=0, tiled=True)  10.4 us
    ppermute x11, starting transfers between devices, xor_swap(): return lax.ppermute(x, axis, [(i, i ^ mask) for i in range(count)])  5.79 us
    unnamed x36, local copies, waits for them, and re-layouts  1.81 us
  transfers between devices with their start and end apart: 14, of which 10 were waited for; matrix products, arithmetic and copies ran while one was open for 0% of the time, Pallas kernels for 16%

profile of v7, /device:TPU:6, one launch (start us, length us, event | category | flops | bytes accessed | tf_op | source)
XLA Modules:
  0.0 83.8 jit_solution(1113674614191798830)
XLA Ops:
  0.7 1.2 %first_edges.1 = (f32[264,128]{1,0:T(8,128)S(1)}, f32[280,128]{1,0:T(8,128)S(1)}) custom-call(f32[2048,128]{1,0:T(8,128)} %bitcast.6, f32[2048,128]{1,0:T(8,128)} %bitcast.8, f32[64,512]{1,0:T(8,128)} %refs_10_.1), custom_call_target="tpu_custom_call" | custom-call | tf_op jit(solution)/shard_map/first_edges/pallas_call | solution.py:691
  1.9 8.0 %collective-permute-start.1 = (f32[280,128]{1,0:T(8,128)S(1)}, f32[280,128]{1,0:T(8,128)S(1)}, u32[]{:S(2)}, u32[]{:S(2)}) collective-permute-start(f32[280,128]{1,0:T(8,128)S(1)} %get-tuple-element.52), channel_id=1, source_target_pairs={{1,2},{3,4},{5,6},{7,8},{9,10},{11,12},{13,14},{15,16},{17,18},{19... | collective-permute-start | bytes 430088 | tf_op jit(solution)/shard_map/ppermute | solution.py:672
  10.1 0.9 %copy-done.4 = bf16[256,256]{1,0:T(8,128)(2,1)S(1)} copy-done((bf16[256,256]{1,0:T(8,128)(2,1)S(1)}, bf16[256,256]{1,0:T(8,128)(2,1)}, u32[]{:S(2)}) %copy-start.4) | copy-done | bytes 131096
  11.0 5.2 %prepare.1 = (f32[16,128,128]{2,1,0:T(8,128)S(1)}, f32[16,128,128]{2,1,0:T(8,128)S(1)}, f32[16,128,128]{2,1,0:T(8,128)S(1)}, f32[16,128,128]{2,1,0:T(8,128)S(1)}...) custom-call(s32[64]{0:T(128)S(1)} %bitcast.10, ...), custom_call_target="tpu_custom_call" | custom-call | flops 1000000000 | bytes 4788756 | tf_op jit(solution)/shard_map/prepare/pallas_call | solution.py:649
  16.8 0.8 advance_0.1
  17.6 0.6 collective-permute-start.2
  19.4 3.6 %collective-permute-start.3 = (f32[512,128]{1,0:T(8,128)S(1)}, f32[512,128]{1,0:T(8,128)S(1)}, u32[]{:S(2)}, u32[]{:S(2)}) collective-permute-start(f32[512,128]{1,0:T(8,128)S(1)} %early_1.1.refs_4_.refs_12_), channel_id=1, source_target_pairs={{1,2},{3,4},{5,6},{7,8},{9,10},{11,12},{13,14},{15,16},{17,18},{19... | collective-permute-start | bytes 786440 | tf_op jit(solution)/shard_map/ppermute | solution.py:672
  23.0 1.5 %inside_0.1 = (f32[16,128,128]{2,1,0:T(8,128)S(1)}, f32[16,128,128]{2,1,0:T(8,128)S(1)}) custom-call(f32[16,128,128]{2,1,0:T(8,128)S(1)} %get-tuple-element.64.refs_0_.refs_1_.refs_2_.refs_3_, f32[16,128,128]{2,1,0:T(8,128)S(1)} %get-tuple-element.65.refs_1_.refs_3_.refs_4_.refs_5_.refs_10_.refs_16_, bf16[256,256]{1,0:T(8,128)(2,1)S(1)} %copy-done.6, ...), custom_call_target="tpu_custom_call" | custom-call | flops 1000000000 | bytes 2359296 | tf_op jit(solution)/shard_map/inside_0/pallas_call | solution.py:649
  24.5 6.2 %collective-permute-done.3.refs_1_.refs_19_ = f32[512,128]{1,0:T(8,128)S(1)} collective-permute-done((f32[512,128]{1,0:T(8,128)S(1)}, f32[512,128]{1,0:T(8,128)S(1)}, u32[]{:S(2)}, u32[]{:S(2)}) %collective-permute-start.3) | collective-permute-done | bytes 262176 | tf_op jit(solution)/shard_map/ppermute | solution.py:672
  30.7 0.9 %advance_1.1 = (f32[16,128,128]{2,1,0:T(8,128)S(1)}, f32[16,128,128]{2,1,0:T(8,128)S(1)}, f32[256,128]{1,0:T(8,128)S(1)}, f32[256,128]{1,0:T(8,128)S(1)}, f32[16,128,128]{2,1,0:T(8,128)S(1)}) custom-call(f32[256,128]{1,0:T(8,128)S(1)} %collective-permute-done.2.refs_0_, f32[512,128]{1,0:T(8,128)S(1)} %collective-permute-done.3.refs_1_.refs_19_, ...), custom_call_target="tpu_custom_call" | custom-call | flops 100000000 | bytes 9157632 | tf_op jit(solution)/shard_map/advance_1/pallas_call | solution.py:649
  31.6 1.5 %inside_1.1 = (f32[16,128,128]{2,1,0:T(8,128)S(1)}, f32[16,128,128]{2,1,0:T(8,128)S(1)}) custom-call(f32[16,128,128]{2,1,0:T(8,128)S(1)} %get-tuple-element.71.refs_0_.refs_2_.refs_3_, f32[16,128,128]{2,1,0:T(8,128)S(1)} %get-tuple-element.72.refs_1_.refs_4_.refs_5_, bf16[256,256]{1,0:T(8,128)(2,1)S(1)} %copy-done.6, bf16[256,256]{1,0:T(8,128)(2,1)S(1)} %copy-done.3), custom_call_target="tpu_custom_call" | custom-call | flops 1000000000 | bytes 2359296 | tf_op jit(solution)/shard_map/inside_1/pallas_call | solution.py:649
  33.1 0.9 %advance_2.1 = (f32[16,128,128]{2,1,0:T(8,128)S(1)}, f32[16,128,128]{2,1,0:T(8,128)S(1)}, f32[256,128]{1,0:T(8,128)S(1)}, f32[16,128,128]{2,1,0:T(8,128)S(1)}) custom-call(f32[256,128]{1,0:T(8,128)S(1)} %collective-permute-done.4.refs_0_, f32[256,128]{1,0:T(8,128)S(1)} %get-tuple-element.70.refs_1_, ...), custom_call_target="tpu_custom_call" | custom-call | flops 100000000 | bytes 9744384 | tf_op jit(solution)/shard_map/advance_2/pallas_call | solution.py:649
  34.1 0.6 collective-permute-start.5
  34.7 0.5 edge_inside_2.1.refs_5_
  35.2 0.5 collective-permute-done.5.refs_0_
  35.9 3.8 %collective-permute-start.6 = (f32[640,128]{1,0:T(8,128)S(1)}, f32[640,128]{1,0:T(8,128)S(1)}, u32[]{:S(2)}, u32[]{:S(2)}) collective-permute-start(f32[640,128]{1,0:T(8,128)S(1)} %early_3.1.refs_4_.refs_12_), channel_id=1, source_target_pairs={{1,2},{3,4},{5,6},{7,8},{9,10},{11,12},{13,14},{15,16},{17,18},{19... | collective-permute-start | bytes 983048 | tf_op jit(solution)/shard_map/ppermute | solution.py:672
  39.6 1.5 %inside_2.1 = (f32[16,128,128]{2,1,0:T(8,128)S(1)}, f32[16,128,128]{2,1,0:T(8,128)S(1)}) custom-call(f32[16,128,128]{2,1,0:T(8,128)S(1)} %get-tuple-element.77.refs_0_.refs_1_.refs_2_.refs_3_, f32[16,128,128]{2,1,0:T(8,128)S(1)} %get-tuple-element.78.refs_1_.refs_3_.refs_4_, bf16[256,256]{1,0:T(8,128)(2,1)S(1)} %copy-done.6, bf16[256,256]{1,0:T(8,128)(2,1)S(1)} %copy-done.3, ...), custom_call_target="tpu_custom_call" | custom-call | flops 1000000000 | bytes 2359296 | tf_op jit(solution)/shard_map/inside_2/pallas_call | solution.py:649
  41.1 6.8 %collective-permute-done.6.refs_1_ = f32[640,128]{1,0:T(8,128)S(1)} collective-permute-done((f32[640,128]{1,0:T(8,128)S(1)}, f32[640,128]{1,0:T(8,128)S(1)}, u32[]{:S(2)}, u32[]{:S(2)}) %collective-permute-start.6) | collective-permute-done | bytes 327712 | tf_op jit(solution)/shard_map/ppermute | solution.py:672
  47.9 1.2 %advance_3.1 = (f32[16,128,128]{2,1,0:T(8,128)S(1)}, f32[128,128]{1,0:T(8,128)S(1)}, f32[128,128]{1,0:T(8,128)S(1)}, f32[16,128,128]{2,1,0:T(8,128)S(1)}, f32[128,128]{1,0:T(8,128)S(1)}) custom-call(f32[256,128]{1,0:T(8,128)S(1)} %collective-permute-done.5.refs_0_, f32[640,128]{1,0:T(8,128)S(1)} %collective-permute-done.6.refs_1_, ...), custom_call_target="tpu_custom_call" | custom-call | flops 100000000 | bytes 13745152 | tf_op jit(solution)/shard_map/advance_3/pallas_call | solution.py:649
  49.2 0.6 shrink.1.refs_0_
  49.8 3.1 %collective-permute-start.9 = (f32[72,512]{1,0:T(8,128)S(1)}, f32[72,512]{1,0:T(8,128)S(1)}, u32[]{:S(2)}, u32[]{:S(2)}) collective-permute-start(f32[72,512]{1,0:T(8,128)S(1)} %shrink.1.refs_0_), channel_id=1, source_target_pairs={{0,192},{64,128},{128,64},{192,0},{1,193},{65,129},{129,65},{193,1... | collective-permute-start | bytes 442376 | tf_op jit(solution)/shard_map/ppermute | solution.py:666
  52.9 0.6 collective-permute-start.8
  54.0 0.8 inside_last.1.refs_4_
  55.6 1.6 %collective-permute-done.9.refs_3_ = f32[72,512]{1,0:T(8,128)S(1)} collective-permute-done((f32[72,512]{1,0:T(8,128)S(1)}, f32[72,512]{1,0:T(8,128)S(1)}, u32[]{:S(2)}, u32[]{:S(2)}) %collective-permute-start.9) | collective-permute-done | bytes 147488 | tf_op jit(solution)/shard_map/ppermute | solution.py:666
  57.2 2.4 %collective-permute-done.8.refs_2_ = f32[72,512]{1,0:T(8,128)S(1)} collective-permute-done((f32[72,512]{1,0:T(8,128)S(1)}, f32[72,512]{1,0:T(8,128)S(1)}, u32[]{:S(2)}, u32[]{:S(2)}) %collective-permute-start.8) | collective-permute-done | bytes 147488 | tf_op jit(solution)/shard_map/ppermute | solution.py:666
  59.7 5.1 %collective-permute-done.11.refs_1_ = f32[72,512]{1,0:T(8,128)S(1)} collective-permute-done((f32[72,512]{1,0:T(8,128)S(1)}, f32[72,512]{1,0:T(8,128)S(1)}, u32[]{:S(2)}, u32[]{:S(2)}) %collective-permute-start.11) | collective-permute-done | bytes 147488 | tf_op jit(solution)/shard_map/ppermute | solution.py:666
  65.0 1.2 %collective-permute-done.12.refs_2_ = f32[24,128]{1,0:T(8,128)S(1)} collective-permute-done((f32[24,128]{1,0:T(8,128)S(1)}, f32[24,128]{1,0:T(8,128)S(1)}, u32[]{:S(2)}, u32[]{:S(2)}) %collective-permute-start.12) | collective-permute-done | bytes 12320 | tf_op jit(solution)/shard_map/ppermute | solution.py:666
  66.3 0.8 copy-done.5
  67.1 1.7 %spread.1 = (f32[2048,128]{1,0:T(8,128)S(1)}, f32[2048,128]{1,0:T(8,128)S(1)}, f32[2048,128]{1,0:T(8,128)S(1)}) custom-call(f32[72,512]{1,0:T(8,128)S(1)} %get-tuple-element.94.refs_0_.refs_1_, f32[16,128,128]{2,1,0:T(8,128)S(1)} %get-tuple-element.81.refs_13_.refs_18_.refs_1_, f32[16,128,128]{2,1,0:T(8,128)S(1)} %get-tuple-element.89.refs_4_.refs_2_.refs_3_, ...), custom_call_target="tpu_custom_call" | custom-call | flops 100000000 | bytes 3497984 | tf_op jit(solution)/shard_map/spread/pallas_call | solution.py:649
  68.8 2.6 %collective-permute-done.13.refs_1_ = f32[8,128]{1,0:T(8,128)S(1)} collective-permute-done((f32[8,128]{1,0:T(8,128)S(1)}, f32[8,128]{1,0:T(8,128)S(1)}, u32[]{:S(2)}, u32[]{:S(2)}) %collective-permute-start.13) | collective-permute-done | bytes 4128 | tf_op jit(solution)/shard_map/ppermute | solution.py:666
  71.4 10.4 %all_to_all.5.refs_0_ = f32[8,8,128]{2,1,0:T(8,128)S(1)} all-to-all(f32[8,8,128]{2,1,0:T(8,128)S(1)} %widen.1), channel_id=1, replica_groups=mesh['y'=4,'xl'=2,'xh'=2,'z'=8,'core'=2] {'z'}, dimensions={0} | all-to-all | bytes 65536 | tf_op jit(solution)/shard_map/all_to_all | solution.py:807
  81.8 1.8 %finish.1 = (f32[64,512]{1,0:T(8,128)}, f32[2048,128]{1,0:T(8,128)}) custom-call(f32[8,8,128]{2,1,0:T(8,128)S(1)} %all_to_all.5.refs_0_, f32[72,512]{1,0:T(8,128)S(1)} %get-tuple-element.94.refs_0_.refs_1_, f32[2048,128]{1,0:T(8,128)S(1)} %get-tuple-element.95.refs_2_, f32[2048,128]{1,0:T(8,128)S(1)} %get-tuple-element.96.refs_3_, ...), custom_call_target="tpu_custom_call" | custom-call | bytes 3325952 | tf_op jit(solution)/shard_map/finish/pallas_call | solution.py:649
  (56 shorter events, 3.8 us)
Async XLA Ops:
  0.6 9.4 %copy-start = (f32[1,128,16,128]{3,2,1,0:T(8,128)S(1)}, f32[1,128,16,128]{3,2,1,0:T(8,128)}, u32[]{:S(2)}) copy-start(f32[1,128,16,128]{3,2,1,0:T(8,128)} %param.21) | copy-start | bytes 3145732
  0.6 9.4 %copy-start.1 = (f32[1,128,16,128]{3,2,1,0:T(8,128)S(1)}, f32[1,128,16,128]{3,2,1,0:T(8,128)}, u32[]{:S(2)}) copy-start(f32[1,128,16,128]{3,2,1,0:T(8,128)} %param.23) | copy-start | bytes 3145732
  0.7 9.4 %copy-start.2 = (bf16[2,128,48]{2,1,0:T(8,128)(2,1)S(1)}, bf16[2,128,48]{2,1,0:T(8,128)(2,1)}, u32[]{:S(2)}) copy-start(bf16[2,128,48]{2,1,0:T(8,128)(2,1)} %constant.27.clone.refs_12_.refs_11_.refs_7_) | copy-start | bytes 73732
  0.7 9.4 %copy-start.15 = (s32[1,64]{1,0:T(1,128)S(1)}, s32[1,64]{1,0:T(1,128)}, u32[]{:S(2)}) copy-start(s32[1,64]{1,0:T(1,128)} %param.26) | copy-start | bytes 772
  0.7 9.4 %copy-start.16 = (s32[64]{0:T(128)S(1)}, s32[64]{0:T(128)}, u32[]{:S(2)}) copy-start(s32[64]{0:T(128)} %refs_1_.2) | copy-start | bytes 772
  0.7 9.4 %copy-start.17 = (f32[5]{0:T(128)S(1)}, f32[5]{0:T(128)}, u32[]{:S(2)}) copy-start(f32[5]{0:T(128)} %refs_2_.8) | copy-start | bytes 64
  1.9 14.4 %collective-permute-start.1 = (f32[280,128]{1,0:T(8,128)S(1)}, f32[280,128]{1,0:T(8,128)S(1)}, u32[]{:S(2)}, u32[]{:S(2)}) collective-permute-start(f32[280,128]{1,0:T(8,128)S(1)} %get-tuple-element.52), channel_id=1, source_target_pairs={{1,2},{3,4},{5,6},{7,8},{9,10},{11,12},{13,14},{15,16},{17,18},{19... | collective-permute-start | bytes 430088 | tf_op jit(solution)/shard_map/ppermute | solution.py:672
  9.9 6.3 %collective-permute-start = (f32[264,128]{1,0:T(8,128)S(1)}, f32[264,128]{1,0:T(8,128)S(1)}, u32[]{:S(2)}, u32[]{:S(2)}) collective-permute-start(f32[264,128]{1,0:T(8,128)S(1)} %get-tuple-element.51), channel_id=1, source_target_pairs={{0,1},{1,0},{2,3},{3,2},{4,5},{5,4},{6,7},{7,6},{8,9},{9,8},{10,11... | collective-permute-start | bytes 405512 | tf_op jit(solution)/shard_map/ppermute | solution.py:666
  10.1 0.9 %copy-start.4 = (bf16[256,256]{1,0:T(8,128)(2,1)S(1)}, bf16[256,256]{1,0:T(8,128)(2,1)}, u32[]{:S(2)}) copy-start(bf16[256,256]{1,0:T(8,128)(2,1)} %constant.32.clone.refs_5_.refs_3_.refs_4_) | copy-start | bytes 393220
  11.0 5.3 %copy-start.10 = (bf16[2,136,16]{2,1,0:T(8,128)(2,1)S(1)}, bf16[2,136,16]{2,1,0:T(8,128)(2,1)}, u32[]{:S(2)}) copy-start(bf16[2,136,16]{2,1,0:T(8,128)(2,1)} %constant.36.clone.refs_4_) | copy-start | bytes 26116
  16.8 1.4 %copy-start.3 = (bf16[256,256]{1,0:T(8,128)(2,1)S(1)}, bf16[256,256]{1,0:T(8,128)(2,1)}, u32[]{:S(2)}) copy-start(bf16[256,256]{1,0:T(8,128)(2,1)} %constant.31.clone.refs_7_.refs_3_.refs_2_) | copy-start | bytes 393220
  16.8 1.4 %copy-start.11 = (bf16[2,16,256]{2,1,0:T(8,128)(2,1)S(1)}, bf16[2,16,256]{2,1,0:T(8,128)(2,1)}, u32[]{:S(2)}) copy-start(bf16[2,16,256]{2,1,0:T(8,128)(2,1)} %constant.28.clone.refs_2_) | copy-start | bytes 49156
  17.6 1.6 %collective-permute-start.2 = (f32[256,128]{1,0:T(8,128)S(1)}, f32[256,128]{1,0:T(8,128)S(1)}, u32[]{:S(2)}, u32[]{:S(2)}) collective-permute-start(f32[256,128]{1,0:T(8,128)S(1)} %get-tuple-element.63), channel_id=1, source_target_pairs={{0,1},{1,0},{2,3},{3,2},{4,5},{5,4},{6,7},{7,6},{8,9},{9,8},{10,11... | collective-permute-start | bytes 393224 | tf_op jit(solution)/shard_map/ppermute | solution.py:666
  18.2 1.0 %copy-start.14 = (bf16[2,16,48]{2,1,0:T(8,128)(2,1)S(1)}, bf16[2,16,48]{2,1,0:T(8,128)(2,1)}, u32[]{:S(2)}) copy-start(bf16[2,16,48]{2,1,0:T(8,128)(2,1)} %constant.29.clone.refs_9_) | copy-start | bytes 9220
  18.7 4.3 %copy-start.6 = (bf16[256,256]{1,0:T(8,128)(2,1)S(1)}, bf16[256,256]{1,0:T(8,128)(2,1)}, u32[]{:S(2)}) copy-start(bf16[256,256]{1,0:T(8,128)(2,1)} %constant.26.clone.refs_6_.refs_2_.refs_1_) | copy-start | bytes 393220
  19.4 11.3 %copy-start.13 = (bf16[2,16,48]{2,1,0:T(8,128)(2,1)S(1)}, bf16[2,16,48]{2,1,0:T(8,128)(2,1)}, u32[]{:S(2)}) copy-start(bf16[2,16,48]{2,1,0:T(8,128)(2,1)} %constant.30.clone.refs_14_) | copy-start | bytes 9220
  19.4 11.3 %collective-permute-start.3 = (f32[512,128]{1,0:T(8,128)S(1)}, f32[512,128]{1,0:T(8,128)S(1)}, u32[]{:S(2)}, u32[]{:S(2)}) collective-permute-start(f32[512,128]{1,0:T(8,128)S(1)} %early_1.1.refs_4_.refs_12_), channel_id=1, source_target_pairs={{1,2},{3,4},{5,6},{7,8},{9,10},{11,12},{13,14},{15,16},{17,18},{19... | collective-permute-start | bytes 786440 | tf_op jit(solution)/shard_map/ppermute | solution.py:672
  31.5 1.6 %collective-permute-start.4 = (f32[256,128]{1,0:T(8,128)S(1)}, f32[256,128]{1,0:T(8,128)S(1)}, u32[]{:S(2)}, u32[]{:S(2)}) collective-permute-start(f32[256,128]{1,0:T(8,128)S(1)} %get-tuple-element.69), channel_id=1, source_target_pairs={{0,1},{1,0},{2,3},{3,2},{4,5},{5,4},{6,7},{7,6},{8,9},{9,8},{10,11... | collective-permute-start | bytes 393224 | tf_op jit(solution)/shard_map/ppermute | solution.py:666
  34.1 1.6 %collective-permute-start.5 = (f32[256,128]{1,0:T(8,128)S(1)}, f32[256,128]{1,0:T(8,128)S(1)}, u32[]{:S(2)}, u32[]{:S(2)}) collective-permute-start(f32[256,128]{1,0:T(8,128)S(1)} %get-tuple-element.76), channel_id=1, source_target_pairs={{0,1},{1,0},{2,3},{3,2},{4,5},{5,4},{6,7},{7,6},{8,9},{9,8},{10,11... | collective-permute-start | bytes 393224 | tf_op jit(solution)/shard_map/ppermute | solution.py:666
  35.9 12.1 %collective-permute-start.6 = (f32[640,128]{1,0:T(8,128)S(1)}, f32[640,128]{1,0:T(8,128)S(1)}, u32[]{:S(2)}, u32[]{:S(2)}) collective-permute-start(f32[640,128]{1,0:T(8,128)S(1)} %early_3.1.refs_4_.refs_12_), channel_id=1, source_target_pairs={{1,2},{3,4},{5,6},{7,8},{9,10},{11,12},{13,14},{15,16},{17,18},{19... | collective-permute-start | bytes 983048 | tf_op jit(solution)/shard_map/ppermute | solution.py:672
  47.9 1.2 %copy-start.8 = (bf16[512,128]{1,0:T(8,128)(2,1)S(1)}, bf16[512,128]{1,0:T(8,128)(2,1)}, u32[]{:S(2)}) copy-start(bf16[512,128]{1,0:T(8,128)(2,1)} %constant.33.clone.refs_4_) | copy-start | bytes 393220
  47.9 1.2 %copy-start.9 = (bf16[2,72,256]{2,1,0:T(8,128)(2,1)S(1)}, bf16[2,72,256]{2,1,0:T(8,128)(2,1)}, u32[]{:S(2)}) copy-start(bf16[2,72,256]{2,1,0:T(8,128)(2,1)} %constant.38.clone.refs_2_) | copy-start | bytes 221188
  47.9 1.2 %copy-start.12 = (bf16[2,72,16]{2,1,0:T(8,128)(2,1)S(1)}, bf16[2,72,16]{2,1,0:T(8,128)(2,1)}, u32[]{:S(2)}) copy-start(bf16[2,72,16]{2,1,0:T(8,128)(2,1)} %constant.34.clone.refs_3_) | copy-start | bytes 13828
  49.8 7.4 %collective-permute-start.9 = (f32[72,512]{1,0:T(8,128)S(1)}, f32[72,512]{1,0:T(8,128)S(1)}, u32[]{:S(2)}, u32[]{:S(2)}) collective-permute-start(f32[72,512]{1,0:T(8,128)S(1)} %shrink.1.refs_0_), channel_id=1, source_target_pairs={{0,192},{64,128},{128,64},{192,0},{1,193},{65,129},{129,65},{193,1... | collective-permute-start | bytes 442376 | tf_op jit(solution)/shard_map/ppermute | solution.py:666
  52.9 6.6 %collective-permute-start.8 = (f32[72,512]{1,0:T(8,128)S(1)}, f32[72,512]{1,0:T(8,128)S(1)}, u32[]{:S(2)}, u32[]{:S(2)}) collective-permute-start(f32[72,512]{1,0:T(8,128)S(1)} %shrink.1.refs_0_), channel_id=1, source_target_pairs={{0,128},{64,192},{128,0},{192,64},{1,129},{65,193},{129,1},{193,65... | collective-permute-start | bytes 442376 | tf_op jit(solution)/shard_map/ppermute | solution.py:666
  53.5 6.0 %collective-permute-start.7 = (f32[72,512]{1,0:T(8,128)S(1)}, f32[72,512]{1,0:T(8,128)S(1)}, u32[]{:S(2)}, u32[]{:S(2)}) collective-permute-start(f32[72,512]{1,0:T(8,128)S(1)} %shrink.1.refs_0_), channel_id=1, source_target_pairs={{0,64},{64,0},{128,192},{192,128},{1,65},{65,1},{129,193},{193,129... | collective-permute-start | bytes 442376 | tf_op jit(solution)/shard_map/ppermute | solution.py:666
  54.0 1.3 %collective-permute-start.10 = (f32[128,128]{1,0:T(8,128)S(1)}, f32[128,128]{1,0:T(8,128)S(1)}, u32[]{:S(2)}, u32[]{:S(2)}) collective-permute-start(f32[128,128]{1,0:T(8,128)S(1)} %get-tuple-element.86), channel_id=1, source_target_pairs={{0,1},{1,0},{2,3},{3,2},{4,5},{5,4},{6,7},{7,6},{8,9},{9,8},{10,11... | collective-permute-start | bytes 196616 | tf_op jit(solution)/shard_map/ppermute | solution.py:666
  59.6 5.2 %collective-permute-start.11 = (f32[72,512]{1,0:T(8,128)S(1)}, f32[72,512]{1,0:T(8,128)S(1)}, u32[]{:S(2)}, u32[]{:S(2)}) collective-permute-start(f32[72,512]{1,0:T(8,128)S(1)} %add_four.1.refs_0_), channel_id=1, source_target_pairs={{0,32},{32,0},{1,33},{33,1},{2,34},{34,2},{3,35},{35,3},{4,36},{36... | collective-permute-start | bytes 442376 | tf_op jit(solution)/shard_map/ppermute | solution.py:666
  64.9 1.3 %collective-permute-start.12 = (f32[24,128]{1,0:T(8,128)S(1)}, f32[24,128]{1,0:T(8,128)S(1)}, u32[]{:S(2)}, u32[]{:S(2)}) collective-permute-start(f32[24,128]{1,0:T(8,128)S(1)} %get-tuple-element.92.refs_1_), channel_id=1, source_target_pairs={{0,1},{1,0},{2,3},{3,2},{4,5},{5,4},{6,7},{7,6},{8,9},{9,8},{10,11... | collective-permute-start | bytes 36872 | tf_op jit(solution)/shard_map/ppermute | solution.py:666
  66.2 0.9 %copy-start.5 = (bf16[256,256]{1,0:T(8,128)(2,1)S(1)}, bf16[256,256]{1,0:T(8,128)(2,1)}, u32[]{:S(2)}) copy-start(bf16[256,256]{1,0:T(8,128)(2,1)} %constant.32.clone.refs_5_.refs_3_.refs_4_) | copy-start | bytes 393220
  66.2 1.0 %copy-start.7 = (bf16[2,128,144]{2,1,0:T(8,128)(2,1)S(1)}, bf16[2,128,144]{2,1,0:T(8,128)(2,1)}, u32[]{:S(2)}) copy-start(bf16[2,128,144]{2,1,0:T(8,128)(2,1)} %constant.37.clone.refs_5_) | copy-start | bytes 221188
  66.2 5.2 %collective-permute-start.13 = (f32[8,128]{1,0:T(8,128)S(1)}, f32[8,128]{1,0:T(8,128)S(1)}, u32[]{:S(2)}, u32[]{:S(2)}) collective-permute-start(f32[8,128]{1,0:T(8,128)S(1)} %get-tuple-element.93.refs_0_), channel_id=1, source_target_pairs={{0,16},{16,0},{1,17},{17,1},{2,18},{18,2},{3,19},{19,3},{4,20},{20... | collective-permute-start | bytes 12296 | tf_op jit(solution)/shard_map/ppermute | solution.py:666

commit v8 on v7

--- a/solution.py
+++ b/solution.py
@@ -195,53 +195,38 @@
         near[start : start + OV] = v[y, pl.ds(row, OV), :]
 
 
-def first_edges(p, q, coef, near, far, p_lo, p_hi, q_lo, q_hi, c_lo, c_hi, sems):
-    core = lax.axis_index("core")
+def first_edge(far_side, p, q, coef, out, p_rows, q_rows, c_rows, sems):
+    core = lax.axis_index("core")
+    end = core if far_side else 1 - core
     block = OV * CY
     copies = [
-        pltpu.make_async_copy(source.at[pl.ds(start, size)], target, sems.at[k])
+        pltpu.make_async_copy(source.at[pl.ds(pl.multiple_of(start, 8), size)], target, sems.at[k])
         for k, (source, start, size, target) in enumerate(
             (
-                (p, 0, block, p_lo),
-                (p, CX * CY - block, block, p_hi),
-                (q, 0, block, q_lo),
-                (q, CX * CY - block, block, q_hi),
-                (coef, 0, 8, c_lo),
-                (coef, CXC - 8, 8, c_hi),
+                (p, end * (CX * CY - block), block, p_rows),
+                (q, end * (CX * CY - block), block, q_rows),
+                (coef, end * (CXC - 8), 8, c_rows),
             )
         )
     ]
     for copy in copies:
         copy.start()
-
-    def fill(low, high, field):
+    for field, rows in enumerate((p_rows, q_rows)):
+        copies[field].wait()
         for y in range(CY):
             start = (field * CY + y) * OV
-            rows = pl.ds(y, OV, stride=CY)
-            first, last = low[rows, :], high[rows, :]
-            near[start : start + OV] = jnp.where(core == 0, last, first)
-            far[start : start + OV] = jnp.where(core == 0, first, last)
-
-    copies[0].wait()
-    copies[1].wait()
-    fill(p_lo, p_hi, 0)
+            out[start : start + OV] = rows[pl.ds(y, OV, stride=CY), :]
     copies[2].wait()
-    copies[3].wait()
-    fill(q_lo, q_hi, 1)
-    copies[4].wait()
-    copies[5].wait()
     base = 2 * CY * OV
-    for row in range(6):
+    count = 6 if far_side else 2
+    for row in range(count):
         for part in range(4):
             lanes = slice(part * 128, part * 128 + 128)
             spot = base + row * 4 + part
-            if row < 2:
-                first = c_lo[row : row + 1, lanes]
-                last = c_hi[6 + row : 7 + row, lanes]
-                near[spot : spot + 1] = jnp.where(core == 0, last, first)
-            first = c_lo[row : row + 1, lanes]
-            last = c_hi[2 + row : 3 + row, lanes]
-            far[spot : spot + 1] = jnp.where(core == 0, first, last)
+            last = 8 - count + row
+            out[spot : spot + 1] = jnp.where(
+                end == 0, c_rows[row : row + 1, lanes], c_rows[last : last + 1, lanes]
+            )
 
 
 def reorder(source, target):
@@ -250,9 +235,10 @@
 
 
 def prepare(
-    signs, index, wavelet, p_now, q_now, grow_z, own_x_in, own_z_in, p_prev_in, q_prev_in, coef_in, grow_own_in,
+    signs, index, wavelet, p_now, q_now,
+    own_x_in, own_z_in, p_prev_in, q_prev_in, coef_in, grow_own_in, grow_z_in,
     p0, q0, p1, q1, lap_p, lap_q, source, amounts, sigma_own,
-    own_x, own_z, p_prev, q_prev, coef, grow_own, sems,
+    own_x, own_z, p_prev, q_prev, coef, grow_own, grow_z, sems,
 ):
     copies = [
         pltpu.make_async_copy(far, near, sems.at[k])
@@ -264,6 +250,7 @@
                 (q_prev_in, q_prev),
                 (coef_in, coef),
                 (grow_own_in, grow_own),
+                (grow_z_in, grow_z),
             )
         )
     ]
@@ -294,8 +281,8 @@
     reorder(p_prev, p1)
     copies[3].wait()
     reorder(q_prev, q1)
-    copies[4].wait()
-    copies[5].wait()
+    for copy in copies[4:]:
+        copy.wait()
 
     def write(y, fine):
         sigma_own[y] = fine
@@ -585,7 +572,7 @@
             base[y] = 2.0 * p[y] - p_before[y] + source[y] * weight
 
 
-def add_four(own, one, two, three, out):
+def add_four(own, two, three, one, out):
     out[...] = (own[...] + one[...]) + (two[...] + three[...])
 
 
@@ -672,12 +659,6 @@
     return lax.ppermute(x, TILE, pairs + [(b, a) for a, b in pairs])
 
 
-def exchange(near, far):
-    far = far_swap(far)
-    near = xor_swap(near, "core", 1)
-    return near, far
-
-
 def on_device(p_now, p_prev, adj_now, adj_next, coef_old, signs, elem_index, wavelet):
     const = {name: jnp.asarray(value) for name, value in constants().items()}
     own_x, own_z, halo_x = const["own_x"], const["own_z"], const["halo_x"]
@@ -685,29 +666,34 @@
     p_now, p_prev, adj_now, adj_next = map(flat, (p_now, p_prev, adj_now, adj_next))
 
     half, edge = rows_of(CY * OV), rows_of(2 * CY * OV)
-    with_two, with_six = rows_of(2 * CY * OV + 8), rows_of(2 * CY * OV + 24)
-    block = pltpu.VMEM((OV * CY, CZ), F32)
-    few = pltpu.VMEM((8, CYC * CZC), F32)
-    near, far = pl.pallas_call(
-        first_edges,
-        out_shape=(with_two, with_six),
-        in_specs=[pl.BlockSpec(memory_space=pltpu.HBM)] * 3,
-        out_specs=(VM, VM),
-        scratch_shapes=[block] * 4 + [few] * 2 + [pltpu.SemaphoreType.DMA((6,))],
-        compiler_params=PARAMS,
-        name="first_edges",
-    )(*(pltpu.with_memory_space_constraint(a, pltpu.HBM) for a in (p_now, adj_now, coef_old)))
-    near, far = exchange(near, far)
+    sources = [pltpu.with_memory_space_constraint(a, pltpu.HBM) for a in (p_now, adj_now, coef_old)]
+
+    def first(far_side, *held):
+        return call(
+            functools.partial(first_edge, far_side),
+            rows_of(2 * CY * OV + (24 if far_side else 8)),
+            *sources,
+            in_specs=[pl.BlockSpec(memory_space=pltpu.HBM)] * 3,
+            scratch=[pltpu.VMEM((OV * CY, CZ), F32)] * 2
+            + [pltpu.VMEM((8, CYC * CZC), F32), pltpu.SemaphoreType.DMA((3,))],
+            name="far_edge" if far_side else "near_edge",
+            held=held,
+        )
+
+    far = first(True)
+    near = xor_swap(first(False, far), "core", 1)
+    far = far_swap(far)
 
     wide = jax.ShapeDtypeStruct((CY, CX + OV, CZ), F32)
     later = [own_x, own_z, p_prev, adj_next, coef_old, const["grow_own"]]
+    later.append(const["grow_z"])
     p, q, p_before, q_before, lap_p, lap_q, source, amounts, sigma_own = call(
         prepare,
         (FIELD,) * 7 + (jax.ShapeDtypeStruct((STEPS + 1, 8, CZ), F32), wide),
-        signs[0], elem_index, wavelet, p_now, adj_now, const["grow_z"],
+        signs[0], elem_index, wavelet, p_now, adj_now,
         *(pltpu.with_memory_space_constraint(a, pltpu.HBM) for a in later),
         flops=10**9, name="prepare", held=(halo_x,),
-        in_specs=[SM] * 3 + [VM] * 3 + [pl.BlockSpec(memory_space=pltpu.HBM)] * len(later),
+        in_specs=[SM] * 3 + [VM] * 2 + [pl.BlockSpec(memory_space=pltpu.HBM)] * len(later),
         scratch=[pltpu.VMEM(a.shape, a.dtype) for a in later]
         + [pltpu.SemaphoreType.DMA((len(later),))],
     )
@@ -785,7 +771,7 @@
     )
     held = (lap_p, base)
     partial = call(
-        add_four, rows_of(ROWS, CYC * CZC), partial, one, two, three, name="add_four", held=held
+        add_four, rows_of(ROWS, CYC * CZC), partial, two, three, one, name="add_four", held=held
     )
     total, mine = call(
         squares, (rows_of(ROWS, CYC * CZC), rows_of(24)), partial, xor_swap(partial, "xl", 1),

time: 84 us -> 84.8 us (level)
  local copies, waits for them, and re-layouts: 1.81 us -> 0.87 us
    pallas_call x22 -> x24, Pallas kernels: 20.7 us -> 22.6 us  [call(): pl.pallas_call(run, out_shape=outs, in_specs=([SM] * smem + [VM] * (count...]
    pallas_call x1 -> x0, Pallas kernels: 1.19 us -> none  [on_device(): pl.pallas_call(first_edges, out_shape=(with_two, with_six), in_specs=[pl....]
    unnamed x36 -> x34, local copies, waits for them, and re-layouts: 1.81 us -> 0.87 us
  transfers between devices with their start and end apart: 14 -> 14, of which waited for: 10 -> 10; matrix products, arithmetic and copies ran while one was open for 0% -> 0% of each run, Pallas kernels for 16% -> 17%
where the time goes in v8:
time: 84.8 us; the launch traced here: 84.5 us
  waiting for transfers between devices  27.8 us (33%)
  Pallas kernels  22.6 us (27%)
  starting transfers between devices  21.6 us (25%)
  blocking collectives  10.4 us (12%)
  between operations  1.23 us (1%)
  local copies, waits for them, and re-layouts  0.87 us (1%)
    pallas_call x24, Pallas kernels, call(): pl.pallas_call(run, out_shape=outs, in_specs=([SM] * smem + [VM] * (count...  22.6 us
    ppermute x3, starting transfers between devices, far_swap(): return lax.ppermute(x, TILE, pairs + [(b, a) for a, b in pairs])  15.3 us
    ppermute x11, waiting for transfers between devices, xor_swap(): return lax.ppermute(x, axis, [(i, i ^ mask) for i in range(count)])  14.6 us
    ppermute x3, waiting for transfers between devices, far_swap(): return lax.ppermute(x, TILE, pairs + [(b, a) for a, b in pairs])  13.2 us
    all_to_all x1, blocking collectives, on_device(): parts = lax.all_to_all(copies, 'z', split_axis=0, concat_axis=0, tiled=True)  10.4 us
    ppermute x11, starting transfers between devices, xor_swap(): return lax.ppermute(x, axis, [(i, i ^ mask) for i in range(count)])  6.23 us
  transfers between devices with their start and end apart: 14, of which 10 were waited for; matrix products, arithmetic and copies ran while one was open for 0% of the time, Pallas kernels for 17%

profile of v8, /device:TPU:6, one launch (start us, length us, event | category | flops | bytes accessed | tf_op | source)
XLA Modules:
  0.0 84.5 jit_solution(4895636554746855887)
XLA Ops:
  0.6 0.9 %far_edge.1.refs_3_ = f32[280,128]{1,0:T(8,128)S(1)} custom-call(f32[2048,128]{1,0:T(8,128)} %bitcast.6, f32[2048,128]{1,0:T(8,128)} %bitcast.9, f32[64,512]{1,0:T(8,128)} %refs_9_.3), custom_call_target="tpu_custom_call" | custom-call | bytes 2228224 | tf_op jit(solution)/shard_map/far_edge/pallas_call | solution.py:636
  1.7 8.2 %collective-permute-start.1 = (f32[280,128]{1,0:T(8,128)S(1)}, f32[280,128]{1,0:T(8,128)S(1)}, u32[]{:S(2)}, u32[]{:S(2)}) collective-permute-start(f32[280,128]{1,0:T(8,128)S(1)} %far_edge.1.refs_3_), channel_id=1, source_target_pairs={{1,2},{3,4},{5,6},{7,8},{9,10},{11,12},{13,14},{15,16},{17,18},{19... | collective-permute-start | bytes 430088 | tf_op jit(solution)/shard_map/ppermute | solution.py:659
  9.8 0.9 %near_edge.1 = f32[264,128]{1,0:T(8,128)S(1)} custom-call(f32[2048,128]{1,0:T(8,128)} %bitcast.7, f32[2048,128]{1,0:T(8,128)} %bitcast.10, f32[64,512]{1,0:T(8,128)} %refs_9_.3, f32[280,128]{1,0:T(8,128)S(1)} %far_edge.1.refs_3_), custom_call_target="tpu_custom_call" | custom-call | bytes 2228224 | tf_op jit(solution)/shard_map/near_edge/pallas_call | solution.py:636
  11.0 5.2 %prepare.1 = (f32[16,128,128]{2,1,0:T(8,128)S(1)}, f32[16,128,128]{2,1,0:T(8,128)S(1)}, f32[16,128,128]{2,1,0:T(8,128)S(1)}, f32[16,128,128]{2,1,0:T(8,128)S(1)}...) custom-call(s32[64]{0:T(128)S(1)} %bitcast.12, ...), custom_call_target="tpu_custom_call" | custom-call | flops 1000000000 | bytes 4788756 | tf_op jit(solution)/shard_map/prepare/pallas_call | solution.py:636
  16.8 0.8 advance_0.1
  17.6 0.6 collective-permute-start.2
  19.4 3.5 %collective-permute-start.3 = (f32[512,128]{1,0:T(8,128)S(1)}, f32[512,128]{1,0:T(8,128)S(1)}, u32[]{:S(2)}, u32[]{:S(2)}) collective-permute-start(f32[512,128]{1,0:T(8,128)S(1)} %early_1.1.refs_4_.refs_12_), channel_id=1, source_target_pairs={{1,2},{3,4},{5,6},{7,8},{9,10},{11,12},{13,14},{15,16},{17,18},{19... | collective-permute-start | bytes 786440 | tf_op jit(solution)/shard_map/ppermute | solution.py:659
  22.9 1.5 %inside_0.1 = (f32[16,128,128]{2,1,0:T(8,128)S(1)}, f32[16,128,128]{2,1,0:T(8,128)S(1)}) custom-call(f32[16,128,128]{2,1,0:T(8,128)S(1)} %get-tuple-element.60.refs_0_.refs_1_.refs_2_.refs_3_, f32[16,128,128]{2,1,0:T(8,128)S(1)} %get-tuple-element.61.refs_1_.refs_3_.refs_4_.refs_5_.refs_10_.refs_16_, bf16[256,256]{1,0:T(8,128)(2,1)S(1)} %copy-done.5, ...), custom_call_target="tpu_custom_call" | custom-call | flops 1000000000 | bytes 2359296 | tf_op jit(solution)/shard_map/inside_0/pallas_call | solution.py:636
  24.4 6.3 %collective-permute-done.3.refs_1_.refs_19_ = f32[512,128]{1,0:T(8,128)S(1)} collective-permute-done((f32[512,128]{1,0:T(8,128)S(1)}, f32[512,128]{1,0:T(8,128)S(1)}, u32[]{:S(2)}, u32[]{:S(2)}) %collective-permute-start.3) | collective-permute-done | bytes 262176 | tf_op jit(solution)/shard_map/ppermute | solution.py:659
  30.7 0.9 %advance_1.1 = (f32[16,128,128]{2,1,0:T(8,128)S(1)}, f32[16,128,128]{2,1,0:T(8,128)S(1)}, f32[256,128]{1,0:T(8,128)S(1)}, f32[256,128]{1,0:T(8,128)S(1)}, f32[16,128,128]{2,1,0:T(8,128)S(1)}) custom-call(f32[256,128]{1,0:T(8,128)S(1)} %collective-permute-done.2.refs_0_, f32[512,128]{1,0:T(8,128)S(1)} %collective-permute-done.3.refs_1_.refs_19_, ...), custom_call_target="tpu_custom_call" | custom-call | flops 100000000 | bytes 9157632 | tf_op jit(solution)/shard_map/advance_1/pallas_call | solution.py:636
  31.6 1.5 %inside_1.1 = (f32[16,128,128]{2,1,0:T(8,128)S(1)}, f32[16,128,128]{2,1,0:T(8,128)S(1)}) custom-call(f32[16,128,128]{2,1,0:T(8,128)S(1)} %get-tuple-element.67.refs_0_.refs_2_.refs_3_, f32[16,128,128]{2,1,0:T(8,128)S(1)} %get-tuple-element.68.refs_1_.refs_4_.refs_5_, bf16[256,256]{1,0:T(8,128)(2,1)S(1)} %copy-done.5, bf16[256,256]{1,0:T(8,128)(2,1)S(1)} %copy-done.3), custom_call_target="tpu_custom_call" | custom-call | flops 1000000000 | bytes 2359296 | tf_op jit(solution)/shard_map/inside_1/pallas_call | solution.py:636
  33.1 0.9 %advance_2.1 = (f32[16,128,128]{2,1,0:T(8,128)S(1)}, f32[16,128,128]{2,1,0:T(8,128)S(1)}, f32[256,128]{1,0:T(8,128)S(1)}, f32[16,128,128]{2,1,0:T(8,128)S(1)}) custom-call(f32[256,128]{1,0:T(8,128)S(1)} %collective-permute-done.4.refs_0_, f32[256,128]{1,0:T(8,128)S(1)} %get-tuple-element.66.refs_1_, ...), custom_call_target="tpu_custom_call" | custom-call | flops 100000000 | bytes 9744384 | tf_op jit(solution)/shard_map/advance_2/pallas_call | solution.py:636
  34.1 0.6 collective-permute-start.5
  35.1 0.5 collective-permute-done.5.refs_0_
  35.8 3.7 %collective-permute-start.6 = (f32[640,128]{1,0:T(8,128)S(1)}, f32[640,128]{1,0:T(8,128)S(1)}, u32[]{:S(2)}, u32[]{:S(2)}) collective-permute-start(f32[640,128]{1,0:T(8,128)S(1)} %early_3.1.refs_4_.refs_12_), channel_id=1, source_target_pairs={{1,2},{3,4},{5,6},{7,8},{9,10},{11,12},{13,14},{15,16},{17,18},{19... | collective-permute-start | bytes 983048 | tf_op jit(solution)/shard_map/ppermute | solution.py:659
  39.5 1.5 %inside_2.1 = (f32[16,128,128]{2,1,0:T(8,128)S(1)}, f32[16,128,128]{2,1,0:T(8,128)S(1)}) custom-call(f32[16,128,128]{2,1,0:T(8,128)S(1)} %get-tuple-element.73.refs_0_.refs_1_.refs_2_.refs_3_, f32[16,128,128]{2,1,0:T(8,128)S(1)} %get-tuple-element.74.refs_1_.refs_3_.refs_4_, bf16[256,256]{1,0:T(8,128)(2,1)S(1)} %copy-done.5, bf16[256,256]{1,0:T(8,128)(2,1)S(1)} %copy-done.3, ...), custom_call_target="tpu_custom_call" | custom-call | flops 1000000000 | bytes 2359296 | tf_op jit(solution)/shard_map/inside_2/pallas_call | solution.py:636
  41.0 6.8 %collective-permute-done.6.refs_1_ = f32[640,128]{1,0:T(8,128)S(1)} collective-permute-done((f32[640,128]{1,0:T(8,128)S(1)}, f32[640,128]{1,0:T(8,128)S(1)}, u32[]{:S(2)}, u32[]{:S(2)}) %collective-permute-start.6) | collective-permute-done | bytes 327712 | tf_op jit(solution)/shard_map/ppermute | solution.py:659
  47.8 1.2 %advance_3.1 = (f32[16,128,128]{2,1,0:T(8,128)S(1)}, f32[128,128]{1,0:T(8,128)S(1)}, f32[128,128]{1,0:T(8,128)S(1)}, f32[16,128,128]{2,1,0:T(8,128)S(1)}, f32[128,128]{1,0:T(8,128)S(1)}) custom-call(f32[256,128]{1,0:T(8,128)S(1)} %collective-permute-done.5.refs_0_, f32[640,128]{1,0:T(8,128)S(1)} %collective-permute-done.6.refs_1_, ...), custom_call_target="tpu_custom_call" | custom-call | flops 100000000 | bytes 13745152 | tf_op jit(solution)/shard_map/advance_3/pallas_call | solution.py:636
  49.1 0.6 shrink.1.refs_0_
  49.7 1.7 %collective-permute-start.9 = (f32[72,512]{1,0:T(8,128)S(1)}, f32[72,512]{1,0:T(8,128)S(1)}, u32[]{:S(2)}, u32[]{:S(2)}) collective-permute-start(f32[72,512]{1,0:T(8,128)S(1)} %shrink.1.refs_0_), channel_id=1, source_target_pairs={{0,64},{64,0},{128,192},{192,128},{1,65},{65,1},{129,193},{193,129... | collective-permute-start | bytes 442376 | tf_op jit(solution)/shard_map/ppermute | solution.py:653
  51.5 2.2 %collective-permute-start.8 = (f32[72,512]{1,0:T(8,128)S(1)}, f32[72,512]{1,0:T(8,128)S(1)}, u32[]{:S(2)}, u32[]{:S(2)}) collective-permute-start(f32[72,512]{1,0:T(8,128)S(1)} %shrink.1.refs_0_), channel_id=1, source_target_pairs={{0,192},{64,128},{128,64},{192,0},{1,193},{65,129},{129,65},{193,1... | collective-permute-start | bytes 442376 | tf_op jit(solution)/shard_map/ppermute | solution.py:653
  53.6 0.7 collective-permute-start.7
  54.4 0.8 inside_last.1.refs_4_
  56.0 1.8 %collective-permute-done.8.refs_2_ = f32[72,512]{1,0:T(8,128)S(1)} collective-permute-done((f32[72,512]{1,0:T(8,128)S(1)}, f32[72,512]{1,0:T(8,128)S(1)}, u32[]{:S(2)}, u32[]{:S(2)}) %collective-permute-start.8) | collective-permute-done | bytes 147488 | tf_op jit(solution)/shard_map/ppermute | solution.py:653
  57.8 2.5 %collective-permute-done.7.refs_1_ = f32[72,512]{1,0:T(8,128)S(1)} collective-permute-done((f32[72,512]{1,0:T(8,128)S(1)}, f32[72,512]{1,0:T(8,128)S(1)}, u32[]{:S(2)}, u32[]{:S(2)}) %collective-permute-start.7) | collective-permute-done | bytes 147488 | tf_op jit(solution)/shard_map/ppermute | solution.py:653
  60.4 5.1 %collective-permute-done.11.refs_1_ = f32[72,512]{1,0:T(8,128)S(1)} collective-permute-done((f32[72,512]{1,0:T(8,128)S(1)}, f32[72,512]{1,0:T(8,128)S(1)}, u32[]{:S(2)}, u32[]{:S(2)}) %collective-permute-start.11) | collective-permute-done | bytes 147488 | tf_op jit(solution)/shard_map/ppermute | solution.py:653
  65.7 1.2 %collective-permute-done.12.refs_2_ = f32[24,128]{1,0:T(8,128)S(1)} collective-permute-done((f32[24,128]{1,0:T(8,128)S(1)}, f32[24,128]{1,0:T(8,128)S(1)}, u32[]{:S(2)}, u32[]{:S(2)}) %collective-permute-start.12) | collective-permute-done | bytes 12320 | tf_op jit(solution)/shard_map/ppermute | solution.py:653
  67.0 0.8 copy-done.6
  67.8 1.7 %spread.1 = (f32[2048,128]{1,0:T(8,128)S(1)}, f32[2048,128]{1,0:T(8,128)S(1)}, f32[2048,128]{1,0:T(8,128)S(1)}) custom-call(f32[72,512]{1,0:T(8,128)S(1)} %get-tuple-element.90.refs_0_.refs_1_, f32[16,128,128]{2,1,0:T(8,128)S(1)} %get-tuple-element.77.refs_13_.refs_18_.refs_1_, f32[16,128,128]{2,1,0:T(8,128)S(1)} %get-tuple-element.85.refs_4_.refs_2_.refs_3_, ...), custom_call_target="tpu_custom_call" | custom-call | flops 100000000 | bytes 3497984 | tf_op jit(solution)/shard_map/spread/pallas_call | solution.py:636
  69.5 2.6 %collective-permute-done.13.refs_1_ = f32[8,128]{1,0:T(8,128)S(1)} collective-permute-done((f32[8,128]{1,0:T(8,128)S(1)}, f32[8,128]{1,0:T(8,128)S(1)}, u32[]{:S(2)}, u32[]{:S(2)}) %collective-permute-start.13) | collective-permute-done | bytes 4128 | tf_op jit(solution)/shard_map/ppermute | solution.py:653
  72.1 10.4 %all_to_all.5.refs_0_ = f32[8,8,128]{2,1,0:T(8,128)S(1)} all-to-all(f32[8,8,128]{2,1,0:T(8,128)S(1)} %widen.1), channel_id=1, replica_groups=mesh['y'=4,'xl'=2,'xh'=2,'z'=8,'core'=2] {'z'}, dimensions={0} | all-to-all | bytes 65536 | tf_op jit(solution)/shard_map/all_to_all | solution.py:793
  82.5 1.8 %finish.1 = (f32[64,512]{1,0:T(8,128)}, f32[2048,128]{1,0:T(8,128)}) custom-call(f32[8,8,128]{2,1,0:T(8,128)S(1)} %all_to_all.5.refs_0_, f32[72,512]{1,0:T(8,128)S(1)} %get-tuple-element.90.refs_0_.refs_1_, f32[2048,128]{1,0:T(8,128)S(1)} %get-tuple-element.91.refs_2_, f32[2048,128]{1,0:T(8,128)S(1)} %get-tuple-element.92.refs_3_, ...), custom_call_target="tpu_custom_call" | custom-call | bytes 3325952 | tf_op jit(solution)/shard_map/finish/pallas_call | solution.py:636
  (55 shorter events, 3.7 us)
Async XLA Ops:
  1.6 9.3 %copy-start = (f32[1,128,16,128]{3,2,1,0:T(8,128)S(1)}, f32[1,128,16,128]{3,2,1,0:T(8,128)}, u32[]{:S(2)}) copy-start(f32[1,128,16,128]{3,2,1,0:T(8,128)} %param.21) | copy-start | bytes 3145732
  1.6 9.3 %copy-start.1 = (f32[1,128,16,128]{3,2,1,0:T(8,128)S(1)}, f32[1,128,16,128]{3,2,1,0:T(8,128)}, u32[]{:S(2)}) copy-start(f32[1,128,16,128]{3,2,1,0:T(8,128)} %param.23) | copy-start | bytes 3145732
  1.6 9.3 %copy-start.2 = (bf16[2,128,48]{2,1,0:T(8,128)(2,1)S(1)}, bf16[2,128,48]{2,1,0:T(8,128)(2,1)}, u32[]{:S(2)}) copy-start(bf16[2,128,48]{2,1,0:T(8,128)(2,1)} %constant.27.clone.refs_12_.refs_11_.refs_7_) | copy-start | bytes 73732
  1.6 9.3 %copy-start.14 = (s32[1,64]{1,0:T(1,128)S(1)}, s32[1,64]{1,0:T(1,128)}, u32[]{:S(2)}) copy-start(s32[1,64]{1,0:T(1,128)} %param.26) | copy-start | bytes 772
  1.6 9.3 %copy-start.15 = (s32[64]{0:T(128)S(1)}, s32[64]{0:T(128)}, u32[]{:S(2)}) copy-start(s32[64]{0:T(128)} %refs_1_.2) | copy-start | bytes 772
  1.6 9.3 %copy-start.16 = (f32[5]{0:T(128)S(1)}, f32[5]{0:T(128)}, u32[]{:S(2)}) copy-start(f32[5]{0:T(128)} %refs_2_.12) | copy-start | bytes 64
  1.7 14.6 %collective-permute-start.1 = (f32[280,128]{1,0:T(8,128)S(1)}, f32[280,128]{1,0:T(8,128)S(1)}, u32[]{:S(2)}, u32[]{:S(2)}) collective-permute-start(f32[280,128]{1,0:T(8,128)S(1)} %far_edge.1.refs_3_), channel_id=1, source_target_pairs={{1,2},{3,4},{5,6},{7,8},{9,10},{11,12},{13,14},{15,16},{17,18},{19... | collective-permute-start | bytes 430088 | tf_op jit(solution)/shard_map/ppermute | solution.py:659
  10.8 5.4 %collective-permute-start = (f32[264,128]{1,0:T(8,128)S(1)}, f32[264,128]{1,0:T(8,128)S(1)}, u32[]{:S(2)}, u32[]{:S(2)}) collective-permute-start(f32[264,128]{1,0:T(8,128)S(1)} %near_edge.1), channel_id=1, source_target_pairs={{0,1},{1,0},{2,3},{3,2},{4,5},{5,4},{6,7},{7,6},{8,9},{9,8},{10,11... | collective-permute-start | bytes 405512 | tf_op jit(solution)/shard_map/ppermute | solution.py:653
  10.9 5.3 %copy-start.4 = (bf16[256,256]{1,0:T(8,128)(2,1)S(1)}, bf16[256,256]{1,0:T(8,128)(2,1)}, u32[]{:S(2)}) copy-start(bf16[256,256]{1,0:T(8,128)(2,1)} %constant.32.clone.refs_11_.refs_3_.refs_4_) | copy-start | bytes 393220
  11.0 5.3 %copy-start.9 = (bf16[2,136,16]{2,1,0:T(8,128)(2,1)S(1)}, bf16[2,136,16]{2,1,0:T(8,128)(2,1)}, u32[]{:S(2)}) copy-start(bf16[2,136,16]{2,1,0:T(8,128)(2,1)} %constant.36.clone.refs_4_) | copy-start | bytes 26116
  16.7 1.4 %copy-start.3 = (bf16[256,256]{1,0:T(8,128)(2,1)S(1)}, bf16[256,256]{1,0:T(8,128)(2,1)}, u32[]{:S(2)}) copy-start(bf16[256,256]{1,0:T(8,128)(2,1)} %constant.31.clone.refs_6_.refs_3_.refs_2_) | copy-start | bytes 393220
  16.8 1.4 %copy-start.10 = (bf16[2,16,256]{2,1,0:T(8,128)(2,1)S(1)}, bf16[2,16,256]{2,1,0:T(8,128)(2,1)}, u32[]{:S(2)}) copy-start(bf16[2,16,256]{2,1,0:T(8,128)(2,1)} %constant.28.clone.refs_2_) | copy-start | bytes 49156
  17.6 1.6 %collective-permute-start.2 = (f32[256,128]{1,0:T(8,128)S(1)}, f32[256,128]{1,0:T(8,128)S(1)}, u32[]{:S(2)}, u32[]{:S(2)}) collective-permute-start(f32[256,128]{1,0:T(8,128)S(1)} %get-tuple-element.59), channel_id=1, source_target_pairs={{0,1},{1,0},{2,3},{3,2},{4,5},{5,4},{6,7},{7,6},{8,9},{9,8},{10,11... | collective-permute-start | bytes 393224 | tf_op jit(solution)/shard_map/ppermute | solution.py:653
  18.2 1.0 %copy-start.13 = (bf16[2,16,48]{2,1,0:T(8,128)(2,1)S(1)}, bf16[2,16,48]{2,1,0:T(8,128)(2,1)}, u32[]{:S(2)}) copy-start(bf16[2,16,48]{2,1,0:T(8,128)(2,1)} %constant.29.clone.refs_9_) | copy-start | bytes 9220
  18.7 4.2 %copy-start.5 = (bf16[256,256]{1,0:T(8,128)(2,1)S(1)}, bf16[256,256]{1,0:T(8,128)(2,1)}, u32[]{:S(2)}) copy-start(bf16[256,256]{1,0:T(8,128)(2,1)} %constant.26.clone.refs_5_.refs_2_.refs_1_) | copy-start | bytes 393220
  19.3 11.3 %copy-start.12 = (bf16[2,16,48]{2,1,0:T(8,128)(2,1)S(1)}, bf16[2,16,48]{2,1,0:T(8,128)(2,1)}, u32[]{:S(2)}) copy-start(bf16[2,16,48]{2,1,0:T(8,128)(2,1)} %constant.30.clone.refs_14_) | copy-start | bytes 9220
  19.4 11.3 %collective-permute-start.3 = (f32[512,128]{1,0:T(8,128)S(1)}, f32[512,128]{1,0:T(8,128)S(1)}, u32[]{:S(2)}, u32[]{:S(2)}) collective-permute-start(f32[512,128]{1,0:T(8,128)S(1)} %early_1.1.refs_4_.refs_12_), channel_id=1, source_target_pairs={{1,2},{3,4},{5,6},{7,8},{9,10},{11,12},{13,14},{15,16},{17,18},{19... | collective-permute-start | bytes 786440 | tf_op jit(solution)/shard_map/ppermute | solution.py:659
  31.5 1.6 %collective-permute-start.4 = (f32[256,128]{1,0:T(8,128)S(1)}, f32[256,128]{1,0:T(8,128)S(1)}, u32[]{:S(2)}, u32[]{:S(2)}) collective-permute-start(f32[256,128]{1,0:T(8,128)S(1)} %get-tuple-element.65), channel_id=1, source_target_pairs={{0,1},{1,0},{2,3},{3,2},{4,5},{5,4},{6,7},{7,6},{8,9},{9,8},{10,11... | collective-permute-start | bytes 393224 | tf_op jit(solution)/shard_map/ppermute | solution.py:653
  34.1 1.6 %collective-permute-start.5 = (f32[256,128]{1,0:T(8,128)S(1)}, f32[256,128]{1,0:T(8,128)S(1)}, u32[]{:S(2)}, u32[]{:S(2)}) collective-permute-start(f32[256,128]{1,0:T(8,128)S(1)} %get-tuple-element.72), channel_id=1, source_target_pairs={{0,1},{1,0},{2,3},{3,2},{4,5},{5,4},{6,7},{7,6},{8,9},{9,8},{10,11... | collective-permute-start | bytes 393224 | tf_op jit(solution)/shard_map/ppermute | solution.py:653
  35.8 12.0 %collective-permute-start.6 = (f32[640,128]{1,0:T(8,128)S(1)}, f32[640,128]{1,0:T(8,128)S(1)}, u32[]{:S(2)}, u32[]{:S(2)}) collective-permute-start(f32[640,128]{1,0:T(8,128)S(1)} %early_3.1.refs_4_.refs_12_), channel_id=1, source_target_pairs={{1,2},{3,4},{5,6},{7,8},{9,10},{11,12},{13,14},{15,16},{17,18},{19... | collective-permute-start | bytes 983048 | tf_op jit(solution)/shard_map/ppermute | solution.py:659
  47.8 1.2 %copy-start.7 = (bf16[512,128]{1,0:T(8,128)(2,1)S(1)}, bf16[512,128]{1,0:T(8,128)(2,1)}, u32[]{:S(2)}) copy-start(bf16[512,128]{1,0:T(8,128)(2,1)} %constant.33.clone.refs_4_) | copy-start | bytes 393220
  47.8 1.2 %copy-start.8 = (bf16[2,72,256]{2,1,0:T(8,128)(2,1)S(1)}, bf16[2,72,256]{2,1,0:T(8,128)(2,1)}, u32[]{:S(2)}) copy-start(bf16[2,72,256]{2,1,0:T(8,128)(2,1)} %constant.38.clone.refs_2_) | copy-start | bytes 221188
  47.8 1.2 %copy-start.11 = (bf16[2,72,16]{2,1,0:T(8,128)(2,1)S(1)}, bf16[2,72,16]{2,1,0:T(8,128)(2,1)}, u32[]{:S(2)}) copy-start(bf16[2,72,16]{2,1,0:T(8,128)(2,1)} %constant.34.clone.refs_3_) | copy-start | bytes 13828
  49.7 6.2 %collective-permute-start.9 = (f32[72,512]{1,0:T(8,128)S(1)}, f32[72,512]{1,0:T(8,128)S(1)}, u32[]{:S(2)}, u32[]{:S(2)}) collective-permute-start(f32[72,512]{1,0:T(8,128)S(1)} %shrink.1.refs_0_), channel_id=1, source_target_pairs={{0,64},{64,0},{128,192},{192,128},{1,65},{65,1},{129,193},{193,129... | collective-permute-start | bytes 442376 | tf_op jit(solution)/shard_map/ppermute | solution.py:653
  51.5 6.4 %collective-permute-start.8 = (f32[72,512]{1,0:T(8,128)S(1)}, f32[72,512]{1,0:T(8,128)S(1)}, u32[]{:S(2)}, u32[]{:S(2)}) collective-permute-start(f32[72,512]{1,0:T(8,128)S(1)} %shrink.1.refs_0_), channel_id=1, source_target_pairs={{0,192},{64,128},{128,64},{192,0},{1,193},{65,129},{129,65},{193,1... | collective-permute-start | bytes 442376 | tf_op jit(solution)/shard_map/ppermute | solution.py:653
  53.6 6.6 %collective-permute-start.7 = (f32[72,512]{1,0:T(8,128)S(1)}, f32[72,512]{1,0:T(8,128)S(1)}, u32[]{:S(2)}, u32[]{:S(2)}) collective-permute-start(f32[72,512]{1,0:T(8,128)S(1)} %shrink.1.refs_0_), channel_id=1, source_target_pairs={{0,128},{64,192},{128,0},{192,64},{1,129},{65,193},{129,1},{193,65... | collective-permute-start | bytes 442376 | tf_op jit(solution)/shard_map/ppermute | solution.py:653
  54.4 1.3 %collective-permute-start.10 = (f32[128,128]{1,0:T(8,128)S(1)}, f32[128,128]{1,0:T(8,128)S(1)}, u32[]{:S(2)}, u32[]{:S(2)}) collective-permute-start(f32[128,128]{1,0:T(8,128)S(1)} %get-tuple-element.82), channel_id=1, source_target_pairs={{0,1},{1,0},{2,3},{3,2},{4,5},{5,4},{6,7},{7,6},{8,9},{9,8},{10,11... | collective-permute-start | bytes 196616 | tf_op jit(solution)/shard_map/ppermute | solution.py:653
  60.3 5.2 %collective-permute-start.11 = (f32[72,512]{1,0:T(8,128)S(1)}, f32[72,512]{1,0:T(8,128)S(1)}, u32[]{:S(2)}, u32[]{:S(2)}) collective-permute-start(f32[72,512]{1,0:T(8,128)S(1)} %add_four.1.refs_0_), channel_id=1, source_target_pairs={{0,32},{32,0},{1,33},{33,1},{2,34},{34,2},{3,35},{35,3},{4,36},{36... | collective-permute-start | bytes 442376 | tf_op jit(solution)/shard_map/ppermute | solution.py:653
  65.6 1.3 %collective-permute-start.12 = (f32[24,128]{1,0:T(8,128)S(1)}, f32[24,128]{1,0:T(8,128)S(1)}, u32[]{:S(2)}, u32[]{:S(2)}) collective-permute-start(f32[24,128]{1,0:T(8,128)S(1)} %get-tuple-element.88.refs_1_), channel_id=1, source_target_pairs={{0,1},{1,0},{2,3},{3,2},{4,5},{5,4},{6,7},{7,6},{8,9},{9,8},{10,11... | collective-permute-start | bytes 36872 | tf_op jit(solution)/shard_map/ppermute | solution.py:653
  66.9 0.9 %copy-start.6 = (bf16[2,128,144]{2,1,0:T(8,128)(2,1)S(1)}, bf16[2,128,144]{2,1,0:T(8,128)(2,1)}, u32[]{:S(2)}) copy-start(bf16[2,128,144]{2,1,0:T(8,128)(2,1)} %constant.37.clone.refs_5_) | copy-start | bytes 221188
  66.9 5.2 %collective-permute-start.13 = (f32[8,128]{1,0:T(8,128)S(1)}, f32[8,128]{1,0:T(8,128)S(1)}, u32[]{:S(2)}, u32[]{:S(2)}) collective-permute-start(f32[8,128]{1,0:T(8,128)S(1)} %get-tuple-element.89.refs_0_), channel_id=1, source_target_pairs={{0,16},{16,0},{1,17},{17,1},{2,18},{18,2},{3,19},{19,3},{4,20},{20... | collective-permute-start | bytes 12296 | tf_op jit(solution)/shard_map/ppermute | solution.py:653

commit v9 on v8

--- a/solution.py
+++ b/solution.py
@@ -195,38 +195,40 @@
         near[start : start + OV] = v[y, pl.ds(row, OV), :]
 
 
-def first_edge(far_side, p, q, coef, out, p_rows, q_rows, c_rows, sems):
-    core = lax.axis_index("core")
-    end = core if far_side else 1 - core
+def first_edges(p, q, coef, far, near, *scratch):
+    core = lax.axis_index("core")
+    sems = scratch[6]
     block = OV * CY
-    copies = [
-        pltpu.make_async_copy(source.at[pl.ds(pl.multiple_of(start, 8), size)], target, sems.at[k])
-        for k, (source, start, size, target) in enumerate(
-            (
-                (p, end * (CX * CY - block), block, p_rows),
-                (q, end * (CX * CY - block), block, q_rows),
-                (coef, end * (CXC - 8), 8, c_rows),
+    ends, copies = (core, 1 - core), []
+    for side, end in enumerate(ends):
+        for k, (source, whole, size) in enumerate(
+            ((p, CX * CY, block), (q, CX * CY, block), (coef, CXC, 8))
+        ):
+            start = pl.multiple_of(end * (whole - size), 8)
+            at = 3 * side + k
+            copies.append(
+                pltpu.make_async_copy(source.at[pl.ds(start, size)], scratch[at], sems.at[at])
             )
-        )
-    ]
     for copy in copies:
         copy.start()
-    for field, rows in enumerate((p_rows, q_rows)):
-        copies[field].wait()
-        for y in range(CY):
-            start = (field * CY + y) * OV
-            out[start : start + OV] = rows[pl.ds(y, OV, stride=CY), :]
-    copies[2].wait()
-    base = 2 * CY * OV
-    count = 6 if far_side else 2
-    for row in range(count):
-        for part in range(4):
-            lanes = slice(part * 128, part * 128 + 128)
-            spot = base + row * 4 + part
-            last = 8 - count + row
-            out[spot : spot + 1] = jnp.where(
-                end == 0, c_rows[row : row + 1, lanes], c_rows[last : last + 1, lanes]
-            )
+    for side, (end, out, count) in enumerate(zip(ends, (far, near), (6, 2))):
+        for field in range(2):
+            copies[3 * side + field].wait()
+            rows = scratch[3 * side + field]
+            for y in range(CY):
+                start = (field * CY + y) * OV
+                out[start : start + OV] = rows[pl.ds(y, OV, stride=CY), :]
+        copies[3 * side + 2].wait()
+        rows = scratch[3 * side + 2]
+        base = 2 * CY * OV
+        for row in range(count):
+            for part in range(4):
+                lanes = slice(part * 128, part * 128 + 128)
+                spot = base + row * 4 + part
+                last = 8 - count + row
+                out[spot : spot + 1] = jnp.where(
+                    end == 0, rows[row : row + 1, lanes], rows[last : last + 1, lanes]
+                )
 
 
 def reorder(source, target):
@@ -572,7 +574,7 @@
             base[y] = 2.0 * p[y] - p_before[y] + source[y] * weight
 
 
-def add_four(own, two, three, one, out):
+def add_four(own, one, two, three, out):
     out[...] = (own[...] + one[...]) + (two[...] + three[...])
 
 
@@ -610,7 +612,7 @@
         rows = slice(c * size, c * size + size)
         held[rows] = zeroth[rows] + rate * (first[rows] + rate * second[rows])
         copies.append(pltpu.make_async_copy(held.at[rows], p_last.at[rows], sems.at[c]))
-        copies[-1].start()
+        copies[-1].start(priority=c % 2)
     direction[...] = total[:CXC] * inverse
     for copy in copies:
         copy.wait()
@@ -668,21 +670,14 @@
     half, edge = rows_of(CY * OV), rows_of(2 * CY * OV)
     sources = [pltpu.with_memory_space_constraint(a, pltpu.HBM) for a in (p_now, adj_now, coef_old)]
 
-    def first(far_side, *held):
-        return call(
-            functools.partial(first_edge, far_side),
-            rows_of(2 * CY * OV + (24 if far_side else 8)),
-            *sources,
-            in_specs=[pl.BlockSpec(memory_space=pltpu.HBM)] * 3,
-            scratch=[pltpu.VMEM((OV * CY, CZ), F32)] * 2
-            + [pltpu.VMEM((8, CYC * CZC), F32), pltpu.SemaphoreType.DMA((3,))],
-            name="far_edge" if far_side else "near_edge",
-            held=held,
-        )
-
-    far = first(True)
-    near = xor_swap(first(False, far), "core", 1)
-    far = far_swap(far)
+    blocks = [pltpu.VMEM((OV * CY, CZ), F32)] * 2 + [pltpu.VMEM((8, CYC * CZC), F32)]
+    far, near = call(
+        first_edges, (rows_of(2 * CY * OV + 24), rows_of(2 * CY * OV + 8)), *sources,
+        in_specs=[pl.BlockSpec(memory_space=pltpu.HBM)] * 3,
+        scratch=blocks * 2 + [pltpu.SemaphoreType.DMA((6,))],
+        name="first_edges",
+    )
+    far, near = far_swap(far), xor_swap(near, "core", 1)
 
     wide = jax.ShapeDtypeStruct((CY, CX + OV, CZ), F32)
     later = [own_x, own_z, p_prev, adj_next, coef_old, const["grow_own"]]
@@ -771,7 +766,7 @@
     )
     held = (lap_p, base)
     partial = call(
-        add_four, rows_of(ROWS, CYC * CZC), partial, two, three, one, name="add_four", held=held
+        add_four, rows_of(ROWS, CYC * CZC), partial, one, two, three, name="add_four", held=held
     )
     total, mine = call(
         squares, (rows_of(ROWS, CYC * CZC), rows_of(24)), partial, xor_swap(partial, "xl", 1),

time: 84.8 us -> 83.2 us (0.981)
  waiting for transfers between devices: 27.8 us -> 25.6 us
  starting transfers between devices: 21.6 us -> 22.9 us
    ppermute x3, waiting for transfers between devices: 13.2 us -> 11.3 us  [far_swap(): return lax.ppermute(x, TILE, pairs + [(b, a) for a, b in pairs])]
    ppermute x3, starting transfers between devices: 15.3 us -> 17.1 us  [far_swap(): return lax.ppermute(x, TILE, pairs + [(b, a) for a, b in pairs])]
    pallas_call x24 -> x23, Pallas kernels: 22.6 us -> 21.9 us  [call(): pl.pallas_call(run, out_shape=outs, in_specs=([SM] * smem + [VM] * (count...]
  transfers between devices with their start and end apart: 14 -> 14, of which waited for: 10 -> 10; matrix products, arithmetic and copies ran while one was open for 0% -> 0% of each run, Pallas kernels for 17% -> 16%
where the time goes in v9:
time: 83.2 us; the launch traced here: 82.9 us
  waiting for transfers between devices  25.6 us (31%)
  starting transfers between devices  22.9 us (28%)
  Pallas kernels  21.9 us (26%)
  blocking collectives  10.4 us (12%)
  between operations  1.21 us (1%)
  local copies, waits for them, and re-layouts  0.86 us (1%)
    pallas_call x23, Pallas kernels, call(): pl.pallas_call(run, out_shape=outs, in_specs=([SM] * smem + [VM] * (count...  21.9 us
    ppermute x3, starting transfers between devices, far_swap(): return lax.ppermute(x, TILE, pairs + [(b, a) for a, b in pairs])  17.1 us
    ppermute x11, waiting for transfers between devices, xor_swap(): return lax.ppermute(x, axis, [(i, i ^ mask) for i in range(count)])  14.3 us
    ppermute x3, waiting for transfers between devices, far_swap(): return lax.ppermute(x, TILE, pairs + [(b, a) for a, b in pairs])  11.3 us
    all_to_all x1, blocking collectives, on_device(): parts = lax.all_to_all(copies, 'z', split_axis=0, concat_axis=0, tiled=True)  10.4 us
    ppermute x11, starting transfers between devices, xor_swap(): return lax.ppermute(x, axis, [(i, i ^ mask) for i in range(count)])  5.77 us
  transfers between devices with their start and end apart: 14, of which 10 were waited for; matrix products, arithmetic and copies ran while one was open for 0% of the time, Pallas kernels for 16%

profile of v9, /device:TPU:6, one launch (start us, length us, event | category | flops | bytes accessed | tf_op | source)
XLA Modules:
  0.0 82.9 jit_solution(7480070872660126312)
XLA Ops:
  0.7 1.2 %first_edges.1 = (f32[280,128]{1,0:T(8,128)S(1)}, f32[264,128]{1,0:T(8,128)S(1)}) custom-call(f32[2048,128]{1,0:T(8,128)} %bitcast.6, f32[2048,128]{1,0:T(8,128)} %bitcast.8, f32[64,512]{1,0:T(8,128)} %refs_9_.3), custom_call_target="tpu_custom_call" | custom-call | bytes 2228224 | tf_op jit(solution)/shard_map/first_edges/pallas_call | solution.py:638
  1.9 8.0 %collective-permute-start.1 = (f32[280,128]{1,0:T(8,128)S(1)}, f32[280,128]{1,0:T(8,128)S(1)}, u32[]{:S(2)}, u32[]{:S(2)}) collective-permute-start(f32[280,128]{1,0:T(8,128)S(1)} %get-tuple-element.52), channel_id=1, source_target_pairs={{1,2},{3,4},{5,6},{7,8},{9,10},{11,12},{13,14},{15,16},{17,18},{19... | collective-permute-start | bytes 430088 | tf_op jit(solution)/shard_map/ppermute | solution.py:661
  10.1 5.3 %prepare.1 = (f32[16,128,128]{2,1,0:T(8,128)S(1)}, f32[16,128,128]{2,1,0:T(8,128)S(1)}, f32[16,128,128]{2,1,0:T(8,128)S(1)}, f32[16,128,128]{2,1,0:T(8,128)S(1)}...) custom-call(s32[64]{0:T(128)S(1)} %bitcast.10, ...), custom_call_target="tpu_custom_call" | custom-call | flops 1000000000 | bytes 4788756 | tf_op jit(solution)/shard_map/prepare/pallas_call | solution.py:638
  15.9 0.8 advance_0.1
  16.7 0.5 collective-permute-start.2
  17.3 0.5 edge_inside_0.1.refs_5_
  18.5 4.4 %collective-permute-start.3 = (f32[512,128]{1,0:T(8,128)S(1)}, f32[512,128]{1,0:T(8,128)S(1)}, u32[]{:S(2)}, u32[]{:S(2)}) collective-permute-start(f32[512,128]{1,0:T(8,128)S(1)} %early_1.1.refs_4_.refs_12_), channel_id=1, source_target_pairs={{1,2},{3,4},{5,6},{7,8},{9,10},{11,12},{13,14},{15,16},{17,18},{19... | collective-permute-start | bytes 786440 | tf_op jit(solution)/shard_map/ppermute | solution.py:661
  22.9 1.5 %inside_0.1 = (f32[16,128,128]{2,1,0:T(8,128)S(1)}, f32[16,128,128]{2,1,0:T(8,128)S(1)}) custom-call(f32[16,128,128]{2,1,0:T(8,128)S(1)} %get-tuple-element.64.refs_0_.refs_1_.refs_2_.refs_3_, f32[16,128,128]{2,1,0:T(8,128)S(1)} %get-tuple-element.65.refs_1_.refs_3_.refs_4_.refs_5_.refs_10_.refs_16_, bf16[256,256]{1,0:T(8,128)(2,1)S(1)} %copy-done.5, ...), custom_call_target="tpu_custom_call" | custom-call | flops 1000000000 | bytes 2359296 | tf_op jit(solution)/shard_map/inside_0/pallas_call | solution.py:638
  24.4 5.4 %collective-permute-done.3.refs_1_.refs_19_ = f32[512,128]{1,0:T(8,128)S(1)} collective-permute-done((f32[512,128]{1,0:T(8,128)S(1)}, f32[512,128]{1,0:T(8,128)S(1)}, u32[]{:S(2)}, u32[]{:S(2)}) %collective-permute-start.3) | collective-permute-done | bytes 262176 | tf_op jit(solution)/shard_map/ppermute | solution.py:661
  29.8 0.9 %advance_1.1 = (f32[16,128,128]{2,1,0:T(8,128)S(1)}, f32[16,128,128]{2,1,0:T(8,128)S(1)}, f32[256,128]{1,0:T(8,128)S(1)}, f32[256,128]{1,0:T(8,128)S(1)}, f32[16,128,128]{2,1,0:T(8,128)S(1)}) custom-call(f32[256,128]{1,0:T(8,128)S(1)} %collective-permute-done.2.refs_0_, f32[512,128]{1,0:T(8,128)S(1)} %collective-permute-done.3.refs_1_.refs_19_, ...), custom_call_target="tpu_custom_call" | custom-call | flops 100000000 | bytes 9157632 | tf_op jit(solution)/shard_map/advance_1/pallas_call | solution.py:638
  30.8 1.5 %inside_1.1 = (f32[16,128,128]{2,1,0:T(8,128)S(1)}, f32[16,128,128]{2,1,0:T(8,128)S(1)}) custom-call(f32[16,128,128]{2,1,0:T(8,128)S(1)} %get-tuple-element.71.refs_0_.refs_2_.refs_3_, f32[16,128,128]{2,1,0:T(8,128)S(1)} %get-tuple-element.72.refs_1_.refs_4_.refs_5_, bf16[256,256]{1,0:T(8,128)(2,1)S(1)} %copy-done.5, bf16[256,256]{1,0:T(8,128)(2,1)S(1)} %copy-done.3), custom_call_target="tpu_custom_call" | custom-call | flops 1000000000 | bytes 2359296 | tf_op jit(solution)/shard_map/inside_1/pallas_call | solution.py:638
  32.3 0.9 %advance_2.1 = (f32[16,128,128]{2,1,0:T(8,128)S(1)}, f32[16,128,128]{2,1,0:T(8,128)S(1)}, f32[256,128]{1,0:T(8,128)S(1)}, f32[16,128,128]{2,1,0:T(8,128)S(1)}) custom-call(f32[256,128]{1,0:T(8,128)S(1)} %collective-permute-done.4.refs_0_, f32[256,128]{1,0:T(8,128)S(1)} %get-tuple-element.70.refs_1_, ...), custom_call_target="tpu_custom_call" | custom-call | flops 100000000 | bytes 9744384 | tf_op jit(solution)/shard_map/advance_2/pallas_call | solution.py:638
  33.2 0.6 collective-permute-start.5
  33.8 0.5 edge_inside_2.1.refs_5_
  34.3 0.5 collective-permute-done.5.refs_0_
  35.0 4.6 %collective-permute-start.6 = (f32[640,128]{1,0:T(8,128)S(1)}, f32[640,128]{1,0:T(8,128)S(1)}, u32[]{:S(2)}, u32[]{:S(2)}) collective-permute-start(f32[640,128]{1,0:T(8,128)S(1)} %early_3.1.refs_4_.refs_12_), channel_id=1, source_target_pairs={{1,2},{3,4},{5,6},{7,8},{9,10},{11,12},{13,14},{15,16},{17,18},{19... | collective-permute-start | bytes 983048 | tf_op jit(solution)/shard_map/ppermute | solution.py:661
  39.6 1.5 %inside_2.1 = (f32[16,128,128]{2,1,0:T(8,128)S(1)}, f32[16,128,128]{2,1,0:T(8,128)S(1)}) custom-call(f32[16,128,128]{2,1,0:T(8,128)S(1)} %get-tuple-element.77.refs_0_.refs_1_.refs_2_.refs_3_, f32[16,128,128]{2,1,0:T(8,128)S(1)} %get-tuple-element.78.refs_1_.refs_3_.refs_4_, bf16[256,256]{1,0:T(8,128)(2,1)S(1)} %copy-done.5, bf16[256,256]{1,0:T(8,128)(2,1)S(1)} %copy-done.3, ...), custom_call_target="tpu_custom_call" | custom-call | flops 1000000000 | bytes 2359296 | tf_op jit(solution)/shard_map/inside_2/pallas_call | solution.py:638
  41.1 6.0 %collective-permute-done.6.refs_1_ = f32[640,128]{1,0:T(8,128)S(1)} collective-permute-done((f32[640,128]{1,0:T(8,128)S(1)}, f32[640,128]{1,0:T(8,128)S(1)}, u32[]{:S(2)}, u32[]{:S(2)}) %collective-permute-start.6) | collective-permute-done | bytes 327712 | tf_op jit(solution)/shard_map/ppermute | solution.py:661
  47.1 1.2 %advance_3.1 = (f32[16,128,128]{2,1,0:T(8,128)S(1)}, f32[128,128]{1,0:T(8,128)S(1)}, f32[128,128]{1,0:T(8,128)S(1)}, f32[16,128,128]{2,1,0:T(8,128)S(1)}, f32[128,128]{1,0:T(8,128)S(1)}) custom-call(f32[256,128]{1,0:T(8,128)S(1)} %collective-permute-done.5.refs_0_, f32[640,128]{1,0:T(8,128)S(1)} %collective-permute-done.6.refs_1_, ...), custom_call_target="tpu_custom_call" | custom-call | flops 100000000 | bytes 13745152 | tf_op jit(solution)/shard_map/advance_3/pallas_call | solution.py:638
  48.3 0.6 shrink.1.refs_0_
  48.9 3.1 %collective-permute-start.9 = (f32[72,512]{1,0:T(8,128)S(1)}, f32[72,512]{1,0:T(8,128)S(1)}, u32[]{:S(2)}, u32[]{:S(2)}) collective-permute-start(f32[72,512]{1,0:T(8,128)S(1)} %shrink.1.refs_0_), channel_id=1, source_target_pairs={{0,192},{64,128},{128,64},{192,0},{1,193},{65,129},{129,65},{193,1... | collective-permute-start | bytes 442376 | tf_op jit(solution)/shard_map/ppermute | solution.py:655
  52.1 0.6 collective-permute-start.8
  53.1 0.8 inside_last.1.refs_4_
  54.7 1.6 %collective-permute-done.9.refs_3_ = f32[72,512]{1,0:T(8,128)S(1)} collective-permute-done((f32[72,512]{1,0:T(8,128)S(1)}, f32[72,512]{1,0:T(8,128)S(1)}, u32[]{:S(2)}, u32[]{:S(2)}) %collective-permute-start.9) | collective-permute-done | bytes 147488 | tf_op jit(solution)/shard_map/ppermute | solution.py:655
  56.4 2.4 %collective-permute-done.8.refs_2_ = f32[72,512]{1,0:T(8,128)S(1)} collective-permute-done((f32[72,512]{1,0:T(8,128)S(1)}, f32[72,512]{1,0:T(8,128)S(1)}, u32[]{:S(2)}, u32[]{:S(2)}) %collective-permute-start.8) | collective-permute-done | bytes 147488 | tf_op jit(solution)/shard_map/ppermute | solution.py:655
  58.9 5.1 %collective-permute-done.11.refs_1_ = f32[72,512]{1,0:T(8,128)S(1)} collective-permute-done((f32[72,512]{1,0:T(8,128)S(1)}, f32[72,512]{1,0:T(8,128)S(1)}, u32[]{:S(2)}, u32[]{:S(2)}) %collective-permute-start.11) | collective-permute-done | bytes 147488 | tf_op jit(solution)/shard_map/ppermute | solution.py:655
  64.1 1.2 %collective-permute-done.12.refs_2_ = f32[24,128]{1,0:T(8,128)S(1)} collective-permute-done((f32[24,128]{1,0:T(8,128)S(1)}, f32[24,128]{1,0:T(8,128)S(1)}, u32[]{:S(2)}, u32[]{:S(2)}) %collective-permute-start.12) | collective-permute-done | bytes 12320 | tf_op jit(solution)/shard_map/ppermute | solution.py:655
  65.4 0.8 copy-done.6
  66.2 1.7 %spread.1 = (f32[2048,128]{1,0:T(8,128)S(1)}, f32[2048,128]{1,0:T(8,128)S(1)}, f32[2048,128]{1,0:T(8,128)S(1)}) custom-call(f32[72,512]{1,0:T(8,128)S(1)} %get-tuple-element.94.refs_0_.refs_1_, f32[16,128,128]{2,1,0:T(8,128)S(1)} %get-tuple-element.81.refs_13_.refs_18_.refs_1_, f32[16,128,128]{2,1,0:T(8,128)S(1)} %get-tuple-element.89.refs_4_.refs_2_.refs_3_, ...), custom_call_target="tpu_custom_call" | custom-call | flops 100000000 | bytes 3497984 | tf_op jit(solution)/shard_map/spread/pallas_call | solution.py:638
  67.9 2.6 %collective-permute-done.13.refs_1_ = f32[8,128]{1,0:T(8,128)S(1)} collective-permute-done((f32[8,128]{1,0:T(8,128)S(1)}, f32[8,128]{1,0:T(8,128)S(1)}, u32[]{:S(2)}, u32[]{:S(2)}) %collective-permute-start.13) | collective-permute-done | bytes 4128 | tf_op jit(solution)/shard_map/ppermute | solution.py:655
  70.5 10.4 %all_to_all.5.refs_0_ = f32[8,8,128]{2,1,0:T(8,128)S(1)} all-to-all(f32[8,8,128]{2,1,0:T(8,128)S(1)} %widen.1), channel_id=1, replica_groups=mesh['y'=4,'xl'=2,'xh'=2,'z'=8,'core'=2] {'z'}, dimensions={0} | all-to-all | bytes 65536 | tf_op jit(solution)/shard_map/all_to_all | solution.py:788
  80.9 1.8 %finish.1 = (f32[64,512]{1,0:T(8,128)}, f32[2048,128]{1,0:T(8,128)}) custom-call(f32[8,8,128]{2,1,0:T(8,128)S(1)} %all_to_all.5.refs_0_, f32[72,512]{1,0:T(8,128)S(1)} %get-tuple-element.94.refs_0_.refs_1_, f32[2048,128]{1,0:T(8,128)S(1)} %get-tuple-element.95.refs_2_, f32[2048,128]{1,0:T(8,128)S(1)} %get-tuple-element.96.refs_3_, ...), custom_call_target="tpu_custom_call" | custom-call | bytes 3325952 | tf_op jit(solution)/shard_map/finish/pallas_call | solution.py:638
  (54 shorter events, 3.2 us)
Async XLA Ops:
  0.6 9.4 %copy-start = (f32[1,128,16,128]{3,2,1,0:T(8,128)S(1)}, f32[1,128,16,128]{3,2,1,0:T(8,128)}, u32[]{:S(2)}) copy-start(f32[1,128,16,128]{3,2,1,0:T(8,128)} %param.21) | copy-start | bytes 3145732
  0.6 9.4 %copy-start.1 = (f32[1,128,16,128]{3,2,1,0:T(8,128)S(1)}, f32[1,128,16,128]{3,2,1,0:T(8,128)}, u32[]{:S(2)}) copy-start(f32[1,128,16,128]{3,2,1,0:T(8,128)} %param.23) | copy-start | bytes 3145732
  0.7 9.4 %copy-start.2 = (bf16[2,128,48]{2,1,0:T(8,128)(2,1)S(1)}, bf16[2,128,48]{2,1,0:T(8,128)(2,1)}, u32[]{:S(2)}) copy-start(bf16[2,128,48]{2,1,0:T(8,128)(2,1)} %constant.27.clone.refs_12_.refs_11_.refs_7_) | copy-start | bytes 73732
  0.7 9.4 %copy-start.14 = (s32[1,64]{1,0:T(1,128)S(1)}, s32[1,64]{1,0:T(1,128)}, u32[]{:S(2)}) copy-start(s32[1,64]{1,0:T(1,128)} %param.26) | copy-start | bytes 772
  0.7 9.4 %copy-start.15 = (s32[64]{0:T(128)S(1)}, s32[64]{0:T(128)}, u32[]{:S(2)}) copy-start(s32[64]{0:T(128)} %refs_1_.2) | copy-start | bytes 772
  0.7 9.4 %copy-start.16 = (f32[5]{0:T(128)S(1)}, f32[5]{0:T(128)}, u32[]{:S(2)}) copy-start(f32[5]{0:T(128)} %refs_2_.10) | copy-start | bytes 64
  1.9 13.5 %collective-permute-start.1 = (f32[280,128]{1,0:T(8,128)S(1)}, f32[280,128]{1,0:T(8,128)S(1)}, u32[]{:S(2)}, u32[]{:S(2)}) collective-permute-start(f32[280,128]{1,0:T(8,128)S(1)} %get-tuple-element.52), channel_id=1, source_target_pairs={{1,2},{3,4},{5,6},{7,8},{9,10},{11,12},{13,14},{15,16},{17,18},{19... | collective-permute-start | bytes 430088 | tf_op jit(solution)/shard_map/ppermute | solution.py:661
  9.9 5.5 %collective-permute-start = (f32[264,128]{1,0:T(8,128)S(1)}, f32[264,128]{1,0:T(8,128)S(1)}, u32[]{:S(2)}, u32[]{:S(2)}) collective-permute-start(f32[264,128]{1,0:T(8,128)S(1)} %get-tuple-element.51), channel_id=1, source_target_pairs={{0,1},{1,0},{2,3},{3,2},{4,5},{5,4},{6,7},{7,6},{8,9},{9,8},{10,11... | collective-permute-start | bytes 405512 | tf_op jit(solution)/shard_map/ppermute | solution.py:655
  10.1 5.3 %copy-start.4 = (bf16[256,256]{1,0:T(8,128)(2,1)S(1)}, bf16[256,256]{1,0:T(8,128)(2,1)}, u32[]{:S(2)}) copy-start(bf16[256,256]{1,0:T(8,128)(2,1)} %constant.32.clone.refs_11_.refs_3_.refs_4_) | copy-start | bytes 393220
  10.1 5.3 %copy-start.9 = (bf16[2,136,16]{2,1,0:T(8,128)(2,1)S(1)}, bf16[2,136,16]{2,1,0:T(8,128)(2,1)}, u32[]{:S(2)}) copy-start(bf16[2,136,16]{2,1,0:T(8,128)(2,1)} %constant.36.clone.refs_4_) | copy-start | bytes 26116
  15.9 1.4 %copy-start.3 = (bf16[256,256]{1,0:T(8,128)(2,1)S(1)}, bf16[256,256]{1,0:T(8,128)(2,1)}, u32[]{:S(2)}) copy-start(bf16[256,256]{1,0:T(8,128)(2,1)} %constant.31.clone.refs_6_.refs_3_.refs_2_) | copy-start | bytes 393220
  15.9 1.4 %copy-start.10 = (bf16[2,16,256]{2,1,0:T(8,128)(2,1)S(1)}, bf16[2,16,256]{2,1,0:T(8,128)(2,1)}, u32[]{:S(2)}) copy-start(bf16[2,16,256]{2,1,0:T(8,128)(2,1)} %constant.28.clone.refs_2_) | copy-start | bytes 49156
  16.7 1.5 %collective-permute-start.2 = (f32[256,128]{1,0:T(8,128)S(1)}, f32[256,128]{1,0:T(8,128)S(1)}, u32[]{:S(2)}, u32[]{:S(2)}) collective-permute-start(f32[256,128]{1,0:T(8,128)S(1)} %get-tuple-element.63), channel_id=1, source_target_pairs={{0,1},{1,0},{2,3},{3,2},{4,5},{5,4},{6,7},{7,6},{8,9},{9,8},{10,11... | collective-permute-start | bytes 393224 | tf_op jit(solution)/shard_map/ppermute | solution.py:655
  17.3 1.0 %copy-start.13 = (bf16[2,16,48]{2,1,0:T(8,128)(2,1)S(1)}, bf16[2,16,48]{2,1,0:T(8,128)(2,1)}, u32[]{:S(2)}) copy-start(bf16[2,16,48]{2,1,0:T(8,128)(2,1)} %constant.29.clone.refs_9_) | copy-start | bytes 9220
  17.8 5.1 %copy-start.5 = (bf16[256,256]{1,0:T(8,128)(2,1)S(1)}, bf16[256,256]{1,0:T(8,128)(2,1)}, u32[]{:S(2)}) copy-start(bf16[256,256]{1,0:T(8,128)(2,1)} %constant.26.clone.refs_5_.refs_2_.refs_1_) | copy-start | bytes 393220
  18.5 11.3 %copy-start.12 = (bf16[2,16,48]{2,1,0:T(8,128)(2,1)S(1)}, bf16[2,16,48]{2,1,0:T(8,128)(2,1)}, u32[]{:S(2)}) copy-start(bf16[2,16,48]{2,1,0:T(8,128)(2,1)} %constant.30.clone.refs_14_) | copy-start | bytes 9220
  18.5 11.3 %collective-permute-start.3 = (f32[512,128]{1,0:T(8,128)S(1)}, f32[512,128]{1,0:T(8,128)S(1)}, u32[]{:S(2)}, u32[]{:S(2)}) collective-permute-start(f32[512,128]{1,0:T(8,128)S(1)} %early_1.1.refs_4_.refs_12_), channel_id=1, source_target_pairs={{1,2},{3,4},{5,6},{7,8},{9,10},{11,12},{13,14},{15,16},{17,18},{19... | collective-permute-start | bytes 786440 | tf_op jit(solution)/shard_map/ppermute | solution.py:661
  30.7 1.6 %collective-permute-start.4 = (f32[256,128]{1,0:T(8,128)S(1)}, f32[256,128]{1,0:T(8,128)S(1)}, u32[]{:S(2)}, u32[]{:S(2)}) collective-permute-start(f32[256,128]{1,0:T(8,128)S(1)} %get-tuple-element.69), channel_id=1, source_target_pairs={{0,1},{1,0},{2,3},{3,2},{4,5},{5,4},{6,7},{7,6},{8,9},{9,8},{10,11... | collective-permute-start | bytes 393224 | tf_op jit(solution)/shard_map/ppermute | solution.py:655
  33.2 1.6 %collective-permute-start.5 = (f32[256,128]{1,0:T(8,128)S(1)}, f32[256,128]{1,0:T(8,128)S(1)}, u32[]{:S(2)}, u32[]{:S(2)}) collective-permute-start(f32[256,128]{1,0:T(8,128)S(1)} %get-tuple-element.76), channel_id=1, source_target_pairs={{0,1},{1,0},{2,3},{3,2},{4,5},{5,4},{6,7},{7,6},{8,9},{9,8},{10,11... | collective-permute-start | bytes 393224 | tf_op jit(solution)/shard_map/ppermute | solution.py:655
  35.0 12.1 %collective-permute-start.6 = (f32[640,128]{1,0:T(8,128)S(1)}, f32[640,128]{1,0:T(8,128)S(1)}, u32[]{:S(2)}, u32[]{:S(2)}) collective-permute-start(f32[640,128]{1,0:T(8,128)S(1)} %early_3.1.refs_4_.refs_12_), channel_id=1, source_target_pairs={{1,2},{3,4},{5,6},{7,8},{9,10},{11,12},{13,14},{15,16},{17,18},{19... | collective-permute-start | bytes 983048 | tf_op jit(solution)/shard_map/ppermute | solution.py:661
  47.0 1.2 %copy-start.7 = (bf16[512,128]{1,0:T(8,128)(2,1)S(1)}, bf16[512,128]{1,0:T(8,128)(2,1)}, u32[]{:S(2)}) copy-start(bf16[512,128]{1,0:T(8,128)(2,1)} %constant.33.clone.refs_4_) | copy-start | bytes 393220
  47.0 1.2 %copy-start.8 = (bf16[2,72,256]{2,1,0:T(8,128)(2,1)S(1)}, bf16[2,72,256]{2,1,0:T(8,128)(2,1)}, u32[]{:S(2)}) copy-start(bf16[2,72,256]{2,1,0:T(8,128)(2,1)} %constant.38.clone.refs_2_) | copy-start | bytes 221188
  47.1 1.2 %copy-start.11 = (bf16[2,72,16]{2,1,0:T(8,128)(2,1)S(1)}, bf16[2,72,16]{2,1,0:T(8,128)(2,1)}, u32[]{:S(2)}) copy-start(bf16[2,72,16]{2,1,0:T(8,128)(2,1)} %constant.34.clone.refs_3_) | copy-start | bytes 13828
  48.9 7.4 %collective-permute-start.9 = (f32[72,512]{1,0:T(8,128)S(1)}, f32[72,512]{1,0:T(8,128)S(1)}, u32[]{:S(2)}, u32[]{:S(2)}) collective-permute-start(f32[72,512]{1,0:T(8,128)S(1)} %shrink.1.refs_0_), channel_id=1, source_target_pairs={{0,192},{64,128},{128,64},{192,0},{1,193},{65,129},{129,65},{193,1... | collective-permute-start | bytes 442376 | tf_op jit(solution)/shard_map/ppermute | solution.py:655
  52.1 6.6 %collective-permute-start.8 = (f32[72,512]{1,0:T(8,128)S(1)}, f32[72,512]{1,0:T(8,128)S(1)}, u32[]{:S(2)}, u32[]{:S(2)}) collective-permute-start(f32[72,512]{1,0:T(8,128)S(1)} %shrink.1.refs_0_), channel_id=1, source_target_pairs={{0,128},{64,192},{128,0},{192,64},{1,129},{65,193},{129,1},{193,65... | collective-permute-start | bytes 442376 | tf_op jit(solution)/shard_map/ppermute | solution.py:655
  52.7 6.1 %collective-permute-start.7 = (f32[72,512]{1,0:T(8,128)S(1)}, f32[72,512]{1,0:T(8,128)S(1)}, u32[]{:S(2)}, u32[]{:S(2)}) collective-permute-start(f32[72,512]{1,0:T(8,128)S(1)} %shrink.1.refs_0_), channel_id=1, source_target_pairs={{0,64},{64,0},{128,192},{192,128},{1,65},{65,1},{129,193},{193,129... | collective-permute-start | bytes 442376 | tf_op jit(solution)/shard_map/ppermute | solution.py:655
  53.1 1.3 %collective-permute-start.10 = (f32[128,128]{1,0:T(8,128)S(1)}, f32[128,128]{1,0:T(8,128)S(1)}, u32[]{:S(2)}, u32[]{:S(2)}) collective-permute-start(f32[128,128]{1,0:T(8,128)S(1)} %get-tuple-element.86), channel_id=1, source_target_pairs={{0,1},{1,0},{2,3},{3,2},{4,5},{5,4},{6,7},{7,6},{8,9},{9,8},{10,11... | collective-permute-start | bytes 196616 | tf_op jit(solution)/shard_map/ppermute | solution.py:655
  58.8 5.2 %collective-permute-start.11 = (f32[72,512]{1,0:T(8,128)S(1)}, f32[72,512]{1,0:T(8,128)S(1)}, u32[]{:S(2)}, u32[]{:S(2)}) collective-permute-start(f32[72,512]{1,0:T(8,128)S(1)} %add_four.1.refs_0_), channel_id=1, source_target_pairs={{0,32},{32,0},{1,33},{33,1},{2,34},{34,2},{3,35},{35,3},{4,36},{36... | collective-permute-start | bytes 442376 | tf_op jit(solution)/shard_map/ppermute | solution.py:655
  64.0 1.3 %collective-permute-start.12 = (f32[24,128]{1,0:T(8,128)S(1)}, f32[24,128]{1,0:T(8,128)S(1)}, u32[]{:S(2)}, u32[]{:S(2)}) collective-permute-start(f32[24,128]{1,0:T(8,128)S(1)} %get-tuple-element.92.refs_1_), channel_id=1, source_target_pairs={{0,1},{1,0},{2,3},{3,2},{4,5},{5,4},{6,7},{7,6},{8,9},{9,8},{10,11... | collective-permute-start | bytes 36872 | tf_op jit(solution)/shard_map/ppermute | solution.py:655
  65.3 0.9 %copy-start.6 = (bf16[2,128,144]{2,1,0:T(8,128)(2,1)S(1)}, bf16[2,128,144]{2,1,0:T(8,128)(2,1)}, u32[]{:S(2)}) copy-start(bf16[2,128,144]{2,1,0:T(8,128)(2,1)} %constant.37.clone.refs_5_) | copy-start | bytes 221188
  65.3 5.2 %collective-permute-start.13 = (f32[8,128]{1,0:T(8,128)S(1)}, f32[8,128]{1,0:T(8,128)S(1)}, u32[]{:S(2)}, u32[]{:S(2)}) collective-permute-start(f32[8,128]{1,0:T(8,128)S(1)} %get-tuple-element.93.refs_0_), channel_id=1, source_target_pairs={{0,16},{16,0},{1,17},{17,1},{2,18},{18,2},{3,19},{19,3},{4,20},{20... | collective-permute-start | bytes 12296 | tf_op jit(solution)/shard_map/ppermute | solution.py:655

commit v10 on v9

--- a/solution.py
+++ b/solution.py
@@ -574,7 +574,7 @@
             base[y] = 2.0 * p[y] - p_before[y] + source[y] * weight
 
 
-def add_four(own, one, two, three, out):
+def add_four(own, one, three, two, out):
     out[...] = (own[...] + one[...]) + (two[...] + three[...])
 
 
@@ -594,16 +594,12 @@
 
 
 def widen(a, b, out):
-    value = a[...] + b[...]
-    for k in range(out.shape[0]):
-        out[k] = value
+    value = jnp.sum(a[...] + b[...], axis=0, keepdims=True)
+    out[...] = jnp.broadcast_to(value, out.shape)
 
 
 def finish(count, parts, total, zeroth, first, second, direction, p_last, held, sems):
-    value = parts[0]
-    for k in range(1, parts.shape[0]):
-        value = value + parts[k]
-    value = jnp.sum(jnp.sum(value, axis=0, keepdims=True), axis=1, keepdims=True)
+    value = jnp.sum(jnp.sum(parts[...], axis=0, keepdims=True), axis=1, keepdims=True)
     inverse = 1.0 / jnp.sqrt(value * (1.0 / count) + EPSILON)
     rate = LEARN * inverse
     size = CX * CY // sems.shape[0]
@@ -766,7 +762,7 @@
     )
     held = (lap_p, base)
     partial = call(
-        add_four, rows_of(ROWS, CYC * CZC), partial, one, two, three, name="add_four", held=held
+        add_four, rows_of(ROWS, CYC * CZC), partial, one, three, two, name="add_four", held=held
     )
     total, mine = call(
         squares, (rows_of(ROWS, CYC * CZC), rows_of(24)), partial, xor_swap(partial, "xl", 1),
@@ -782,7 +778,7 @@
     )
     deep = lax.axis_size("z")
     copies = call(
-        widen, jax.ShapeDtypeStruct((deep, 8, 128), F32),
+        widen, rows_of(deep),
         squared_sum, xor_swap(squared_sum, "xh", 1), name="widen", held=terms,
     )
     parts = lax.all_to_all(copies, "z", split_axis=0, concat_axis=0, tiled=True)

time: 83.2 us -> 83.1 us (level)
  no operation moved by 1% of the time
where the time goes in v10:
time: 83.1 us; the launch traced here: 82.5 us
  waiting for transfers between devices  25.4 us (31%)
  starting transfers between devices  23 us (28%)
  Pallas kernels  21.9 us (26%)
  blocking collectives  10 us (12%)
  between operations  1.21 us (1%)
  local copies, waits for them, and re-layouts  0.86 us (1%)
    pallas_call x23, Pallas kernels, call(): pl.pallas_call(run, out_shape=outs, in_specs=([SM] * smem + [VM] * (count...  21.9 us
    ppermute x3, starting transfers between devices, far_swap(): return lax.ppermute(x, TILE, pairs + [(b, a) for a, b in pairs])  17.1 us
    ppermute x11, waiting for transfers between devices, xor_swap(): return lax.ppermute(x, axis, [(i, i ^ mask) for i in range(count)])  14.1 us
    ppermute x3, waiting for transfers between devices, far_swap(): return lax.ppermute(x, TILE, pairs + [(b, a) for a, b in pairs])  11.3 us
    all_to_all x1, blocking collectives, on_device(): parts = lax.all_to_all(copies, 'z', split_axis=0, concat_axis=0, tiled=True)  10 us
    ppermute x11, starting transfers between devices, xor_swap(): return lax.ppermute(x, axis, [(i, i ^ mask) for i in range(count)])  5.91 us
  transfers between devices with their start and end apart: 14, of which 10 were waited for; matrix products, arithmetic and copies ran while one was open for 0% of the time, Pallas kernels for 16%

profile of v10, /device:TPU:6, one launch (start us, length us, event | category | flops | bytes accessed | tf_op | source)
XLA Modules:
  0.0 82.5 jit_solution(10222656262789878480)
XLA Ops:
  0.7 1.2 %first_edges.1 = (f32[280,128]{1,0:T(8,128)S(1)}, f32[264,128]{1,0:T(8,128)S(1)}) custom-call(f32[2048,128]{1,0:T(8,128)} %bitcast.10, f32[2048,128]{1,0:T(8,128)} %bitcast.12, f32[64,512]{1,0:T(8,128)} %refs_9_.3), custom_call_target="tpu_custom_call" | custom-call | bytes 2228224 | tf_op jit(solution)/shard_map/first_edges/pallas_call | solution.py:634
  1.9 8.0 %collective-permute-start.1 = (f32[280,128]{1,0:T(8,128)S(1)}, f32[280,128]{1,0:T(8,128)S(1)}, u32[]{:S(2)}, u32[]{:S(2)}) collective-permute-start(f32[280,128]{1,0:T(8,128)S(1)} %get-tuple-element.52), channel_id=1, source_target_pairs={{1,2},{3,4},{5,6},{7,8},{9,10},{11,12},{13,14},{15,16},{17,18},{19... | collective-permute-start | bytes 430088 | tf_op jit(solution)/shard_map/ppermute | solution.py:657
  10.1 5.3 %prepare.1 = (f32[16,128,128]{2,1,0:T(8,128)S(1)}, f32[16,128,128]{2,1,0:T(8,128)S(1)}, f32[16,128,128]{2,1,0:T(8,128)S(1)}, f32[16,128,128]{2,1,0:T(8,128)S(1)}...) custom-call(s32[64]{0:T(128)S(1)} %bitcast.16, ...), custom_call_target="tpu_custom_call" | custom-call | flops 1000000000 | bytes 4788756 | tf_op jit(solution)/shard_map/prepare/pallas_call | solution.py:634
  15.9 0.8 advance_0.1
  16.7 0.5 collective-permute-start.2
  17.3 0.5 edge_inside_0.1.refs_5_
  18.5 4.4 %collective-permute-start.3 = (f32[512,128]{1,0:T(8,128)S(1)}, f32[512,128]{1,0:T(8,128)S(1)}, u32[]{:S(2)}, u32[]{:S(2)}) collective-permute-start(f32[512,128]{1,0:T(8,128)S(1)} %early_1.1.refs_4_.refs_12_), channel_id=1, source_target_pairs={{1,2},{3,4},{5,6},{7,8},{9,10},{11,12},{13,14},{15,16},{17,18},{19... | collective-permute-start | bytes 786440 | tf_op jit(solution)/shard_map/ppermute | solution.py:657
  22.9 1.5 %inside_0.1 = (f32[16,128,128]{2,1,0:T(8,128)S(1)}, f32[16,128,128]{2,1,0:T(8,128)S(1)}) custom-call(f32[16,128,128]{2,1,0:T(8,128)S(1)} %get-tuple-element.64.refs_0_.refs_1_.refs_2_.refs_3_, f32[16,128,128]{2,1,0:T(8,128)S(1)} %get-tuple-element.65.refs_1_.refs_3_.refs_4_.refs_5_.refs_10_.refs_16_, bf16[256,256]{1,0:T(8,128)(2,1)S(1)} %copy-done.5, ...), custom_call_target="tpu_custom_call" | custom-call | flops 1000000000 | bytes 2359296 | tf_op jit(solution)/shard_map/inside_0/pallas_call | solution.py:634
  24.4 5.4 %collective-permute-done.3.refs_1_.refs_19_ = f32[512,128]{1,0:T(8,128)S(1)} collective-permute-done((f32[512,128]{1,0:T(8,128)S(1)}, f32[512,128]{1,0:T(8,128)S(1)}, u32[]{:S(2)}, u32[]{:S(2)}) %collective-permute-start.3) | collective-permute-done | bytes 262176 | tf_op jit(solution)/shard_map/ppermute | solution.py:657
  29.8 0.9 %advance_1.1 = (f32[16,128,128]{2,1,0:T(8,128)S(1)}, f32[16,128,128]{2,1,0:T(8,128)S(1)}, f32[256,128]{1,0:T(8,128)S(1)}, f32[256,128]{1,0:T(8,128)S(1)}, f32[16,128,128]{2,1,0:T(8,128)S(1)}) custom-call(f32[256,128]{1,0:T(8,128)S(1)} %collective-permute-done.2.refs_0_, f32[512,128]{1,0:T(8,128)S(1)} %collective-permute-done.3.refs_1_.refs_19_, ...), custom_call_target="tpu_custom_call" | custom-call | flops 100000000 | bytes 9157632 | tf_op jit(solution)/shard_map/advance_1/pallas_call | solution.py:634
  30.8 1.5 %inside_1.1 = (f32[16,128,128]{2,1,0:T(8,128)S(1)}, f32[16,128,128]{2,1,0:T(8,128)S(1)}) custom-call(f32[16,128,128]{2,1,0:T(8,128)S(1)} %get-tuple-element.71.refs_0_.refs_2_.refs_3_, f32[16,128,128]{2,1,0:T(8,128)S(1)} %get-tuple-element.72.refs_1_.refs_4_.refs_5_, bf16[256,256]{1,0:T(8,128)(2,1)S(1)} %copy-done.5, bf16[256,256]{1,0:T(8,128)(2,1)S(1)} %copy-done.3), custom_call_target="tpu_custom_call" | custom-call | flops 1000000000 | bytes 2359296 | tf_op jit(solution)/shard_map/inside_1/pallas_call | solution.py:634
  32.3 0.9 %advance_2.1 = (f32[16,128,128]{2,1,0:T(8,128)S(1)}, f32[16,128,128]{2,1,0:T(8,128)S(1)}, f32[256,128]{1,0:T(8,128)S(1)}, f32[16,128,128]{2,1,0:T(8,128)S(1)}) custom-call(f32[256,128]{1,0:T(8,128)S(1)} %collective-permute-done.4.refs_0_, f32[256,128]{1,0:T(8,128)S(1)} %get-tuple-element.70.refs_1_, ...), custom_call_target="tpu_custom_call" | custom-call | flops 100000000 | bytes 9744384 | tf_op jit(solution)/shard_map/advance_2/pallas_call | solution.py:634
  33.2 0.6 collective-permute-start.5
  33.8 0.5 edge_inside_2.1.refs_5_
  34.3 0.5 collective-permute-done.5.refs_0_
  35.0 4.6 %collective-permute-start.6 = (f32[640,128]{1,0:T(8,128)S(1)}, f32[640,128]{1,0:T(8,128)S(1)}, u32[]{:S(2)}, u32[]{:S(2)}) collective-permute-start(f32[640,128]{1,0:T(8,128)S(1)} %early_3.1.refs_4_.refs_12_), channel_id=1, source_target_pairs={{1,2},{3,4},{5,6},{7,8},{9,10},{11,12},{13,14},{15,16},{17,18},{19... | collective-permute-start | bytes 983048 | tf_op jit(solution)/shard_map/ppermute | solution.py:657
  39.6 1.5 %inside_2.1 = (f32[16,128,128]{2,1,0:T(8,128)S(1)}, f32[16,128,128]{2,1,0:T(8,128)S(1)}) custom-call(f32[16,128,128]{2,1,0:T(8,128)S(1)} %get-tuple-element.77.refs_0_.refs_1_.refs_2_.refs_3_, f32[16,128,128]{2,1,0:T(8,128)S(1)} %get-tuple-element.78.refs_1_.refs_3_.refs_4_, bf16[256,256]{1,0:T(8,128)(2,1)S(1)} %copy-done.5, bf16[256,256]{1,0:T(8,128)(2,1)S(1)} %copy-done.3, ...), custom_call_target="tpu_custom_call" | custom-call | flops 1000000000 | bytes 2359296 | tf_op jit(solution)/shard_map/inside_2/pallas_call | solution.py:634
  41.1 5.9 %collective-permute-done.6.refs_1_ = f32[640,128]{1,0:T(8,128)S(1)} collective-permute-done((f32[640,128]{1,0:T(8,128)S(1)}, f32[640,128]{1,0:T(8,128)S(1)}, u32[]{:S(2)}, u32[]{:S(2)}) %collective-permute-start.6) | collective-permute-done | bytes 327712 | tf_op jit(solution)/shard_map/ppermute | solution.py:657
  47.0 1.2 %advance_3.1 = (f32[16,128,128]{2,1,0:T(8,128)S(1)}, f32[128,128]{1,0:T(8,128)S(1)}, f32[128,128]{1,0:T(8,128)S(1)}, f32[16,128,128]{2,1,0:T(8,128)S(1)}, f32[128,128]{1,0:T(8,128)S(1)}) custom-call(f32[256,128]{1,0:T(8,128)S(1)} %collective-permute-done.5.refs_0_, f32[640,128]{1,0:T(8,128)S(1)} %collective-permute-done.6.refs_1_, ...), custom_call_target="tpu_custom_call" | custom-call | flops 100000000 | bytes 13745152 | tf_op jit(solution)/shard_map/advance_3/pallas_call | solution.py:634
  48.3 0.6 shrink.1.refs_0_
  48.9 3.2 %collective-permute-start.9 = (f32[72,512]{1,0:T(8,128)S(1)}, f32[72,512]{1,0:T(8,128)S(1)}, u32[]{:S(2)}, u32[]{:S(2)}) collective-permute-start(f32[72,512]{1,0:T(8,128)S(1)} %shrink.1.refs_0_), channel_id=1, source_target_pairs={{0,128},{64,192},{128,0},{192,64},{1,129},{65,193},{129,1},{193,65... | collective-permute-start | bytes 442376 | tf_op jit(solution)/shard_map/ppermute | solution.py:651
  52.2 1.1 %collective-permute-start.8 = (f32[72,512]{1,0:T(8,128)S(1)}, f32[72,512]{1,0:T(8,128)S(1)}, u32[]{:S(2)}, u32[]{:S(2)}) collective-permute-start(f32[72,512]{1,0:T(8,128)S(1)} %shrink.1.refs_0_), channel_id=1, source_target_pairs={{0,192},{64,128},{128,64},{192,0},{1,193},{65,129},{129,65},{193,1... | collective-permute-start | bytes 442376 | tf_op jit(solution)/shard_map/ppermute | solution.py:651
  53.2 0.8 inside_last.1.refs_4_
  54.8 2.2 %collective-permute-done.9.refs_3_ = f32[72,512]{1,0:T(8,128)S(1)} collective-permute-done((f32[72,512]{1,0:T(8,128)S(1)}, f32[72,512]{1,0:T(8,128)S(1)}, u32[]{:S(2)}, u32[]{:S(2)}) %collective-permute-start.9) | collective-permute-done | bytes 147488 | tf_op jit(solution)/shard_map/ppermute | solution.py:651
  57.1 1.6 %collective-permute-done.8.refs_2_ = f32[72,512]{1,0:T(8,128)S(1)} collective-permute-done((f32[72,512]{1,0:T(8,128)S(1)}, f32[72,512]{1,0:T(8,128)S(1)}, u32[]{:S(2)}, u32[]{:S(2)}) %collective-permute-start.8) | collective-permute-done | bytes 147488 | tf_op jit(solution)/shard_map/ppermute | solution.py:651
  58.8 5.1 %collective-permute-done.11.refs_1_ = f32[72,512]{1,0:T(8,128)S(1)} collective-permute-done((f32[72,512]{1,0:T(8,128)S(1)}, f32[72,512]{1,0:T(8,128)S(1)}, u32[]{:S(2)}, u32[]{:S(2)}) %collective-permute-start.11) | collective-permute-done | bytes 147488 | tf_op jit(solution)/shard_map/ppermute | solution.py:651
  64.1 1.2 %collective-permute-done.12.refs_2_ = f32[24,128]{1,0:T(8,128)S(1)} collective-permute-done((f32[24,128]{1,0:T(8,128)S(1)}, f32[24,128]{1,0:T(8,128)S(1)}, u32[]{:S(2)}, u32[]{:S(2)}) %collective-permute-start.12) | collective-permute-done | bytes 12320 | tf_op jit(solution)/shard_map/ppermute | solution.py:651
  65.4 0.8 copy-done.6
  66.1 1.7 %spread.1 = (f32[2048,128]{1,0:T(8,128)S(1)}, f32[2048,128]{1,0:T(8,128)S(1)}, f32[2048,128]{1,0:T(8,128)S(1)}) custom-call(f32[72,512]{1,0:T(8,128)S(1)} %get-tuple-element.94.refs_0_.refs_1_, f32[16,128,128]{2,1,0:T(8,128)S(1)} %get-tuple-element.81.refs_13_.refs_18_.refs_1_, f32[16,128,128]{2,1,0:T(8,128)S(1)} %get-tuple-element.89.refs_4_.refs_2_.refs_3_, ...), custom_call_target="tpu_custom_call" | custom-call | flops 100000000 | bytes 3497984 | tf_op jit(solution)/shard_map/spread/pallas_call | solution.py:634
  67.8 2.6 %collective-permute-done.13.refs_1_ = f32[8,128]{1,0:T(8,128)S(1)} collective-permute-done((f32[8,128]{1,0:T(8,128)S(1)}, f32[8,128]{1,0:T(8,128)S(1)}, u32[]{:S(2)}, u32[]{:S(2)}) %collective-permute-start.13) | collective-permute-done | bytes 4128 | tf_op jit(solution)/shard_map/ppermute | solution.py:651
  70.5 10.0 %all_to_all.11 = f32[8,1,128]{2,1,0:T(1,128)S(1)} all-to-all(f32[8,1,128]{2,1,0:T(1,128)S(1)} %bitcast.15), channel_id=1, replica_groups=mesh['y'=4,'xl'=2,'xh'=2,'z'=8,'core'=2] {'z'}, dimensions={0} | all-to-all | bytes 8192 | tf_op jit(solution)/shard_map/all_to_all | solution.py:784
  80.5 1.8 %finish.1 = (f32[64,512]{1,0:T(8,128)}, f32[2048,128]{1,0:T(8,128)}) custom-call(f32[8,128]{1,0:T(8,128)S(1)} %bitcast.14, f32[72,512]{1,0:T(8,128)S(1)} %get-tuple-element.94.refs_0_.refs_1_, f32[2048,128]{1,0:T(8,128)S(1)} %get-tuple-element.95.refs_2_, f32[2048,128]{1,0:T(8,128)S(1)} %get-tuple-element.96.refs_3_, f32[2048,128]{1,0:T(8,128)S(1)} %get-tuple-element.97.refs_4_), custom_call_target="tpu_custom_call" | custom-call | bytes 3297280 | tf_op jit(solution)/shard_map/finish/pallas_call | solution.py:634
  (54 shorter events, 2.8 us)
Async XLA Ops:
  0.6 9.4 %copy-start = (f32[1,128,16,128]{3,2,1,0:T(8,128)S(1)}, f32[1,128,16,128]{3,2,1,0:T(8,128)}, u32[]{:S(2)}) copy-start(f32[1,128,16,128]{3,2,1,0:T(8,128)} %param.21) | copy-start | bytes 3145732
  0.6 9.4 %copy-start.1 = (f32[1,128,16,128]{3,2,1,0:T(8,128)S(1)}, f32[1,128,16,128]{3,2,1,0:T(8,128)}, u32[]{:S(2)}) copy-start(f32[1,128,16,128]{3,2,1,0:T(8,128)} %param.23) | copy-start | bytes 3145732
  0.7 9.4 %copy-start.2 = (bf16[2,128,48]{2,1,0:T(8,128)(2,1)S(1)}, bf16[2,128,48]{2,1,0:T(8,128)(2,1)}, u32[]{:S(2)}) copy-start(bf16[2,128,48]{2,1,0:T(8,128)(2,1)} %constant.27.clone.refs_12_.refs_11_.refs_7_) | copy-start | bytes 73732
  0.7 9.4 %copy-start.14 = (s32[1,64]{1,0:T(1,128)S(1)}, s32[1,64]{1,0:T(1,128)}, u32[]{:S(2)}) copy-start(s32[1,64]{1,0:T(1,128)} %param.26) | copy-start | bytes 772
  0.7 9.4 %copy-start.15 = (s32[64]{0:T(128)S(1)}, s32[64]{0:T(128)}, u32[]{:S(2)}) copy-start(s32[64]{0:T(128)} %refs_1_.2) | copy-start | bytes 772
  0.7 9.4 %copy-start.16 = (f32[5]{0:T(128)S(1)}, f32[5]{0:T(128)}, u32[]{:S(2)}) copy-start(f32[5]{0:T(128)} %refs_2_.10) | copy-start | bytes 64
  1.9 13.5 %collective-permute-start.1 = (f32[280,128]{1,0:T(8,128)S(1)}, f32[280,128]{1,0:T(8,128)S(1)}, u32[]{:S(2)}, u32[]{:S(2)}) collective-permute-start(f32[280,128]{1,0:T(8,128)S(1)} %get-tuple-element.52), channel_id=1, source_target_pairs={{1,2},{3,4},{5,6},{7,8},{9,10},{11,12},{13,14},{15,16},{17,18},{19... | collective-permute-start | bytes 430088 | tf_op jit(solution)/shard_map/ppermute | solution.py:657
  9.9 5.5 %collective-permute-start = (f32[264,128]{1,0:T(8,128)S(1)}, f32[264,128]{1,0:T(8,128)S(1)}, u32[]{:S(2)}, u32[]{:S(2)}) collective-permute-start(f32[264,128]{1,0:T(8,128)S(1)} %get-tuple-element.51), channel_id=1, source_target_pairs={{0,1},{1,0},{2,3},{3,2},{4,5},{5,4},{6,7},{7,6},{8,9},{9,8},{10,11... | collective-permute-start | bytes 405512 | tf_op jit(solution)/shard_map/ppermute | solution.py:651
  10.1 5.3 %copy-start.4 = (bf16[256,256]{1,0:T(8,128)(2,1)S(1)}, bf16[256,256]{1,0:T(8,128)(2,1)}, u32[]{:S(2)}) copy-start(bf16[256,256]{1,0:T(8,128)(2,1)} %constant.32.clone.refs_11_.refs_3_.refs_4_) | copy-start | bytes 393220
  10.1 5.3 %copy-start.9 = (bf16[2,136,16]{2,1,0:T(8,128)(2,1)S(1)}, bf16[2,136,16]{2,1,0:T(8,128)(2,1)}, u32[]{:S(2)}) copy-start(bf16[2,136,16]{2,1,0:T(8,128)(2,1)} %constant.36.clone.refs_4_) | copy-start | bytes 26116
  15.9 1.4 %copy-start.3 = (bf16[256,256]{1,0:T(8,128)(2,1)S(1)}, bf16[256,256]{1,0:T(8,128)(2,1)}, u32[]{:S(2)}) copy-start(bf16[256,256]{1,0:T(8,128)(2,1)} %constant.31.clone.refs_6_.refs_3_.refs_2_) | copy-start | bytes 393220
  15.9 1.4 %copy-start.10 = (bf16[2,16,256]{2,1,0:T(8,128)(2,1)S(1)}, bf16[2,16,256]{2,1,0:T(8,128)(2,1)}, u32[]{:S(2)}) copy-start(bf16[2,16,256]{2,1,0:T(8,128)(2,1)} %constant.28.clone.refs_2_) | copy-start | bytes 49156
  16.7 1.5 %collective-permute-start.2 = (f32[256,128]{1,0:T(8,128)S(1)}, f32[256,128]{1,0:T(8,128)S(1)}, u32[]{:S(2)}, u32[]{:S(2)}) collective-permute-start(f32[256,128]{1,0:T(8,128)S(1)} %get-tuple-element.63), channel_id=1, source_target_pairs={{0,1},{1,0},{2,3},{3,2},{4,5},{5,4},{6,7},{7,6},{8,9},{9,8},{10,11... | collective-permute-start | bytes 393224 | tf_op jit(solution)/shard_map/ppermute | solution.py:651
  17.3 1.0 %copy-start.13 = (bf16[2,16,48]{2,1,0:T(8,128)(2,1)S(1)}, bf16[2,16,48]{2,1,0:T(8,128)(2,1)}, u32[]{:S(2)}) copy-start(bf16[2,16,48]{2,1,0:T(8,128)(2,1)} %constant.29.clone.refs_9_) | copy-start | bytes 9220
  17.8 5.1 %copy-start.5 = (bf16[256,256]{1,0:T(8,128)(2,1)S(1)}, bf16[256,256]{1,0:T(8,128)(2,1)}, u32[]{:S(2)}) copy-start(bf16[256,256]{1,0:T(8,128)(2,1)} %constant.26.clone.refs_5_.refs_2_.refs_1_) | copy-start | bytes 393220
  18.5 11.3 %copy-start.12 = (bf16[2,16,48]{2,1,0:T(8,128)(2,1)S(1)}, bf16[2,16,48]{2,1,0:T(8,128)(2,1)}, u32[]{:S(2)}) copy-start(bf16[2,16,48]{2,1,0:T(8,128)(2,1)} %constant.30.clone.refs_14_) | copy-start | bytes 9220
  18.5 11.3 %collective-permute-start.3 = (f32[512,128]{1,0:T(8,128)S(1)}, f32[512,128]{1,0:T(8,128)S(1)}, u32[]{:S(2)}, u32[]{:S(2)}) collective-permute-start(f32[512,128]{1,0:T(8,128)S(1)} %early_1.1.refs_4_.refs_12_), channel_id=1, source_target_pairs={{1,2},{3,4},{5,6},{7,8},{9,10},{11,12},{13,14},{15,16},{17,18},{19... | collective-permute-start | bytes 786440 | tf_op jit(solution)/shard_map/ppermute | solution.py:657
  30.7 1.6 %collective-permute-start.4 = (f32[256,128]{1,0:T(8,128)S(1)}, f32[256,128]{1,0:T(8,128)S(1)}, u32[]{:S(2)}, u32[]{:S(2)}) collective-permute-start(f32[256,128]{1,0:T(8,128)S(1)} %get-tuple-element.69), channel_id=1, source_target_pairs={{0,1},{1,0},{2,3},{3,2},{4,5},{5,4},{6,7},{7,6},{8,9},{9,8},{10,11... | collective-permute-start | bytes 393224 | tf_op jit(solution)/shard_map/ppermute | solution.py:651
  33.2 1.6 %collective-permute-start.5 = (f32[256,128]{1,0:T(8,128)S(1)}, f32[256,128]{1,0:T(8,128)S(1)}, u32[]{:S(2)}, u32[]{:S(2)}) collective-permute-start(f32[256,128]{1,0:T(8,128)S(1)} %get-tuple-element.76), channel_id=1, source_target_pairs={{0,1},{1,0},{2,3},{3,2},{4,5},{5,4},{6,7},{7,6},{8,9},{9,8},{10,11... | collective-permute-start | bytes 393224 | tf_op jit(solution)/shard_map/ppermute | solution.py:651
  35.0 12.1 %collective-permute-start.6 = (f32[640,128]{1,0:T(8,128)S(1)}, f32[640,128]{1,0:T(8,128)S(1)}, u32[]{:S(2)}, u32[]{:S(2)}) collective-permute-start(f32[640,128]{1,0:T(8,128)S(1)} %early_3.1.refs_4_.refs_12_), channel_id=1, source_target_pairs={{1,2},{3,4},{5,6},{7,8},{9,10},{11,12},{13,14},{15,16},{17,18},{19... | collective-permute-start | bytes 983048 | tf_op jit(solution)/shard_map/ppermute | solution.py:657
  47.0 1.2 %copy-start.7 = (bf16[512,128]{1,0:T(8,128)(2,1)S(1)}, bf16[512,128]{1,0:T(8,128)(2,1)}, u32[]{:S(2)}) copy-start(bf16[512,128]{1,0:T(8,128)(2,1)} %constant.33.clone.refs_4_) | copy-start | bytes 393220
  47.0 1.2 %copy-start.8 = (bf16[2,72,256]{2,1,0:T(8,128)(2,1)S(1)}, bf16[2,72,256]{2,1,0:T(8,128)(2,1)}, u32[]{:S(2)}) copy-start(bf16[2,72,256]{2,1,0:T(8,128)(2,1)} %constant.38.clone.refs_2_) | copy-start | bytes 221188
  47.0 1.2 %copy-start.11 = (bf16[2,72,16]{2,1,0:T(8,128)(2,1)S(1)}, bf16[2,72,16]{2,1,0:T(8,128)(2,1)}, u32[]{:S(2)}) copy-start(bf16[2,72,16]{2,1,0:T(8,128)(2,1)} %constant.34.clone.refs_3_) | copy-start | bytes 13828
  48.9 8.2 %collective-permute-start.9 = (f32[72,512]{1,0:T(8,128)S(1)}, f32[72,512]{1,0:T(8,128)S(1)}, u32[]{:S(2)}, u32[]{:S(2)}) collective-permute-start(f32[72,512]{1,0:T(8,128)S(1)} %shrink.1.refs_0_), channel_id=1, source_target_pairs={{0,128},{64,192},{128,0},{192,64},{1,129},{65,193},{129,1},{193,65... | collective-permute-start | bytes 442376 | tf_op jit(solution)/shard_map/ppermute | solution.py:651
  52.2 6.5 %collective-permute-start.8 = (f32[72,512]{1,0:T(8,128)S(1)}, f32[72,512]{1,0:T(8,128)S(1)}, u32[]{:S(2)}, u32[]{:S(2)}) collective-permute-start(f32[72,512]{1,0:T(8,128)S(1)} %shrink.1.refs_0_), channel_id=1, source_target_pairs={{0,192},{64,128},{128,64},{192,0},{1,193},{65,129},{129,65},{193,1... | collective-permute-start | bytes 442376 | tf_op jit(solution)/shard_map/ppermute | solution.py:651
  53.2 5.4 %collective-permute-start.7 = (f32[72,512]{1,0:T(8,128)S(1)}, f32[72,512]{1,0:T(8,128)S(1)}, u32[]{:S(2)}, u32[]{:S(2)}) collective-permute-start(f32[72,512]{1,0:T(8,128)S(1)} %shrink.1.refs_0_), channel_id=1, source_target_pairs={{0,64},{64,0},{128,192},{192,128},{1,65},{65,1},{129,193},{193,129... | collective-permute-start | bytes 442376 | tf_op jit(solution)/shard_map/ppermute | solution.py:651
  53.2 1.3 %collective-permute-start.10 = (f32[128,128]{1,0:T(8,128)S(1)}, f32[128,128]{1,0:T(8,128)S(1)}, u32[]{:S(2)}, u32[]{:S(2)}) collective-permute-start(f32[128,128]{1,0:T(8,128)S(1)} %get-tuple-element.86), channel_id=1, source_target_pairs={{0,1},{1,0},{2,3},{3,2},{4,5},{5,4},{6,7},{7,6},{8,9},{9,8},{10,11... | collective-permute-start | bytes 196616 | tf_op jit(solution)/shard_map/ppermute | solution.py:651
  58.7 5.2 %collective-permute-start.11 = (f32[72,512]{1,0:T(8,128)S(1)}, f32[72,512]{1,0:T(8,128)S(1)}, u32[]{:S(2)}, u32[]{:S(2)}) collective-permute-start(f32[72,512]{1,0:T(8,128)S(1)} %add_four.1.refs_0_), channel_id=1, source_target_pairs={{0,32},{32,0},{1,33},{33,1},{2,34},{34,2},{3,35},{35,3},{4,36},{36... | collective-permute-start | bytes 442376 | tf_op jit(solution)/shard_map/ppermute | solution.py:651
  64.0 1.3 %collective-permute-start.12 = (f32[24,128]{1,0:T(8,128)S(1)}, f32[24,128]{1,0:T(8,128)S(1)}, u32[]{:S(2)}, u32[]{:S(2)}) collective-permute-start(f32[24,128]{1,0:T(8,128)S(1)} %get-tuple-element.92.refs_1_), channel_id=1, source_target_pairs={{0,1},{1,0},{2,3},{3,2},{4,5},{5,4},{6,7},{7,6},{8,9},{9,8},{10,11... | collective-permute-start | bytes 36872 | tf_op jit(solution)/shard_map/ppermute | solution.py:651
  65.2 0.9 %copy-start.6 = (bf16[2,128,144]{2,1,0:T(8,128)(2,1)S(1)}, bf16[2,128,144]{2,1,0:T(8,128)(2,1)}, u32[]{:S(2)}) copy-start(bf16[2,128,144]{2,1,0:T(8,128)(2,1)} %constant.37.clone.refs_5_) | copy-start | bytes 221188
  65.3 5.2 %collective-permute-start.13 = (f32[8,128]{1,0:T(8,128)S(1)}, f32[8,128]{1,0:T(8,128)S(1)}, u32[]{:S(2)}, u32[]{:S(2)}) collective-permute-start(f32[8,128]{1,0:T(8,128)S(1)} %get-tuple-element.93.refs_0_), channel_id=1, source_target_pairs={{0,16},{16,0},{1,17},{17,1},{2,18},{18,2},{3,19},{19,3},{4,20},{20... | collective-permute-start | bytes 12296 | tf_op jit(solution)/shard_map/ppermute | solution.py:651

commit v11 on v10

--- a/solution.py
+++ b/solution.py
@@ -598,20 +598,12 @@
     out[...] = jnp.broadcast_to(value, out.shape)
 
 
-def finish(count, parts, total, zeroth, first, second, direction, p_last, held, sems):
+def finish(count, parts, total, zeroth, first, second, direction, p_last):
     value = jnp.sum(jnp.sum(parts[...], axis=0, keepdims=True), axis=1, keepdims=True)
     inverse = 1.0 / jnp.sqrt(value * (1.0 / count) + EPSILON)
     rate = LEARN * inverse
-    size = CX * CY // sems.shape[0]
-    copies = []
-    for c in range(sems.shape[0]):
-        rows = slice(c * size, c * size + size)
-        held[rows] = zeroth[rows] + rate * (first[rows] + rate * second[rows])
-        copies.append(pltpu.make_async_copy(held.at[rows], p_last.at[rows], sems.at[c]))
-        copies[-1].start(priority=c % 2)
+    p_last[...] = zeroth[...] + rate * (first[...] + rate * second[...])
     direction[...] = total[:CXC] * inverse
-    for copy in copies:
-        copy.wait()
 
 
 VM = pl.BlockSpec(memory_space=pltpu.VMEM)
@@ -785,10 +777,8 @@
     count = float(lax.axis_size(TILE) * CXC * CYC * CZC)
     direction, p_last = call(
         functools.partial(finish, count),
-        (rows_of(CXC, CYC * CZC), pltpu.HBM((CX * CY, CZ), F32)),
+        (rows_of(CXC, CYC * CZC), rows_of(CX * CY)),
         parts, total, *terms, name="finish",
-        scratch=[pltpu.VMEM((CX * CY, CZ), F32), pltpu.SemaphoreType.DMA((4,))],
-        out_specs=(VM, pl.BlockSpec(memory_space=pltpu.HBM)),
     )
     return direction, p_last.reshape(1, CX, CY, CZ)
 

time: 83.1 us -> 82.5 us (level)
  transfers between devices with their start and end apart: 14 -> 14, of which waited for: 10 -> 10; matrix products, arithmetic and copies ran while one was open for 0% -> 0% of each run, Pallas kernels for 16% -> 17%
where the time goes in v11:
time: 82.5 us; the launch traced here: 81.9 us
  waiting for transfers between devices  25.4 us (31%)
  starting transfers between devices  23 us (28%)
  Pallas kernels  21.5 us (26%)
  blocking collectives  10 us (12%)
  between operations  1.05 us (1%)
  local copies, waits for them, and re-layouts  0.86 us (1%)
    pallas_call x23, Pallas kernels, call(): pl.pallas_call(run, out_shape=outs, in_specs=([SM] * smem + [VM] * (count...  21.5 us
    ppermute x3, starting transfers between devices, far_swap(): return lax.ppermute(x, TILE, pairs + [(b, a) for a, b in pairs])  17.1 us
    ppermute x11, waiting for transfers between devices, xor_swap(): return lax.ppermute(x, axis, [(i, i ^ mask) for i in range(count)])  14.1 us
    ppermute x3, waiting for transfers between devices, far_swap(): return lax.ppermute(x, TILE, pairs + [(b, a) for a, b in pairs])  11.3 us
    all_to_all x1, blocking collectives, on_device(): parts = lax.all_to_all(copies, 'z', split_axis=0, concat_axis=0, tiled=True)  10 us
    ppermute x11, starting transfers between devices, xor_swap(): return lax.ppermute(x, axis, [(i, i ^ mask) for i in range(count)])  5.91 us
  transfers between devices with their start and end apart: 14, of which 10 were waited for; matrix products, arithmetic and copies ran while one was open for 0% of the time, Pallas kernels for 17%

profile of v11, /device:TPU:6, one launch (start us, length us, event | category | flops | bytes accessed | tf_op | source)
XLA Modules:
  0.0 81.9 jit_solution(11786067362352989654)
XLA Ops:
  0.7 1.2 %first_edges.1 = (f32[280,128]{1,0:T(8,128)S(1)}, f32[264,128]{1,0:T(8,128)S(1)}) custom-call(f32[2048,128]{1,0:T(8,128)} %bitcast.10, f32[2048,128]{1,0:T(8,128)} %bitcast.12, f32[64,512]{1,0:T(8,128)} %refs_9_.3), custom_call_target="tpu_custom_call" | custom-call | bytes 2228224 | tf_op jit(solution)/shard_map/first_edges/pallas_call | solution.py:626
  1.9 8.0 %collective-permute-start.1 = (f32[280,128]{1,0:T(8,128)S(1)}, f32[280,128]{1,0:T(8,128)S(1)}, u32[]{:S(2)}, u32[]{:S(2)}) collective-permute-start(f32[280,128]{1,0:T(8,128)S(1)} %get-tuple-element.52), channel_id=1, source_target_pairs={{1,2},{3,4},{5,6},{7,8},{9,10},{11,12},{13,14},{15,16},{17,18},{19... | collective-permute-start | bytes 430088 | tf_op jit(solution)/shard_map/ppermute | solution.py:649
  10.1 5.3 %prepare.1 = (f32[16,128,128]{2,1,0:T(8,128)S(1)}, f32[16,128,128]{2,1,0:T(8,128)S(1)}, f32[16,128,128]{2,1,0:T(8,128)S(1)}, f32[16,128,128]{2,1,0:T(8,128)S(1)}...) custom-call(s32[64]{0:T(128)S(1)} %bitcast.16, ...), custom_call_target="tpu_custom_call" | custom-call | flops 1000000000 | bytes 4788756 | tf_op jit(solution)/shard_map/prepare/pallas_call | solution.py:626
  15.9 0.8 %advance_0.1 = (f32[16,128,128]{2,1,0:T(8,128)S(1)}, f32[16,128,128]{2,1,0:T(8,128)S(1)}, f32[256,128]{1,0:T(8,128)S(1)}, f32[16,128,128]{2,1,0:T(8,128)S(1)}) custom-call(f32[264,128]{1,0:T(8,128)S(1)} %collective-permute-done.refs_1_.refs_0_, f32[280,128]{1,0:T(8,128)S(1)} %collective-permute-done.1.refs_2_.refs_1_, ...), custom_call_target="tpu_custom_call" | custom-call | flops 100000000 | bytes 8712192 | tf_op jit(solution)/shard_map/advance_0/pallas_call | solution.py:626
  16.7 0.5 collective-permute-start.2
  17.3 0.5 edge_inside_0.1.refs_5_
  18.5 4.4 %collective-permute-start.3 = (f32[512,128]{1,0:T(8,128)S(1)}, f32[512,128]{1,0:T(8,128)S(1)}, u32[]{:S(2)}, u32[]{:S(2)}) collective-permute-start(f32[512,128]{1,0:T(8,128)S(1)} %early_1.1.refs_4_.refs_12_), channel_id=1, source_target_pairs={{1,2},{3,4},{5,6},{7,8},{9,10},{11,12},{13,14},{15,16},{17,18},{19... | collective-permute-start | bytes 786440 | tf_op jit(solution)/shard_map/ppermute | solution.py:649
  22.9 1.5 %inside_0.1 = (f32[16,128,128]{2,1,0:T(8,128)S(1)}, f32[16,128,128]{2,1,0:T(8,128)S(1)}) custom-call(f32[16,128,128]{2,1,0:T(8,128)S(1)} %get-tuple-element.64.refs_0_.refs_1_.refs_2_.refs_3_, f32[16,128,128]{2,1,0:T(8,128)S(1)} %get-tuple-element.65.refs_1_.refs_3_.refs_4_.refs_5_.refs_10_.refs_16_, bf16[256,256]{1,0:T(8,128)(2,1)S(1)} %copy-done.5, ...), custom_call_target="tpu_custom_call" | custom-call | flops 1000000000 | bytes 2359296 | tf_op jit(solution)/shard_map/inside_0/pallas_call | solution.py:626
  24.4 5.4 %collective-permute-done.3.refs_1_.refs_19_ = f32[512,128]{1,0:T(8,128)S(1)} collective-permute-done((f32[512,128]{1,0:T(8,128)S(1)}, f32[512,128]{1,0:T(8,128)S(1)}, u32[]{:S(2)}, u32[]{:S(2)}) %collective-permute-start.3) | collective-permute-done | bytes 262176 | tf_op jit(solution)/shard_map/ppermute | solution.py:649
  29.8 0.9 %advance_1.1 = (f32[16,128,128]{2,1,0:T(8,128)S(1)}, f32[16,128,128]{2,1,0:T(8,128)S(1)}, f32[256,128]{1,0:T(8,128)S(1)}, f32[256,128]{1,0:T(8,128)S(1)}, f32[16,128,128]{2,1,0:T(8,128)S(1)}) custom-call(f32[256,128]{1,0:T(8,128)S(1)} %collective-permute-done.2.refs_0_, f32[512,128]{1,0:T(8,128)S(1)} %collective-permute-done.3.refs_1_.refs_19_, ...), custom_call_target="tpu_custom_call" | custom-call | flops 100000000 | bytes 9157632 | tf_op jit(solution)/shard_map/advance_1/pallas_call | solution.py:626
  30.8 1.5 %inside_1.1 = (f32[16,128,128]{2,1,0:T(8,128)S(1)}, f32[16,128,128]{2,1,0:T(8,128)S(1)}) custom-call(f32[16,128,128]{2,1,0:T(8,128)S(1)} %get-tuple-element.71.refs_0_.refs_2_.refs_3_, f32[16,128,128]{2,1,0:T(8,128)S(1)} %get-tuple-element.72.refs_1_.refs_4_.refs_5_, bf16[256,256]{1,0:T(8,128)(2,1)S(1)} %copy-done.5, bf16[256,256]{1,0:T(8,128)(2,1)S(1)} %copy-done.3), custom_call_target="tpu_custom_call" | custom-call | flops 1000000000 | bytes 2359296 | tf_op jit(solution)/shard_map/inside_1/pallas_call | solution.py:626
  32.3 0.9 %advance_2.1 = (f32[16,128,128]{2,1,0:T(8,128)S(1)}, f32[16,128,128]{2,1,0:T(8,128)S(1)}, f32[256,128]{1,0:T(8,128)S(1)}, f32[16,128,128]{2,1,0:T(8,128)S(1)}) custom-call(f32[256,128]{1,0:T(8,128)S(1)} %collective-permute-done.4.refs_0_, f32[256,128]{1,0:T(8,128)S(1)} %get-tuple-element.70.refs_1_, ...), custom_call_target="tpu_custom_call" | custom-call | flops 100000000 | bytes 9744384 | tf_op jit(solution)/shard_map/advance_2/pallas_call | solution.py:626
  33.2 0.6 collective-permute-start.5
  33.8 0.5 edge_inside_2.1.refs_5_
  34.3 0.5 collective-permute-done.5.refs_0_
  35.0 4.6 %collective-permute-start.6 = (f32[640,128]{1,0:T(8,128)S(1)}, f32[640,128]{1,0:T(8,128)S(1)}, u32[]{:S(2)}, u32[]{:S(2)}) collective-permute-start(f32[640,128]{1,0:T(8,128)S(1)} %early_3.1.refs_4_.refs_12_), channel_id=1, source_target_pairs={{1,2},{3,4},{5,6},{7,8},{9,10},{11,12},{13,14},{15,16},{17,18},{19... | collective-permute-start | bytes 983048 | tf_op jit(solution)/shard_map/ppermute | solution.py:649
  39.6 1.5 %inside_2.1 = (f32[16,128,128]{2,1,0:T(8,128)S(1)}, f32[16,128,128]{2,1,0:T(8,128)S(1)}) custom-call(f32[16,128,128]{2,1,0:T(8,128)S(1)} %get-tuple-element.77.refs_0_.refs_1_.refs_2_.refs_3_, f32[16,128,128]{2,1,0:T(8,128)S(1)} %get-tuple-element.78.refs_1_.refs_3_.refs_4_, bf16[256,256]{1,0:T(8,128)(2,1)S(1)} %copy-done.5, bf16[256,256]{1,0:T(8,128)(2,1)S(1)} %copy-done.3, ...), custom_call_target="tpu_custom_call" | custom-call | flops 1000000000 | bytes 2359296 | tf_op jit(solution)/shard_map/inside_2/pallas_call | solution.py:626
  41.1 5.9 %collective-permute-done.6.refs_1_ = f32[640,128]{1,0:T(8,128)S(1)} collective-permute-done((f32[640,128]{1,0:T(8,128)S(1)}, f32[640,128]{1,0:T(8,128)S(1)}, u32[]{:S(2)}, u32[]{:S(2)}) %collective-permute-start.6) | collective-permute-done | bytes 327712 | tf_op jit(solution)/shard_map/ppermute | solution.py:649
  47.0 1.2 %advance_3.1 = (f32[16,128,128]{2,1,0:T(8,128)S(1)}, f32[128,128]{1,0:T(8,128)S(1)}, f32[128,128]{1,0:T(8,128)S(1)}, f32[16,128,128]{2,1,0:T(8,128)S(1)}, f32[128,128]{1,0:T(8,128)S(1)}) custom-call(f32[256,128]{1,0:T(8,128)S(1)} %collective-permute-done.5.refs_0_, f32[640,128]{1,0:T(8,128)S(1)} %collective-permute-done.6.refs_1_, ...), custom_call_target="tpu_custom_call" | custom-call | flops 100000000 | bytes 13745152 | tf_op jit(solution)/shard_map/advance_3/pallas_call | solution.py:626
  48.3 0.6 shrink.1.refs_0_
  48.9 3.2 %collective-permute-start.9 = (f32[72,512]{1,0:T(8,128)S(1)}, f32[72,512]{1,0:T(8,128)S(1)}, u32[]{:S(2)}, u32[]{:S(2)}) collective-permute-start(f32[72,512]{1,0:T(8,128)S(1)} %shrink.1.refs_0_), channel_id=1, source_target_pairs={{0,128},{64,192},{128,0},{192,64},{1,129},{65,193},{129,1},{193,65... | collective-permute-start | bytes 442376 | tf_op jit(solution)/shard_map/ppermute | solution.py:643
  52.2 1.1 %collective-permute-start.8 = (f32[72,512]{1,0:T(8,128)S(1)}, f32[72,512]{1,0:T(8,128)S(1)}, u32[]{:S(2)}, u32[]{:S(2)}) collective-permute-start(f32[72,512]{1,0:T(8,128)S(1)} %shrink.1.refs_0_), channel_id=1, source_target_pairs={{0,192},{64,128},{128,64},{192,0},{1,193},{65,129},{129,65},{193,1... | collective-permute-start | bytes 442376 | tf_op jit(solution)/shard_map/ppermute | solution.py:643
  53.2 0.8 inside_last.1.refs_4_
  54.8 2.2 %collective-permute-done.9.refs_3_ = f32[72,512]{1,0:T(8,128)S(1)} collective-permute-done((f32[72,512]{1,0:T(8,128)S(1)}, f32[72,512]{1,0:T(8,128)S(1)}, u32[]{:S(2)}, u32[]{:S(2)}) %collective-permute-start.9) | collective-permute-done | bytes 147488 | tf_op jit(solution)/shard_map/ppermute | solution.py:643
  57.1 1.6 %collective-permute-done.8.refs_2_ = f32[72,512]{1,0:T(8,128)S(1)} collective-permute-done((f32[72,512]{1,0:T(8,128)S(1)}, f32[72,512]{1,0:T(8,128)S(1)}, u32[]{:S(2)}, u32[]{:S(2)}) %collective-permute-start.8) | collective-permute-done | bytes 147488 | tf_op jit(solution)/shard_map/ppermute | solution.py:643
  58.8 5.1 %collective-permute-done.11.refs_1_ = f32[72,512]{1,0:T(8,128)S(1)} collective-permute-done((f32[72,512]{1,0:T(8,128)S(1)}, f32[72,512]{1,0:T(8,128)S(1)}, u32[]{:S(2)}, u32[]{:S(2)}) %collective-permute-start.11) | collective-permute-done | bytes 147488 | tf_op jit(solution)/shard_map/ppermute | solution.py:643
  64.1 1.2 %collective-permute-done.12.refs_2_ = f32[24,128]{1,0:T(8,128)S(1)} collective-permute-done((f32[24,128]{1,0:T(8,128)S(1)}, f32[24,128]{1,0:T(8,128)S(1)}, u32[]{:S(2)}, u32[]{:S(2)}) %collective-permute-start.12) | collective-permute-done | bytes 12320 | tf_op jit(solution)/shard_map/ppermute | solution.py:643
  65.4 0.8 copy-done.6
  66.1 1.7 %spread.1 = (f32[2048,128]{1,0:T(8,128)S(1)}, f32[2048,128]{1,0:T(8,128)S(1)}, f32[2048,128]{1,0:T(8,128)S(1)}) custom-call(f32[72,512]{1,0:T(8,128)S(1)} %get-tuple-element.94.refs_0_.refs_1_, f32[16,128,128]{2,1,0:T(8,128)S(1)} %get-tuple-element.81.refs_13_.refs_18_.refs_1_, f32[16,128,128]{2,1,0:T(8,128)S(1)} %get-tuple-element.89.refs_4_.refs_2_.refs_3_, ...), custom_call_target="tpu_custom_call" | custom-call | flops 100000000 | bytes 3497984 | tf_op jit(solution)/shard_map/spread/pallas_call | solution.py:626
  67.8 2.6 %collective-permute-done.13.refs_1_ = f32[8,128]{1,0:T(8,128)S(1)} collective-permute-done((f32[8,128]{1,0:T(8,128)S(1)}, f32[8,128]{1,0:T(8,128)S(1)}, u32[]{:S(2)}, u32[]{:S(2)}) %collective-permute-start.13) | collective-permute-done | bytes 4128 | tf_op jit(solution)/shard_map/ppermute | solution.py:643
  70.5 10.0 %all_to_all.11 = f32[8,1,128]{2,1,0:T(1,128)S(1)} all-to-all(f32[8,1,128]{2,1,0:T(1,128)S(1)} %bitcast.15), channel_id=1, replica_groups=mesh['y'=4,'xl'=2,'xh'=2,'z'=8,'core'=2] {'z'}, dimensions={0} | all-to-all | bytes 8192 | tf_op jit(solution)/shard_map/all_to_all | solution.py:776
  80.5 1.4 %finish.1 = (f32[64,512]{1,0:T(8,128)}, f32[2048,128]{1,0:T(8,128)}) custom-call(f32[8,128]{1,0:T(8,128)S(1)} %bitcast.14, f32[72,512]{1,0:T(8,128)S(1)} %get-tuple-element.94.refs_0_.refs_1_, f32[2048,128]{1,0:T(8,128)S(1)} %get-tuple-element.95.refs_2_, f32[2048,128]{1,0:T(8,128)S(1)} %get-tuple-element.96.refs_3_, f32[2048,128]{1,0:T(8,128)S(1)} %get-tuple-element.97.refs_4_), custom_call_target="tpu_custom_call" | custom-call | bytes 3297280 | tf_op jit(solution)/shard_map/finish/pallas_call | solution.py:626
  (54 shorter events, 2.8 us)
Async XLA Ops:
  0.6 9.4 %copy-start = (f32[1,128,16,128]{3,2,1,0:T(8,128)S(1)}, f32[1,128,16,128]{3,2,1,0:T(8,128)}, u32[]{:S(2)}) copy-start(f32[1,128,16,128]{3,2,1,0:T(8,128)} %param.21) | copy-start | bytes 3145732
  0.6 9.4 %copy-start.1 = (f32[1,128,16,128]{3,2,1,0:T(8,128)S(1)}, f32[1,128,16,128]{3,2,1,0:T(8,128)}, u32[]{:S(2)}) copy-start(f32[1,128,16,128]{3,2,1,0:T(8,128)} %param.23) | copy-start | bytes 3145732
  0.7 9.4 %copy-start.2 = (bf16[2,128,48]{2,1,0:T(8,128)(2,1)S(1)}, bf16[2,128,48]{2,1,0:T(8,128)(2,1)}, u32[]{:S(2)}) copy-start(bf16[2,128,48]{2,1,0:T(8,128)(2,1)} %constant.27.clone.refs_12_.refs_11_.refs_7_) | copy-start | bytes 73732
  0.7 9.4 %copy-start.14 = (s32[1,64]{1,0:T(1,128)S(1)}, s32[1,64]{1,0:T(1,128)}, u32[]{:S(2)}) copy-start(s32[1,64]{1,0:T(1,128)} %param.26) | copy-start | bytes 772
  0.7 9.4 %copy-start.15 = (s32[64]{0:T(128)S(1)}, s32[64]{0:T(128)}, u32[]{:S(2)}) copy-start(s32[64]{0:T(128)} %refs_1_.2) | copy-start | bytes 772
  0.7 9.4 %copy-start.16 = (f32[5]{0:T(128)S(1)}, f32[5]{0:T(128)}, u32[]{:S(2)}) copy-start(f32[5]{0:T(128)} %refs_2_.10) | copy-start | bytes 64
  1.9 13.5 %collective-permute-start.1 = (f32[280,128]{1,0:T(8,128)S(1)}, f32[280,128]{1,0:T(8,128)S(1)}, u32[]{:S(2)}, u32[]{:S(2)}) collective-permute-start(f32[280,128]{1,0:T(8,128)S(1)} %get-tuple-element.52), channel_id=1, source_target_pairs={{1,2},{3,4},{5,6},{7,8},{9,10},{11,12},{13,14},{15,16},{17,18},{19... | collective-permute-start | bytes 430088 | tf_op jit(solution)/shard_map/ppermute | solution.py:649
  9.9 5.5 %collective-permute-start = (f32[264,128]{1,0:T(8,128)S(1)}, f32[264,128]{1,0:T(8,128)S(1)}, u32[]{:S(2)}, u32[]{:S(2)}) collective-permute-start(f32[264,128]{1,0:T(8,128)S(1)} %get-tuple-element.51), channel_id=1, source_target_pairs={{0,1},{1,0},{2,3},{3,2},{4,5},{5,4},{6,7},{7,6},{8,9},{9,8},{10,11... | collective-permute-start | bytes 405512 | tf_op jit(solution)/shard_map/ppermute | solution.py:643
  10.1 5.3 %copy-start.4 = (bf16[256,256]{1,0:T(8,128)(2,1)S(1)}, bf16[256,256]{1,0:T(8,128)(2,1)}, u32[]{:S(2)}) copy-start(bf16[256,256]{1,0:T(8,128)(2,1)} %constant.32.clone.refs_11_.refs_3_.refs_4_) | copy-start | bytes 393220
  10.1 5.3 %copy-start.9 = (bf16[2,136,16]{2,1,0:T(8,128)(2,1)S(1)}, bf16[2,136,16]{2,1,0:T(8,128)(2,1)}, u32[]{:S(2)}) copy-start(bf16[2,136,16]{2,1,0:T(8,128)(2,1)} %constant.36.clone.refs_4_) | copy-start | bytes 26116
  15.9 1.4 %copy-start.3 = (bf16[256,256]{1,0:T(8,128)(2,1)S(1)}, bf16[256,256]{1,0:T(8,128)(2,1)}, u32[]{:S(2)}) copy-start(bf16[256,256]{1,0:T(8,128)(2,1)} %constant.31.clone.refs_6_.refs_3_.refs_2_) | copy-start | bytes 393220
  15.9 1.4 %copy-start.10 = (bf16[2,16,256]{2,1,0:T(8,128)(2,1)S(1)}, bf16[2,16,256]{2,1,0:T(8,128)(2,1)}, u32[]{:S(2)}) copy-start(bf16[2,16,256]{2,1,0:T(8,128)(2,1)} %constant.28.clone.refs_2_) | copy-start | bytes 49156
  16.7 1.5 %collective-permute-start.2 = (f32[256,128]{1,0:T(8,128)S(1)}, f32[256,128]{1,0:T(8,128)S(1)}, u32[]{:S(2)}, u32[]{:S(2)}) collective-permute-start(f32[256,128]{1,0:T(8,128)S(1)} %get-tuple-element.63), channel_id=1, source_target_pairs={{0,1},{1,0},{2,3},{3,2},{4,5},{5,4},{6,7},{7,6},{8,9},{9,8},{10,11... | collective-permute-start | bytes 393224 | tf_op jit(solution)/shard_map/ppermute | solution.py:643
  17.3 1.0 %copy-start.13 = (bf16[2,16,48]{2,1,0:T(8,128)(2,1)S(1)}, bf16[2,16,48]{2,1,0:T(8,128)(2,1)}, u32[]{:S(2)}) copy-start(bf16[2,16,48]{2,1,0:T(8,128)(2,1)} %constant.29.clone.refs_9_) | copy-start | bytes 9220
  17.8 5.1 %copy-start.5 = (bf16[256,256]{1,0:T(8,128)(2,1)S(1)}, bf16[256,256]{1,0:T(8,128)(2,1)}, u32[]{:S(2)}) copy-start(bf16[256,256]{1,0:T(8,128)(2,1)} %constant.26.clone.refs_5_.refs_2_.refs_1_) | copy-start | bytes 393220
  18.5 11.3 %copy-start.12 = (bf16[2,16,48]{2,1,0:T(8,128)(2,1)S(1)}, bf16[2,16,48]{2,1,0:T(8,128)(2,1)}, u32[]{:S(2)}) copy-start(bf16[2,16,48]{2,1,0:T(8,128)(2,1)} %constant.30.clone.refs_14_) | copy-start | bytes 9220
  18.5 11.3 %collective-permute-start.3 = (f32[512,128]{1,0:T(8,128)S(1)}, f32[512,128]{1,0:T(8,128)S(1)}, u32[]{:S(2)}, u32[]{:S(2)}) collective-permute-start(f32[512,128]{1,0:T(8,128)S(1)} %early_1.1.refs_4_.refs_12_), channel_id=1, source_target_pairs={{1,2},{3,4},{5,6},{7,8},{9,10},{11,12},{13,14},{15,16},{17,18},{19... | collective-permute-start | bytes 786440 | tf_op jit(solution)/shard_map/ppermute | solution.py:649
  30.7 1.6 %collective-permute-start.4 = (f32[256,128]{1,0:T(8,128)S(1)}, f32[256,128]{1,0:T(8,128)S(1)}, u32[]{:S(2)}, u32[]{:S(2)}) collective-permute-start(f32[256,128]{1,0:T(8,128)S(1)} %get-tuple-element.69), channel_id=1, source_target_pairs={{0,1},{1,0},{2,3},{3,2},{4,5},{5,4},{6,7},{7,6},{8,9},{9,8},{10,11... | collective-permute-start | bytes 393224 | tf_op jit(solution)/shard_map/ppermute | solution.py:643
  33.2 1.6 %collective-permute-start.5 = (f32[256,128]{1,0:T(8,128)S(1)}, f32[256,128]{1,0:T(8,128)S(1)}, u32[]{:S(2)}, u32[]{:S(2)}) collective-permute-start(f32[256,128]{1,0:T(8,128)S(1)} %get-tuple-element.76), channel_id=1, source_target_pairs={{0,1},{1,0},{2,3},{3,2},{4,5},{5,4},{6,7},{7,6},{8,9},{9,8},{10,11... | collective-permute-start | bytes 393224 | tf_op jit(solution)/shard_map/ppermute | solution.py:643
  35.0 12.1 %collective-permute-start.6 = (f32[640,128]{1,0:T(8,128)S(1)}, f32[640,128]{1,0:T(8,128)S(1)}, u32[]{:S(2)}, u32[]{:S(2)}) collective-permute-start(f32[640,128]{1,0:T(8,128)S(1)} %early_3.1.refs_4_.refs_12_), channel_id=1, source_target_pairs={{1,2},{3,4},{5,6},{7,8},{9,10},{11,12},{13,14},{15,16},{17,18},{19... | collective-permute-start | bytes 983048 | tf_op jit(solution)/shard_map/ppermute | solution.py:649
  47.0 1.2 %copy-start.7 = (bf16[512,128]{1,0:T(8,128)(2,1)S(1)}, bf16[512,128]{1,0:T(8,128)(2,1)}, u32[]{:S(2)}) copy-start(bf16[512,128]{1,0:T(8,128)(2,1)} %constant.33.clone.refs_4_) | copy-start | bytes 393220
  47.0 1.2 %copy-start.8 = (bf16[2,72,256]{2,1,0:T(8,128)(2,1)S(1)}, bf16[2,72,256]{2,1,0:T(8,128)(2,1)}, u32[]{:S(2)}) copy-start(bf16[2,72,256]{2,1,0:T(8,128)(2,1)} %constant.38.clone.refs_2_) | copy-start | bytes 221188
  47.0 1.2 %copy-start.11 = (bf16[2,72,16]{2,1,0:T(8,128)(2,1)S(1)}, bf16[2,72,16]{2,1,0:T(8,128)(2,1)}, u32[]{:S(2)}) copy-start(bf16[2,72,16]{2,1,0:T(8,128)(2,1)} %constant.34.clone.refs_3_) | copy-start | bytes 13828
  48.9 8.2 %collective-permute-start.9 = (f32[72,512]{1,0:T(8,128)S(1)}, f32[72,512]{1,0:T(8,128)S(1)}, u32[]{:S(2)}, u32[]{:S(2)}) collective-permute-start(f32[72,512]{1,0:T(8,128)S(1)} %shrink.1.refs_0_), channel_id=1, source_target_pairs={{0,128},{64,192},{128,0},{192,64},{1,129},{65,193},{129,1},{193,65... | collective-permute-start | bytes 442376 | tf_op jit(solution)/shard_map/ppermute | solution.py:643
  52.2 6.5 %collective-permute-start.8 = (f32[72,512]{1,0:T(8,128)S(1)}, f32[72,512]{1,0:T(8,128)S(1)}, u32[]{:S(2)}, u32[]{:S(2)}) collective-permute-start(f32[72,512]{1,0:T(8,128)S(1)} %shrink.1.refs_0_), channel_id=1, source_target_pairs={{0,192},{64,128},{128,64},{192,0},{1,193},{65,129},{129,65},{193,1... | collective-permute-start | bytes 442376 | tf_op jit(solution)/shard_map/ppermute | solution.py:643
  53.2 5.4 %collective-permute-start.7 = (f32[72,512]{1,0:T(8,128)S(1)}, f32[72,512]{1,0:T(8,128)S(1)}, u32[]{:S(2)}, u32[]{:S(2)}) collective-permute-start(f32[72,512]{1,0:T(8,128)S(1)} %shrink.1.refs_0_), channel_id=1, source_target_pairs={{0,64},{64,0},{128,192},{192,128},{1,65},{65,1},{129,193},{193,129... | collective-permute-start | bytes 442376 | tf_op jit(solution)/shard_map/ppermute | solution.py:643
  53.2 1.3 %collective-permute-start.10 = (f32[128,128]{1,0:T(8,128)S(1)}, f32[128,128]{1,0:T(8,128)S(1)}, u32[]{:S(2)}, u32[]{:S(2)}) collective-permute-start(f32[128,128]{1,0:T(8,128)S(1)} %get-tuple-element.86), channel_id=1, source_target_pairs={{0,1},{1,0},{2,3},{3,2},{4,5},{5,4},{6,7},{7,6},{8,9},{9,8},{10,11... | collective-permute-start | bytes 196616 | tf_op jit(solution)/shard_map/ppermute | solution.py:643
  58.7 5.2 %collective-permute-start.11 = (f32[72,512]{1,0:T(8,128)S(1)}, f32[72,512]{1,0:T(8,128)S(1)}, u32[]{:S(2)}, u32[]{:S(2)}) collective-permute-start(f32[72,512]{1,0:T(8,128)S(1)} %add_four.1.refs_0_), channel_id=1, source_target_pairs={{0,32},{32,0},{1,33},{33,1},{2,34},{34,2},{3,35},{35,3},{4,36},{36... | collective-permute-start | bytes 442376 | tf_op jit(solution)/shard_map/ppermute | solution.py:643
  64.0 1.3 %collective-permute-start.12 = (f32[24,128]{1,0:T(8,128)S(1)}, f32[24,128]{1,0:T(8,128)S(1)}, u32[]{:S(2)}, u32[]{:S(2)}) collective-permute-start(f32[24,128]{1,0:T(8,128)S(1)} %get-tuple-element.92.refs_1_), channel_id=1, source_target_pairs={{0,1},{1,0},{2,3},{3,2},{4,5},{5,4},{6,7},{7,6},{8,9},{9,8},{10,11... | collective-permute-start | bytes 36872 | tf_op jit(solution)/shard_map/ppermute | solution.py:643
  65.2 0.9 %copy-start.6 = (bf16[2,128,144]{2,1,0:T(8,128)(2,1)S(1)}, bf16[2,128,144]{2,1,0:T(8,128)(2,1)}, u32[]{:S(2)}) copy-start(bf16[2,128,144]{2,1,0:T(8,128)(2,1)} %constant.37.clone.refs_5_) | copy-start | bytes 221188
  65.3 5.2 %collective-permute-start.13 = (f32[8,128]{1,0:T(8,128)S(1)}, f32[8,128]{1,0:T(8,128)S(1)}, u32[]{:S(2)}, u32[]{:S(2)}) collective-permute-start(f32[8,128]{1,0:T(8,128)S(1)} %get-tuple-element.93.refs_0_), channel_id=1, source_target_pairs={{0,16},{16,0},{1,17},{17,1},{2,18},{18,2},{3,19},{19,3},{4,20},{20... | collective-permute-start | bytes 12296 | tf_op jit(solution)/shard_map/ppermute | solution.py:643

commit v12 on v11

--- a/solution.py
+++ b/solution.py
@@ -521,6 +521,13 @@
     own[...] = cat(pieces, 1)
 
 
+def advance_and_shrink(*refs):
+    fields, matrices = refs[:20], refs[20:23]
+    p_new, near, far, own, image, image_far = refs[23:]
+    advance(3, *fields, p_new, near, far, image, image_far)
+    shrink(image, image_far, *matrices, own)
+
+
 def fold(value):
     rows = value[0:8]
     for r in range(1, value.shape[0] // 8):
@@ -702,12 +709,15 @@
             outs = (FIELD, FIELD, edge, FIELD)
         else:
             args += [sent, beyond, const["cross_x"], laps[0], qs[1], gathered, sigma, older_far]
-            outs = (FIELD, half, half, FIELD, half)
-        result = call(body, outs, *args, flops=10**8, name=name)
-        if step == 3:
-            p_new, near, far, image, image_far = result
+            args += [const["shrink_x"], const["shrink_far"], const["shrink_z"]]
+            p_new, near, far, partial = call(
+                advance_and_shrink, (FIELD, half, half, rows_of(ROWS, CYC * CZC)), *args,
+                scratch=[pltpu.VMEM((CY, CX, CZ), F32), pltpu.VMEM((CY * OV, CZ), F32)],
+                flops=2 * 10**8, name="advance_3",
+            )
             p, p_before = p_new, p
             continue
+        result = call(body, outs, *args, flops=10**8, name=name)
         p_new, q_new, *edges, other = result
         if step < 2:
             laps.append(other)
@@ -740,11 +750,6 @@
             held=(sent,),
         )
 
-    partial = call(
-        shrink, rows_of(ROWS, CYC * CZC),
-        image, image_far, const["shrink_x"], const["shrink_far"], const["shrink_z"],
-        flops=10**8, name="shrink",
-    )
     two, three, one = (xor_swap(partial, "y", m) for m in (2, 3, 1))
     near = xor_swap(near, "core", 1)
     lap_p = call(inside_one, FIELD, p, own_x, own_z, flops=5 * 10**8, name="inside_last")

time: 82.5 us -> 83 us (level)
    pallas_call x23 -> x22, Pallas kernels: 21.5 us -> 21.9 us  [call(): pl.pallas_call(run, out_shape=outs, in_specs=([SM] * smem + [VM] * (count...]
  transfers between devices with their start and end apart: 14 -> 14, of which waited for: 10 -> 10; matrix products, arithmetic and copies ran while one was open for 0% -> 0% of each run, Pallas kernels for 17% -> 16%
where the time goes in v12:
time: 83 us; the launch traced here: 82.4 us
  waiting for transfers between devices  25.4 us (31%)
  starting transfers between devices  23.1 us (28%)
  Pallas kernels  21.9 us (26%)
  blocking collectives  10 us (12%)
  between operations  1.06 us (1%)
  local copies, waits for them, and re-layouts  0.87 us (1%)
    pallas_call x22, Pallas kernels, call(): pl.pallas_call(run, out_shape=outs, in_specs=([SM] * smem + [VM] * (count...  21.9 us
    ppermute x3, starting transfers between devices, far_swap(): return lax.ppermute(x, TILE, pairs + [(b, a) for a, b in pairs])  17.2 us
    ppermute x11, waiting for transfers between devices, xor_swap(): return lax.ppermute(x, axis, [(i, i ^ mask) for i in range(count)])  14.1 us
    ppermute x3, waiting for transfers between devices, far_swap(): return lax.ppermute(x, TILE, pairs + [(b, a) for a, b in pairs])  11.3 us
    all_to_all x1, blocking collectives, on_device(): parts = lax.all_to_all(copies, 'z', split_axis=0, concat_axis=0, tiled=True)  10 us
    ppermute x11, starting transfers between devices, xor_swap(): return lax.ppermute(x, axis, [(i, i ^ mask) for i in range(count)])  5.93 us
  transfers between devices with their start and end apart: 14, of which 10 were waited for; matrix products, arithmetic and copies ran while one was open for 0% of the time, Pallas kernels for 16%

profile of v12, /device:TPU:6, one launch (start us, length us, event | category | flops | bytes accessed | tf_op | source)
XLA Modules:
  0.0 82.4 jit_solution(9144963499039333073)
XLA Ops:
  0.7 1.2 %first_edges.1 = (f32[280,128]{1,0:T(8,128)S(1)}, f32[264,128]{1,0:T(8,128)S(1)}) custom-call(f32[2048,128]{1,0:T(8,128)} %bitcast.10, f32[2048,128]{1,0:T(8,128)} %bitcast.12, f32[64,512]{1,0:T(8,128)} %refs_9_.3), custom_call_target="tpu_custom_call" | custom-call | bytes 2228224 | tf_op jit(solution)/shard_map/first_edges/pallas_call | solution.py:633
  1.9 8.0 %collective-permute-start.1 = (f32[280,128]{1,0:T(8,128)S(1)}, f32[280,128]{1,0:T(8,128)S(1)}, u32[]{:S(2)}, u32[]{:S(2)}) collective-permute-start(f32[280,128]{1,0:T(8,128)S(1)} %get-tuple-element.51), channel_id=1, source_target_pairs={{1,2},{3,4},{5,6},{7,8},{9,10},{11,12},{13,14},{15,16},{17,18},{19... | collective-permute-start | bytes 430088 | tf_op jit(solution)/shard_map/ppermute | solution.py:656
  10.1 5.3 %prepare.1 = (f32[16,128,128]{2,1,0:T(8,128)S(1)}, f32[16,128,128]{2,1,0:T(8,128)S(1)}, f32[16,128,128]{2,1,0:T(8,128)S(1)}, f32[16,128,128]{2,1,0:T(8,128)S(1)}...) custom-call(s32[64]{0:T(128)S(1)} %bitcast.16, ...), custom_call_target="tpu_custom_call" | custom-call | flops 1000000000 | bytes 4788756 | tf_op jit(solution)/shard_map/prepare/pallas_call | solution.py:633
  15.9 0.9 %advance_0.1 = (f32[16,128,128]{2,1,0:T(8,128)S(1)}, f32[16,128,128]{2,1,0:T(8,128)S(1)}, f32[256,128]{1,0:T(8,128)S(1)}, f32[16,128,128]{2,1,0:T(8,128)S(1)}) custom-call(f32[264,128]{1,0:T(8,128)S(1)} %collective-permute-done.refs_1_.refs_0_, f32[280,128]{1,0:T(8,128)S(1)} %collective-permute-done.1.refs_2_.refs_1_, ...), custom_call_target="tpu_custom_call" | custom-call | flops 100000000 | bytes 8712192 | tf_op jit(solution)/shard_map/advance_0/pallas_call | solution.py:633
  16.8 0.6 collective-permute-start.2
  17.4 0.5 edge_inside_0.1.refs_5_
  17.9 0.5 collective-permute-done.2.refs_0_
  18.6 4.4 %collective-permute-start.3 = (f32[512,128]{1,0:T(8,128)S(1)}, f32[512,128]{1,0:T(8,128)S(1)}, u32[]{:S(2)}, u32[]{:S(2)}) collective-permute-start(f32[512,128]{1,0:T(8,128)S(1)} %early_1.1.refs_4_.refs_12_), channel_id=1, source_target_pairs={{1,2},{3,4},{5,6},{7,8},{9,10},{11,12},{13,14},{15,16},{17,18},{19... | collective-permute-start | bytes 786440 | tf_op jit(solution)/shard_map/ppermute | solution.py:656
  23.0 1.5 %inside_0.1 = (f32[16,128,128]{2,1,0:T(8,128)S(1)}, f32[16,128,128]{2,1,0:T(8,128)S(1)}) custom-call(f32[16,128,128]{2,1,0:T(8,128)S(1)} %get-tuple-element.63.refs_0_.refs_1_.refs_2_.refs_3_, f32[16,128,128]{2,1,0:T(8,128)S(1)} %get-tuple-element.64.refs_1_.refs_3_.refs_4_.refs_5_.refs_10_.refs_16_, bf16[256,256]{1,0:T(8,128)(2,1)S(1)} %copy-done.5, ...), custom_call_target="tpu_custom_call" | custom-call | flops 1000000000 | bytes 2359296 | tf_op jit(solution)/shard_map/inside_0/pallas_call | solution.py:633
  24.5 5.4 %collective-permute-done.3.refs_1_.refs_19_ = f32[512,128]{1,0:T(8,128)S(1)} collective-permute-done((f32[512,128]{1,0:T(8,128)S(1)}, f32[512,128]{1,0:T(8,128)S(1)}, u32[]{:S(2)}, u32[]{:S(2)}) %collective-permute-start.3) | collective-permute-done | bytes 262176 | tf_op jit(solution)/shard_map/ppermute | solution.py:656
  29.9 0.9 %advance_1.1 = (f32[16,128,128]{2,1,0:T(8,128)S(1)}, f32[16,128,128]{2,1,0:T(8,128)S(1)}, f32[256,128]{1,0:T(8,128)S(1)}, f32[256,128]{1,0:T(8,128)S(1)}, f32[16,128,128]{2,1,0:T(8,128)S(1)}) custom-call(f32[256,128]{1,0:T(8,128)S(1)} %collective-permute-done.2.refs_0_, f32[512,128]{1,0:T(8,128)S(1)} %collective-permute-done.3.refs_1_.refs_19_, ...), custom_call_target="tpu_custom_call" | custom-call | flops 100000000 | bytes 9157632 | tf_op jit(solution)/shard_map/advance_1/pallas_call | solution.py:633
  30.9 1.5 %inside_1.1 = (f32[16,128,128]{2,1,0:T(8,128)S(1)}, f32[16,128,128]{2,1,0:T(8,128)S(1)}) custom-call(f32[16,128,128]{2,1,0:T(8,128)S(1)} %get-tuple-element.70.refs_0_.refs_2_.refs_3_, f32[16,128,128]{2,1,0:T(8,128)S(1)} %get-tuple-element.71.refs_1_.refs_4_.refs_5_, bf16[256,256]{1,0:T(8,128)(2,1)S(1)} %copy-done.5, bf16[256,256]{1,0:T(8,128)(2,1)S(1)} %copy-done.3), custom_call_target="tpu_custom_call" | custom-call | flops 1000000000 | bytes 2359296 | tf_op jit(solution)/shard_map/inside_1/pallas_call | solution.py:633
  32.4 1.0 %advance_2.1 = (f32[16,128,128]{2,1,0:T(8,128)S(1)}, f32[16,128,128]{2,1,0:T(8,128)S(1)}, f32[256,128]{1,0:T(8,128)S(1)}, f32[16,128,128]{2,1,0:T(8,128)S(1)}) custom-call(f32[256,128]{1,0:T(8,128)S(1)} %collective-permute-done.4.refs_0_, f32[256,128]{1,0:T(8,128)S(1)} %get-tuple-element.69.refs_1_, ...), custom_call_target="tpu_custom_call" | custom-call | flops 100000000 | bytes 9744384 | tf_op jit(solution)/shard_map/advance_2/pallas_call | solution.py:633
  33.5 0.6 collective-permute-start.5
  34.0 0.5 edge_inside_2.1.refs_5_
  34.5 0.5 collective-permute-done.5.refs_0_
  35.3 4.7 %collective-permute-start.6 = (f32[640,128]{1,0:T(8,128)S(1)}, f32[640,128]{1,0:T(8,128)S(1)}, u32[]{:S(2)}, u32[]{:S(2)}) collective-permute-start(f32[640,128]{1,0:T(8,128)S(1)} %early_3.1.refs_4_.refs_12_), channel_id=1, source_target_pairs={{1,2},{3,4},{5,6},{7,8},{9,10},{11,12},{13,14},{15,16},{17,18},{19... | collective-permute-start | bytes 983048 | tf_op jit(solution)/shard_map/ppermute | solution.py:656
  40.0 1.5 %inside_2.1 = (f32[16,128,128]{2,1,0:T(8,128)S(1)}, f32[16,128,128]{2,1,0:T(8,128)S(1)}) custom-call(f32[16,128,128]{2,1,0:T(8,128)S(1)} %get-tuple-element.76.refs_0_.refs_1_.refs_2_.refs_3_, f32[16,128,128]{2,1,0:T(8,128)S(1)} %get-tuple-element.77.refs_1_.refs_3_.refs_4_, bf16[256,256]{1,0:T(8,128)(2,1)S(1)} %copy-done.5, bf16[256,256]{1,0:T(8,128)(2,1)S(1)} %copy-done.3, ...), custom_call_target="tpu_custom_call" | custom-call | flops 1000000000 | bytes 2359296 | tf_op jit(solution)/shard_map/inside_2/pallas_call | solution.py:633
  41.5 5.9 %collective-permute-done.6.refs_1_ = f32[640,128]{1,0:T(8,128)S(1)} collective-permute-done((f32[640,128]{1,0:T(8,128)S(1)}, f32[640,128]{1,0:T(8,128)S(1)}, u32[]{:S(2)}, u32[]{:S(2)}) %collective-permute-start.6) | collective-permute-done | bytes 327712 | tf_op jit(solution)/shard_map/ppermute | solution.py:656
  47.5 1.9 %advance_3.1 = (f32[16,128,128]{2,1,0:T(8,128)S(1)}, f32[128,128]{1,0:T(8,128)S(1)}, f32[128,128]{1,0:T(8,128)S(1)}, f32[72,512]{1,0:T(8,128)S(1)}) custom-call(f32[256,128]{1,0:T(8,128)S(1)} %collective-permute-done.5.refs_0_, f32[640,128]{1,0:T(8,128)S(1)} %collective-permute-done.6.refs_1_, ...), custom_call_target="tpu_custom_call" | custom-call | flops 200000000 | bytes 13954560 | tf_op jit(solution)/shard_map/advance_3/pallas_call | solution.py:633
  49.4 3.2 %collective-permute-start.9 = (f32[72,512]{1,0:T(8,128)S(1)}, f32[72,512]{1,0:T(8,128)S(1)}, u32[]{:S(2)}, u32[]{:S(2)}) collective-permute-start(f32[72,512]{1,0:T(8,128)S(1)} %get-tuple-element.83.refs_0_), channel_id=1, source_target_pairs={{0,128},{64,192},{128,0},{192,64},{1,129},{65,193},{129,1},{193,65... | collective-permute-start | bytes 442376 | tf_op jit(solution)/shard_map/ppermute | solution.py:650
  52.6 1.1 %collective-permute-start.8 = (f32[72,512]{1,0:T(8,128)S(1)}, f32[72,512]{1,0:T(8,128)S(1)}, u32[]{:S(2)}, u32[]{:S(2)}) collective-permute-start(f32[72,512]{1,0:T(8,128)S(1)} %get-tuple-element.83.refs_0_), channel_id=1, source_target_pairs={{0,192},{64,128},{128,64},{192,0},{1,193},{65,129},{129,65},{193,1... | collective-permute-start | bytes 442376 | tf_op jit(solution)/shard_map/ppermute | solution.py:650
  53.7 0.8 inside_last.1.refs_4_
  55.3 2.2 %collective-permute-done.9.refs_3_ = f32[72,512]{1,0:T(8,128)S(1)} collective-permute-done((f32[72,512]{1,0:T(8,128)S(1)}, f32[72,512]{1,0:T(8,128)S(1)}, u32[]{:S(2)}, u32[]{:S(2)}) %collective-permute-start.9) | collective-permute-done | bytes 147488 | tf_op jit(solution)/shard_map/ppermute | solution.py:650
  57.5 1.6 %collective-permute-done.8.refs_2_ = f32[72,512]{1,0:T(8,128)S(1)} collective-permute-done((f32[72,512]{1,0:T(8,128)S(1)}, f32[72,512]{1,0:T(8,128)S(1)}, u32[]{:S(2)}, u32[]{:S(2)}) %collective-permute-start.8) | collective-permute-done | bytes 147488 | tf_op jit(solution)/shard_map/ppermute | solution.py:650
  59.2 5.1 %collective-permute-done.11.refs_1_ = f32[72,512]{1,0:T(8,128)S(1)} collective-permute-done((f32[72,512]{1,0:T(8,128)S(1)}, f32[72,512]{1,0:T(8,128)S(1)}, u32[]{:S(2)}, u32[]{:S(2)}) %collective-permute-start.11) | collective-permute-done | bytes 147488 | tf_op jit(solution)/shard_map/ppermute | solution.py:650
  64.5 1.2 %collective-permute-done.12.refs_2_ = f32[24,128]{1,0:T(8,128)S(1)} collective-permute-done((f32[24,128]{1,0:T(8,128)S(1)}, f32[24,128]{1,0:T(8,128)S(1)}, u32[]{:S(2)}, u32[]{:S(2)}) %collective-permute-start.12) | collective-permute-done | bytes 12320 | tf_op jit(solution)/shard_map/ppermute | solution.py:650
  65.8 0.8 copy-done.7
  66.6 1.7 %spread.1 = (f32[2048,128]{1,0:T(8,128)S(1)}, f32[2048,128]{1,0:T(8,128)S(1)}, f32[2048,128]{1,0:T(8,128)S(1)}) custom-call(f32[72,512]{1,0:T(8,128)S(1)} %get-tuple-element.92.refs_0_.refs_1_, f32[16,128,128]{2,1,0:T(8,128)S(1)} %get-tuple-element.80.refs_13_.refs_18_.refs_1_, f32[16,128,128]{2,1,0:T(8,128)S(1)} %get-tuple-element.87.refs_4_.refs_2_.refs_3_, ...), custom_call_target="tpu_custom_call" | custom-call | flops 100000000 | bytes 3497984 | tf_op jit(solution)/shard_map/spread/pallas_call | solution.py:633
  68.3 2.6 %collective-permute-done.13.refs_1_ = f32[8,128]{1,0:T(8,128)S(1)} collective-permute-done((f32[8,128]{1,0:T(8,128)S(1)}, f32[8,128]{1,0:T(8,128)S(1)}, u32[]{:S(2)}, u32[]{:S(2)}) %collective-permute-start.13) | collective-permute-done | bytes 4128 | tf_op jit(solution)/shard_map/ppermute | solution.py:650
  70.9 10.0 %all_to_all.11 = f32[8,1,128]{2,1,0:T(1,128)S(1)} all-to-all(f32[8,1,128]{2,1,0:T(1,128)S(1)} %bitcast.15), channel_id=1, replica_groups=mesh['y'=4,'xl'=2,'xh'=2,'z'=8,'core'=2] {'z'}, dimensions={0} | all-to-all | bytes 8192 | tf_op jit(solution)/shard_map/all_to_all | solution.py:781
  81.0 1.4 %finish.1 = (f32[64,512]{1,0:T(8,128)}, f32[2048,128]{1,0:T(8,128)}) custom-call(f32[8,128]{1,0:T(8,128)S(1)} %bitcast.14, f32[72,512]{1,0:T(8,128)S(1)} %get-tuple-element.92.refs_0_.refs_1_, f32[2048,128]{1,0:T(8,128)S(1)} %get-tuple-element.93.refs_2_, f32[2048,128]{1,0:T(8,128)S(1)} %get-tuple-element.94.refs_3_, f32[2048,128]{1,0:T(8,128)S(1)} %get-tuple-element.95.refs_4_), custom_call_target="tpu_custom_call" | custom-call | bytes 3297280 | tf_op jit(solution)/shard_map/finish/pallas_call | solution.py:633
  (53 shorter events, 2.3 us)
Async XLA Ops:
  0.6 9.4 %copy-start = (f32[1,128,16,128]{3,2,1,0:T(8,128)S(1)}, f32[1,128,16,128]{3,2,1,0:T(8,128)}, u32[]{:S(2)}) copy-start(f32[1,128,16,128]{3,2,1,0:T(8,128)} %param.21) | copy-start | bytes 3145732
  0.6 9.4 %copy-start.1 = (f32[1,128,16,128]{3,2,1,0:T(8,128)S(1)}, f32[1,128,16,128]{3,2,1,0:T(8,128)}, u32[]{:S(2)}) copy-start(f32[1,128,16,128]{3,2,1,0:T(8,128)} %param.23) | copy-start | bytes 3145732
  0.7 9.4 %copy-start.2 = (bf16[2,128,48]{2,1,0:T(8,128)(2,1)S(1)}, bf16[2,128,48]{2,1,0:T(8,128)(2,1)}, u32[]{:S(2)}) copy-start(bf16[2,128,48]{2,1,0:T(8,128)(2,1)} %constant.27.clone.refs_12_.refs_11_.refs_7_) | copy-start | bytes 73732
  0.7 9.4 %copy-start.14 = (s32[1,64]{1,0:T(1,128)S(1)}, s32[1,64]{1,0:T(1,128)}, u32[]{:S(2)}) copy-start(s32[1,64]{1,0:T(1,128)} %param.26) | copy-start | bytes 772
  0.7 9.4 %copy-start.15 = (s32[64]{0:T(128)S(1)}, s32[64]{0:T(128)}, u32[]{:S(2)}) copy-start(s32[64]{0:T(128)} %refs_1_.2) | copy-start | bytes 772
  0.7 9.4 %copy-start.16 = (f32[5]{0:T(128)S(1)}, f32[5]{0:T(128)}, u32[]{:S(2)}) copy-start(f32[5]{0:T(128)} %refs_2_.9) | copy-start | bytes 64
  1.9 13.5 %collective-permute-start.1 = (f32[280,128]{1,0:T(8,128)S(1)}, f32[280,128]{1,0:T(8,128)S(1)}, u32[]{:S(2)}, u32[]{:S(2)}) collective-permute-start(f32[280,128]{1,0:T(8,128)S(1)} %get-tuple-element.51), channel_id=1, source_target_pairs={{1,2},{3,4},{5,6},{7,8},{9,10},{11,12},{13,14},{15,16},{17,18},{19... | collective-permute-start | bytes 430088 | tf_op jit(solution)/shard_map/ppermute | solution.py:656
  9.9 5.5 %collective-permute-start = (f32[264,128]{1,0:T(8,128)S(1)}, f32[264,128]{1,0:T(8,128)S(1)}, u32[]{:S(2)}, u32[]{:S(2)}) collective-permute-start(f32[264,128]{1,0:T(8,128)S(1)} %get-tuple-element.50), channel_id=1, source_target_pairs={{0,1},{1,0},{2,3},{3,2},{4,5},{5,4},{6,7},{7,6},{8,9},{9,8},{10,11... | collective-permute-start | bytes 405512 | tf_op jit(solution)/shard_map/ppermute | solution.py:650
  10.1 5.3 %copy-start.4 = (bf16[256,256]{1,0:T(8,128)(2,1)S(1)}, bf16[256,256]{1,0:T(8,128)(2,1)}, u32[]{:S(2)}) copy-start(bf16[256,256]{1,0:T(8,128)(2,1)} %constant.32.clone.refs_11_.refs_3_.refs_4_) | copy-start | bytes 393220
  10.1 5.3 %copy-start.9 = (bf16[2,136,16]{2,1,0:T(8,128)(2,1)S(1)}, bf16[2,136,16]{2,1,0:T(8,128)(2,1)}, u32[]{:S(2)}) copy-start(bf16[2,136,16]{2,1,0:T(8,128)(2,1)} %constant.36.clone.refs_4_) | copy-start | bytes 26116
  15.9 1.5 %copy-start.3 = (bf16[256,256]{1,0:T(8,128)(2,1)S(1)}, bf16[256,256]{1,0:T(8,128)(2,1)}, u32[]{:S(2)}) copy-start(bf16[256,256]{1,0:T(8,128)(2,1)} %constant.31.clone.refs_6_.refs_3_.refs_2_) | copy-start | bytes 393220
  15.9 1.5 %copy-start.10 = (bf16[2,16,256]{2,1,0:T(8,128)(2,1)S(1)}, bf16[2,16,256]{2,1,0:T(8,128)(2,1)}, u32[]{:S(2)}) copy-start(bf16[2,16,256]{2,1,0:T(8,128)(2,1)} %constant.28.clone.refs_2_) | copy-start | bytes 49156
  16.8 1.5 %collective-permute-start.2 = (f32[256,128]{1,0:T(8,128)S(1)}, f32[256,128]{1,0:T(8,128)S(1)}, u32[]{:S(2)}, u32[]{:S(2)}) collective-permute-start(f32[256,128]{1,0:T(8,128)S(1)} %get-tuple-element.62), channel_id=1, source_target_pairs={{0,1},{1,0},{2,3},{3,2},{4,5},{5,4},{6,7},{7,6},{8,9},{9,8},{10,11... | collective-permute-start | bytes 393224 | tf_op jit(solution)/shard_map/ppermute | solution.py:650
  17.4 1.0 %copy-start.13 = (bf16[2,16,48]{2,1,0:T(8,128)(2,1)S(1)}, bf16[2,16,48]{2,1,0:T(8,128)(2,1)}, u32[]{:S(2)}) copy-start(bf16[2,16,48]{2,1,0:T(8,128)(2,1)} %constant.29.clone.refs_9_) | copy-start | bytes 9220
  17.9 5.1 %copy-start.5 = (bf16[256,256]{1,0:T(8,128)(2,1)S(1)}, bf16[256,256]{1,0:T(8,128)(2,1)}, u32[]{:S(2)}) copy-start(bf16[256,256]{1,0:T(8,128)(2,1)} %constant.26.clone.refs_5_.refs_2_.refs_1_) | copy-start | bytes 393220
  18.6 11.3 %copy-start.12 = (bf16[2,16,48]{2,1,0:T(8,128)(2,1)S(1)}, bf16[2,16,48]{2,1,0:T(8,128)(2,1)}, u32[]{:S(2)}) copy-start(bf16[2,16,48]{2,1,0:T(8,128)(2,1)} %constant.30.clone.refs_14_) | copy-start | bytes 9220
  18.6 11.3 %collective-permute-start.3 = (f32[512,128]{1,0:T(8,128)S(1)}, f32[512,128]{1,0:T(8,128)S(1)}, u32[]{:S(2)}, u32[]{:S(2)}) collective-permute-start(f32[512,128]{1,0:T(8,128)S(1)} %early_1.1.refs_4_.refs_12_), channel_id=1, source_target_pairs={{1,2},{3,4},{5,6},{7,8},{9,10},{11,12},{13,14},{15,16},{17,18},{19... | collective-permute-start | bytes 786440 | tf_op jit(solution)/shard_map/ppermute | solution.py:656
  30.8 1.6 %collective-permute-start.4 = (f32[256,128]{1,0:T(8,128)S(1)}, f32[256,128]{1,0:T(8,128)S(1)}, u32[]{:S(2)}, u32[]{:S(2)}) collective-permute-start(f32[256,128]{1,0:T(8,128)S(1)} %get-tuple-element.68), channel_id=1, source_target_pairs={{0,1},{1,0},{2,3},{3,2},{4,5},{5,4},{6,7},{7,6},{8,9},{9,8},{10,11... | collective-permute-start | bytes 393224 | tf_op jit(solution)/shard_map/ppermute | solution.py:650
  33.5 1.6 %collective-permute-start.5 = (f32[256,128]{1,0:T(8,128)S(1)}, f32[256,128]{1,0:T(8,128)S(1)}, u32[]{:S(2)}, u32[]{:S(2)}) collective-permute-start(f32[256,128]{1,0:T(8,128)S(1)} %get-tuple-element.75), channel_id=1, source_target_pairs={{0,1},{1,0},{2,3},{3,2},{4,5},{5,4},{6,7},{7,6},{8,9},{9,8},{10,11... | collective-permute-start | bytes 393224 | tf_op jit(solution)/shard_map/ppermute | solution.py:650
  35.2 12.2 %copy-start.6 = (bf16[512,128]{1,0:T(8,128)(2,1)S(1)}, bf16[512,128]{1,0:T(8,128)(2,1)}, u32[]{:S(2)}) copy-start(bf16[512,128]{1,0:T(8,128)(2,1)} %constant.33.clone.refs_22_) | copy-start | bytes 393220
  35.2 12.2 %copy-start.8 = (bf16[2,72,256]{2,1,0:T(8,128)(2,1)S(1)}, bf16[2,72,256]{2,1,0:T(8,128)(2,1)}, u32[]{:S(2)}) copy-start(bf16[2,72,256]{2,1,0:T(8,128)(2,1)} %constant.38.clone.refs_20_) | copy-start | bytes 221188
  35.2 12.2 %copy-start.11 = (bf16[2,72,16]{2,1,0:T(8,128)(2,1)S(1)}, bf16[2,72,16]{2,1,0:T(8,128)(2,1)}, u32[]{:S(2)}) copy-start(bf16[2,72,16]{2,1,0:T(8,128)(2,1)} %constant.34.clone.refs_21_) | copy-start | bytes 13828
  35.3 12.2 %collective-permute-start.6 = (f32[640,128]{1,0:T(8,128)S(1)}, f32[640,128]{1,0:T(8,128)S(1)}, u32[]{:S(2)}, u32[]{:S(2)}) collective-permute-start(f32[640,128]{1,0:T(8,128)S(1)} %early_3.1.refs_4_.refs_12_), channel_id=1, source_target_pairs={{1,2},{3,4},{5,6},{7,8},{9,10},{11,12},{13,14},{15,16},{17,18},{19... | collective-permute-start | bytes 983048 | tf_op jit(solution)/shard_map/ppermute | solution.py:656
  49.4 8.2 %collective-permute-start.9 = (f32[72,512]{1,0:T(8,128)S(1)}, f32[72,512]{1,0:T(8,128)S(1)}, u32[]{:S(2)}, u32[]{:S(2)}) collective-permute-start(f32[72,512]{1,0:T(8,128)S(1)} %get-tuple-element.83.refs_0_), channel_id=1, source_target_pairs={{0,128},{64,192},{128,0},{192,64},{1,129},{65,193},{129,1},{193,65... | collective-permute-start | bytes 442376 | tf_op jit(solution)/shard_map/ppermute | solution.py:650
  52.6 6.5 %collective-permute-start.8 = (f32[72,512]{1,0:T(8,128)S(1)}, f32[72,512]{1,0:T(8,128)S(1)}, u32[]{:S(2)}, u32[]{:S(2)}) collective-permute-start(f32[72,512]{1,0:T(8,128)S(1)} %get-tuple-element.83.refs_0_), channel_id=1, source_target_pairs={{0,192},{64,128},{128,64},{192,0},{1,193},{65,129},{129,65},{193,1... | collective-permute-start | bytes 442376 | tf_op jit(solution)/shard_map/ppermute | solution.py:650
  53.7 5.4 %collective-permute-start.7 = (f32[72,512]{1,0:T(8,128)S(1)}, f32[72,512]{1,0:T(8,128)S(1)}, u32[]{:S(2)}, u32[]{:S(2)}) collective-permute-start(f32[72,512]{1,0:T(8,128)S(1)} %get-tuple-element.83.refs_0_), channel_id=1, source_target_pairs={{0,64},{64,0},{128,192},{192,128},{1,65},{65,1},{129,193},{193,129... | collective-permute-start | bytes 442376 | tf_op jit(solution)/shard_map/ppermute | solution.py:650
  53.7 1.3 %collective-permute-start.10 = (f32[128,128]{1,0:T(8,128)S(1)}, f32[128,128]{1,0:T(8,128)S(1)}, u32[]{:S(2)}, u32[]{:S(2)}) collective-permute-start(f32[128,128]{1,0:T(8,128)S(1)} %get-tuple-element.84), channel_id=1, source_target_pairs={{0,1},{1,0},{2,3},{3,2},{4,5},{5,4},{6,7},{7,6},{8,9},{9,8},{10,11... | collective-permute-start | bytes 196616 | tf_op jit(solution)/shard_map/ppermute | solution.py:650
  59.1 5.2 %collective-permute-start.11 = (f32[72,512]{1,0:T(8,128)S(1)}, f32[72,512]{1,0:T(8,128)S(1)}, u32[]{:S(2)}, u32[]{:S(2)}) collective-permute-start(f32[72,512]{1,0:T(8,128)S(1)} %add_four.1.refs_0_), channel_id=1, source_target_pairs={{0,32},{32,0},{1,33},{33,1},{2,34},{34,2},{3,35},{35,3},{4,36},{36... | collective-permute-start | bytes 442376 | tf_op jit(solution)/shard_map/ppermute | solution.py:650
  64.4 1.3 %collective-permute-start.12 = (f32[24,128]{1,0:T(8,128)S(1)}, f32[24,128]{1,0:T(8,128)S(1)}, u32[]{:S(2)}, u32[]{:S(2)}) collective-permute-start(f32[24,128]{1,0:T(8,128)S(1)} %get-tuple-element.90.refs_1_), channel_id=1, source_target_pairs={{0,1},{1,0},{2,3},{3,2},{4,5},{5,4},{6,7},{7,6},{8,9},{9,8},{10,11... | collective-permute-start | bytes 36872 | tf_op jit(solution)/shard_map/ppermute | solution.py:650
  65.7 0.9 %copy-start.7 = (bf16[2,128,144]{2,1,0:T(8,128)(2,1)S(1)}, bf16[2,128,144]{2,1,0:T(8,128)(2,1)}, u32[]{:S(2)}) copy-start(bf16[2,128,144]{2,1,0:T(8,128)(2,1)} %constant.37.clone.refs_5_) | copy-start | bytes 221188
  65.7 5.2 %collective-permute-start.13 = (f32[8,128]{1,0:T(8,128)S(1)}, f32[8,128]{1,0:T(8,128)S(1)}, u32[]{:S(2)}, u32[]{:S(2)}) collective-permute-start(f32[8,128]{1,0:T(8,128)S(1)} %get-tuple-element.91.refs_0_), channel_id=1, source_target_pairs={{0,16},{16,0},{1,17},{17,1},{2,18},{18,2},{3,19},{19,3},{4,20},{20... | collective-permute-start | bytes 12296 | tf_op jit(solution)/shard_map/ppermute | solution.py:650
